TPU v7x, 32 devices: a whole 2x2x4 slice. The times are simulated.
32 devices in a mesh: dp: 16 (over z, y, x), mp: 2 (over core).
Axes of the slice: x: 2, y: 2, z: 4, core: 2. Of those that a mesh axis runs over, the one named last changes fastest.
Arguments:
- tokens: bfloat16 [16384, 768], P(('dp', 'mp')), may hold values from -8 to 8
- segment_ids: int32 [16, 1024], P('dp'), may hold values from 0 to 16, never falling along the last dimension, each value on 1 to 512 neighbouring positions
- query_weight: bfloat16 [768, 768], P(None, 'mp'), may hold values from -0.21875 to 0.21875
- key_weight: bfloat16 [768, 768], P(None, 'mp'), may hold values from -0.21875 to 0.21875
- value_weight: bfloat16 [768, 768], P(None, 'mp'), may hold values from -0.21875 to 0.21875
- output_weight: bfloat16 [768, 768], P('mp'), may hold values from -0.875 to 0.875
- inner_weight: bfloat16 [768, 3072], P(None, 'mp'), may hold values from -0.21875 to 0.21875
- outer_weight: bfloat16 [3072, 768], P('mp'), may hold values from -0.109375 to 0.109375
- mixer_down: bfloat16 [768, 64], replicated, may hold values from -0.21875 to 0.21875
- mixer_down_bias: bfloat16 [64], replicated, may hold values from -3 to 3
- mixer_up: bfloat16 [64, 768], replicated, may hold values from -0.75 to 0.75
- mixer_up_bias: bfloat16 [768], replicated, may hold values from -3 to 3
- dense_down: bfloat16 [768, 64], replicated, may hold values from -0.21875 to 0.21875
- dense_down_bias: bfloat16 [64], replicated, may hold values from -3 to 3
- dense_up: bfloat16 [64, 768], replicated, may hold values from -0.75 to 0.75
- dense_up_bias: bfloat16 [768], replicated, may hold values from -3 to 3
- first_gain: bfloat16 [768], replicated, may hold values from 0.5 to 1.5
- first_shift: bfloat16 [768], replicated, may hold values from -3 to 3
- second_gain: bfloat16 [768], replicated, may hold values from 0.5 to 1.5
- second_shift: bfloat16 [768], replicated, may hold values from -3 to 3
- output_grad: bfloat16 [16384, 768], P(('dp', 'mp')), may hold values from -6 to 6
Outputs:
- activations: bfloat16 [16384, 768], P(('dp', 'mp'))
- input_grad: bfloat16 [16384, 768], P(('dp', 'mp'))
- mixer_down_grad: float32 [768, 64], replicated
- mixer_down_bias_grad: float32 [64], replicated
- mixer_up_grad: float32 [64, 768], replicated
- mixer_up_bias_grad: float32 [768], replicated
- dense_down_grad: float32 [768, 64], replicated
- dense_down_bias_grad: float32 [64], replicated
- dense_up_grad: float32 [64, 768], replicated
- dense_up_bias_grad: float32 [768], replicated
- first_gain_grad: float32 [768], replicated
- first_shift_grad: float32 [768], replicated
- second_gain_grad: float32 [768], replicated
- second_shift_grad: float32 [768], replicated
- norm_ratios: float32 [2], replicated
Inputs may be any that keep to these rules, and one draw needn't show every extreme that they name: `segment_ids`: each row numbers the items of one packed batch from 0, never falling.
All inputs are finite; a program needn't handle non-finite values.
Results may differ from a plain program's by a relative error of at most 0.019.
Values may be sent and summed in bfloat16 or wider, within the bound.
No kernel may reach another device: no remote copies, remote signals or barrier semaphores. Data moves between devices by JAX's collectives and lax.ppermute only.
A program may use at most 128 MiB of HBM per device.

v0:
```python
import jax
import jax.numpy as jnp
from jax import lax
from jax.sharding import PartitionSpec as P

HEAD_DIM = 64


EPS = 1e-12
block_limit = 512


def gelu_value(values):
    return jax.nn.gelu(values, approximate=False)


def gelu_slope(values):
    return (
        0.5 * (1.0 + jax.scipy.special.erf(values * 0.7071067811865476))
        + values * jnp.exp(-0.5 * values * values) * 0.3989422804014327
    )


def times_transpose(left, right):
    return lax.dot_general(
        left, right, (((1,), (1,)), ((), ())), preferred_element_type=jnp.float32
    )


def contract_rows(left, right):
    return lax.dot_general(
        left, right, (((0,), (0,)), ((), ())), preferred_element_type=jnp.float32
    )


def norm_forward(residual, gain, shift):
    mean = jnp.mean(residual, -1, keepdims=True)
    centred = residual - mean
    reciprocal = lax.rsqrt(jnp.mean(centred * centred, -1, keepdims=True) + EPS)
    normed = centred * reciprocal
    return (normed * gain + shift, normed, reciprocal)


def norm_backward(upstream, normed, reciprocal, gain):
    scaled = upstream * gain
    inflow = reciprocal * (
        scaled
        - jnp.mean(scaled, -1, keepdims=True)
        - normed * jnp.mean(scaled * normed, -1, keepdims=True)
    )
    return (inflow, jnp.sum(upstream * normed, 0), jnp.sum(upstream, 0))


def adapter_forward(inflow, down, down_bias, up, up_bias):
    inflow_low = inflow.astype(jnp.bfloat16)
    inner = jnp.dot(inflow_low, down, preferred_element_type=jnp.float32) + down_bias.astype(
        jnp.float32
    )
    active = gelu_value(inner).astype(jnp.bfloat16)
    outflow = jnp.dot(active, up, preferred_element_type=jnp.float32) + up_bias.astype(jnp.float32)
    return (outflow, (inflow_low, inner, active))


def adapter_backward(grad_out, kept, down, up):
    inflow_low, inner, active = kept
    grad_top = grad_out.astype(jnp.bfloat16)
    up_grad = contract_rows(active, grad_top)
    up_bias_grad = jnp.sum(grad_top.astype(jnp.float32), 0)
    grad_mid = (times_transpose(grad_top, up) * gelu_slope(inner)).astype(jnp.bfloat16)
    down_grad = contract_rows(inflow_low, grad_mid)
    down_bias_grad = jnp.sum(grad_mid.astype(jnp.float32), 0)
    inflow_grad = times_transpose(grad_mid, down)
    return (inflow_grad, (down_grad, down_bias_grad, up_grad, up_bias_grad))


def score_block(query_rows, query_seg, keys, key_seg, scale):
    scores = (
        jnp.einsum("qhd,khd->hqk", query_rows, keys, preferred_element_type=jnp.float32) * scale
    )
    same = query_seg[:, None] == key_seg[None, :]
    return jnp.where(same[None], scores, -1e30)


def attention_forward(queries, keys, values, seg_row, block, scale):
    count = queries.shape[0] // block

    def one_block(index):
        start = index * block
        rows = lax.dynamic_slice_in_dim(queries, start, block, 0)
        row_seg = lax.dynamic_slice_in_dim(seg_row, start, block, 0)
        scores = score_block(rows, row_seg, keys, seg_row, scale)
        peak = jnp.max(scores, -1, keepdims=True)
        exponent = jnp.exp(scores - peak)
        total = jnp.sum(exponent, -1, keepdims=True)
        shares = (exponent / total).astype(jnp.bfloat16)
        mixed = jnp.einsum("hqk,khd->qhd", shares, values, preferred_element_type=jnp.float32)
        return (mixed.astype(jnp.bfloat16), (peak + jnp.log(total))[..., 0])

    mixed, log_totals = lax.map(one_block, jnp.arange(count))
    return (mixed.reshape(queries.shape), log_totals)


def attention_backward(queries, keys, values, seg_row, log_totals, mixed_grad, block, scale):
    count = queries.shape[0] // block

    def one_block(carry, index):
        key_grad, value_grad = carry
        start = index * block
        rows = lax.dynamic_slice_in_dim(queries, start, block, 0)
        row_seg = lax.dynamic_slice_in_dim(seg_row, start, block, 0)
        grad_rows = lax.dynamic_slice_in_dim(mixed_grad, start, block, 0)
        scores = score_block(rows, row_seg, keys, seg_row, scale)
        shares = jnp.exp(scores - log_totals[index][..., None])
        value_grad = value_grad + jnp.einsum(
            "hqk,qhd->khd",
            shares.astype(jnp.bfloat16),
            grad_rows,
            preferred_element_type=jnp.float32,
        )
        share_grad = jnp.einsum(
            "qhd,khd->hqk", grad_rows, values, preferred_element_type=jnp.float32
        )
        score_grad = (
            shares * (share_grad - jnp.sum(shares * share_grad, -1, keepdims=True))
        ).astype(jnp.bfloat16)
        query_grad = (
            jnp.einsum("hqk,khd->qhd", score_grad, keys, preferred_element_type=jnp.float32) * scale
        ).astype(jnp.bfloat16)
        key_grad = (
            key_grad
            + jnp.einsum("hqk,qhd->khd", score_grad, rows, preferred_element_type=jnp.float32)
            * scale
        )
        return ((key_grad, value_grad), query_grad)

    zeros = jnp.zeros(keys.shape, jnp.float32)
    (key_grad, value_grad), query_grad = lax.scan(one_block, (zeros, zeros), jnp.arange(count))
    return (
        query_grad.reshape(queries.shape),
        key_grad.astype(jnp.bfloat16),
        value_grad.astype(jnp.bfloat16),
    )


def per_device(
    tokens,
    segment_ids,
    query_weight,
    key_weight,
    value_weight,
    output_weight,
    inner_weight,
    outer_weight,
    mixer_down,
    mixer_down_bias,
    mixer_up,
    mixer_up_bias,
    dense_down,
    dense_down_bias,
    dense_up,
    dense_up_bias,
    first_gain,
    first_shift,
    second_gain,
    second_shift,
    output_grad,
):
    shard_rows = tokens.shape[0]
    group_rows = shard_rows * lax.axis_size("mp")
    seg_row = segment_ids[0]
    block = min(block_limit, group_rows)
    scale = HEAD_DIM ** (-0.5)
    width = query_weight.shape[1]
    local_heads = width // HEAD_DIM
    head_shape = (group_rows, local_heads, HEAD_DIM)
    gain_one = first_gain.astype(jnp.float32)
    gain_two = second_gain.astype(jnp.float32)
    piece = lax.all_gather(tokens, "mp", axis=0, tiled=True)
    projected = jnp.concatenate(
        [
            jnp.dot(piece, query_weight, preferred_element_type=jnp.float32).astype(jnp.bfloat16),
            jnp.dot(piece, key_weight, preferred_element_type=jnp.float32).astype(jnp.bfloat16),
            jnp.dot(piece, value_weight, preferred_element_type=jnp.float32).astype(jnp.bfloat16),
        ],
        1,
    )
    queries = projected[:, :width].reshape(head_shape)
    keys = projected[:, width : 2 * width].reshape(head_shape)
    values = projected[:, 2 * width :].reshape(head_shape)
    mixed, log_totals = attention_forward(queries, keys, values, seg_row, block, scale)
    mixed_flat = mixed.reshape(group_rows, width)
    attended = lax.psum_scatter(
        jnp.dot(mixed_flat, output_weight, preferred_element_type=jnp.float32),
        "mp",
        scatter_dimension=0,
        tiled=True,
    )
    token_values = tokens.astype(jnp.float32)
    mixer_out, mixer_kept = adapter_forward(
        attended, mixer_down, mixer_down_bias, mixer_up, mixer_up_bias
    )
    hidden, normed_one, recip_one = norm_forward(
        token_values + attended + mixer_out, gain_one, first_shift.astype(jnp.float32)
    )
    hidden_low = hidden.astype(jnp.bfloat16)
    inner = jnp.dot(
        lax.all_gather(hidden_low, "mp", axis=0, tiled=True),
        inner_weight,
        preferred_element_type=jnp.float32,
    )
    inner_low = gelu_value(inner).astype(jnp.bfloat16)
    dense_in = lax.psum_scatter(
        jnp.dot(inner_low, outer_weight, preferred_element_type=jnp.float32).astype(jnp.bfloat16),
        "mp",
        scatter_dimension=0,
        tiled=True,
    ).astype(jnp.float32)
    dense_out, dense_kept = adapter_forward(
        dense_in, dense_down, dense_down_bias, dense_up, dense_up_bias
    )
    result, normed_two, recip_two = norm_forward(
        hidden + dense_in + dense_out, gain_two, second_shift.astype(jnp.float32)
    )
    mixer_square = jnp.sum(mixer_out * mixer_out)
    dense_square = jnp.sum(dense_out * dense_out)
    input_square = jnp.sum(token_values * token_values)
    mixer_square, dense_square, input_square = lax.psum(
        (mixer_square, dense_square, input_square), ("dp", "mp")
    )
    upstream = output_grad.astype(jnp.float32)
    second_grad, second_gain_grad, second_shift_grad = norm_backward(
        upstream, normed_two, recip_two, gain_two
    )
    dense_back, dense_grads = adapter_backward(second_grad, dense_kept, dense_down, dense_up)
    dense_in_grad = (second_grad + dense_back).astype(jnp.bfloat16)
    inner_full = times_transpose(
        lax.all_gather(dense_in_grad, "mp", axis=0, tiled=True), outer_weight
    )
    inner_grad = (inner_full * gelu_slope(inner)).astype(jnp.bfloat16)
    hidden_back = lax.psum_scatter(
        times_transpose(inner_grad, inner_weight).astype(jnp.bfloat16),
        "mp",
        scatter_dimension=0,
        tiled=True,
    ).astype(jnp.float32)
    hidden_grad = second_grad + hidden_back
    first_grad, first_gain_grad, first_shift_grad = norm_backward(
        hidden_grad, normed_one, recip_one, gain_one
    )
    mixer_back, mixer_grads = adapter_backward(first_grad, mixer_kept, mixer_down, mixer_up)
    attended_grad = (first_grad + mixer_back).astype(jnp.bfloat16)
    mixed_grad = (
        times_transpose(lax.all_gather(attended_grad, "mp", axis=0, tiled=True), output_weight)
        .astype(jnp.bfloat16)
        .reshape(head_shape)
    )
    query_grad, key_grad, value_grad = attention_backward(
        queries, keys, values, seg_row, log_totals, mixed_grad, block, scale
    )
    query_flat = query_grad.reshape(group_rows, width)
    key_flat = key_grad.reshape(group_rows, width)
    value_flat = value_grad.reshape(group_rows, width)
    total = times_transpose(query_flat, query_weight)
    total = total + times_transpose(key_flat, key_weight)
    input_back = lax.psum_scatter(
        (total + times_transpose(value_flat, value_weight)).astype(jnp.bfloat16),
        "mp",
        scatter_dimension=0,
        tiled=True,
    ).astype(jnp.float32)
    input_grad = (first_grad + input_back).astype(jnp.bfloat16)
    summed = lax.psum(
        (
            mixer_grads[0],
            mixer_grads[1],
            mixer_grads[2],
            mixer_grads[3],
            dense_grads[0],
            dense_grads[1],
            dense_grads[2],
            dense_grads[3],
            first_gain_grad,
            first_shift_grad,
            second_gain_grad,
            second_shift_grad,
        ),
        ("dp", "mp"),
    )
    ratios = jnp.sqrt(jnp.stack([mixer_square, dense_square]) / input_square)
    return (
        result.astype(jnp.bfloat16),
        input_grad,
        summed[0],
        summed[1],
        summed[2],
        summed[3],
        summed[4],
        summed[5],
        summed[6],
        summed[7],
        summed[8],
        summed[9],
        summed[10],
        summed[11],
        ratios,
    )


def solution(mesh):
    placed = (
        P(("dp", "mp"), None),
        P("dp", None),
        P(None, "mp"),
        P(None, "mp"),
        P(None, "mp"),
        P("mp", None),
        P(None, "mp"),
        P("mp", None),
        P(),
        P(),
        P(),
        P(),
        P(),
        P(),
        P(),
        P(),
        P(),
        P(),
        P(),
        P(),
        P(("dp", "mp"), None),
    )
    return jax.shard_map(
        per_device,
        mesh=mesh,
        in_specs=placed,
        out_specs=(
            P(("dp", "mp"), None),
            P(("dp", "mp"), None),
            P(),
            P(),
            P(),
            P(),
            P(),
            P(),
            P(),
            P(),
            P(),
            P(),
            P(),
            P(),
            P(),
        ),
        check_vma=False,
    )
```

profile of v0, /device:TPU:0, one launch (start us, length us, event | category | flops | bytes accessed | tf_op | source)
XLA Modules:
  0.0 461.9 jit_solution(3610006697994505217)
XLA Ops:
  8.0 14.1 %all-gather.5.cloned.1.call-done = bf16[1024,768]{1,0:T(8,128)(2,1)} async-done(((bf16[512,768]{1,0:T(8,128)(2,1)}), bf16[1024,768]{1,0:T(8,128)(2,1)}) %all-gather.5.cloned.1.call-update) | async-done | bytes 1572880 | tf_op jit(solution)/shard_map/all_gather | solution.py:178
  29.1 27.5 %while.27 = (s32[]{:T(128)}, bf16[2,512,6,64]{1,3,2,0:T(8,128)(2,1)}, f32[2,6,512]{2,1,0:T(8,128)S(1)}, s32[2]{0:T(128)S(1)}, s32[1024]{0:T(1024)S(1)}, /*index=...) while((s32[]{:T(128)}, ...), condition=%wide.region_3.4_spmd, body=%wide.region_0.3_spmd.sunk | while | flops 843772928 | bytes 45472476 | solution.py:99
  37.8 5.0 %fusion.214 = bf16[2,512,6,64]{1,3,2,0:T(8,128)(2,1)} fusion(bf16[2,512,6,64]{1,3,2,0:T(8,128)(2,1)} %get-tuple-element.408, s32[]{:T(128)} %get-tuple-element.407, bf16[1024,6,64]{0,2,1:T(8,128)(2,1)S(1)} %copy-done.10, f32[6,512,1024]{2,1,0:T(8,128)S(1)} %get-tuple-element.378, f32[6,512]{1,0:T(8,128)S(1)} %fusion.213, ...), kind=kOutput, calls=%fused_computation.8.clone.1 | convolution fusion | flops 418578432 | bytes 14311936 | tf_op jit(solution)/shard_map/while/body/eval_jaxpr/hqk,khd->qhd/dot_general | solution.py:96
  51.5 5.0 %fusion.214 = bf16[2,512,6,64]{1,3,2,0:T(8,128)(2,1)} fusion(bf16[2,512,6,64]{1,3,2,0:T(8,128)(2,1)} %get-tuple-element.408, s32[]{:T(128)} %get-tuple-element.407, bf16[1024,6,64]{0,2,1:T(8,128)(2,1)S(1)} %copy-done.10, f32[6,512,1024]{2,1,0:T(8,128)S(1)} %get-tuple-element.378, f32[6,512]{1,0:T(8,128)S(1)} %fusion.213, ...), kind=kOutput, calls=%fused_computation.8.clone.1 | convolution fusion | flops 418578432 | bytes 14311936 | tf_op jit(solution)/shard_map/while/body/eval_jaxpr/hqk,khd->qhd/dot_general | solution.py:96
  61.6 12.1 %reduce-scatter.5.cloned.1.call-done = f32[512,768]{1,0:T(8,128)} async-done(((f32[1024,768]{1,0:T(8,128)}), f32[512,768]{1,0:T(8,128)}) %reduce-scatter.5.cloned.1.call-update) | async-done | bytes 1572880 | tf_op jit(solution)/shard_map/reduce_scatter | solution.py:192
  81.3 10.9 %all-gather.7.cloned.1.call-done = bf16[1024,768]{1,0:T(8,128)(2,1)} async-done(((bf16[512,768]{1,0:T(8,128)(2,1)}), bf16[1024,768]{1,0:T(8,128)(2,1)}) %all-gather.7.cloned.1.call-update) | async-done | bytes 1572880 | tf_op jit(solution)/shard_map/all_gather | solution.py:207
  99.0 17.3 %fusion.53 = bf16[1024,768]{1,0:T(8,128)(2,1)} fusion(bf16[1536,768]{1,0:T(8,128)(2,1)S(1)} %copy-done.52, f32[1024,1536]{1,0:T(8,128)S(1)} %fusion.147), kind=kOutput, calls=%fused_computation.78 | convolution fusion | flops 2518941696 | bytes 10223616 | tf_op jit(solution)/shard_map/dot_general | solution.py:213
  116.5 10.3 %reduce-scatter.7.cloned.1.call-done = bf16[512,768]{1,0:T(8,128)(2,1)} async-done(((bf16[1024,768]{1,0:T(8,128)(2,1)}), bf16[512,768]{1,0:T(8,128)(2,1)}) %reduce-scatter.7.cloned.1.call-update) | async-done | bytes 786448 | tf_op jit(solution)/shard_map/reduce_scatter | solution.py:212
  138.0 11.1 %all-gather.9.cloned.1.call-done = bf16[1024,768]{1,0:T(8,128)(2,1)} async-done(((bf16[512,768]{1,0:T(8,128)(2,1)}), bf16[1024,768]{1,0:T(8,128)(2,1)}) %all-gather.9.cloned.1.call-update) | async-done | bytes 1572880 | tf_op jit(solution)/shard_map/all_gather | solution.py:237
  149.1 10.5 %convolution_convert_fusion = bf16[1024,768]{1,0:T(8,128)(2,1)} fusion(bf16[768,1536]{1,0:T(8,128)(2,1)S(1)} %copy-done, f32[1024,1536]{1,0:T(8,128)} %copy-done.56, bf16[1024,768]{1,0:T(8,128)(2,1)} %all-gather.9.cloned.1.call-done, bf16[1536,768]{1,0:T(8,128)(2,1)} %param.32), kind=kOutput, calls=%fused_computation.79 | convolution fusion | flops 4848353280 | bytes 14155776 | tf_op jit(solution)/shard_map/dot_general | solution.py:25
  159.8 10.1 %reduce-scatter.9.cloned.1.call-done = bf16[512,768]{1,0:T(8,128)(2,1)} async-done(((bf16[1024,768]{1,0:T(8,128)(2,1)}), bf16[512,768]{1,0:T(8,128)(2,1)}) %reduce-scatter.9.cloned.1.call-update) | async-done | bytes 786448 | tf_op jit(solution)/shard_map/reduce_scatter | solution.py:240
  177.8 11.1 %all-gather.11.cloned.1.call-done = bf16[1024,768]{1,0:T(8,128)(2,1)} async-done(((bf16[512,768]{1,0:T(8,128)(2,1)}), bf16[1024,768]{1,0:T(8,128)(2,1)}) %all-gather.11.cloned.1.call-update) | async-done | bytes 1572880 | tf_op jit(solution)/shard_map/all_gather | solution.py:253
  192.9 98.8 %while.28 = (s32[]{:T(128)}, f32[1024,6,64]{0,2,1:T(8,128)S(1)}, f32[1024,6,64]{0,2,1:T(8,128)}, bf16[2,512,6,64]{1,3,2,0:T(8,128)(2,1)}, s32[2]{0:T(128)S(1)}, ...) while((s32[]{:T(128)}, f32[1024,6,64]{0,2,1:T(8,128)S(1)}, ...), condition=%wide.region_17.18_spmd.clone, body=%wide.region_15.17_spmd.clone.sunk | while | flops 2063332352 | bytes 179538384 | solution.py:137
  194.2 7.4 %fusion.224 = f32[6,512,1024]{2,1,0:T(8,128)} fusion(bf16[1024,6,64]{0,2,1:T(8,128)(2,1)S(1)} %get-tuple-element.475, bf16[1024,6,64]{0,2,1:T(8,128)(2,1)} %get-tuple-element.472, s32[]{:T(128)S(6)} %select_n.64), kind=kOutput, calls=%fused_computation.33.clone.1 | convolution fusion | flops 402653184 | bytes 13762564 | tf_op jit(solution)/shard_map/while/body/eval_jaxpr/qhd,khd->hqk/dot_general | solution.py:78
  204.0 11.6 %multiply_reduce_fusion.9 = (f32[6,512]{1,0:T(8,128)S(1)}, f32[6,512,1024]{2,1,0:T(8,128)}) fusion(f32[6,512,1024]{2,1,0:T(8,128)} %fusion.224, f32[6,512]{1,0:T(8,128)S(1)} %dynamic-slice_bitcast_fusion.2, pred[512,1024]{1,0:T(8,128)(4,1)S(1)} %broadcast_compare_fusion.5, bf16[1024,6,64]{0,2,1:T(8,128)(2,1)} %get-tuple-element.478, ...), kind=kOutput, calls=%fused_computation.17.clone.1 | convolution fusion | flops 418378752 | bytes 26894340 | tf_op jit(solution)/shard_map/while/body/eval_jaxpr/qhd,khd->hqk/dot_general | solution.py:120
  216.9 9.6 %multiply_convert_fusion.2 = bf16[6,512,1024]{2,1,0:T(8,128)(2,1)} fusion(f32[6,512,1024]{2,1,0:T(8,128)} %get-tuple-element.392, f32[6,512,1024]{2,1,0:T(8,128)S(1)} %bitcast.121, f32[6,512]{1,0:T(8,128)S(1)} %get-tuple-element.393, f32[6,512]{1,0:T(8,128)S(1)} %dynamic-slice_bitcast_fusion.2, pred[512,1024]{1,0:T(8,128)(4,1)S(1)} %broadcast_compare_fusion.5), kind=kLoop, calls=%fused_computation.16.clone.1 | loop fusion | flops 18874368 | bytes 32006144 | tf_op jit(solution)/shard_map/while/body/eval_jaxpr/convert_element_type | solution.py:125
  226.6 4.4 bitcast_add_fusion.4
  234.3 7.7 %bitcast_add_fusion.5 = f32[1024,6,64]{0,2,1:T(8,128)} fusion(f32[1024,6,64]{0,2,1:T(8,128)} %get-tuple-element.452, f32[6,512,1024]{2,1,0:T(8,128)} %fusion.224, f32[6,512]{1,0:T(8,128)S(1)} %dynamic-slice_bitcast_fusion.2, pred[512,1024]{1,0:T(8,128)(4,1)S(1)} %broadcast_compare_fusion.5, pred[]{:T(512)S(6)} %compare.3, ...), kind=kOutput, calls=%fused_computation.22.clone.1 | convolution fusion | flops 416022528 | bytes 16662533 | tf_op jit(solution)/shard_map/while/body/eval_jaxpr/hqk,qhd->khd/dot_general | solution.py:114
  243.3 7.4 %fusion.224 = f32[6,512,1024]{2,1,0:T(8,128)} fusion(bf16[1024,6,64]{0,2,1:T(8,128)(2,1)S(1)} %get-tuple-element.475, bf16[1024,6,64]{0,2,1:T(8,128)(2,1)} %get-tuple-element.472, s32[]{:T(128)S(6)} %select_n.64), kind=kOutput, calls=%fused_computation.33.clone.1 | convolution fusion | flops 402653184 | bytes 13762564 | tf_op jit(solution)/shard_map/while/body/eval_jaxpr/qhd,khd->hqk/dot_general | solution.py:78
  253.0 11.6 %multiply_reduce_fusion.9 = (f32[6,512]{1,0:T(8,128)S(1)}, f32[6,512,1024]{2,1,0:T(8,128)}) fusion(f32[6,512,1024]{2,1,0:T(8,128)} %fusion.224, f32[6,512]{1,0:T(8,128)S(1)} %dynamic-slice_bitcast_fusion.2, pred[512,1024]{1,0:T(8,128)(4,1)S(1)} %broadcast_compare_fusion.5, bf16[1024,6,64]{0,2,1:T(8,128)(2,1)} %get-tuple-element.478, ...), kind=kOutput, calls=%fused_computation.17.clone.1 | convolution fusion | flops 418378752 | bytes 26894340 | tf_op jit(solution)/shard_map/while/body/eval_jaxpr/qhd,khd->hqk/dot_general | solution.py:120
  266.0 9.6 %multiply_convert_fusion.2 = bf16[6,512,1024]{2,1,0:T(8,128)(2,1)} fusion(f32[6,512,1024]{2,1,0:T(8,128)} %get-tuple-element.392, f32[6,512,1024]{2,1,0:T(8,128)S(1)} %bitcast.121, f32[6,512]{1,0:T(8,128)S(1)} %get-tuple-element.393, f32[6,512]{1,0:T(8,128)S(1)} %dynamic-slice_bitcast_fusion.2, pred[512,1024]{1,0:T(8,128)(4,1)S(1)} %broadcast_compare_fusion.5), kind=kLoop, calls=%fused_computation.16.clone.1 | loop fusion | flops 18874368 | bytes 32006144 | tf_op jit(solution)/shard_map/while/body/eval_jaxpr/convert_element_type | solution.py:125
  283.4 8.1 %bitcast_add_fusion.5 = f32[1024,6,64]{0,2,1:T(8,128)} fusion(f32[1024,6,64]{0,2,1:T(8,128)} %get-tuple-element.452, f32[6,512,1024]{2,1,0:T(8,128)} %fusion.224, f32[6,512]{1,0:T(8,128)S(1)} %dynamic-slice_bitcast_fusion.2, pred[512,1024]{1,0:T(8,128)(4,1)S(1)} %broadcast_compare_fusion.5, pred[]{:T(512)S(6)} %compare.3, ...), kind=kOutput, calls=%fused_computation.22.clone.1 | convolution fusion | flops 416022528 | bytes 16662533 | tf_op jit(solution)/shard_map/while/body/eval_jaxpr/hqk,qhd->khd/dot_general | solution.py:114
  305.8 41.6 %all-reduce = (f32[64]{0:T(128)}, f32[768]{0:T(1024)}, f32[64]{0:T(128)}, f32[768]{0:T(1024)}, f32[768]{0:T(1024)}, /*index=5*/f32[768]{0:T(1024)}, f32[768]{0:T...) all-reduce(f32[64]{0:T(128)S(1)} %copy-done.51, ...), channel_id=1, replica_groups=mesh['dp'=16,'mp'=2] {'dp','mp'}, use_global_device_ids=true, to_apply=%region_21.22 | all-reduce | flops 4739 | bytes 37912 | tf_op jit(solution)/shard_map/psum | solution.py:272
  352.5 96.0 %all-reduce.4.cloned.1.call-done = (f32[768,64]{0,1:T(8,128)}, f32[64,768]{1,0:T(8,128)}, f32[768,64]{0,1:T(8,128)}, f32[64,768]{1,0:T(8,128)}) async-done(((f32[768,64]{0,1:T(8,128)}, f32[64,768]{1,0:T(8,128)}, f32[768,64]{0,1:T(8,128)}, f32[64,768]{1,0:T(8,128)}), (f32[768,64]{0,1:T(8,128)}, f32[64,768]{1,0:T(8,128)}, f32[768,64]{0,1:T(8,128)}, f32[64,768]{1,0:T(8,128)})) %all-reduce.4.cloned.1.call-update) | async-done | bytes 786448 | tf_op jit(solution)/shard_map/psum | solution.py:272
  (242 shorter events, 107.6 us)
Async XLA Ops:
  7.2 85.0 %copy-start = (bf16[768,1536]{1,0:T(8,128)(2,1)S(1)}, bf16[768,1536]{1,0:T(8,128)(2,1)}, u32[]{:S(2)}) copy-start(bf16[768,1536]{1,0:T(8,128)(2,1)} %param.31) | copy-start | bytes 7077892
  7.2 14.9 %all-gather.5.cloned.1.call-start = ((), (), s32[]{:S(2)}) async-start(), calls=%async_computation.4 | async-start | bytes 2359296 | tf_op jit(solution)/shard_map/all_gather | solution.py:178
  7.9 65.7 %reduce-scatter.5.cloned.1.call-start = ((), (), s32[]{:S(2)}) async-start(), calls=%async_computation.5 | async-start | bytes 4718592 | tf_op jit(solution)/shard_map/reduce_scatter | solution.py:192
  58.7 14.9 %copy-start.34 = (bf16[768,64]{0,1:T(8,128)(2,1)S(1)}, bf16[768,64]{0,1:T(8,128)(2,1)}, u32[]{:S(2)}) copy-start(bf16[768,64]{0,1:T(8,128)(2,1)} %param.33) | copy-start | bytes 294916
  61.4 14.0 %copy-start.36 = (bf16[64,768]{1,0:T(8,128)(2,1)S(1)}, bf16[64,768]{1,0:T(8,128)(2,1)}, u32[]{:S(2)}) copy-start(bf16[64,768]{1,0:T(8,128)(2,1)} %param.35) | copy-start | bytes 294916
  61.4 30.7 %all-gather.7.cloned.1.call-start = ((), (), s32[]{:S(2)}) async-start(), calls=%async_computation.6 | async-start | bytes 2359296 | tf_op jit(solution)/shard_map/all_gather | solution.py:207
  75.4 99.8 %copy-start.31 = (f32[512,64]{0,1:T(8,128)}, f32[512,64]{0,1:T(8,128)S(1)}, u32[]{:S(2)}) copy-start(f32[512,64]{0,1:T(8,128)S(1)} %convolution_add_fusion.3) | copy-start | bytes 393220
  81.1 45.7 %reduce-scatter.7.cloned.1.call-start = ((), (), s32[]{:S(2)}) async-start(), calls=%async_computation.7 | async-start | bytes 2359296 | tf_op jit(solution)/shard_map/reduce_scatter | solution.py:212
  99.0 17.4 %copy-start.55 = (bf16[64]{0:T(256)(128)(2,1)S(1)}, bf16[64]{0:T(256)(128)(2,1)}, u32[]{:S(2)}) copy-start(bf16[64]{0:T(256)(128)(2,1)} %param.38) | copy-start | bytes 388
  99.0 17.5 %copy-start.47 = (bf16[768]{0:T(1024)(128)(2,1)S(1)}, bf16[768]{0:T(1024)(128)(2,1)}, u32[]{:S(2)}) copy-start(bf16[768]{0:T(1024)(128)(2,1)} %param.40) | copy-start | bytes 4612
  99.0 17.5 %copy-start.48 = (bf16[768]{0:T(1024)(128)(2,1)S(1)}, bf16[768]{0:T(1024)(128)(2,1)}, u32[]{:S(2)}) copy-start(bf16[768]{0:T(1024)(128)(2,1)} %param.43) | copy-start | bytes 4612
  99.0 17.5 %copy-start.49 = (bf16[768]{0:T(1024)(128)(2,1)S(1)}, bf16[768]{0:T(1024)(128)(2,1)}, u32[]{:S(2)}) copy-start(bf16[768]{0:T(1024)(128)(2,1)} %param.44) | copy-start | bytes 4612
  99.0 27.8 %copy-start.33 = (bf16[768,64]{0,1:T(8,128)(2,1)S(1)}, bf16[768,64]{0,1:T(8,128)(2,1)}, u32[]{:S(2)}) copy-start(bf16[768,64]{0,1:T(8,128)(2,1)} %param.37) | copy-start | bytes 294916
  116.4 32.7 %all-gather.9.cloned.1.call-start = ((), (), s32[]{:S(2)}) async-start(), calls=%async_computation.8 | async-start | bytes 2359296 | tf_op jit(solution)/shard_map/all_gather | solution.py:237
  137.9 32.0 %reduce-scatter.9.cloned.1.call-start = ((), (), s32[]{:S(2)}) async-start(), calls=%async_computation.9 | async-start | bytes 2359296 | tf_op jit(solution)/shard_map/reduce_scatter | solution.py:240
  159.5 14.5 %copy-start.4 = (f32[512,768]{1,0:T(8,128)S(1)}, f32[512,768]{1,0:T(8,128)}, u32[]{:S(2)}) copy-start(f32[512,768]{1,0:T(8,128)} %copy-done.3) | copy-start | bytes 4718596
  159.5 29.3 %all-gather.11.cloned.1.call-start = ((), (), s32[]{:S(2)}) async-start(), calls=%async_computation.10 | async-start | bytes 2359296 | tf_op jit(solution)/shard_map/all_gather | solution.py:253
  175.3 13.6 %copy-start.19 = (bf16[384,768]{1,0:T(8,128)(2,1)S(1)}, bf16[384,768]{1,0:T(8,128)(2,1)}, u32[]{:S(2)}) copy-start(bf16[384,768]{1,0:T(8,128)(2,1)} %param.30) | copy-start | bytes 1769476
  176.2 15.7 %copy-start.27 = (bf16[512,64]{0,1:T(8,128)(2,1)}, bf16[512,64]{0,1:T(8,128)(2,1)S(1)}, u32[]{:S(2)}) copy-start(bf16[512,64]{0,1:T(8,128)(2,1)S(1)} %get-tuple-element.253) | copy-start | bytes 196612
  177.7 172.1 %reduce-scatter.11.cloned.1.call-start = ((), (), s32[]{:S(2)}) async-start(), calls=%async_computation.11 | async-start | bytes 2359296 | tf_op jit(solution)/shard_map/reduce_scatter | solution.py:265
  204.0 13.0 %slice-start.2 = ((s8[12582912]{0:T(1024)(128)(4,1)}), s8[4194304]{0:T(1024)(128)(4,1)S(1)}, s32[]{:S(2)}) async-start(s8[12582912]{0:T(1024)(128)(4,1)} %bitcast.120), calls=%async_computation.15 | async-start | bytes 8388608 | tf_op jit(solution)/shard_map/while
  253.0 13.0 %slice-start.2 = ((s8[12582912]{0:T(1024)(128)(4,1)}), s8[4194304]{0:T(1024)(128)(4,1)S(1)}, s32[]{:S(2)}) async-start(s8[12582912]{0:T(1024)(128)(4,1)} %bitcast.120), calls=%async_computation.15 | async-start | bytes 8388608 | tf_op jit(solution)/shard_map/while
  300.0 148.5 %all-reduce.4.cloned.1.call-start = ((), (), s32[]{:S(2)}) async-start(), calls=%async_computation.12 | async-start | bytes 1572864 | tf_op jit(solution)/shard_map/psum | solution.py:272
  304.5 150.4 %copy-start.1 = (bf16[768,1536]{1,0:T(8,128)(2,1)S(1)}, bf16[768,1536]{1,0:T(8,128)(2,1)}, u32[]{:S(2)}) copy-start(bf16[768,1536]{1,0:T(8,128)(2,1)} %param.31) | copy-start | bytes 7077892
  (53 other events, 195.6 us)
Sparse Core Ops, SparseCore 0:
  9.6 12.4 all-gather.4
  61.6 12.0 reduce-scatter.4
  81.2 10.9 all-gather.6
  116.5 10.2 reduce-scatter.6
  138.0 10.9 all-gather.8
  159.7 10.2 reduce-scatter.8
  177.8 10.9 all-gather.10
  300.1 10.2 reduce-scatter.10
  317.2 131.2 all-reduce.3
where the time goes:
time: 470 us; the launch traced here: 462 us
  waiting for transfers between devices  176 us (37%)
  matrix products  151 us (32%)
  other arithmetic  44.7 us (10%)
  blocking collectives  41.6 us (9%)
  local copies, waits for them, and re-layouts  25.2 us (5%)
  between operations  14.9 us (3%)
  loops' own time  6.95 us (1%)
    psum x1, waiting for transfers between devices, per_device(): lax.psum((mixer_grads[0], mixer_grads[1], mixer_grads[2], mixer_grads[3],...  96 us
    psum x1, blocking collectives, per_device(): lax.psum((mixer_grads[0], mixer_grads[1], mixer_grads[2], mixer_grads[3],...  41.6 us
    dot_general x2, matrix products, one_block(): jnp.einsum('qhd,khd->hqk', grad_rows, values, preferred_element_type=jnp....  23.3 us
    dot_general x9, matrix products, times_transpose(): lax.dot_general(left, right, (((1,), (1,)), ((), ())), preferred_element_...  22.3 us
    dot_general x4, matrix products, score_block(): jnp.einsum('qhd,khd->hqk', query_rows, keys, preferred_element_type=jnp.f...  21.5 us
    convert_element_type x2, other arithmetic, one_block(): score_grad = (shares * (share_grad - jnp.sum(shares * share_grad, -1, kee...  19.2 us
    dot_general x1, matrix products, per_device(): jnp.dot(inner_low, outer_weight, preferred_element_type=jnp.float32)  17.3 us
    dot_general x2, matrix products, one_block(): jnp.einsum('hqk,qhd->khd', shares.astype(jnp.bfloat16), grad_rows, prefer...  15.8 us
  transfers between devices with their start and end apart: 9, of which 8 were waited for; matrix products, arithmetic and copies ran while one was open for 2% of the time, Pallas kernels for 0%

commit v1 on v0

v1 whole, which is shorter than its diff:
```python
import functools

import jax
import jax.numpy as jnp
from jax import lax
from jax.experimental import pallas as pl
from jax.experimental.pallas import tpu as pltpu
from jax.sharding import PartitionSpec as P

F32 = jnp.float32
BF16 = jnp.bfloat16
HEAD_DIM = 64
PAIR = 2 * HEAD_DIM
EPS = 1e-12
LOG2E = 1.4426950408889634
LN2 = 0.6931471805599453
ROOT_HALF = 0.7071067811865476
ROOT_TWO_PI = 0.3989422804014327
MASKED = -1e30
BLOCK = 256
MIB = 1 << 20

VM = pl.BlockSpec(memory_space=pltpu.VMEM)
SM = pl.BlockSpec(memory_space=pltpu.SMEM)


def dot(left, right):
    return jnp.dot(left, right, preferred_element_type=F32)


def dot_nt(left, right):
    return lax.dot_general(left, right, (((1,), (1,)), ((), ())), preferred_element_type=F32)


def dot_tn(left, right):
    return lax.dot_general(left, right, (((0,), (0,)), ((), ())), preferred_element_type=F32)


def aligned(index, size):
    return pl.ds(pl.multiple_of(index * size, size), size)


def split_pair(pair):
    lane = lax.broadcasted_iota(jnp.int32, pair.shape, 1)
    zero = jnp.zeros_like(pair)
    return jnp.where(lane < HEAD_DIM, pair, zero), jnp.where(lane < HEAD_DIM, zero, pair)


def stack_heads(source, target, block):
    first, second = split_pair(source)
    for t in range(source.shape[0] // block):
        target[pl.ds(2 * t * block, block), :] = first[t * block : (t + 1) * block]
        target[pl.ds((2 * t + 1) * block, block), :] = second[t * block : (t + 1) * block]


def fill_columns(row_ref, column_ref):
    for t in range(row_ref.shape[1] // 128):
        span = slice(t * 128, (t + 1) * 128)
        column_ref[span, :] = jnp.broadcast_to(row_ref[0:1, span], (128, 128)).T


def block_ranges(seg_row, block):
    ids = seg_row.reshape(-1)
    first = ids[::block]
    last = ids[block - 1 :: block]
    low = jnp.sum((ids[None, :] < first[:, None]).astype(jnp.int32), 1) // block
    high = (jnp.sum((ids[None, :] <= last[:, None]).astype(jnp.int32), 1) + block - 1) // block
    return jnp.stack([low, high])


def project_kernel(x_ref, wq_ref, wk_ref, wv_ref, out_ref):
    width = wq_ref.shape[1]
    x = x_ref[...]
    out_ref[:, :width] = (dot(x, wq_ref[...]) * (HEAD_DIM**-0.5 * LOG2E)).astype(BF16)
    out_ref[:, width : 2 * width] = dot(x, wk_ref[...]).astype(BF16)
    out_ref[:, 2 * width :] = dot(x, wv_ref[...]).astype(BF16)


def project(x, wq, wk, wv):
    rows, width = x.shape[0], wq.shape[1]
    return pl.pallas_call(
        project_kernel,
        out_shape=jax.ShapeDtypeStruct((rows, 3 * width), BF16),
        in_specs=[VM] * 4,
        out_specs=VM,
        compiler_params=pltpu.CompilerParams(vmem_limit_bytes=16 * MIB),
        cost_estimate=pl.CostEstimate(flops=2 * rows * x.shape[1] * 3 * width, bytes_accessed=5 * MIB, transcendentals=0),
        name="project",
    )(x, wq, wk, wv)


def attention_kernel(
    rng_ref, half_ref, seg_ref, own_ref, x_ref, wq_ref, wk_ref, wv_ref,
    qkv_ref, keep_ref, send_ref, lse_ref,
    seg_col, keys, values, scores, peaks, totals, mix,
):
    half = own_ref.shape[0]
    count, width = qkv_ref.shape[0], wq_ref.shape[1]
    pairs, heads, block = width // PAIR, width // HEAD_DIM, BLOCK
    here, there = half_ref[0], 1 - half_ref[0]
    fill_columns(seg_ref, seg_col)
    qkv_ref[aligned(here, half), :] = own_ref[...]
    project_kernel(x_ref, wq_ref, wk_ref, wv_ref, qkv_ref.at[aligned(there, half), :])
    for p in range(pairs):
        first, second = split_pair(qkv_ref[:, width + p * PAIR : width + (p + 1) * PAIR])
        keys[2 * p], keys[2 * p + 1] = first, second
        stack_heads(qkv_ref[:, 2 * width + p * PAIR : 2 * width + (p + 1) * PAIR], values.at[p], block)

    def query_block(g, carry):
        rows = aligned(g, block)
        low, high = rng_ref[0, g], rng_ref[1, g]
        peaks[...] = jnp.full(peaks.shape, MASKED, F32)
        totals[...] = jnp.zeros(totals.shape, F32)
        mix[...] = jnp.zeros(mix.shape, F32)

        def score_pass(j, c):
            cols = aligned(j, block)
            same = seg_col[rows, 0:1] == seg_ref[0:1, cols]
            for h in range(heads):
                p = h // 2
                s = dot_nt(qkv_ref[rows, p * PAIR : (p + 1) * PAIR], keys[h, cols, :])
                s = jnp.where(same, s, MASKED)
                scores[h, :, cols] = s
                top = peaks[h]
                for t in range(block // 128):
                    top = jnp.maximum(top, s[:, t * 128 : (t + 1) * 128])
                peaks[h] = top
            return c

        lax.fori_loop(low, high, score_pass, 0)
        for h in range(heads):
            peaks[h] = jnp.broadcast_to(jnp.max(peaks[h], -1, keepdims=True), (block, 128))

        def mix_pass(j, c):
            cols = aligned(j, block)
            for p in range(pairs):
                parts = []
                for h in (2 * p, 2 * p + 1):
                    peak = jnp.concatenate([peaks[h]] * (block // 128), 1)
                    e = jnp.exp2(scores[h, :, cols] - peak)
                    total = totals[h]
                    for t in range(block // 128):
                        total = total + e[:, t * 128 : (t + 1) * 128]
                    totals[h] = total
                    parts.append(e.astype(BF16))
                mix[:, p * PAIR : (p + 1) * PAIR] += dot(jnp.concatenate(parts, 1), values[p, aligned(j, 2 * block), :])
            return c

        lax.fori_loop(low, high, mix_pass, 0)
        lane = lax.broadcasted_iota(jnp.int32, (block, 128), 1)
        lse = jnp.zeros((block, 128), F32)
        outs = []
        for p in range(pairs):
            sums = [jnp.sum(totals[h], -1, keepdims=True) for h in (2 * p, 2 * p + 1)]
            for a in range(2):
                lse = jnp.where(lane == 2 * p + a, peaks[2 * p + a] + jnp.log2(sums[a]), lse)
            scale = jnp.where(lane < HEAD_DIM, 1.0 / sums[0], 1.0 / sums[1])
            outs.append((mix[:, p * PAIR : (p + 1) * PAIR] * scale).astype(BF16))
        lse_ref[:, rows] = lse.T[0:8, :]
        result = jnp.concatenate(outs, 1)
        per_half = half // block

        @pl.when(g // per_half == here)
        def _():
            keep_ref[aligned(g % per_half, block), :] = result

        @pl.when(g // per_half != here)
        def _():
            send_ref[aligned(g % per_half, block), :] = result

        return carry

    lax.fori_loop(0, count // block, query_block, 0)


def attention(rng, half_index, seg, own, x, wq, wk, wv):
    half, width = own.shape[0], wq.shape[1]
    count, pairs = 2 * half, width // PAIR
    return pl.pallas_call(
        attention_kernel,
        out_shape=(
            jax.ShapeDtypeStruct((count, 3 * width), BF16),
            jax.ShapeDtypeStruct((half, width), BF16),
            jax.ShapeDtypeStruct((half, width), BF16),
            jax.ShapeDtypeStruct((8, count), F32),
        ),
        in_specs=[SM, SM] + [VM] * 6,
        out_specs=(VM,) * 4,
        scratch_shapes=[
            pltpu.VMEM((count, 128), F32),
            pltpu.VMEM((2 * pairs, count, PAIR), BF16),
            pltpu.VMEM((pairs, 2 * count, PAIR), BF16),
            pltpu.VMEM((2 * pairs, BLOCK, count), F32),
            pltpu.VMEM((2 * pairs, BLOCK, 128), F32),
            pltpu.VMEM((2 * pairs, BLOCK, 128), F32),
            pltpu.VMEM((BLOCK, width), F32),
        ],
        compiler_params=pltpu.CompilerParams(vmem_limit_bytes=32 * MIB),
        cost_estimate=pl.CostEstimate(flops=10**10, bytes_accessed=8 * MIB, transcendentals=10**6),
        name="attention",
    )(rng, half_index, seg, own, x, wq, wk, wv)


def attention_grad_kernel(
    rng_ref, half_ref, seg_ref, qkv_ref, keep_ref, send_ref, own_ref, other_ref, lse_ref, wq_ref, wk_ref, wv_ref, first_ref,
    away_ref, home_ref,
    seg_col, keys, values, queries, grads, grad, delta, dq, dk, dv, dqkv,
):
    half = own_ref.shape[0]
    count, width = qkv_ref.shape[0], wq_ref.shape[1]
    pairs, block = width // PAIR, BLOCK
    here, there = half_ref[0], 1 - half_ref[0]
    fill_columns(seg_ref, seg_col)
    grad[aligned(here, half), :] = own_ref[...]
    grad[aligned(there, half), :] = other_ref[...]
    row = lax.broadcasted_iota(jnp.int32, (8, width), 0)
    column = lax.broadcasted_iota(jnp.int32, (8, width), 1)
    pick = jnp.where(column // HEAD_DIM == row, 1.0, 0.0).astype(BF16)
    for which, mixed_ref, up_ref in ((here, keep_ref, own_ref), (there, send_ref, other_ref)):
        product = mixed_ref[...].astype(F32) * up_ref[...].astype(F32)
        high = product.astype(BF16)
        low = (product - high.astype(F32)).astype(BF16)
        delta[:, aligned(which, half)] = dot_nt(pick, high) + dot_nt(pick, low)
    for p in range(pairs):
        cols = slice(p * PAIR, (p + 1) * PAIR)
        stack_heads(qkv_ref[:, cols], queries.at[p], block)
        stack_heads(qkv_ref[:, width + p * PAIR : width + (p + 1) * PAIR], keys.at[p], block)
        stack_heads(qkv_ref[:, 2 * width + p * PAIR : 2 * width + (p + 1) * PAIR], values.at[p], block)
        stack_heads(grad[:, cols], grads.at[p], block)
    dk[...] = jnp.zeros(dk.shape, F32)
    dv[...] = jnp.zeros(dv.shape, F32)

    def query_block(g, carry):
        rows = aligned(g, block)
        low, high = rng_ref[0, g], rng_ref[1, g]
        dq[...] = jnp.zeros(dq.shape, F32)

        def key_block(j, c):
            span = aligned(j, block)
            same = seg_col[span, 0:1] == seg_ref[0:1, rows]
            for p in range(pairs):
                cols = slice(p * PAIR, (p + 1) * PAIR)
                s2 = dot_nt(keys[p, aligned(j, 2 * block), :], qkv_ref[rows, cols])
                d2 = dot_nt(values[p, aligned(j, 2 * block), :], grad[rows, cols])
                shares, slopes = [], []
                for a in range(2):
                    h = 2 * p + a
                    s = jnp.where(same, s2[a * block : (a + 1) * block] - lse_ref[h : h + 1, rows], MASKED)
                    e = jnp.exp2(s)
                    d = e * (d2[a * block : (a + 1) * block] - delta[h : h + 1, rows])
                    shares.append(e.astype(BF16))
                    slopes.append(d.astype(BF16))
                dv[span, cols] += dot(jnp.concatenate(shares, 1), grads[p, aligned(g, 2 * block), :])
                dk[span, cols] += dot(jnp.concatenate(slopes, 1), queries[p, aligned(g, 2 * block), :])
                dq[:, cols] += dot_tn(jnp.concatenate(slopes, 0), keys[p, aligned(j, 2 * block), :])
            return c

        lax.fori_loop(low, high, key_block, 0)
        dqkv[rows, :width] = (dq[...] * HEAD_DIM**-0.5).astype(BF16)
        return carry

    lax.fori_loop(0, count // block, query_block, 0)
    dqkv[:, width : 2 * width] = (dk[...] * LN2).astype(BF16)
    dqkv[:, 2 * width :] = dv[...].astype(BF16)

    def input_part(which):
        rows = aligned(which, half)
        return (
            dot_nt(dqkv[rows, :width], wq_ref[...])
            + dot_nt(dqkv[rows, width : 2 * width], wk_ref[...])
            + dot_nt(dqkv[rows, 2 * width :], wv_ref[...])
        )

    away_ref[...] = input_part(there).astype(BF16)
    home_ref[...] = input_part(here) + first_ref[...]


def attention_grad(rng, half_index, seg, qkv, keep, send, own, other, lse, wq, wk, wv, first_grad):
    half, width = own.shape
    count, pairs, features = 2 * half, width // PAIR, wq.shape[0]
    return pl.pallas_call(
        attention_grad_kernel,
        out_shape=(
            jax.ShapeDtypeStruct((half, features), BF16),
            jax.ShapeDtypeStruct((half, features), F32),
        ),
        in_specs=[SM, SM] + [VM] * 11,
        out_specs=(VM,) * 2,
        scratch_shapes=[pltpu.VMEM((count, 128), F32)]
        + [pltpu.VMEM((pairs, 2 * count, PAIR), BF16)] * 4
        + [
            pltpu.VMEM((count, width), BF16),
            pltpu.VMEM((8, count), F32),
            pltpu.VMEM((BLOCK, width), F32),
            pltpu.VMEM((count, width), F32),
            pltpu.VMEM((count, width), F32),
            pltpu.VMEM((count, 3 * width), BF16),
        ],
        compiler_params=pltpu.CompilerParams(vmem_limit_bytes=40 * MIB),
        cost_estimate=pl.CostEstimate(flops=2 * 10**10, bytes_accessed=10 * MIB, transcendentals=10**6),
        name="attention_grad",
    )(rng, half_index, seg, qkv, keep, send, own, other, lse, wq, wk, wv, first_grad)


def gelu_both(v):
    part = 0.5 + 0.5 * lax.erf(v * ROOT_HALF)
    return v * part, part + v * jnp.exp(-0.5 * v * v) * ROOT_TWO_PI


def norm(values, gain, shift):
    mean = jnp.mean(values, -1, keepdims=True)
    centred = values - mean
    reciprocal = lax.rsqrt(jnp.mean(centred * centred, -1, keepdims=True) + EPS)
    normed = centred * reciprocal
    return normed * gain + shift, normed, reciprocal


def norm_grad(upstream, normed, reciprocal, gain):
    scaled = upstream * gain
    return reciprocal * (
        scaled - jnp.mean(scaled, -1, keepdims=True) - normed * jnp.mean(scaled * normed, -1, keepdims=True)
    )


def column_sum(values):
    return jnp.sum(values, 0, keepdims=True)


def middle_kernel(
    x_ref, keep_ref, got_ref, wo_ref, wo2_ref, w1_ref, w12_ref, w2_ref, w22_ref,
    md_ref, mdb_ref, mu_ref, mub_ref, dd_ref, ddb_ref, du_ref, dub_ref,
    fg_ref, fs_ref, sg_ref, ss_ref, up_ref,
    act_ref, first_ref, own_ref, away_ref, big_ref, small_ref,
    slope_ref, hidden_ref, normed_ref,
):
    rows, features = x_ref.shape
    adapt = md_ref.shape[1]
    x = x_ref[...].astype(F32)
    attended = dot(keep_ref[...], wo_ref[...]) + dot(got_ref[...], wo2_ref[...])
    attended_low = attended.astype(BF16)
    mixer_active, mixer_slope = gelu_both(dot(attended_low, md_ref[...]) + mdb_ref[...].astype(F32))
    mixer_active = mixer_active.astype(BF16)
    mixer_out = dot(mixer_active, mu_ref[...]) + mub_ref[...].astype(F32)
    hidden, normed_one, reciprocal_one = norm(x + attended + mixer_out, fg_ref[...].astype(F32), fs_ref[...].astype(F32))
    normed_ref[...] = normed_one
    hidden_ref[...] = hidden
    mixer_square = jnp.sum(column_sum(mixer_out * mixer_out), -1, keepdims=True)
    input_square = jnp.sum(column_sum(x * x), -1, keepdims=True)
    hidden_low = hidden.astype(BF16)
    chunk = 512
    units = w1_ref.shape[1]
    dense_in = jnp.zeros((rows, features), F32)
    for s, (win, wout) in enumerate(((w1_ref, w2_ref), (w12_ref, w22_ref))):
        for c in range(units // chunk):
            span = slice(c * chunk, (c + 1) * chunk)
            value, slope = gelu_both(dot(hidden_low, win[:, span]))
            slope_ref[:, s * units + c * chunk : s * units + (c + 1) * chunk] = slope.astype(BF16)
            dense_in = dense_in + dot(value.astype(BF16), wout[span, :])
    dense_low = dense_in.astype(BF16)
    dense_active, dense_slope = gelu_both(dot(dense_low, dd_ref[...]) + ddb_ref[...].astype(F32))
    dense_active = dense_active.astype(BF16)
    dense_out = dot(dense_active, du_ref[...]) + dub_ref[...].astype(F32)
    second_gain = sg_ref[...].astype(F32)
    result, normed_two, reciprocal_two = norm(hidden_ref[...] + dense_in + dense_out, second_gain, ss_ref[...].astype(F32))
    act_ref[...] = result.astype(BF16)
    dense_square = jnp.sum(column_sum(dense_out * dense_out), -1, keepdims=True)

    upstream = up_ref[...].astype(F32)
    small_ref[4:5, :] = column_sum(upstream * normed_two)
    small_ref[5:6, :] = column_sum(upstream)
    second_grad = norm_grad(upstream, normed_two, reciprocal_two, second_gain)
    dense_top = second_grad.astype(BF16)
    big_ref[3 * adapt : 4 * adapt, :] = dot_tn(dense_active, dense_top).astype(BF16)
    small_ref[1:2, :] = column_sum(dense_top.astype(F32))
    dense_mid = (dot_nt(dense_top, du_ref[...]) * dense_slope).astype(BF16)
    big_ref[2 * adapt : 3 * adapt, :] = dot_tn(dense_mid, dense_low).astype(BF16)
    dense_mid_sum = column_sum(dense_mid.astype(F32))
    dense_in_grad = (second_grad + dot_nt(dense_mid, dd_ref[...])).astype(BF16)
    hidden_grad = second_grad
    for s, (win, wout) in enumerate(((w1_ref, w2_ref), (w12_ref, w22_ref))):
        for c in range(units // chunk):
            span = slice(c * chunk, (c + 1) * chunk)
            slope = slope_ref[:, s * units + c * chunk : s * units + (c + 1) * chunk].astype(F32)
            inner_grad = (dot_nt(dense_in_grad, wout[span, :]) * slope).astype(BF16)
            hidden_grad = hidden_grad + dot_nt(inner_grad, win[:, span])
    normed_one = normed_ref[...]
    small_ref[2:3, :] = column_sum(hidden_grad * normed_one)
    small_ref[3:4, :] = column_sum(hidden_grad)
    first_grad = norm_grad(hidden_grad, normed_one, reciprocal_one, fg_ref[...].astype(F32))
    first_ref[...] = first_grad
    mixer_top = first_grad.astype(BF16)
    big_ref[adapt : 2 * adapt, :] = dot_tn(mixer_active, mixer_top).astype(BF16)
    small_ref[0:1, :] = column_sum(mixer_top.astype(F32))
    mixer_mid = (dot_nt(mixer_top, mu_ref[...]) * mixer_slope).astype(BF16)
    big_ref[0:adapt, :] = dot_tn(mixer_mid, attended_low).astype(BF16)
    mixer_mid_sum = column_sum(mixer_mid.astype(F32))
    attended_grad = (first_grad + dot_nt(mixer_mid, md_ref[...])).astype(BF16)
    own_ref[...] = dot_nt(attended_grad, wo_ref[...]).astype(BF16)
    away_ref[...] = dot_nt(attended_grad, wo2_ref[...]).astype(BF16)
    lane = lax.broadcasted_iota(jnp.int32, (1, 128), 1)
    squares = jnp.where(lane == 0, mixer_square, jnp.where(lane == 1, dense_square, jnp.where(lane == 2, input_square, 0.0)))
    small_ref[6:7, :] = jnp.concatenate(
        [mixer_mid_sum, dense_mid_sum, squares, jnp.zeros((1, features - 2 * adapt - 128), F32)], 1
    )
    small_ref[7:8, :] = jnp.zeros((1, features), F32)


def middle(x, keep, got, weights, adapters, up):
    rows, features = x.shape
    width = keep.shape[1]
    adapt = adapters[0].shape[1]
    units = weights[2].shape[1]
    return pl.pallas_call(
        middle_kernel,
        out_shape=(
            jax.ShapeDtypeStruct((rows, features), BF16),
            jax.ShapeDtypeStruct((rows, features), F32),
            jax.ShapeDtypeStruct((rows, width), BF16),
            jax.ShapeDtypeStruct((rows, width), BF16),
            jax.ShapeDtypeStruct((4 * adapt, features), BF16),
            jax.ShapeDtypeStruct((8, features), F32),
        ),
        in_specs=[VM] * 22,
        out_specs=(VM,) * 6,
        scratch_shapes=[
            pltpu.VMEM((rows, 2 * units), BF16),
            pltpu.VMEM((rows, features), F32),
            pltpu.VMEM((rows, features), F32),
        ],
        compiler_params=pltpu.CompilerParams(vmem_limit_bytes=56 * MIB),
        cost_estimate=pl.CostEstimate(flops=2 * 10**10, bytes_accessed=16 * MIB, transcendentals=10**6),
        name="middle",
    )(x, keep, got, *weights, *adapters, up)


def swap_cores(value):
    return lax.ppermute(value, "mp", [(0, 1), (1, 0)])


def high_low(value):
    high = value.astype(BF16)
    return high, (value - high.astype(F32)).astype(BF16)


def reduce_gradients(big, small, half_index):
    rows = big.shape[0] // 2
    high, low = high_low(small)
    mine = lax.dynamic_slice_in_dim(big, half_index * rows, rows, 0)
    theirs = lax.dynamic_slice_in_dim(big, (1 - half_index) * rows, rows, 0)
    tail = jnp.concatenate([high, low], 0)
    got = swap_cores(jnp.concatenate([theirs, tail], 0))

    def combine(held_big, held_tail, received):
        total = held_big.astype(F32) + received[:rows].astype(F32)
        held = held_tail.astype(F32)
        arrived = received[rows:].astype(F32)
        vector = (held[:8] + held[8:]) + (arrived[:8] + arrived[8:])
        return total, vector

    total, vector = combine(mine, tail, got)
    devices = lax.axis_size("dp")
    step = 1
    while step < devices:
        packed = jnp.concatenate([total.astype(BF16), *high_low(vector)], 0)
        got = lax.ppermute(packed, "dp", [(i, i ^ step) for i in range(devices)])
        total, vector = combine(packed[:rows], packed[rows:], got)
        step *= 2
    other = swap_cores(total.astype(BF16)).astype(F32)
    mine = total.astype(BF16).astype(F32)
    lower = jnp.where(half_index == 0, mine, other)
    upper = jnp.where(half_index == 0, other, mine)
    return lower, upper, vector


def per_device(
    tokens, segment_ids, query_weight, key_weight, value_weight, output_weight, inner_weight, outer_weight,
    mixer_down, mixer_down_bias, mixer_up, mixer_up_bias, dense_down, dense_down_bias, dense_up, dense_up_bias,
    first_gain, first_shift, second_gain, second_shift, output_grad,
):
    half_index = lax.axis_index("mp")
    position = half_index.astype(jnp.int32).reshape(1)
    other_tokens = swap_cores(tokens)
    other_output = swap_cores(output_weight)
    other_inner = swap_cores(inner_weight)
    other_outer = swap_cores(outer_weight)
    rng = block_ranges(segment_ids, BLOCK)
    seg = segment_ids.astype(F32)
    own = project(tokens, query_weight, key_weight, value_weight)
    qkv, keep, send, lse = attention(rng, position, seg, own, other_tokens, query_weight, key_weight, value_weight)
    got = swap_cores(send)
    row = lambda v: v.reshape(1, -1)
    adapters = (
        mixer_down, row(mixer_down_bias), mixer_up, row(mixer_up_bias),
        dense_down, row(dense_down_bias), dense_up, row(dense_up_bias),
        row(first_gain), row(first_shift), row(second_gain), row(second_shift),
    )
    weights = (output_weight, other_output, inner_weight, other_inner, outer_weight, other_outer)
    result, first_grad, own_grad, away_grad, big, small = middle(tokens, keep, got, weights, adapters, output_grad)
    got_grad = swap_cores(away_grad)
    lower, upper, vector = reduce_gradients(big, small, half_index)
    away, home = attention_grad(
        rng, position, seg, qkv, keep, send, own_grad, got_grad, lse, query_weight, key_weight, value_weight, first_grad
    )
    input_grad = (home + swap_cores(away).astype(F32)).astype(BF16)
    adapt = mixer_down.shape[1]
    return (
        result,
        input_grad,
        lower[:adapt].T,
        vector[6, :adapt],
        lower[adapt:],
        vector[0],
        upper[:adapt].T,
        vector[6, adapt : 2 * adapt],
        upper[adapt:],
        vector[1],
        vector[2],
        vector[3],
        vector[4],
        vector[5],
        jnp.sqrt(vector[6, 2 * adapt : 2 * adapt + 2] / vector[6, 2 * adapt + 2]),
    )


def solution(mesh):
    tokens = P(("dp", "mp"), None)
    columns, rows, whole = P(None, "mp"), P("mp", None), P()
    return jax.shard_map(
        per_device,
        mesh=mesh,
        in_specs=(tokens, P("dp", None), columns, columns, columns, rows, columns, rows) + (whole,) * 12 + (tokens,),
        out_specs=(tokens, tokens) + (whole,) * 13,
        check_vma=False,
    )
```

time: 470 us -> 122 us (0.26); the launches traced: 462 us -> 121 us
  waiting for transfers between devices: 176 us -> 18.6 us
  matrix products: 151 us -> 0 us
  Pallas kernels: 0 us -> 63 us
  blocking collectives: 41.6 us -> 0 us
  other arithmetic: 44.7 us -> 7.12 us
  between operations: 14.9 us -> 1.02 us
  starting transfers between devices: 0.75 us -> 9.82 us
  loops' own time: 6.95 us -> 0 us
    dot_general x37 -> x0, matrix products: 151 us -> none  [the longest x2 23.3 us: one_block(): jnp.einsum('qhd,khd->hqk', grad_rows, values, preferred_element_type=jnp....]
    psum x1 -> x0, waiting for transfers between devices: 96 us -> none  [per_device(): lax.psum((mixer_grads[0], mixer_grads[1], mixer_grads[2], mixer_grads[3],...]
    pallas_call x0 -> x4, Pallas kernels: none -> 63 us  [the longest x1 24.5 us: middle(): pl.pallas_call(middle_kernel, out_shape=(jax.ShapeDtypeStruct((rows, feat...]
    all_gather x4 -> x0, waiting for transfers between devices: 47.2 us -> none  [the longest x1 14.1 us: per_device(): piece = lax.all_gather(tokens, 'mp', axis=0, tiled=True)]
    psum x1 -> x0, blocking collectives: 41.6 us -> none  [per_device(): lax.psum((mixer_grads[0], mixer_grads[1], mixer_grads[2], mixer_grads[3],...]
    reduce_scatter x4 -> x0, waiting for transfers between devices: 32.5 us -> none  [the longest x1 12.1 us: per_device(): lax.psum_scatter(jnp.dot(mixed_flat, output_weight, preferred_element_typ...]
    convert_element_type x14 -> x22, other arithmetic: 24.7 us -> 5.56 us  [the longest x4 2.07 us: reduce_gradients(): packed = jnp.concatenate([total.astype(BF16), *high_low(vector)], 0)]
    ppermute x0 -> x13, waiting for transfers between devices: none -> 18.6 us  [the longest x4 17.2 us: reduce_gradients(): got = lax.ppermute(packed, 'dp', [(i, i ^ step) for i in range(devices)])]
  transfers between devices with their start and end apart: 9 -> 13, of which waited for: 8 -> 4; matrix products, arithmetic and copies ran while one was open for 2% -> 11% of each run, Pallas kernels for 0% -> 32%
where the time goes in v1:
time: 122 us; the launch traced here: 121 us
  Pallas kernels  63 us (52%)
  local copies, waits for them, and re-layouts  21.3 us (17%)
  waiting for transfers between devices  18.6 us (15%)
  starting transfers between devices  9.82 us (8%)
  other arithmetic  7.12 us (6%)
    pallas_call x1, Pallas kernels, middle(): pl.pallas_call(middle_kernel, out_shape=(jax.ShapeDtypeStruct((rows, feat...  24.5 us
    pallas_call x1, Pallas kernels, attention_grad(): pl.pallas_call(attention_grad_kernel, out_shape=(jax.ShapeDtypeStruct((ha...  21.9 us
    ppermute x4, waiting for transfers between devices, reduce_gradients(): got = lax.ppermute(packed, 'dp', [(i, i ^ step) for i in range(devices)])  17.2 us
    pallas_call x1, Pallas kernels, attention(): pl.pallas_call(attention_kernel, out_shape=(jax.ShapeDtypeStruct((count,...  15.2 us
    unnamed x48, local copies, waits for them, and re-layouts  12 us
    ppermute x4, starting transfers between devices, reduce_gradients(): got = lax.ppermute(packed, 'dp', [(i, i ^ step) for i in range(devices)])  7.51 us
    reshape x6, local copies, waits for them, and re-layouts, per_device(): row = lambda v: v.reshape(1, -1)  3.49 us
  transfers between devices with their start and end apart: 13, of which 4 were waited for; matrix products, arithmetic and copies ran while one was open for 11% of the time, Pallas kernels for 32%

profile of v1, /device:TPU:0, one launch (start us, length us, event | category | flops | bytes accessed | tf_op | source)
XLA Modules:
  0.0 120.9 jit_solution(15721592312485194551)
XLA Ops:
  4.0 1.1 copy-done
  5.1 1.1 copy-done.1
  6.2 1.1 copy-done.3
  7.3 1.1 copy-done.5
  8.3 1.4 %project.1.own_ref = bf16[512,1152]{1,0:T(8,128)(2,1)S(1)} custom-call(bf16[512,768]{1,0:T(8,128)(2,1)S(1)} %copy-done, bf16[768,384]{1,0:T(8,128)(2,1)S(1)} %copy-done.1, bf16[768,384]{1,0:T(8,128)(2,1)S(1)} %copy-done.3, bf16[768,384]{1,0:T(8,128)(2,1)S(1)} %copy-done.5), custom_call_target="tpu_custom_call" | custom-call | flops 905969664 | bytes 5242880 | tf_op jit(solution)/shard_map/project/pallas_call | solution.py:81
  10.1 15.2 %attention.1 = (bf16[1024,1152]{1,0:T(8,128)(2,1)S(1)}, bf16[512,384]{1,0:T(8,128)(2,1)S(1)}, bf16[512,384]{1,0:T(8,128)(2,1)S(1)}, f32[8,1024]{1,0:T(8,128)S(1)}) custom-call(s32[2,4]{1,0:T(2,128)S(1)} %pad_add_fusion.rng_ref, s32[1]{0:T(128)} %bitcast.3.half_ref, f32[1,1024]{1,0:T(1,128)S(1)} %convert_element_type.144.seg_ref, ...), custom_call_target="tpu_custom_call" | custom-call | flops 10000000000 | bytes 8388608 | tf_op jit(solution)/shard_map/attention/pallas_call | solution.py:179
  25.3 1.4 %copy-done.7 = bf16[1024,1152]{1,0:T(8,128)(2,1)} copy-done((bf16[1024,1152]{1,0:T(8,128)(2,1)}, bf16[1024,1152]{1,0:T(8,128)(2,1)S(1)}, u32[]{:S(2)}) %copy-start.7) | copy-done | bytes 2359320
  33.8 24.5 %middle.1 = (bf16[512,768]{1,0:T(8,128)(2,1)}, f32[512,768]{1,0:T(8,128)}, bf16[512,384]{1,0:T(8,128)(2,1)}, bf16[512,384]{1,0:T(8,128)(2,1)}, bf16[256,768]{1,0:T(8,128)(2,1)}, /*index=5*/f32[8,768]{1,0:T(8,128)}) custom-call(bf16[512,768]{1,0:T(8,128)(2,1)} %x_ref.3, bf16[512,384]{1,0:T(8,128)(2,1)} %copy-done.10, bf16[512,384]{1,0:T(8,128)(2,1)} %copy-done.22, ...), custom_call_target="tpu_custom_call" | custom-call | flops 20000000000 | bytes 16777216 | tf_op jit(solution)/shard_map/middle/pallas_call | solution.py:413
  58.4 0.8 subtract_convert_fusion.4
  59.2 0.9 constant_dynamic-slice_fusion
  60.3 1.4 %collective-permute-done.7 = bf16[144,768]{1,0:T(8,128)(2,1)S(1)} collective-permute-done((bf16[144,768]{1,0:T(8,128)(2,1)S(1)}, bf16[144,768]{1,0:T(8,128)(2,1)S(1)}, u32[]{:S(2)}, u32[]{:S(2)}) %collective-permute-start.7) | collective-permute-done | bytes 221216 | tf_op jit(solution)/shard_map/ppermute | solution.py:437
  61.7 1.0 add_convert_fusion.5
  62.8 7.4 %collective-permute-done.8 = bf16[144,768]{1,0:T(8,128)(2,1)S(1)} collective-permute-done((bf16[144,768]{1,0:T(8,128)(2,1)S(1)}, bf16[144,768]{1,0:T(8,128)(2,1)S(1)}, u32[]{:S(2)}, u32[]{:S(2)}) %collective-permute-start.8) | collective-permute-done | bytes 221216 | tf_op jit(solution)/shard_map/ppermute | solution.py:465
  70.4 3.0 %collective-permute-start.9 = (bf16[144,768]{1,0:T(8,128)(2,1)S(1)}, bf16[144,768]{1,0:T(8,128)(2,1)S(1)}, u32[]{:S(2)}, u32[]{:S(2)}) collective-permute-start(bf16[144,768]{1,0:T(8,128)(2,1)S(1)} %pad_maximum_fusion.2), channel_id=1, source_target_pairs={{0,4},{2,6},{4,0},{6,2},{8,12},{10,14},{12,8},{14,10},{16,20},{18,... | collective-permute-start | bytes 663560 | tf_op jit(solution)/shard_map/ppermute | solution.py:465
  73.4 5.1 %collective-permute-done.9 = bf16[144,768]{1,0:T(8,128)(2,1)S(1)} collective-permute-done((bf16[144,768]{1,0:T(8,128)(2,1)S(1)}, bf16[144,768]{1,0:T(8,128)(2,1)S(1)}, u32[]{:S(2)}, u32[]{:S(2)}) %collective-permute-start.9) | collective-permute-done | bytes 221216 | tf_op jit(solution)/shard_map/ppermute | solution.py:465
  78.6 1.9 %collective-permute-start.10 = (bf16[144,768]{1,0:T(8,128)(2,1)S(1)}, bf16[144,768]{1,0:T(8,128)(2,1)}, u32[]{:S(2)}, u32[]{:S(2)}) collective-permute-start(bf16[144,768]{1,0:T(8,128)(2,1)S(1)} %pad_maximum_fusion.3), channel_id=1, source_target_pairs={{0,8},{2,10},{4,12},{6,14},{8,0},{10,2},{12,4},{14,6},{16,24},{18,... | collective-permute-start | bytes 663560 | tf_op jit(solution)/shard_map/ppermute | solution.py:465
  80.5 4.6 %collective-permute-done.10 = bf16[144,768]{1,0:T(8,128)(2,1)} collective-permute-done((bf16[144,768]{1,0:T(8,128)(2,1)S(1)}, bf16[144,768]{1,0:T(8,128)(2,1)}, u32[]{:S(2)}, u32[]{:S(2)}) %collective-permute-start.10) | collective-permute-done | bytes 221216 | tf_op jit(solution)/shard_map/ppermute | solution.py:465
  85.9 1.0 add_convert_fusion.2
  86.9 2.6 %collective-permute-start.11 = (bf16[144,768]{1,0:T(8,128)(2,1)S(1)}, bf16[144,768]{1,0:T(8,128)(2,1)S(1)}, u32[]{:S(2)}, u32[]{:S(2)}) collective-permute-start(bf16[144,768]{1,0:T(8,128)(2,1)S(1)} %pad_maximum_fusion.4), channel_id=1, source_target_pairs={{0,16},{2,18},{4,20},{6,22},{8,24},{10,26},{12,28},{14,30},{16,0},... | collective-permute-start | bytes 663560 | tf_op jit(solution)/shard_map/ppermute | solution.py:465
  89.5 1.7 %copy-done.8 = bf16[1024,1152]{1,0:T(8,128)(2,1)S(1)} copy-done((bf16[1024,1152]{1,0:T(8,128)(2,1)S(1)}, bf16[1024,1152]{1,0:T(8,128)(2,1)}, u32[]{:S(2)}) %copy-start.8) | copy-done | bytes 2359320
  91.1 1.4 %copy-done.9 = f32[512,768]{1,0:T(8,128)S(1)} copy-done((f32[512,768]{1,0:T(8,128)S(1)}, f32[512,768]{1,0:T(8,128)}, u32[]{:S(2)}) %copy-start.9) | copy-done | bytes 1572888
  92.5 21.9 %attention_grad.1 = (bf16[512,768]{1,0:T(8,128)(2,1)S(1)}, f32[512,768]{1,0:T(8,128)S(1)}) custom-call(s32[2,4]{1,0:T(2,128)S(1)} %pad_add_fusion.rng_ref, s32[1]{0:T(128)} %bitcast.3.half_ref, f32[1,1024]{1,0:T(1,128)S(1)} %convert_element_type.144.seg_ref, bf16[1024,1152]{1,0:T(8,128)(2,1)S(1)} %copy-done.8, bf16[512,384]{1,0:T(8,128)(2,1)S(1)} %copy-done.11, ...), custom_call_target="tpu_custom_call" | custom-call | flops 20000000000 | bytes 10485760 | tf_op jit(solution)/shard_map/attention_grad/pallas_call | solution.py:281
  116.4 1.2 fusion.6
  118.2 1.1 add_convert_fusion
  (101 shorter events, 16.1 us)
Async XLA Ops:
  0.6 32.4 %collective-permute-start.3 = (bf16[768,1536]{1,0:T(8,128)(2,1)}, bf16[768,1536]{1,0:T(8,128)(2,1)}, u32[]{:S(2)}, u32[]{:S(2)}) collective-permute-start(bf16[768,1536]{1,0:T(8,128)(2,1)} %w1_ref.1), channel_id=1, source_target_pairs={{0,1},{1,0},{2,3},{3,2},{4,5},{5,4},{6,7},{7,6},{8,9},{9,8},{10,11... | collective-permute-start | bytes 7077896 | tf_op jit(solution)/shard_map/ppermute | solution.py:437
  1.2 31.9 %collective-permute-start.4 = (bf16[1536,768]{1,0:T(8,128)(2,1)}, bf16[1536,768]{1,0:T(8,128)(2,1)}, u32[]{:S(2)}, u32[]{:S(2)}) collective-permute-start(bf16[1536,768]{1,0:T(8,128)(2,1)} %w2_ref.1), channel_id=1, source_target_pairs={{0,1},{1,0},{2,3},{3,2},{4,5},{5,4},{6,7},{7,6},{8,9},{9,8},{10,11... | collective-permute-start | bytes 7077896 | tf_op jit(solution)/shard_map/ppermute | solution.py:437
  1.2 8.7 %collective-permute-start = (bf16[512,768]{1,0:T(8,128)(2,1)}, bf16[512,768]{1,0:T(8,128)(2,1)S(1)}, u32[]{:S(2)}, u32[]{:S(2)}) collective-permute-start(bf16[512,768]{1,0:T(8,128)(2,1)} %x_ref.3), channel_id=1, source_target_pairs={{0,1},{1,0},{2,3},{3,2},{4,5},{5,4},{6,7},{7,6},{8,9},{9,8},{10,11... | collective-permute-start | bytes 2359304 | tf_op jit(solution)/shard_map/ppermute | solution.py:437
  1.7 31.4 %collective-permute-start.2 = (bf16[384,768]{1,0:T(8,128)(2,1)}, bf16[384,768]{1,0:T(8,128)(2,1)}, u32[]{:S(2)}, u32[]{:S(2)}) collective-permute-start(bf16[384,768]{1,0:T(8,128)(2,1)} %wo_ref.1), channel_id=1, source_target_pairs={{0,1},{1,0},{2,3},{3,2},{4,5},{5,4},{6,7},{7,6},{8,9},{9,8},{10,11... | collective-permute-start | bytes 1769480 | tf_op jit(solution)/shard_map/ppermute | solution.py:437
  8.3 1.7 %copy-start.6 = (bf16[768,384]{1,0:T(8,128)(2,1)S(1)}, bf16[768,384]{1,0:T(8,128)(2,1)}, u32[]{:S(2)}) copy-start(bf16[768,384]{1,0:T(8,128)(2,1)} %wv_ref.5) | copy-start | bytes 1769476
  10.0 17.9 %copy-start.13 = (bf16[768,64]{0,1:T(8,128)(2,1)S(1)}, bf16[768,64]{0,1:T(8,128)(2,1)}, u32[]{:S(2)}) copy-start(bf16[768,64]{0,1:T(8,128)(2,1)} %param.29) | copy-start | bytes 294916
  10.0 18.7 %copy-start.14 = (bf16[768,64]{0,1:T(8,128)(2,1)S(1)}, bf16[768,64]{0,1:T(8,128)(2,1)}, u32[]{:S(2)}) copy-start(bf16[768,64]{0,1:T(8,128)(2,1)} %param.33) | copy-start | bytes 294916
  10.1 19.5 %copy-start.16 = (bf16[768]{0:T(1024)(128)(2,1)S(1)}, bf16[768]{0:T(1024)(128)(2,1)}, u32[]{:S(2)}) copy-start(bf16[768]{0:T(1024)(128)(2,1)} %param.32) | copy-start | bytes 4612
  10.1 20.1 %copy-start.17 = (bf16[768]{0:T(1024)(128)(2,1)S(1)}, bf16[768]{0:T(1024)(128)(2,1)}, u32[]{:S(2)}) copy-start(bf16[768]{0:T(1024)(128)(2,1)} %param.36) | copy-start | bytes 4612
  10.1 20.6 %copy-start.18 = (bf16[768]{0:T(1024)(128)(2,1)S(1)}, bf16[768]{0:T(1024)(128)(2,1)}, u32[]{:S(2)}) copy-start(bf16[768]{0:T(1024)(128)(2,1)} %param.37) | copy-start | bytes 4612
  10.1 21.2 %copy-start.19 = (bf16[768]{0:T(1024)(128)(2,1)S(1)}, bf16[768]{0:T(1024)(128)(2,1)}, u32[]{:S(2)}) copy-start(bf16[768]{0:T(1024)(128)(2,1)} %param.38) | copy-start | bytes 4612
  10.1 21.8 %copy-start.20 = (bf16[768]{0:T(1024)(128)(2,1)S(1)}, bf16[768]{0:T(1024)(128)(2,1)}, u32[]{:S(2)}) copy-start(bf16[768]{0:T(1024)(128)(2,1)} %param.39) | copy-start | bytes 4612
  10.1 22.4 %copy-start.21 = (bf16[768]{0:T(1024)(128)(2,1)S(1)}, bf16[768]{0:T(1024)(128)(2,1)}, u32[]{:S(2)}) copy-start(bf16[768]{0:T(1024)(128)(2,1)} %param.40) | copy-start | bytes 4612
  27.5 5.6 %collective-permute-start.1 = (bf16[512,384]{1,0:T(8,128)(2,1)S(1)}, bf16[512,384]{1,0:T(8,128)(2,1)S(1)}, u32[]{:S(2)}, u32[]{:S(2)}) collective-permute-start(bf16[512,384]{1,0:T(8,128)(2,1)S(1)} %get-tuple-element.28.send_ref), channel_id=1, source_target_pairs={{0,1},{1,0},{2,3},{3,2},{4,5},{5,4},{6,7},{7,6},{8,9},{9,8},{10,11... | collective-permute-start | bytes 1179656 | tf_op jit(solution)/shard_map/ppermute | solution.py:437
  60.2 1.5 %collective-permute-start.7 = (bf16[144,768]{1,0:T(8,128)(2,1)S(1)}, bf16[144,768]{1,0:T(8,128)(2,1)S(1)}, u32[]{:S(2)}, u32[]{:S(2)}) collective-permute-start(bf16[144,768]{1,0:T(8,128)(2,1)S(1)} %pad_maximum_fusion), channel_id=1, source_target_pairs={{0,1},{1,0},{2,3},{3,2},{4,5},{5,4},{6,7},{7,6},{8,9},{9,8},{10,11... | collective-permute-start | bytes 663560 | tf_op jit(solution)/shard_map/ppermute | solution.py:437
  62.7 7.5 %collective-permute-start.8 = (bf16[144,768]{1,0:T(8,128)(2,1)S(1)}, bf16[144,768]{1,0:T(8,128)(2,1)S(1)}, u32[]{:S(2)}, u32[]{:S(2)}) collective-permute-start(bf16[144,768]{1,0:T(8,128)(2,1)S(1)} %pad_maximum_fusion.1), channel_id=1, source_target_pairs={{0,2},{2,0},{4,6},{6,4},{8,10},{10,8},{12,14},{14,12},{16,18},{18,... | collective-permute-start | bytes 663560 | tf_op jit(solution)/shard_map/ppermute | solution.py:465
  70.3 19.1 %copy-start.11 = (bf16[512,384]{1,0:T(8,128)(2,1)S(1)}, bf16[512,384]{1,0:T(8,128)(2,1)}, u32[]{:S(2)}) copy-start(bf16[512,384]{1,0:T(8,128)(2,1)} %copy-done.10) | copy-start | bytes 1179652
  70.4 19.1 %copy-start.12 = (bf16[512,384]{1,0:T(8,128)(2,1)S(1)}, bf16[512,384]{1,0:T(8,128)(2,1)}, u32[]{:S(2)}) copy-start(bf16[512,384]{1,0:T(8,128)(2,1)} %get-tuple-element.31.own_ref) | copy-start | bytes 1179652
  70.4 8.2 %collective-permute-start.9 = (bf16[144,768]{1,0:T(8,128)(2,1)S(1)}, bf16[144,768]{1,0:T(8,128)(2,1)S(1)}, u32[]{:S(2)}, u32[]{:S(2)}) collective-permute-start(bf16[144,768]{1,0:T(8,128)(2,1)S(1)} %pad_maximum_fusion.2), channel_id=1, source_target_pairs={{0,4},{2,6},{4,0},{6,2},{8,12},{10,14},{12,8},{14,10},{16,20},{18,... | collective-permute-start | bytes 663560 | tf_op jit(solution)/shard_map/ppermute | solution.py:465
  78.6 6.5 %collective-permute-start.10 = (bf16[144,768]{1,0:T(8,128)(2,1)S(1)}, bf16[144,768]{1,0:T(8,128)(2,1)}, u32[]{:S(2)}, u32[]{:S(2)}) collective-permute-start(bf16[144,768]{1,0:T(8,128)(2,1)S(1)} %pad_maximum_fusion.3), channel_id=1, source_target_pairs={{0,8},{2,10},{4,12},{6,14},{8,0},{10,2},{12,4},{14,6},{16,24},{18,... | collective-permute-start | bytes 663560 | tf_op jit(solution)/shard_map/ppermute | solution.py:465
  80.5 8.9 %collective-permute-start.5 = (bf16[512,384]{1,0:T(8,128)(2,1)}, bf16[512,384]{1,0:T(8,128)(2,1)S(1)}, u32[]{:S(2)}, u32[]{:S(2)}) collective-permute-start(bf16[512,384]{1,0:T(8,128)(2,1)} %get-tuple-element.32), channel_id=1, source_target_pairs={{0,1},{1,0},{2,3},{3,2},{4,5},{5,4},{6,7},{7,6},{8,9},{9,8},{10,11... | collective-permute-start | bytes 1179656 | tf_op jit(solution)/shard_map/ppermute | solution.py:437
  86.9 27.7 %collective-permute-start.11 = (bf16[144,768]{1,0:T(8,128)(2,1)S(1)}, bf16[144,768]{1,0:T(8,128)(2,1)S(1)}, u32[]{:S(2)}, u32[]{:S(2)}) collective-permute-start(bf16[144,768]{1,0:T(8,128)(2,1)S(1)} %pad_maximum_fusion.4), channel_id=1, source_target_pairs={{0,16},{2,18},{4,20},{6,22},{8,24},{10,26},{12,28},{14,30},{16,0},... | collective-permute-start | bytes 663560 | tf_op jit(solution)/shard_map/ppermute | solution.py:465
  114.5 3.7 %collective-permute-start.6 = (bf16[512,768]{1,0:T(8,128)(2,1)S(1)}, bf16[512,768]{1,0:T(8,128)(2,1)S(1)}, u32[]{:S(2)}, u32[]{:S(2)}) collective-permute-start(bf16[512,768]{1,0:T(8,128)(2,1)S(1)} %get-tuple-element.36), channel_id=1, source_target_pairs={{0,1},{1,0},{2,3},{3,2},{4,5},{5,4},{6,7},{7,6},{8,9},{9,8},{10,11... | collective-permute-start | bytes 2359304 | tf_op jit(solution)/shard_map/ppermute | solution.py:437
  115.2 4.0 %collective-permute-start.12 = (bf16[128,768]{1,0:T(8,128)(2,1)S(1)}, bf16[128,768]{1,0:T(8,128)(2,1)S(1)}, u32[]{:S(2)}, u32[]{:S(2)}) collective-permute-start(bf16[128,768]{1,0:T(8,128)(2,1)S(1)} %add_convert_fusion.1), channel_id=1, source_target_pairs={{0,1},{1,0},{2,3},{3,2},{4,5},{5,4},{6,7},{7,6},{8,9},{9,8},{10,11... | collective-permute-start | bytes 589832 | tf_op jit(solution)/shard_map/ppermute | solution.py:437
  (12 other events, 15.1 us)

commit v2 on v1

v2 whole, which is shorter than its diff:
```python
import functools

import jax
import jax.numpy as jnp
from jax import lax
from jax.experimental import pallas as pl
from jax.experimental.pallas import tpu as pltpu
from jax.sharding import PartitionSpec as P

F32 = jnp.float32
BF16 = jnp.bfloat16
HEAD_DIM = 64
PAIR = 2 * HEAD_DIM
EPS = 1e-12
LOG2E = 1.4426950408889634
LN2 = 0.6931471805599453
ROOT_HALF = 0.7071067811865476
ROOT_TWO_PI = 0.3989422804014327
MASKED = -1e30
BLOCK = 256
MIB = 1 << 20

VM = pl.BlockSpec(memory_space=pltpu.VMEM)
SM = pl.BlockSpec(memory_space=pltpu.SMEM)
HB = pl.BlockSpec(memory_space=pltpu.HBM)


def dot(left, right):
    return jnp.dot(left, right, preferred_element_type=F32)


def dot_nt(left, right):
    return lax.dot_general(left, right, (((1,), (1,)), ((), ())), preferred_element_type=F32)


def dot_tn(left, right):
    return lax.dot_general(left, right, (((0,), (0,)), ((), ())), preferred_element_type=F32)


def aligned(index, size):
    return pl.ds(pl.multiple_of(index * size, size), size)


def split_pair(pair):
    lane = lax.broadcasted_iota(jnp.int32, pair.shape, 1)
    zero = jnp.zeros_like(pair)
    return jnp.where(lane < HEAD_DIM, pair, zero), jnp.where(lane < HEAD_DIM, zero, pair)


def stack_heads(source, target, block):
    first, second = split_pair(source)
    for t in range(source.shape[0] // block):
        target[pl.ds(2 * t * block, block), :] = first[t * block : (t + 1) * block]
        target[pl.ds((2 * t + 1) * block, block), :] = second[t * block : (t + 1) * block]


def fill_columns(row_ref, column_ref):
    for t in range(row_ref.shape[1] // 128):
        span = slice(t * 128, (t + 1) * 128)
        column_ref[span, :] = jnp.broadcast_to(row_ref[0:1, span], (128, 128)).T


def start_all(sources, buffers, sems):
    copies = [pltpu.make_async_copy(src, dst, sems.at[i]) for i, (src, dst) in enumerate(zip(sources, buffers))]
    for copy in copies:
        copy.start()
    return copies


def write_projection(x, weights, copies, out_ref):
    width = weights[0].shape[1]
    for i, weight in enumerate(weights):
        if copies:
            copies[i].wait()
        part = dot(x, weight[...])
        if i == 0:
            part = part * (HEAD_DIM**-0.5 * LOG2E)
        out_ref[:, i * width : (i + 1) * width] = part.astype(BF16)


def project_kernel(x_ref, wq_ref, wk_ref, wv_ref, out_ref, x_buf, wq, wk, wv, sems):
    copies = start_all((x_ref, wq_ref, wk_ref, wv_ref), (x_buf, wq, wk, wv), sems)
    copies[0].wait()
    write_projection(x_buf[...], (wq, wk, wv), copies[1:], out_ref)


def project(x, wq, wk, wv):
    rows, width = x.shape[0], wq.shape[1]
    return pl.pallas_call(
        project_kernel,
        out_shape=jax.ShapeDtypeStruct((rows, 3 * width), BF16),
        in_specs=[HB] * 4,
        out_specs=VM,
        scratch_shapes=[pltpu.VMEM(v.shape, BF16) for v in (x, wq, wk, wv)] + [pltpu.SemaphoreType.DMA((4,))],
        compiler_params=pltpu.CompilerParams(vmem_limit_bytes=12 * MIB),
        cost_estimate=pl.CostEstimate(flops=2 * rows * x.shape[1] * 3 * width, bytes_accessed=5 * MIB, transcendentals=0),
        name="project",
    )(x, wq, wk, wv)


def attention_kernel(
    half_ref, ids_ref, seg_ref, own_ref, x_ref, wq_ref, wk_ref, wv_ref,
    qkv_ref, keep_ref, send_ref, inverse_ref, rng_ref, *rest,
):
    half = own_ref.shape[0]
    count, width = qkv_ref.shape[0], wq_ref.shape[1]
    pairs, heads, block = width // PAIR, width // HEAD_DIM, BLOCK
    share_refs = rest[:pairs]
    seg_row, seg_col, keys, values, scores, peaks, totals, mix, wq, wk, wv, sems = rest[pairs:]
    here, there = half_ref[0], 1 - half_ref[0]
    copies = start_all((wq_ref, wk_ref, wv_ref), (wq, wk, wv), sems)
    seg_row[...] = seg_ref[...].astype(F32)
    fill_columns(seg_row, seg_col)
    ids = seg_row[...]
    for g in range(count // block):
        first = ids_ref[0, g * block].astype(F32)
        last = ids_ref[0, (g + 1) * block - 1].astype(F32)
        rng_ref[0, g] = jnp.sum(jnp.where(ids < first, 1.0, 0.0)).astype(jnp.int32) // block
        rng_ref[1, g] = (jnp.sum(jnp.where(ids <= last, 1.0, 0.0)).astype(jnp.int32) + block - 1) // block
    qkv_ref[aligned(here, half), :] = own_ref[...]
    write_projection(x_ref[...], (wq, wk, wv), copies, qkv_ref.at[aligned(there, half), :])
    for p in range(pairs):
        stack_heads(qkv_ref[:, width + p * PAIR : width + (p + 1) * PAIR], keys.at[p], block)
        stack_heads(qkv_ref[:, 2 * width + p * PAIR : 2 * width + (p + 1) * PAIR], values.at[p], block)

    def query_block(g, carry):
        rows = aligned(g, block)
        low, high = rng_ref[0, g], rng_ref[1, g]
        peaks[...] = jnp.full(peaks.shape, MASKED, F32)
        totals[...] = jnp.zeros(totals.shape, F32)
        mix[...] = jnp.zeros(mix.shape, F32)

        def score_pass(j, c):
            both = aligned(j, 2 * block)
            same = seg_col[rows, 0:1] == seg_row[0:1, aligned(j, block)]
            for p in range(pairs):
                s2 = dot_nt(qkv_ref[rows, p * PAIR : (p + 1) * PAIR], keys[p, both, :])
                for a in range(2):
                    s = jnp.where(same, s2[:, a * block : (a + 1) * block], MASKED)
                    scores[p, :, aligned(2 * j + a, block)] = s
                    top = peaks[2 * p + a]
                    for t in range(block // 128):
                        top = jnp.maximum(top, s[:, t * 128 : (t + 1) * 128])
                    peaks[2 * p + a] = top
            return c

        lax.fori_loop(low, high, score_pass, 0)
        for h in range(heads):
            peaks[h] = jnp.broadcast_to(jnp.max(peaks[h], -1, keepdims=True), (block, 128))

        def mix_pass(j, c):
            both = aligned(j, 2 * block)
            for p in range(pairs):
                parts = []
                for a in range(2):
                    peak = jnp.concatenate([peaks[2 * p + a]] * (block // 128), 1)
                    e = jnp.exp2(scores[p, :, aligned(2 * j + a, block)] - peak)
                    total = totals[2 * p + a]
                    for t in range(block // 128):
                        total = total + e[:, t * 128 : (t + 1) * 128]
                    totals[2 * p + a] = total
                    parts.append(e.astype(BF16))
                shares = jnp.concatenate(parts, 1)
                share_refs[p][rows, both] = shares
                mix[:, p * PAIR : (p + 1) * PAIR] += dot(shares, values[p, both, :])
            return c

        lax.fori_loop(low, high, mix_pass, 0)
        lane = lax.broadcasted_iota(jnp.int32, (block, 128), 1)
        outs = []
        for p in range(pairs):
            sums = [jnp.sum(totals[h], -1, keepdims=True) for h in (2 * p, 2 * p + 1)]
            scale = jnp.where(lane < HEAD_DIM, 1.0 / sums[0], 1.0 / sums[1])
            inverse_ref[rows, p * PAIR : (p + 1) * PAIR] = scale
            outs.append((mix[:, p * PAIR : (p + 1) * PAIR] * scale).astype(BF16))
        result = jnp.concatenate(outs, 1)
        per_half = half // block

        @pl.when(g // per_half == here)
        def _():
            keep_ref[aligned(g % per_half, block), :] = result

        @pl.when(g // per_half != here)
        def _():
            send_ref[aligned(g % per_half, block), :] = result

        return carry

    lax.fori_loop(0, count // block, query_block, 0)


def attention(half_index, seg, own, x, wq, wk, wv):
    half, width = own.shape[0], wq.shape[1]
    count, pairs = 2 * half, width // PAIR
    return pl.pallas_call(
        attention_kernel,
        out_shape=(
            jax.ShapeDtypeStruct((count, 3 * width), BF16),
            jax.ShapeDtypeStruct((half, width), BF16),
            jax.ShapeDtypeStruct((half, width), BF16),
            jax.ShapeDtypeStruct((count, width), F32),
            jax.ShapeDtypeStruct((2, count // BLOCK), jnp.int32),
        )
        + (jax.ShapeDtypeStruct((count, 2 * count), BF16),) * pairs,
        in_specs=[SM, SM] + [VM] * 3 + [HB] * 3,
        out_specs=(VM,) * 4 + (SM,) + (VM,) * pairs,
        scratch_shapes=[
            pltpu.VMEM((1, count), F32),
            pltpu.VMEM((count, 128), F32),
            pltpu.VMEM((pairs, 2 * count, PAIR), BF16),
            pltpu.VMEM((pairs, 2 * count, PAIR), BF16),
            pltpu.VMEM((pairs, BLOCK, 2 * count), F32),
            pltpu.VMEM((2 * pairs, BLOCK, 128), F32),
            pltpu.VMEM((2 * pairs, BLOCK, 128), F32),
            pltpu.VMEM((BLOCK, width), F32),
        ]
        + [pltpu.VMEM(wq.shape, BF16)] * 3
        + [pltpu.SemaphoreType.DMA((3,))],
        compiler_params=pltpu.CompilerParams(vmem_limit_bytes=40 * MIB),
        cost_estimate=pl.CostEstimate(flops=10**10, bytes_accessed=8 * MIB, transcendentals=10**6),
        name="attention",
    )(half_index, seg, seg, own, x, wq, wk, wv)


def pair_grad_kernel(
    p, half_ref, rng_ref, qkv_ref, keep_ref, send_ref, own_ref, other_ref, inverse_ref, share_ref,
    dq_ref, dk_ref, dv_ref,
    keys, values, grad, turned_grad, turned_query, delta, dq, dk, dv,
):
    half = own_ref.shape[0]
    count, block = qkv_ref.shape[0], BLOCK
    width = keep_ref.shape[1]
    cols = slice(p * PAIR, (p + 1) * PAIR)
    here, there = half_ref[0], 1 - half_ref[0]
    lane = lax.broadcasted_iota(jnp.int32, (half, PAIR), 1)
    for which, mixed_ref, up_ref in ((here, keep_ref, own_ref), (there, send_ref, other_ref)):
        rows = aligned(which, half)
        scaled = (up_ref[:, cols].astype(F32) * inverse_ref[rows, cols]).astype(BF16)
        grad[rows, :] = scaled
        product = mixed_ref[:, cols].astype(F32) * scaled.astype(F32)
        for a in range(2):
            side = jnp.where(lane // HEAD_DIM == a, product, 0.0)
            delta[a, rows, :] = jnp.broadcast_to(jnp.sum(side, -1, keepdims=True), (half, PAIR))
    stack_heads(qkv_ref[:, width + p * PAIR : width + (p + 1) * PAIR], keys, block)
    stack_heads(qkv_ref[:, 2 * width + p * PAIR : 2 * width + (p + 1) * PAIR], values, block)
    turned_grad[...] = grad[...].T
    turned_query[...] = qkv_ref[:, cols].T
    dk[...] = jnp.zeros(dk.shape, F32)
    dv[...] = jnp.zeros(dv.shape, F32)

    def query_block(g, carry):
        rows = aligned(g, block)
        low, high = rng_ref[0, g], rng_ref[1, g]
        dq[...] = jnp.zeros(dq.shape, F32)

        def key_block(j, c):
            both = aligned(j, 2 * block)
            span = aligned(j, block)
            d2 = dot_nt(grad[rows, :], values[both, :])
            shares = share_ref[rows, both]
            slopes = []
            for a in range(2):
                side = slice(a * block, (a + 1) * block)
                level = jnp.concatenate([delta[a, rows, :]] * (block // 128), 1)
                slopes.append((shares[:, side].astype(F32) * (d2[:, side] - level)).astype(BF16))
            dq[...] += dot(jnp.concatenate(slopes, 1), keys[both, :])
            for a in range(2):
                head = slice(a * HEAD_DIM, (a + 1) * HEAD_DIM)
                dv[head, span] += dot(turned_grad[head, rows], shares[:, a * block : (a + 1) * block])
                dk[head, span] += dot(turned_query[head, rows], slopes[a])
            return c

        lax.fori_loop(low, high, key_block, 0)
        dq_ref[rows, :] = (dq[...] * HEAD_DIM**-0.5).astype(BF16)
        return carry

    lax.fori_loop(0, count // block, query_block, 0)
    dk_ref[...] = (dk[...] * LN2).T.astype(BF16)
    dv_ref[...] = dv[...].T.astype(BF16)


def pair_grad(p, half_index, rng, qkv, keep, send, own, other, inverse, shares):
    half = own.shape[0]
    count = 2 * half
    return pl.pallas_call(
        functools.partial(pair_grad_kernel, p),
        out_shape=(jax.ShapeDtypeStruct((count, PAIR), BF16),) * 3,
        in_specs=[SM, SM] + [VM] * 7,
        out_specs=(VM,) * 3,
        scratch_shapes=[pltpu.VMEM((2 * count, PAIR), BF16)] * 2
        + [
            pltpu.VMEM((count, PAIR), BF16),
            pltpu.VMEM((PAIR, count), BF16),
            pltpu.VMEM((PAIR, count), BF16),
            pltpu.VMEM((2, count, PAIR), F32),
            pltpu.VMEM((BLOCK, PAIR), F32),
            pltpu.VMEM((PAIR, count), F32),
            pltpu.VMEM((PAIR, count), F32),
        ],
        compiler_params=pltpu.CompilerParams(vmem_limit_bytes=16 * MIB),
        cost_estimate=pl.CostEstimate(flops=4 * 10**9, bytes_accessed=8 * MIB, transcendentals=0),
        name=f"pair_grad_{p}",
    )(half_index, rng, qkv, keep, send, own, other, inverse, shares)


def input_part(half_ref, flip, pieces, weights, half):
    which = 1 - half_ref[0] if flip else half_ref[0]
    rows = aligned(which, half)
    left = jnp.concatenate([piece[rows, :] for piece in pieces], 1)
    right = jnp.concatenate([weight[...] for weight in weights], 1)
    return dot_nt(left, right)


def away_kernel(half_ref, *refs):
    out_ref = refs[-1]
    out_ref[...] = input_part(half_ref, True, refs[:-4], refs[-4:-1], out_ref.shape[0]).astype(BF16)


def home_kernel(half_ref, first_ref, got_ref, *refs):
    out_ref = refs[-1]
    part = input_part(half_ref, False, refs[:-4], refs[-4:-1], out_ref.shape[0])
    out_ref[...] = (part + first_ref[...] + got_ref[...].astype(F32)).astype(BF16)


def input_call(kernel, half_index, extra, pieces, weights, name):
    half, features = pieces[0].shape[0] // 2, weights[0].shape[0]
    return pl.pallas_call(
        kernel,
        out_shape=jax.ShapeDtypeStruct((half, features), BF16),
        in_specs=[SM] + [VM] * (len(extra) + len(pieces) + len(weights)),
        out_specs=VM,
        compiler_params=pltpu.CompilerParams(vmem_limit_bytes=16 * MIB),
        cost_estimate=pl.CostEstimate(flops=10**9, bytes_accessed=6 * MIB, transcendentals=0),
        name=name,
    )(half_index, *extra, *pieces, *weights)


def gelu_both(v):
    part = 0.5 + 0.5 * lax.erf(v * ROOT_HALF)
    return v * part, part + v * jnp.exp(-0.5 * v * v) * ROOT_TWO_PI


def norm(values, gain, shift):
    mean = jnp.mean(values, -1, keepdims=True)
    centred = values - mean
    reciprocal = lax.rsqrt(jnp.mean(centred * centred, -1, keepdims=True) + EPS)
    normed = centred * reciprocal
    return normed * gain + shift, normed, reciprocal


def norm_grad(upstream, normed, reciprocal, gain):
    scaled = upstream * gain
    return reciprocal * (
        scaled - jnp.mean(scaled, -1, keepdims=True) - normed * jnp.mean(scaled * normed, -1, keepdims=True)
    )


def column_sum(values):
    return jnp.sum(values, 0, keepdims=True)


def middle_kernel(
    half_ref, x_ref, keep_ref, got_ref, up_ref,
    mdb_ref, mub_ref, ddb_ref, dub_ref, fg_ref, fs_ref, sg_ref, ss_ref,
    wo_hbm, wo2_hbm, md_hbm, mu_hbm, w1_hbm, w12_hbm, w2_hbm, w22_hbm, dd_hbm, du_hbm,
    act_hbm, first_ref, own_ref, away_ref, mine_ref, theirs_ref,
    wo_ref, wo2_ref, md_ref, mu_ref, w1_ref, w12_ref, w2_ref, w22_ref, dd_ref, du_ref,
    slope_ref, hidden_ref, normed_ref, act_ref, big_ref, small_ref, sems, act_sem,
):
    rows, features = x_ref.shape
    adapt = md_ref.shape[0]
    names = ("wo", "wo2", "md", "mu", "w1", "w2", "w12", "w22", "dd", "du")
    waits = dict(
        zip(
            names,
            start_all(
                (wo_hbm, wo2_hbm, md_hbm, mu_hbm, w1_hbm, w2_hbm, w12_hbm, w22_hbm, dd_hbm, du_hbm),
                (wo_ref, wo2_ref, md_ref, mu_ref, w1_ref, w2_ref, w12_ref, w22_ref, dd_ref, du_ref),
                sems,
            ),
        )
    )

    def vector(ref):
        return ref[...].astype(F32).reshape(1, -1)

    x = x_ref[...].astype(F32)
    waits["wo"].wait()
    attended = dot(keep_ref[...], wo_ref[...])
    waits["wo2"].wait()
    attended = attended + dot(got_ref[...], wo2_ref[...])
    attended_low = attended.astype(BF16)
    waits["md"].wait()
    waits["mu"].wait()
    mixer_active, mixer_slope = gelu_both(dot_nt(attended_low, md_ref[...]) + vector(mdb_ref))
    mixer_active = mixer_active.astype(BF16)
    mixer_out = dot(mixer_active, mu_ref[...]) + vector(mub_ref)
    hidden, normed_one, reciprocal_one = norm(x + attended + mixer_out, vector(fg_ref), vector(fs_ref))
    normed_ref[...] = normed_one
    hidden_ref[...] = hidden
    mixer_square = jnp.sum(column_sum(mixer_out * mixer_out), -1, keepdims=True)
    input_square = jnp.sum(column_sum(x * x), -1, keepdims=True)
    hidden_low = hidden.astype(BF16)
    chunk = 512
    units = w1_ref.shape[1]
    sides = ((w1_ref, w2_ref, "w1", "w2"), (w12_ref, w22_ref, "w12", "w22"))
    dense_in = jnp.zeros((rows, features), F32)
    for s, (win, wout, first, second) in enumerate(sides):
        waits[first].wait()
        waits[second].wait()
        for c in range(units // chunk):
            span = slice(c * chunk, (c + 1) * chunk)
            value, slope = gelu_both(dot(hidden_low, win[:, span]))
            slope_ref[:, s * units + c * chunk : s * units + (c + 1) * chunk] = slope.astype(BF16)
            dense_in = dense_in + dot(value.astype(BF16), wout[span, :])
    dense_low = dense_in.astype(BF16)
    waits["dd"].wait()
    waits["du"].wait()
    dense_active, dense_slope = gelu_both(dot_nt(dense_low, dd_ref[...]) + vector(ddb_ref))
    dense_active = dense_active.astype(BF16)
    dense_out = dot(dense_active, du_ref[...]) + vector(dub_ref)
    second_gain = vector(sg_ref)
    result, normed_two, reciprocal_two = norm(hidden_ref[...] + dense_in + dense_out, second_gain, vector(ss_ref))
    act_ref[...] = result.astype(BF16)
    act_copy = pltpu.make_async_copy(act_ref, act_hbm, act_sem)
    act_copy.start()
    dense_square = jnp.sum(column_sum(dense_out * dense_out), -1, keepdims=True)

    upstream = up_ref[...].astype(F32)
    small_ref[4:5, :] = column_sum(upstream * normed_two)
    small_ref[5:6, :] = column_sum(upstream)
    second_grad = norm_grad(upstream, normed_two, reciprocal_two, second_gain)
    dense_top = second_grad.astype(BF16)
    big_ref[3 * adapt : 4 * adapt, :] = dot_tn(dense_active, dense_top).astype(BF16)
    small_ref[1:2, :] = column_sum(dense_top.astype(F32))
    dense_mid = (dot_nt(dense_top, du_ref[...]) * dense_slope).astype(BF16)
    big_ref[2 * adapt : 3 * adapt, :] = dot_tn(dense_mid, dense_low).astype(BF16)
    dense_mid_sum = column_sum(dense_mid.astype(F32))
    dense_in_grad = (second_grad + dot(dense_mid, dd_ref[...])).astype(BF16)
    hidden_grad = second_grad
    for s, (win, wout, _, _) in enumerate(sides):
        for c in range(units // chunk):
            span = slice(c * chunk, (c + 1) * chunk)
            slope = slope_ref[:, s * units + c * chunk : s * units + (c + 1) * chunk].astype(F32)
            inner_grad = (dot_nt(dense_in_grad, wout[span, :]) * slope).astype(BF16)
            hidden_grad = hidden_grad + dot_nt(inner_grad, win[:, span])
    normed_one = normed_ref[...]
    small_ref[2:3, :] = column_sum(hidden_grad * normed_one)
    small_ref[3:4, :] = column_sum(hidden_grad)
    first_grad = norm_grad(hidden_grad, normed_one, reciprocal_one, vector(fg_ref))
    first_ref[...] = first_grad
    mixer_top = first_grad.astype(BF16)
    big_ref[adapt : 2 * adapt, :] = dot_tn(mixer_active, mixer_top).astype(BF16)
    small_ref[0:1, :] = column_sum(mixer_top.astype(F32))
    mixer_mid = (dot_nt(mixer_top, mu_ref[...]) * mixer_slope).astype(BF16)
    big_ref[0:adapt, :] = dot_tn(mixer_mid, attended_low).astype(BF16)
    mixer_mid_sum = column_sum(mixer_mid.astype(F32))
    attended_grad = (first_grad + dot(mixer_mid, md_ref[...])).astype(BF16)
    own_ref[...] = dot_nt(attended_grad, wo_ref[...]).astype(BF16)
    away_ref[...] = dot_nt(attended_grad, wo2_ref[...]).astype(BF16)
    lane = lax.broadcasted_iota(jnp.int32, (1, 128), 1)
    squares = jnp.where(lane == 0, mixer_square, jnp.where(lane == 1, dense_square, jnp.where(lane == 2, input_square, 0.0)))
    small_ref[6:7, :] = jnp.concatenate(
        [mixer_mid_sum, dense_mid_sum, squares, jnp.zeros((1, features - 2 * adapt - 128), F32)], 1
    )
    small_ref[7:8, :] = jnp.zeros((1, features), F32)
    tail = tail_of(small_ref[...])
    share = 2 * adapt
    for out_ref, which in ((mine_ref, half_ref[0]), (theirs_ref, 1 - half_ref[0])):
        out_ref[:share, :] = big_ref[aligned(which, share), :]
        out_ref[share:, :] = tail
    act_copy.wait()


def tail_of(vectors):
    high = vectors.astype(BF16)
    return jnp.concatenate([high, (vectors - high.astype(F32)).astype(BF16)], 0)


def vectors_of(tail):
    wide = tail.astype(F32)
    return wide[:8] + wide[8:]


def middle(half_index, x, keep, got, up, vectors, matrices):
    rows, features = x.shape
    width = keep.shape[1]
    adapt = matrices[2].shape[0]
    units = matrices[4].shape[1]
    packed = jax.ShapeDtypeStruct((2 * adapt + 16, features), BF16)
    return pl.pallas_call(
        middle_kernel,
        out_shape=(
            jax.ShapeDtypeStruct((rows, features), BF16),
            jax.ShapeDtypeStruct((rows, features), F32),
            jax.ShapeDtypeStruct((rows, width), BF16),
            jax.ShapeDtypeStruct((rows, width), BF16),
            packed,
            packed,
        ),
        in_specs=[SM] + [VM] * 12 + [HB] * 10,
        out_specs=(HB,) + (VM,) * 5,
        scratch_shapes=[pltpu.VMEM(m.shape, BF16) for m in matrices]
        + [
            pltpu.VMEM((rows, 2 * units), BF16),
            pltpu.VMEM((rows, features), F32),
            pltpu.VMEM((rows, features), F32),
            pltpu.VMEM((rows, features), BF16),
            pltpu.VMEM((4 * adapt, features), BF16),
            pltpu.VMEM((8, features), F32),
            pltpu.SemaphoreType.DMA((10,)),
            pltpu.SemaphoreType.DMA,
        ],
        compiler_params=pltpu.CompilerParams(vmem_limit_bytes=40 * MIB),
        cost_estimate=pl.CostEstimate(flops=2 * 10**10, bytes_accessed=16 * MIB, transcendentals=10**6),
        name="middle",
    )(half_index, x, keep, got, up, *vectors, *matrices)


def combine_kernel(held_ref, got_ref, out_ref):
    rows = held_ref.shape[0] - 16
    out_ref[:rows, :] = (held_ref[:rows, :].astype(F32) + got_ref[:rows, :].astype(F32)).astype(BF16)
    out_ref[rows:, :] = tail_of(vectors_of(held_ref[rows:, :]) + vectors_of(got_ref[rows:, :]))


def combine(held, got):
    return pl.pallas_call(
        combine_kernel,
        out_shape=jax.ShapeDtypeStruct(held.shape, BF16),
        in_specs=[VM] * 2,
        out_specs=VM,
        compiler_params=pltpu.CompilerParams(vmem_limit_bytes=4 * MIB),
        cost_estimate=pl.CostEstimate(flops=10**5, bytes_accessed=MIB, transcendentals=0),
        name="combine",
    )(held, got)


def finish_kernel(half_ref, held_ref, got_ref, md_ref, mu_ref, dd_ref, du_ref, vec_ref, bias_ref, ratio_ref):
    adapt = md_ref.shape[0]

    def write(first_ref, second_ref):
        md_ref[...] = first_ref[:adapt, :].astype(F32)
        mu_ref[...] = first_ref[adapt : 2 * adapt, :].astype(F32)
        dd_ref[...] = second_ref[:adapt, :].astype(F32)
        du_ref[...] = second_ref[adapt : 2 * adapt, :].astype(F32)

    @pl.when(half_ref[0] == 0)
    def _():
        write(held_ref, got_ref)

    @pl.when(half_ref[0] != 0)
    def _():
        write(got_ref, held_ref)

    vectors = vectors_of(held_ref[2 * adapt :, :])
    vec_ref[...] = vectors
    last = vectors[6:7, :]
    bias_ref[0:1, :] = last[:, :adapt]
    bias_ref[1:2, :] = last[:, adapt : 2 * adapt]
    squares = last[:, 2 * adapt : 2 * adapt + 128]
    lane = lax.broadcasted_iota(jnp.int32, (1, 128), 1)
    base = jnp.sum(jnp.where(lane == 2, squares, 0.0), -1, keepdims=True)
    ratio_ref[...] = jnp.sqrt(squares / base)


def finish(half_index, held, got, adapt):
    features = held.shape[1]
    matrix = jax.ShapeDtypeStruct((adapt, features), F32)
    return pl.pallas_call(
        finish_kernel,
        out_shape=(matrix,) * 4
        + (
            jax.ShapeDtypeStruct((8, features), F32),
            jax.ShapeDtypeStruct((2, adapt), F32),
            jax.ShapeDtypeStruct((1, 128), F32),
        ),
        in_specs=[SM, VM, VM],
        out_specs=(VM,) * 7,
        compiler_params=pltpu.CompilerParams(vmem_limit_bytes=4 * MIB),
        name="finish",
    )(half_index, held, got)


def swap_cores(value):
    return lax.ppermute(value, "mp", [(0, 1), (1, 0)])


def tie(*values):
    return lax.optimization_barrier(values)


def per_device(
    tokens, segment_ids, query_weight, key_weight, value_weight, output_weight, inner_weight, outer_weight,
    mixer_down, mixer_down_bias, mixer_up, mixer_up_bias, dense_down, dense_down_bias, dense_up, dense_up_bias,
    first_gain, first_shift, second_gain, second_shift, output_grad,
):
    half_index = lax.axis_index("mp").astype(jnp.int32).reshape(1)
    devices = lax.axis_size("dp")
    adapt = mixer_down.shape[1]
    other_tokens = swap_cores(tokens)
    own = project(tokens, query_weight, key_weight, value_weight)
    other_tokens, output_late, inner_late, outer_late = tie(other_tokens, output_weight, inner_weight, outer_weight)
    other_output = swap_cores(output_late)
    other_inner = swap_cores(inner_late)
    other_outer = swap_cores(outer_late)
    qkv, keep, send, inverse, rng, *shares = attention(
        half_index, segment_ids, own, other_tokens, query_weight, key_weight, value_weight
    )
    got = swap_cores(send)
    vectors = (
        mixer_down_bias, mixer_up_bias, dense_down_bias, dense_up_bias, first_gain, first_shift, second_gain, second_shift,
    )
    matrices = (
        output_weight, other_output, mixer_down.T, mixer_up,
        inner_weight, other_inner, outer_weight, other_outer, dense_down.T, dense_up,
    )
    result, first_grad, own_grad, away_grad, mine, theirs = middle(
        half_index, tokens, keep, got, output_grad, vectors, matrices
    )
    got_grad = swap_cores(away_grad)
    packed = combine(mine, swap_cores(theirs))

    steps = []
    while 2 ** len(steps) < devices:
        steps.append(2 ** len(steps))
    steps.reverse()
    pairs = len(shares)
    grads = []
    away = None
    weights = (query_weight, key_weight, value_weight)
    for n, step in enumerate(steps):
        arriving = lax.ppermute(packed, "dp", [(i, i ^ step) for i in range(devices)])
        if n < pairs:
            got_grad, packed = tie(got_grad, packed)
            parts = pair_grad(n, half_index, rng, qkv, keep, send, own_grad, got_grad, inverse, shares[n])
            arriving, *parts = tie(arriving, *parts)
            grads.append(parts)
        elif n == pairs:
            pieces = [grads[p][i] for i in range(3) for p in range(pairs)]
            away = swap_cores(input_call(away_kernel, half_index, (), pieces, weights, "away"))
            input_grad = input_call(home_kernel, half_index, (first_grad, away), pieces, weights, "home")
            arriving, input_grad = tie(arriving, input_grad)
        packed = combine(packed, arriving)
    md, mu, dd, du, vec, bias, ratio = finish(half_index, packed, swap_cores(packed), adapt)
    return (
        result, input_grad, md.T, bias[0], mu, vec[0], dd.T, bias[1], du, vec[1], vec[2], vec[3], vec[4], vec[5], ratio[0, :2],
    )


def solution(mesh):
    tokens = P(("dp", "mp"), None)
    columns, rows, whole = P(None, "mp"), P("mp", None), P()
    return jax.shard_map(
        per_device,
        mesh=mesh,
        in_specs=(tokens, P("dp", None), columns, columns, columns, rows, columns, rows) + (whole,) * 12 + (tokens,),
        out_specs=(tokens, tokens) + (whole,) * 13,
        check_vma=False,
    )
```

time: 122 us -> 103 us (0.84)
  local copies, waits for them, and re-layouts: 21.3 us -> 10.3 us
  other arithmetic: 7.12 us -> 0 us
  Pallas kernels: 63 us -> 68.6 us
  waiting for transfers between devices: 18.6 us -> 13.3 us
    ppermute x4, waiting for transfers between devices: 17.2 us -> 5.34 us  [per_device(): lax.ppermute(packed, 'dp', [(i, i ^ step) for i in range(devices)])]
    ppermute x9, waiting for transfers between devices: 1.4 us -> 7.93 us  [swap_cores(): return lax.ppermute(value, 'mp', [(0, 1), (1, 0)])]
    convert_element_type x22 -> x0, other arithmetic: 5.56 us -> none  [the longest x4 2.07 us: reduce_gradients(): packed = jnp.concatenate([total.astype(BF16), *high_low(vector)], 0)]
    pallas_call x1, Pallas kernels: 15.2 us -> 19.8 us  [attention(): pl.pallas_call(attention_kernel, out_shape=(jax.ShapeDtypeStruct((count,...]
    slice x6 -> x1, local copies, waits for them, and re-layouts: 4.3 us -> 0.64 us  [per_device(): vec[5]]
    reshape x6 -> x0, local copies, waits for them, and re-layouts: 3.49 us -> none  [per_device(): row = lambda v: v.reshape(1, -1)]
    unnamed x48 -> x58, local copies, waits for them, and re-layouts: 12 us -> 8.64 us
    pallas_call x1 -> x11, Pallas kernels: 21.9 us -> 24.7 us  [the longest x3 20.1 us: pair_grad(): pl.pallas_call(functools.partial(pair_grad_kernel, p), out_shape=(jax.Sha...]
  transfers between devices with their start and end apart: 13 -> 13, of which waited for: 4 -> 7; matrix products, arithmetic and copies ran while one was open for 11% -> 0% of each run, Pallas kernels for 32% -> 43%
where the time goes in v2:
time: 103 us
  Pallas kernels  68.6 us (67%)
  waiting for transfers between devices  13.3 us (13%)
  local copies, waits for them, and re-layouts  10.3 us (10%)
  starting transfers between devices  9.51 us (9%)
  between operations  1.06 us (1%)
    pallas_call x1, Pallas kernels, middle(): pl.pallas_call(middle_kernel, out_shape=(jax.ShapeDtypeStruct((rows, feat...  21.8 us
    pallas_call x3, Pallas kernels, pair_grad(): pl.pallas_call(functools.partial(pair_grad_kernel, p), out_shape=(jax.Sha...  20.1 us
    pallas_call x1, Pallas kernels, attention(): pl.pallas_call(attention_kernel, out_shape=(jax.ShapeDtypeStruct((count,...  19.8 us
    unnamed x58, local copies, waits for them, and re-layouts  8.64 us
    ppermute x9, waiting for transfers between devices, swap_cores(): return lax.ppermute(value, 'mp', [(0, 1), (1, 0)])  7.93 us
    ppermute x4, starting transfers between devices, per_device(): lax.ppermute(packed, 'dp', [(i, i ^ step) for i in range(devices)])  7.19 us
    ppermute x4, waiting for transfers between devices, per_device(): lax.ppermute(packed, 'dp', [(i, i ^ step) for i in range(devices)])  5.34 us
    pallas_call x2, Pallas kernels, input_call(): pl.pallas_call(kernel, out_shape=jax.ShapeDtypeStruct((half, features), B...  3.35 us
  transfers between devices with their start and end apart: 13, of which 7 were waited for; matrix products, arithmetic and copies ran while one was open for 0% of the time, Pallas kernels for 43%

profile of v2, /device:TPU:0, one launch (start us, length us, event | category | flops | bytes accessed | tf_op | source)
XLA Modules:
  0.0 102.7 jit_solution(12159231700588115314)
XLA Ops:
  1.2 2.1 %collective-permute-done.x_ref = bf16[512,768]{1,0:T(8,128)(2,1)S(1)} collective-permute-done((bf16[512,768]{1,0:T(8,128)(2,1)}, bf16[512,768]{1,0:T(8,128)(2,1)S(1)}, u32[]{:S(2)}, u32[]{:S(2)}) %collective-permute-start) | collective-permute-done | bytes 786464 | tf_op jit(solution)/shard_map/ppermute | solution.py:585
  3.8 1.1 %copy-done = bf16[768,384]{1,0:T(8,128)(2,1)S(1)} copy-done((bf16[768,384]{1,0:T(8,128)(2,1)S(1)}, bf16[768,384]{1,0:T(8,128)(2,1)}, u32[]{:S(2)}) %copy-start) | copy-done | bytes 589848
  4.9 1.1 %copy-done.2 = bf16[768,384]{1,0:T(8,128)(2,1)S(1)} copy-done((bf16[768,384]{1,0:T(8,128)(2,1)S(1)}, bf16[768,384]{1,0:T(8,128)(2,1)}, u32[]{:S(2)}) %copy-start.2) | copy-done | bytes 589848
  5.9 1.1 %copy-done.4 = bf16[768,384]{1,0:T(8,128)(2,1)S(1)} copy-done((bf16[768,384]{1,0:T(8,128)(2,1)S(1)}, bf16[768,384]{1,0:T(8,128)(2,1)}, u32[]{:S(2)}) %copy-start.4) | copy-done | bytes 589848
  7.0 1.1 %copy-done.6 = bf16[512,768]{1,0:T(8,128)(2,1)S(1)} copy-done((bf16[512,768]{1,0:T(8,128)(2,1)S(1)}, bf16[512,768]{1,0:T(8,128)(2,1)}, u32[]{:S(2)}) %copy-start.6) | copy-done | bytes 786456
  8.1 2.2 %project.1.own_ref = bf16[512,1152]{1,0:T(8,128)(2,1)S(1)} custom-call(bf16[512,768]{1,0:T(8,128)(2,1)S(1)} %copy-done.6, bf16[768,384]{1,0:T(8,128)(2,1)S(1)} %copy-done, bf16[768,384]{1,0:T(8,128)(2,1)S(1)} %copy-done.2, bf16[768,384]{1,0:T(8,128)(2,1)S(1)} %copy-done.4), custom_call_target="tpu_custom_call" | custom-call | flops 905969664 | bytes 5242880 | tf_op jit(solution)/shard_map/project/pallas_call | solution.py:89
  11.0 19.8 %attention.1 = (bf16[1024,1152]{1,0:T(8,128)(2,1)S(1)}, bf16[512,384]{1,0:T(8,128)(2,1)S(1)}, bf16[512,384]{1,0:T(8,128)(2,1)S(1)}, f32[1024,384]{1,0:T(8,128)S(...) custom-call(s32[1]{0:T(128)} %bitcast.half_ref, ...), custom_call_target="tpu_custom_call" | custom-call | flops 10000000000 | bytes 8388608 | tf_op jit(solution)/shard_map/attention/pallas_call | solution.py:195
  30.9 2.0 %copy-done.27 = bf16[1024,2048]{1,0:T(8,128)(2,1)} copy-done((bf16[1024,2048]{1,0:T(8,128)(2,1)}, bf16[1024,2048]{1,0:T(8,128)(2,1)S(1)}, u32[]{:S(2)}) %copy-start.27) | copy-done | bytes 4194328
  33.0 1.6 %collective-permute-done.1.got_ref = bf16[512,384]{1,0:T(8,128)(2,1)S(1)} collective-permute-done((bf16[512,384]{1,0:T(8,128)(2,1)S(1)}, bf16[512,384]{1,0:T(8,128)(2,1)S(1)}, u32[]{:S(2)}, u32[]{:S(2)}) %collective-permute-start.1) | collective-permute-done | bytes 393248 | tf_op jit(solution)/shard_map/ppermute | solution.py:585
  34.8 21.8 %middle.1 = (bf16[512,768]{1,0:T(8,128)(2,1)}, f32[512,768]{1,0:T(8,128)S(1)}, bf16[512,384]{1,0:T(8,128)(2,1)S(1)}, bf16[512,384]{1,0:T(8,128)(2,1)S(1)}, bf16[...) custom-call(s32[1]{0:T(128)} %bitcast.half_ref, bf16[512,768]{1,0:T(8,128)(2,1)S(1)} %copy-done.7, ...), custom_call_target="tpu_custom_call" | custom-call | flops 20000000000 | bytes 16777216 | tf_op jit(solution)/shard_map/middle/pallas_call | solution.py:491
  57.1 1.5 %collective-permute-done.6.got_ref = bf16[144,768]{1,0:T(8,128)(2,1)S(1)} collective-permute-done((bf16[144,768]{1,0:T(8,128)(2,1)S(1)}, bf16[144,768]{1,0:T(8,128)(2,1)S(1)}, u32[]{:S(2)}, u32[]{:S(2)}) %collective-permute-start.6) | collective-permute-done | bytes 221216 | tf_op jit(solution)/shard_map/ppermute | solution.py:585
  58.7 3.8 %collective-permute-start.7 = (bf16[144,768]{1,0:T(8,128)(2,1)S(1)}, bf16[144,768]{1,0:T(8,128)(2,1)S(1)}, u32[]{:S(2)}, u32[]{:S(2)}) collective-permute-start(bf16[144,768]{1,0:T(8,128)(2,1)S(1)} %combine.5.held_ref), channel_id=1, source_target_pairs={{0,16},{2,18},{4,20},{6,22},{8,24},{10,26},{12,28},{14,30},{16,0},... | collective-permute-start | bytes 663560 | tf_op jit(solution)/shard_map/ppermute | solution.py:632
  62.5 2.2 %copy-done.28 = bf16[1024,2048]{1,0:T(8,128)(2,1)S(1)} copy-done((bf16[1024,2048]{1,0:T(8,128)(2,1)S(1)}, bf16[1024,2048]{1,0:T(8,128)(2,1)}, u32[]{:S(2)}) %copy-start.28) | copy-done | bytes 4194328
  64.7 6.7 %pair_grad_0.1 = (bf16[1024,128]{1,0:T(8,128)(2,1)S(1)}, bf16[1024,128]{1,0:T(8,128)(2,1)S(1)}, bf16[1024,128]{1,0:T(8,128)(2,1)S(1)}) custom-call(s32[1]{0:T(128)} %bitcast.half_ref, s32[2,4]{1,0:T(2,128)S(1)} %get-tuple-element.81.rng_ref, bf16[1024,1152]{1,0:T(8,128)(2,1)S(1)} %get-tuple-element.82.qkv_ref, ...), custom_call_target="tpu_custom_call" | custom-call | flops 4000000000 | bytes 8388608 | tf_op jit(solution)/shard_map/pair_grad_0/pallas_call | solution.py:285
  71.4 1.8 %collective-permute-done.7.got_ref = bf16[144,768]{1,0:T(8,128)(2,1)S(1)} collective-permute-done((bf16[144,768]{1,0:T(8,128)(2,1)S(1)}, bf16[144,768]{1,0:T(8,128)(2,1)S(1)}, u32[]{:S(2)}, u32[]{:S(2)}) %collective-permute-start.7) | collective-permute-done | bytes 221216 | tf_op jit(solution)/shard_map/ppermute | solution.py:632
  74.1 6.7 %pair_grad_1.1 = (bf16[1024,128]{1,0:T(8,128)(2,1)S(1)}, bf16[1024,128]{1,0:T(8,128)(2,1)S(1)}, bf16[1024,128]{1,0:T(8,128)(2,1)S(1)}) custom-call(s32[1]{0:T(128)} %bitcast.half_ref, s32[2,4]{1,0:T(2,128)S(1)} %get-tuple-element.81.rng_ref, bf16[1024,1152]{1,0:T(8,128)(2,1)S(1)} %get-tuple-element.82.qkv_ref, ...), custom_call_target="tpu_custom_call" | custom-call | flops 4000000000 | bytes 8388608 | tf_op jit(solution)/shard_map/pair_grad_1/pallas_call | solution.py:285
  80.9 1.6 %collective-permute-start.9 = (bf16[144,768]{1,0:T(8,128)(2,1)S(1)}, bf16[144,768]{1,0:T(8,128)(2,1)S(1)}, u32[]{:S(2)}, u32[]{:S(2)}) collective-permute-start(bf16[144,768]{1,0:T(8,128)(2,1)S(1)} %combine.7.held_ref), channel_id=1, source_target_pairs={{0,4},{2,6},{4,0},{6,2},{8,12},{10,14},{12,8},{14,10},{16,20},{18,... | collective-permute-start | bytes 663560 | tf_op jit(solution)/shard_map/ppermute | solution.py:632
  82.5 6.7 %pair_grad_2.1 = (bf16[1024,128]{1,0:T(8,128)(2,1)S(1)}, bf16[1024,128]{1,0:T(8,128)(2,1)S(1)}, bf16[1024,128]{1,0:T(8,128)(2,1)S(1)}) custom-call(s32[1]{0:T(128)} %bitcast.half_ref, s32[2,4]{1,0:T(2,128)S(1)} %get-tuple-element.81.rng_ref, bf16[1024,1152]{1,0:T(8,128)(2,1)S(1)} %get-tuple-element.82.qkv_ref, ...), custom_call_target="tpu_custom_call" | custom-call | flops 4000000000 | bytes 8388608 | tf_op jit(solution)/shard_map/pair_grad_2/pallas_call | solution.py:285
  89.2 1.2 %away.1 = bf16[512,768]{1,0:T(8,128)(2,1)S(1)} custom-call(s32[1]{0:T(128)} %bitcast.half_ref, bf16[1024,128]{1,0:T(8,128)(2,1)S(1)} %get-tuple-element.105.refs_0_, bf16[1024,128]{1,0:T(8,128)(2,1)S(1)} %get-tuple-element.106.refs_1_, bf16[1024,128]{1,0:T(8,128)(2,1)S(1)} %get-tuple-element.107.refs_2_, bf16[1024,128]{1,0:T(8,128)(2,1)S(1)} %get-tuple-element.108.refs_3_, ...), custom_call_target="tpu_custom_call" | custom-call | flops 1000000000 | bytes 6291456 | tf_op jit(solution)/shard_map/away/pallas_call | solution.py:327
  90.6 1.0 collective-permute-start.10
  91.6 1.2 %collective-permute-done.11.got_ref = bf16[512,768]{1,0:T(8,128)(2,1)S(1)} collective-permute-done((bf16[512,768]{1,0:T(8,128)(2,1)S(1)}, bf16[512,768]{1,0:T(8,128)(2,1)S(1)}, u32[]{:S(2)}, u32[]{:S(2)}) %collective-permute-start.11) | collective-permute-done | bytes 786464 | tf_op jit(solution)/shard_map/ppermute | solution.py:585
  92.8 2.1 %home.1 = bf16[512,768]{1,0:T(8,128)(2,1)} custom-call(s32[1]{0:T(128)} %bitcast.half_ref, f32[512,768]{1,0:T(8,128)S(1)} %get-tuple-element.104.first_ref, bf16[512,768]{1,0:T(8,128)(2,1)S(1)} %collective-permute-done.11.got_ref, bf16[1024,128]{1,0:T(8,128)(2,1)S(1)} %get-tuple-element.105.refs_0_, bf16[1024,128]{1,0:T(8,128)(2,1)S(1)} %get-tuple-element.106.refs_1_, ...), custom_call_target="tpu_custom_call" | custom-call | flops 1000000000 | bytes 6291456 | tf_op jit(solution)/shard_map/home/pallas_call | solution.py:327
  94.9 3.6 %collective-permute-done.10.got_ref = bf16[144,768]{1,0:T(8,128)(2,1)S(1)} collective-permute-done((bf16[144,768]{1,0:T(8,128)(2,1)S(1)}, bf16[144,768]{1,0:T(8,128)(2,1)S(1)}, u32[]{:S(2)}, u32[]{:S(2)}) %collective-permute-start.10) | collective-permute-done | bytes 221216 | tf_op jit(solution)/shard_map/ppermute | solution.py:632
  98.6 1.5 %collective-permute-done.12.got_ref = bf16[144,768]{1,0:T(8,128)(2,1)S(1)} collective-permute-done((bf16[144,768]{1,0:T(8,128)(2,1)S(1)}, bf16[144,768]{1,0:T(8,128)(2,1)S(1)}, u32[]{:S(2)}, u32[]{:S(2)}) %collective-permute-start.12) | collective-permute-done | bytes 221216 | tf_op jit(solution)/shard_map/ppermute | solution.py:585
  (77 shorter events, 6.2 us)
Async XLA Ops:
  0.7 2.6 %collective-permute-start = (bf16[512,768]{1,0:T(8,128)(2,1)}, bf16[512,768]{1,0:T(8,128)(2,1)S(1)}, u32[]{:S(2)}, u32[]{:S(2)}) collective-permute-start(bf16[512,768]{1,0:T(8,128)(2,1)} %x_ref.3), channel_id=1, source_target_pairs={{0,1},{1,0},{2,3},{3,2},{4,5},{5,4},{6,7},{7,6},{8,9},{9,8},{10,11... | collective-permute-start | bytes 2359304 | tf_op jit(solution)/shard_map/ppermute | solution.py:585
  3.3 31.3 %collective-permute-start.3 = (bf16[768,1536]{1,0:T(8,128)(2,1)}, bf16[768,1536]{1,0:T(8,128)(2,1)S(1)}, u32[]{:S(2)}, u32[]{:S(2)}) collective-permute-start(bf16[768,1536]{1,0:T(8,128)(2,1)} %w1_hbm.1), channel_id=1, source_target_pairs={{0,1},{1,0},{2,3},{3,2},{4,5},{5,4},{6,7},{7,6},{8,9},{9,8},{10,11... | collective-permute-start | bytes 7077896 | tf_op jit(solution)/shard_map/ppermute | solution.py:585
  3.7 30.9 %collective-permute-start.4 = (bf16[1536,768]{1,0:T(8,128)(2,1)}, bf16[1536,768]{1,0:T(8,128)(2,1)}, u32[]{:S(2)}, u32[]{:S(2)}) collective-permute-start(bf16[1536,768]{1,0:T(8,128)(2,1)} %w2_hbm.1), channel_id=1, source_target_pairs={{0,1},{1,0},{2,3},{3,2},{4,5},{5,4},{6,7},{7,6},{8,9},{9,8},{10,11... | collective-permute-start | bytes 7077896 | tf_op jit(solution)/shard_map/ppermute | solution.py:585
  10.4 24.2 %collective-permute-start.2 = (bf16[384,768]{1,0:T(8,128)(2,1)S(1)}, bf16[384,768]{1,0:T(8,128)(2,1)S(1)}, u32[]{:S(2)}, u32[]{:S(2)}) collective-permute-start(bf16[384,768]{1,0:T(8,128)(2,1)S(1)} %copy-done.11), channel_id=1, source_target_pairs={{0,1},{1,0},{2,3},{3,2},{4,5},{5,4},{6,7},{7,6},{8,9},{9,8},{10,11... | collective-permute-start | bytes 1769480 | tf_op jit(solution)/shard_map/ppermute | solution.py:585
  10.8 23.8 %copy-start.7 = (bf16[512,768]{1,0:T(8,128)(2,1)S(1)}, bf16[512,768]{1,0:T(8,128)(2,1)}, u32[]{:S(2)}) copy-start(bf16[512,768]{1,0:T(8,128)(2,1)} %x_ref.3) | copy-start | bytes 2359300
  10.8 23.8 %copy-start.8 = (bf16[768,1536]{1,0:T(8,128)(2,1)S(1)}, bf16[768,1536]{1,0:T(8,128)(2,1)}, u32[]{:S(2)}) copy-start(bf16[768,1536]{1,0:T(8,128)(2,1)} %w1_hbm.1) | copy-start | bytes 7077892
  10.9 23.8 %copy-start.9 = (bf16[1536,768]{1,0:T(8,128)(2,1)S(1)}, bf16[1536,768]{1,0:T(8,128)(2,1)}, u32[]{:S(2)}) copy-start(bf16[1536,768]{1,0:T(8,128)(2,1)} %w2_hbm.1) | copy-start | bytes 7077892
  10.9 23.8 %copy-start.10 = (bf16[512,768]{1,0:T(8,128)(2,1)S(1)}, bf16[512,768]{1,0:T(8,128)(2,1)}, u32[]{:S(2)}) copy-start(bf16[512,768]{1,0:T(8,128)(2,1)} %up_ref.1) | copy-start | bytes 2359300
  10.9 23.8 %copy-start.12 = (bf16[768,64]{0,1:T(8,128)(2,1)S(1)}, bf16[768,64]{0,1:T(8,128)(2,1)}, u32[]{:S(2)}) copy-start(bf16[768,64]{0,1:T(8,128)(2,1)} %param.29) | copy-start | bytes 294916
  10.9 23.8 %copy-start.13 = (bf16[64,768]{1,0:T(8,128)(2,1)S(1)}, bf16[64,768]{1,0:T(8,128)(2,1)}, u32[]{:S(2)}) copy-start(bf16[64,768]{1,0:T(8,128)(2,1)} %mu_hbm.1) | copy-start | bytes 294916
  10.9 23.8 %copy-start.14 = (bf16[768,64]{0,1:T(8,128)(2,1)S(1)}, bf16[768,64]{0,1:T(8,128)(2,1)}, u32[]{:S(2)}) copy-start(bf16[768,64]{0,1:T(8,128)(2,1)} %param.33) | copy-start | bytes 294916
  10.9 23.8 %copy-start.15 = (bf16[64,768]{1,0:T(8,128)(2,1)S(1)}, bf16[64,768]{1,0:T(8,128)(2,1)}, u32[]{:S(2)}) copy-start(bf16[64,768]{1,0:T(8,128)(2,1)} %du_hbm.1) | copy-start | bytes 294916
  10.9 23.8 %copy-start.17 = (bf16[768]{0:T(1024)(128)(2,1)S(1)}, bf16[768]{0:T(1024)(128)(2,1)}, u32[]{:S(2)}) copy-start(bf16[768]{0:T(1024)(128)(2,1)} %mub_ref.1) | copy-start | bytes 4612
  10.9 23.8 %copy-start.18 = (bf16[768]{0:T(1024)(128)(2,1)S(1)}, bf16[768]{0:T(1024)(128)(2,1)}, u32[]{:S(2)}) copy-start(bf16[768]{0:T(1024)(128)(2,1)} %dub_ref.1) | copy-start | bytes 4612
  11.0 23.8 %copy-start.19 = (bf16[768]{0:T(1024)(128)(2,1)S(1)}, bf16[768]{0:T(1024)(128)(2,1)}, u32[]{:S(2)}) copy-start(bf16[768]{0:T(1024)(128)(2,1)} %fg_ref.1) | copy-start | bytes 4612
  32.9 1.7 %collective-permute-start.1 = (bf16[512,384]{1,0:T(8,128)(2,1)S(1)}, bf16[512,384]{1,0:T(8,128)(2,1)S(1)}, u32[]{:S(2)}, u32[]{:S(2)}) collective-permute-start(bf16[512,384]{1,0:T(8,128)(2,1)S(1)} %get-tuple-element.71.send_ref), channel_id=1, source_target_pairs={{0,1},{1,0},{2,3},{3,2},{4,5},{5,4},{6,7},{7,6},{8,9},{9,8},{10,11... | collective-permute-start | bytes 1179656 | tf_op jit(solution)/shard_map/ppermute | solution.py:585
  56.6 6.0 %collective-permute-start.5 = (bf16[512,384]{1,0:T(8,128)(2,1)S(1)}, bf16[512,384]{1,0:T(8,128)(2,1)S(1)}, u32[]{:S(2)}, u32[]{:S(2)}) collective-permute-start(bf16[512,384]{1,0:T(8,128)(2,1)S(1)} %get-tuple-element.76), channel_id=1, source_target_pairs={{0,1},{1,0},{2,3},{3,2},{4,5},{5,4},{6,7},{7,6},{8,9},{9,8},{10,11... | collective-permute-start | bytes 1179656 | tf_op jit(solution)/shard_map/ppermute | solution.py:585
  56.8 1.9 %collective-permute-start.6 = (bf16[144,768]{1,0:T(8,128)(2,1)S(1)}, bf16[144,768]{1,0:T(8,128)(2,1)S(1)}, u32[]{:S(2)}, u32[]{:S(2)}) collective-permute-start(bf16[144,768]{1,0:T(8,128)(2,1)S(1)} %get-tuple-element.78), channel_id=1, source_target_pairs={{0,1},{1,0},{2,3},{3,2},{4,5},{5,4},{6,7},{7,6},{8,9},{9,8},{10,11... | collective-permute-start | bytes 663560 | tf_op jit(solution)/shard_map/ppermute | solution.py:585
  58.7 14.5 %collective-permute-start.7 = (bf16[144,768]{1,0:T(8,128)(2,1)S(1)}, bf16[144,768]{1,0:T(8,128)(2,1)S(1)}, u32[]{:S(2)}, u32[]{:S(2)}) collective-permute-start(bf16[144,768]{1,0:T(8,128)(2,1)S(1)} %combine.5.held_ref), channel_id=1, source_target_pairs={{0,16},{2,18},{4,20},{6,22},{8,24},{10,26},{12,28},{14,30},{16,0},... | collective-permute-start | bytes 663560 | tf_op jit(solution)/shard_map/ppermute | solution.py:632
  73.3 7.5 %collective-permute-start.8 = (bf16[144,768]{1,0:T(8,128)(2,1)S(1)}, bf16[144,768]{1,0:T(8,128)(2,1)S(1)}, u32[]{:S(2)}, u32[]{:S(2)}) collective-permute-start(bf16[144,768]{1,0:T(8,128)(2,1)S(1)} %combine.6.held_ref), channel_id=1, source_target_pairs={{0,8},{2,10},{4,12},{6,14},{8,0},{10,2},{12,4},{14,6},{16,24},{18,... | collective-permute-start | bytes 663560 | tf_op jit(solution)/shard_map/ppermute | solution.py:632
  80.9 8.3 %collective-permute-start.9 = (bf16[144,768]{1,0:T(8,128)(2,1)S(1)}, bf16[144,768]{1,0:T(8,128)(2,1)S(1)}, u32[]{:S(2)}, u32[]{:S(2)}) collective-permute-start(bf16[144,768]{1,0:T(8,128)(2,1)S(1)} %combine.7.held_ref), channel_id=1, source_target_pairs={{0,4},{2,6},{4,0},{6,2},{8,12},{10,14},{12,8},{14,10},{16,20},{18,... | collective-permute-start | bytes 663560 | tf_op jit(solution)/shard_map/ppermute | solution.py:632
  90.5 2.4 %collective-permute-start.11 = (bf16[512,768]{1,0:T(8,128)(2,1)S(1)}, bf16[512,768]{1,0:T(8,128)(2,1)S(1)}, u32[]{:S(2)}, u32[]{:S(2)}) collective-permute-start(bf16[512,768]{1,0:T(8,128)(2,1)S(1)} %away.1), channel_id=1, source_target_pairs={{0,1},{1,0},{2,3},{3,2},{4,5},{5,4},{6,7},{7,6},{8,9},{9,8},{10,11... | collective-permute-start | bytes 2359304 | tf_op jit(solution)/shard_map/ppermute | solution.py:585
  90.6 7.9 %collective-permute-start.10 = (bf16[144,768]{1,0:T(8,128)(2,1)S(1)}, bf16[144,768]{1,0:T(8,128)(2,1)S(1)}, u32[]{:S(2)}, u32[]{:S(2)}) collective-permute-start(bf16[144,768]{1,0:T(8,128)(2,1)S(1)} %combine.8.held_ref), channel_id=1, source_target_pairs={{0,2},{2,0},{4,6},{6,4},{8,10},{10,8},{12,14},{14,12},{16,18},{18,... | collective-permute-start | bytes 663560 | tf_op jit(solution)/shard_map/ppermute | solution.py:632
  98.6 1.5 %collective-permute-start.12 = (bf16[144,768]{1,0:T(8,128)(2,1)S(1)}, bf16[144,768]{1,0:T(8,128)(2,1)S(1)}, u32[]{:S(2)}, u32[]{:S(2)}) collective-permute-start(bf16[144,768]{1,0:T(8,128)(2,1)S(1)} %combine.9.held_ref), channel_id=1, source_target_pairs={{0,1},{1,0},{2,3},{3,2},{4,5},{5,4},{6,7},{7,6},{8,9},{9,8},{10,11... | collective-permute-start | bytes 663560 | tf_op jit(solution)/shard_map/ppermute | solution.py:585
  (18 other events, 165.6 us)

commit v3 on v2

--- a/solution.py
+++ b/solution.py
@@ -100,13 +100,13 @@
 
 def attention_kernel(
     half_ref, ids_ref, seg_ref, own_ref, x_ref, wq_ref, wk_ref, wv_ref,
-    qkv_ref, keep_ref, send_ref, inverse_ref, rng_ref, *rest,
+    kv_ref, queries_ref, keep_ref, send_ref, factor_ref, rng_ref, *rest,
 ):
     half = own_ref.shape[0]
-    count, width = qkv_ref.shape[0], wq_ref.shape[1]
-    pairs, heads, block = width // PAIR, width // HEAD_DIM, BLOCK
+    count, width = kv_ref.shape[0], wq_ref.shape[1]
+    pairs, block = width // PAIR, BLOCK
     share_refs = rest[:pairs]
-    seg_row, seg_col, keys, values, scores, peaks, totals, mix, wq, wk, wv, sems = rest[pairs:]
+    seg_row, seg_col, fresh, turned, bias, peaks, totals, mix, wq, wk, wv, sems = rest[pairs:]
     here, there = half_ref[0], 1 - half_ref[0]
     copies = start_all((wq_ref, wk_ref, wv_ref), (wq, wk, wv), sems)
     seg_row[...] = seg_ref[...].astype(F32)
@@ -117,63 +117,52 @@
         last = ids_ref[0, (g + 1) * block - 1].astype(F32)
         rng_ref[0, g] = jnp.sum(jnp.where(ids < first, 1.0, 0.0)).astype(jnp.int32) // block
         rng_ref[1, g] = (jnp.sum(jnp.where(ids <= last, 1.0, 0.0)).astype(jnp.int32) + block - 1) // block
-    qkv_ref[aligned(here, half), :] = own_ref[...]
-    write_projection(x_ref[...], (wq, wk, wv), copies, qkv_ref.at[aligned(there, half), :])
-    for p in range(pairs):
-        stack_heads(qkv_ref[:, width + p * PAIR : width + (p + 1) * PAIR], keys.at[p], block)
-        stack_heads(qkv_ref[:, 2 * width + p * PAIR : 2 * width + (p + 1) * PAIR], values.at[p], block)
+    write_projection(x_ref[...], (wq, wk, wv), copies, fresh)
+    for source, which in ((own_ref, here), (fresh, there)):
+        kv_ref[aligned(which, half), :] = source[:, width:]
+        for p in range(pairs):
+            cols = slice(p * PAIR, (p + 1) * PAIR)
+            stack_heads(source[:, cols], queries_ref.at[p, aligned(which, 2 * half), :], block)
+            turned[cols, aligned(which, half)] = source[:, 2 * width + p * PAIR : 2 * width + (p + 1) * PAIR].T
 
     def query_block(g, carry):
-        rows = aligned(g, block)
-        low, high = rng_ref[0, g], rng_ref[1, g]
+        rows, both = aligned(g, block), aligned(g, 2 * block)
         peaks[...] = jnp.full(peaks.shape, MASKED, F32)
         totals[...] = jnp.zeros(totals.shape, F32)
         mix[...] = jnp.zeros(mix.shape, F32)
-
-        def score_pass(j, c):
-            both = aligned(j, 2 * block)
-            same = seg_col[rows, 0:1] == seg_row[0:1, aligned(j, block)]
+        factor_ref[:, :, both] = jnp.full((pairs, 8, 2 * block), MASKED, F32)
+
+        def key_block(j, c):
+            span = aligned(j, block)
+            bias[...] = jnp.where(seg_col[span, 0:1] == seg_row[0:1, rows], 0.0, MASKED)
             for p in range(pairs):
-                s2 = dot_nt(qkv_ref[rows, p * PAIR : (p + 1) * PAIR], keys[p, both, :])
+                s = dot_nt(kv_ref[span, p * PAIR : (p + 1) * PAIR], queries_ref[p, both, :])
+                hide = bias[...]
+                s = s + jnp.concatenate([hide, hide], 1)
+                old = peaks[p]
+                top = jnp.maximum(old, jnp.max(s, 0, keepdims=True))
+                e = jnp.exp2(s - top)
+                drop = jnp.exp2(old - top)
+                peaks[p] = top
+                totals[p] = totals[p] * drop + jnp.sum(e, 0, keepdims=True)
+                factor_ref[p, pl.ds(j, 1), both] = top
+                e = e.astype(BF16)
+                share_refs[p][span, both] = e
                 for a in range(2):
-                    s = jnp.where(same, s2[:, a * block : (a + 1) * block], MASKED)
-                    scores[p, :, aligned(2 * j + a, block)] = s
-                    top = peaks[2 * p + a]
-                    for t in range(block // 128):
-                        top = jnp.maximum(top, s[:, t * 128 : (t + 1) * 128])
-                    peaks[2 * p + a] = top
+                    side = slice(a * block, (a + 1) * block)
+                    head = slice(p * PAIR + a * HEAD_DIM, p * PAIR + (a + 1) * HEAD_DIM)
+                    mix[head, :] = mix[head, :] * drop[:, side] + dot(turned[head, span], e[:, side])
             return c
 
-        lax.fori_loop(low, high, score_pass, 0)
-        for h in range(heads):
-            peaks[h] = jnp.broadcast_to(jnp.max(peaks[h], -1, keepdims=True), (block, 128))
-
-        def mix_pass(j, c):
-            both = aligned(j, 2 * block)
-            for p in range(pairs):
-                parts = []
-                for a in range(2):
-                    peak = jnp.concatenate([peaks[2 * p + a]] * (block // 128), 1)
-                    e = jnp.exp2(scores[p, :, aligned(2 * j + a, block)] - peak)
-                    total = totals[2 * p + a]
-                    for t in range(block // 128):
-                        total = total + e[:, t * 128 : (t + 1) * 128]
-                    totals[2 * p + a] = total
-                    parts.append(e.astype(BF16))
-                shares = jnp.concatenate(parts, 1)
-                share_refs[p][rows, both] = shares
-                mix[:, p * PAIR : (p + 1) * PAIR] += dot(shares, values[p, both, :])
-            return c
-
-        lax.fori_loop(low, high, mix_pass, 0)
-        lane = lax.broadcasted_iota(jnp.int32, (block, 128), 1)
+        lax.fori_loop(rng_ref[0, g], rng_ref[1, g], key_block, 0)
         outs = []
         for p in range(pairs):
-            sums = [jnp.sum(totals[h], -1, keepdims=True) for h in (2 * p, 2 * p + 1)]
-            scale = jnp.where(lane < HEAD_DIM, 1.0 / sums[0], 1.0 / sums[1])
-            inverse_ref[rows, p * PAIR : (p + 1) * PAIR] = scale
-            outs.append((mix[:, p * PAIR : (p + 1) * PAIR] * scale).astype(BF16))
-        result = jnp.concatenate(outs, 1)
+            inverse = 1.0 / totals[p]
+            factor_ref[p, :, both] = jnp.exp2(factor_ref[p, :, both] - peaks[p]) * inverse
+            for a in range(2):
+                head = slice(p * PAIR + a * HEAD_DIM, p * PAIR + (a + 1) * HEAD_DIM)
+                outs.append((mix[head, :] * inverse[:, a * block : (a + 1) * block]).astype(BF16))
+        result = jnp.concatenate(outs, 0).T
         per_half = half // block
 
         @pl.when(g // per_half == here)
@@ -195,112 +184,101 @@
     return pl.pallas_call(
         attention_kernel,
         out_shape=(
-            jax.ShapeDtypeStruct((count, 3 * width), BF16),
+            jax.ShapeDtypeStruct((count, 2 * width), BF16),
+            jax.ShapeDtypeStruct((pairs, 2 * count, PAIR), BF16),
             jax.ShapeDtypeStruct((half, width), BF16),
             jax.ShapeDtypeStruct((half, width), BF16),
-            jax.ShapeDtypeStruct((count, width), F32),
+            jax.ShapeDtypeStruct((pairs, 8, 2 * count), F32),
             jax.ShapeDtypeStruct((2, count // BLOCK), jnp.int32),
         )
         + (jax.ShapeDtypeStruct((count, 2 * count), BF16),) * pairs,
         in_specs=[SM, SM] + [VM] * 3 + [HB] * 3,
-        out_specs=(VM,) * 4 + (SM,) + (VM,) * pairs,
+        out_specs=(VM,) * 5 + (SM,) + (VM,) * pairs,
         scratch_shapes=[
             pltpu.VMEM((1, count), F32),
             pltpu.VMEM((count, 128), F32),
-            pltpu.VMEM((pairs, 2 * count, PAIR), BF16),
-            pltpu.VMEM((pairs, 2 * count, PAIR), BF16),
-            pltpu.VMEM((pairs, BLOCK, 2 * count), F32),
-            pltpu.VMEM((2 * pairs, BLOCK, 128), F32),
-            pltpu.VMEM((2 * pairs, BLOCK, 128), F32),
-            pltpu.VMEM((BLOCK, width), F32),
+            pltpu.VMEM((half, 3 * width), BF16),
+            pltpu.VMEM((width, count), BF16),
+            pltpu.VMEM((BLOCK, BLOCK), F32),
+            pltpu.VMEM((pairs, 1, 2 * BLOCK), F32),
+            pltpu.VMEM((pairs, 1, 2 * BLOCK), F32),
+            pltpu.VMEM((width, BLOCK), F32),
         ]
         + [pltpu.VMEM(wq.shape, BF16)] * 3
         + [pltpu.SemaphoreType.DMA((3,))],
-        compiler_params=pltpu.CompilerParams(vmem_limit_bytes=40 * MIB),
+        compiler_params=pltpu.CompilerParams(vmem_limit_bytes=16 * MIB),
         cost_estimate=pl.CostEstimate(flops=10**10, bytes_accessed=8 * MIB, transcendentals=10**6),
         name="attention",
     )(half_index, seg, seg, own, x, wq, wk, wv)
 
 
 def pair_grad_kernel(
-    p, half_ref, rng_ref, qkv_ref, keep_ref, send_ref, own_ref, other_ref, inverse_ref, share_ref,
+    p, half_ref, rng_ref, kv_ref, queries_ref, keep_ref, send_ref, own_ref, other_ref, factor_ref, share_ref,
     dq_ref, dk_ref, dv_ref,
-    keys, values, grad, turned_grad, turned_query, delta, dq, dk, dv,
+    grads, turned, delta, dq, dk, dv,
 ):
-    half = own_ref.shape[0]
-    count, block = qkv_ref.shape[0], BLOCK
-    width = keep_ref.shape[1]
+    half, width = keep_ref.shape
+    count, block = kv_ref.shape[0], BLOCK
     cols = slice(p * PAIR, (p + 1) * PAIR)
     here, there = half_ref[0], 1 - half_ref[0]
-    lane = lax.broadcasted_iota(jnp.int32, (half, PAIR), 1)
+    row = lax.broadcasted_iota(jnp.int32, (8, PAIR), 0)
+    column = lax.broadcasted_iota(jnp.int32, (8, PAIR), 1)
+    pick = jnp.where(column // HEAD_DIM == row, 1.0, 0.0).astype(BF16)
     for which, mixed_ref, up_ref in ((here, keep_ref, own_ref), (there, send_ref, other_ref)):
-        rows = aligned(which, half)
-        scaled = (up_ref[:, cols].astype(F32) * inverse_ref[rows, cols]).astype(BF16)
-        grad[rows, :] = scaled
-        product = mixed_ref[:, cols].astype(F32) * scaled.astype(F32)
-        for a in range(2):
-            side = jnp.where(lane // HEAD_DIM == a, product, 0.0)
-            delta[a, rows, :] = jnp.broadcast_to(jnp.sum(side, -1, keepdims=True), (half, PAIR))
-    stack_heads(qkv_ref[:, width + p * PAIR : width + (p + 1) * PAIR], keys, block)
-    stack_heads(qkv_ref[:, 2 * width + p * PAIR : 2 * width + (p + 1) * PAIR], values, block)
-    turned_grad[...] = grad[...].T
-    turned_query[...] = qkv_ref[:, cols].T
+        product = mixed_ref[:, cols].astype(F32) * up_ref[:, cols].astype(F32)
+        high = product.astype(BF16)
+        low = (product - high.astype(F32)).astype(BF16)
+        delta[:, aligned(which, half)] = dot_nt(pick, high) + dot_nt(pick, low)
+        stack_heads(up_ref[:, cols], grads.at[aligned(which, 2 * half), :], block)
+    turned[...] = kv_ref[:, cols].T
     dk[...] = jnp.zeros(dk.shape, F32)
     dv[...] = jnp.zeros(dv.shape, F32)
 
     def query_block(g, carry):
-        rows = aligned(g, block)
-        low, high = rng_ref[0, g], rng_ref[1, g]
+        rows, both = aligned(g, block), aligned(g, 2 * block)
         dq[...] = jnp.zeros(dq.shape, F32)
 
         def key_block(j, c):
-            both = aligned(j, 2 * block)
             span = aligned(j, block)
-            d2 = dot_nt(grad[rows, :], values[both, :])
-            shares = share_ref[rows, both]
-            slopes = []
-            for a in range(2):
-                side = slice(a * block, (a + 1) * block)
-                level = jnp.concatenate([delta[a, rows, :]] * (block // 128), 1)
-                slopes.append((shares[:, side].astype(F32) * (d2[:, side] - level)).astype(BF16))
-            dq[...] += dot(jnp.concatenate(slopes, 1), keys[both, :])
+            d = dot_nt(kv_ref[span, width + p * PAIR : width + (p + 1) * PAIR], grads[both, :])
+            shares = share_ref[span, both].astype(F32) * factor_ref[p, pl.ds(j, 1), both]
+            level = jnp.concatenate([delta[0:1, rows], delta[1:2, rows]], 1)
+            slopes = (shares * (d - level)).astype(BF16)
+            dv[span, :] += dot(shares.astype(BF16), grads[both, :])
+            dk[span, :] += dot(slopes, queries_ref[p, both, :])
             for a in range(2):
                 head = slice(a * HEAD_DIM, (a + 1) * HEAD_DIM)
-                dv[head, span] += dot(turned_grad[head, rows], shares[:, a * block : (a + 1) * block])
-                dk[head, span] += dot(turned_query[head, rows], slopes[a])
+                dq[head, :] += dot(turned[head, span], slopes[:, a * block : (a + 1) * block])
             return c
 
-        lax.fori_loop(low, high, key_block, 0)
-        dq_ref[rows, :] = (dq[...] * HEAD_DIM**-0.5).astype(BF16)
+        lax.fori_loop(rng_ref[0, g], rng_ref[1, g], key_block, 0)
+        dq_ref[rows, :] = (dq[...] * HEAD_DIM**-0.5).astype(BF16).T
         return carry
 
     lax.fori_loop(0, count // block, query_block, 0)
-    dk_ref[...] = (dk[...] * LN2).T.astype(BF16)
-    dv_ref[...] = dv[...].T.astype(BF16)
-
-
-def pair_grad(p, half_index, rng, qkv, keep, send, own, other, inverse, shares):
-    half = own.shape[0]
-    count = 2 * half
+    dk_ref[...] = (dk[...] * LN2).astype(BF16)
+    dv_ref[...] = dv[...].astype(BF16)
+
+
+def pair_grad(p, half_index, rng, kv, queries, keep, send, own, other, factor, shares):
+    count = kv.shape[0]
     return pl.pallas_call(
         functools.partial(pair_grad_kernel, p),
         out_shape=(jax.ShapeDtypeStruct((count, PAIR), BF16),) * 3,
-        in_specs=[SM, SM] + [VM] * 7,
+        in_specs=[SM, SM] + [VM] * 8,
         out_specs=(VM,) * 3,
-        scratch_shapes=[pltpu.VMEM((2 * count, PAIR), BF16)] * 2
-        + [
-            pltpu.VMEM((count, PAIR), BF16),
+        scratch_shapes=[
+            pltpu.VMEM((2 * count, PAIR), BF16),
             pltpu.VMEM((PAIR, count), BF16),
-            pltpu.VMEM((PAIR, count), BF16),
-            pltpu.VMEM((2, count, PAIR), F32),
-            pltpu.VMEM((BLOCK, PAIR), F32),
-            pltpu.VMEM((PAIR, count), F32),
-            pltpu.VMEM((PAIR, count), F32),
+            pltpu.VMEM((8, count), F32),
+            pltpu.VMEM((PAIR, BLOCK), F32),
+            pltpu.VMEM((count, PAIR), F32),
+            pltpu.VMEM((count, PAIR), F32),
         ],
-        compiler_params=pltpu.CompilerParams(vmem_limit_bytes=16 * MIB),
+        compiler_params=pltpu.CompilerParams(vmem_limit_bytes=12 * MIB),
         cost_estimate=pl.CostEstimate(flops=4 * 10**9, bytes_accessed=8 * MIB, transcendentals=0),
         name=f"pair_grad_{p}",
-    )(half_index, rng, qkv, keep, send, own, other, inverse, shares)
+    )(half_index, rng, kv, queries, keep, send, own, other, factor, shares)
 
 
 def input_part(half_ref, flip, pieces, weights, half):
@@ -603,7 +581,7 @@
     other_output = swap_cores(output_late)
     other_inner = swap_cores(inner_late)
     other_outer = swap_cores(outer_late)
-    qkv, keep, send, inverse, rng, *shares = attention(
+    kv, queries, keep, send, factor, rng, *shares = attention(
         half_index, segment_ids, own, other_tokens, query_weight, key_weight, value_weight
     )
     got = swap_cores(send)
@@ -632,7 +610,7 @@
         arriving = lax.ppermute(packed, "dp", [(i, i ^ step) for i in range(devices)])
         if n < pairs:
             got_grad, packed = tie(got_grad, packed)
-            parts = pair_grad(n, half_index, rng, qkv, keep, send, own_grad, got_grad, inverse, shares[n])
+            parts = pair_grad(n, half_index, rng, kv, queries, keep, send, own_grad, got_grad, factor, shares[n])
             arriving, *parts = tie(arriving, *parts)
             grads.append(parts)
         elif n == pairs:

time: 103 us -> 106 us (1.029)
  local copies, waits for them, and re-layouts: 10.3 us -> 17.5 us
  Pallas kernels: 68.6 us -> 64.9 us
  waiting for transfers between devices: 13.3 us -> 10.8 us
  starting transfers between devices: 9.51 us -> 10.9 us
    unnamed x58 -> x66, local copies, waits for them, and re-layouts: 8.64 us -> 15.8 us
    pallas_call x3, Pallas kernels: 20.1 us -> 17.9 us  [pair_grad(): pl.pallas_call(functools.partial(pair_grad_kernel, p), out_shape=(jax.Sha...]
    ppermute x4, waiting for transfers between devices: 5.34 us -> 3.56 us  [per_device(): lax.ppermute(packed, 'dp', [(i, i ^ step) for i in range(devices)])]
    pallas_call x1, Pallas kernels: 19.8 us -> 18.4 us  [attention(): pl.pallas_call(attention_kernel, out_shape=(jax.ShapeDtypeStruct((count,...]
    ppermute x4, starting transfers between devices: 7.19 us -> 8.59 us  [per_device(): lax.ppermute(packed, 'dp', [(i, i ^ step) for i in range(devices)])]
  transfers between devices with their start and end apart: 13 -> 13, of which waited for: 7 -> 6; matrix products, arithmetic and copies ran while one was open for 0% -> 0% of each run, Pallas kernels for 43% -> 39%
where the time goes in v3:
time: 106 us; the launch traced here: 105 us
  Pallas kernels  64.9 us (61%)
  local copies, waits for them, and re-layouts  17.5 us (17%)
  starting transfers between devices  10.9 us (10%)
  waiting for transfers between devices  10.8 us (10%)
  between operations  1.08 us (1%)
    pallas_call x1, Pallas kernels, middle(): pl.pallas_call(middle_kernel, out_shape=(jax.ShapeDtypeStruct((rows, feat...  21.8 us
    pallas_call x1, Pallas kernels, attention(): pl.pallas_call(attention_kernel, out_shape=(jax.ShapeDtypeStruct((count,...  18.4 us
    pallas_call x3, Pallas kernels, pair_grad(): pl.pallas_call(functools.partial(pair_grad_kernel, p), out_shape=(jax.Sha...  17.9 us
    unnamed x66, local copies, waits for them, and re-layouts  15.8 us
    ppermute x4, starting transfers between devices, per_device(): lax.ppermute(packed, 'dp', [(i, i ^ step) for i in range(devices)])  8.59 us
    ppermute x9, waiting for transfers between devices, swap_cores(): return lax.ppermute(value, 'mp', [(0, 1), (1, 0)])  7.21 us
    ppermute x4, waiting for transfers between devices, per_device(): lax.ppermute(packed, 'dp', [(i, i ^ step) for i in range(devices)])  3.56 us
    pallas_call x2, Pallas kernels, input_call(): pl.pallas_call(kernel, out_shape=jax.ShapeDtypeStruct((half, features), B...  3.35 us
  transfers between devices with their start and end apart: 13, of which 6 were waited for; matrix products, arithmetic and copies ran while one was open for 0% of the time, Pallas kernels for 39%

profile of v3, /device:TPU:0, one launch (start us, length us, event | category | flops | bytes accessed | tf_op | source)
XLA Modules:
  0.0 105.1 jit_solution(9664942107225224992)
XLA Ops:
  1.2 2.1 %collective-permute-done.x_ref = bf16[512,768]{1,0:T(8,128)(2,1)S(1)} collective-permute-done((bf16[512,768]{1,0:T(8,128)(2,1)}, bf16[512,768]{1,0:T(8,128)(2,1)S(1)}, u32[]{:S(2)}, u32[]{:S(2)}) %collective-permute-start) | collective-permute-done | bytes 786464 | tf_op jit(solution)/shard_map/ppermute | solution.py:563
  8.1 2.2 %project.1.own_ref = bf16[512,1152]{1,0:T(8,128)(2,1)S(1)} custom-call(bf16[512,768]{1,0:T(8,128)(2,1)S(1)} %copy-done.6, bf16[768,384]{1,0:T(8,128)(2,1)S(1)} %copy-done, bf16[768,384]{1,0:T(8,128)(2,1)S(1)} %copy-done.2, bf16[768,384]{1,0:T(8,128)(2,1)S(1)} %copy-done.4), custom_call_target="tpu_custom_call" | custom-call | flops 905969664 | bytes 5242880 | tf_op jit(solution)/shard_map/project/pallas_call | solution.py:89
  11.0 18.4 %attention.1 = (bf16[1024,768]{1,0:T(8,128)(2,1)S(1)}, bf16[3,2048,128]{2,1,0:T(8,128)(2,1)S(1)}, bf16[512,384]{1,0:T(8,128)(2,1)S(1)}, bf16[512,384]{1,0:T(8,12...) custom-call(s32[1]{0:T(128)} %bitcast.half_ref, ...), custom_call_target="tpu_custom_call" | custom-call | flops 10000000000 | bytes 8388608 | tf_op jit(solution)/shard_map/attention/pallas_call | solution.py:184
  29.4 2.0 %copy-done.25 = bf16[1024,2048]{1,0:T(8,128)(2,1)} copy-done((bf16[1024,2048]{1,0:T(8,128)(2,1)}, bf16[1024,2048]{1,0:T(8,128)(2,1)S(1)}, u32[]{:S(2)}) %copy-start.25) | copy-done | bytes 4194328
  31.4 2.0 %copy-done.27 = bf16[1024,2048]{1,0:T(8,128)(2,1)} copy-done((bf16[1024,2048]{1,0:T(8,128)(2,1)}, bf16[1024,2048]{1,0:T(8,128)(2,1)S(1)}, u32[]{:S(2)}) %copy-start.27) | copy-done | bytes 4194328
  33.4 1.2 %copy-done.29 = bf16[1024,768]{1,0:T(8,128)(2,1)} copy-done((bf16[1024,768]{1,0:T(8,128)(2,1)}, bf16[1024,768]{1,0:T(8,128)(2,1)S(1)}, u32[]{:S(2)}) %copy-start.29) | copy-done | bytes 1572888
  34.6 1.2 %copy-done.31 = bf16[3,2048,128]{2,1,0:T(8,128)(2,1)} copy-done((bf16[3,2048,128]{2,1,0:T(8,128)(2,1)}, bf16[3,2048,128]{2,1,0:T(8,128)(2,1)S(1)}, u32[]{:S(2)}) %copy-start.31) | copy-done | bytes 1572888
  35.9 1.6 %collective-permute-done.1.got_ref = bf16[512,384]{1,0:T(8,128)(2,1)S(1)} collective-permute-done((bf16[512,384]{1,0:T(8,128)(2,1)S(1)}, bf16[512,384]{1,0:T(8,128)(2,1)S(1)}, u32[]{:S(2)}, u32[]{:S(2)}) %collective-permute-start.1) | collective-permute-done | bytes 393248 | tf_op jit(solution)/shard_map/ppermute | solution.py:563
  37.7 21.8 %middle.1 = (bf16[512,768]{1,0:T(8,128)(2,1)}, f32[512,768]{1,0:T(8,128)S(1)}, bf16[512,384]{1,0:T(8,128)(2,1)S(1)}, bf16[512,384]{1,0:T(8,128)(2,1)S(1)}, bf16[...) custom-call(s32[1]{0:T(128)} %bitcast.half_ref, bf16[512,768]{1,0:T(8,128)(2,1)S(1)} %copy-done.7, ...), custom_call_target="tpu_custom_call" | custom-call | flops 20000000000 | bytes 16777216 | tf_op jit(solution)/shard_map/middle/pallas_call | solution.py:469
  60.0 1.5 %collective-permute-done.6.got_ref = bf16[144,768]{1,0:T(8,128)(2,1)S(1)} collective-permute-done((bf16[144,768]{1,0:T(8,128)(2,1)S(1)}, bf16[144,768]{1,0:T(8,128)(2,1)S(1)}, u32[]{:S(2)}, u32[]{:S(2)}) %collective-permute-start.6) | collective-permute-done | bytes 221216 | tf_op jit(solution)/shard_map/ppermute | solution.py:563
  61.6 3.8 %collective-permute-start.7 = (bf16[144,768]{1,0:T(8,128)(2,1)S(1)}, bf16[144,768]{1,0:T(8,128)(2,1)S(1)}, u32[]{:S(2)}, u32[]{:S(2)}) collective-permute-start(bf16[144,768]{1,0:T(8,128)(2,1)S(1)} %combine.5.held_ref), channel_id=1, source_target_pairs={{0,16},{2,18},{4,20},{6,22},{8,24},{10,26},{12,28},{14,30},{16,0},... | collective-permute-start | bytes 663560 | tf_op jit(solution)/shard_map/ppermute | solution.py:610
  65.4 2.2 %copy-done.28 = bf16[1024,2048]{1,0:T(8,128)(2,1)S(1)} copy-done((bf16[1024,2048]{1,0:T(8,128)(2,1)S(1)}, bf16[1024,2048]{1,0:T(8,128)(2,1)}, u32[]{:S(2)}) %copy-start.28) | copy-done | bytes 4194328
  67.6 1.4 %copy-done.30 = bf16[1024,768]{1,0:T(8,128)(2,1)S(1)} copy-done((bf16[1024,768]{1,0:T(8,128)(2,1)S(1)}, bf16[1024,768]{1,0:T(8,128)(2,1)}, u32[]{:S(2)}) %copy-start.30) | copy-done | bytes 1572888
  69.0 1.4 %copy-done.32 = bf16[3,2048,128]{2,1,0:T(8,128)(2,1)S(1)} copy-done((bf16[3,2048,128]{2,1,0:T(8,128)(2,1)S(1)}, bf16[3,2048,128]{2,1,0:T(8,128)(2,1)}, u32[]{:S(2)}) %copy-start.32) | copy-done | bytes 1572888
  70.4 6.0 %pair_grad_0.1 = (bf16[1024,128]{1,0:T(8,128)(2,1)S(1)}, bf16[1024,128]{1,0:T(8,128)(2,1)S(1)}, bf16[1024,128]{1,0:T(8,128)(2,1)S(1)}) custom-call(s32[1]{0:T(128)} %bitcast.half_ref, s32[2,4]{1,0:T(2,128)S(1)} %get-tuple-element.82.rng_ref, bf16[1024,768]{1,0:T(8,128)(2,1)S(1)} %copy-done.30, bf16[3,2048,128]{2,1,0:T(8,128)(2,1)S(1)} %copy-done.32, ...), custom_call_target="tpu_custom_call" | custom-call | flops 4000000000 | bytes 8388608 | tf_op jit(solution)/shard_map/pair_grad_0/pallas_call | solution.py:265
  76.5 1.6 %collective-permute-start.8 = (bf16[144,768]{1,0:T(8,128)(2,1)S(1)}, bf16[144,768]{1,0:T(8,128)(2,1)S(1)}, u32[]{:S(2)}, u32[]{:S(2)}) collective-permute-start(bf16[144,768]{1,0:T(8,128)(2,1)S(1)} %combine.6.held_ref), channel_id=1, source_target_pairs={{0,8},{2,10},{4,12},{6,14},{8,0},{10,2},{12,4},{14,6},{16,24},{18,... | collective-permute-start | bytes 663560 | tf_op jit(solution)/shard_map/ppermute | solution.py:610
  78.1 6.0 %pair_grad_1.1 = (bf16[1024,128]{1,0:T(8,128)(2,1)S(1)}, bf16[1024,128]{1,0:T(8,128)(2,1)S(1)}, bf16[1024,128]{1,0:T(8,128)(2,1)S(1)}) custom-call(s32[1]{0:T(128)} %bitcast.half_ref, s32[2,4]{1,0:T(2,128)S(1)} %get-tuple-element.82.rng_ref, bf16[1024,768]{1,0:T(8,128)(2,1)S(1)} %copy-done.30, bf16[3,2048,128]{2,1,0:T(8,128)(2,1)S(1)} %copy-done.32, ...), custom_call_target="tpu_custom_call" | custom-call | flops 4000000000 | bytes 8388608 | tf_op jit(solution)/shard_map/pair_grad_1/pallas_call | solution.py:265
  84.2 1.4 %collective-permute-start.9 = (bf16[144,768]{1,0:T(8,128)(2,1)S(1)}, bf16[144,768]{1,0:T(8,128)(2,1)S(1)}, u32[]{:S(2)}, u32[]{:S(2)}) collective-permute-start(bf16[144,768]{1,0:T(8,128)(2,1)S(1)} %combine.7.held_ref), channel_id=1, source_target_pairs={{0,4},{2,6},{4,0},{6,2},{8,12},{10,14},{12,8},{14,10},{16,20},{18,... | collective-permute-start | bytes 663560 | tf_op jit(solution)/shard_map/ppermute | solution.py:610
  85.6 6.0 %pair_grad_2.1 = (bf16[1024,128]{1,0:T(8,128)(2,1)S(1)}, bf16[1024,128]{1,0:T(8,128)(2,1)S(1)}, bf16[1024,128]{1,0:T(8,128)(2,1)S(1)}) custom-call(s32[1]{0:T(128)} %bitcast.half_ref, s32[2,4]{1,0:T(2,128)S(1)} %get-tuple-element.82.rng_ref, bf16[1024,768]{1,0:T(8,128)(2,1)S(1)} %copy-done.30, bf16[3,2048,128]{2,1,0:T(8,128)(2,1)S(1)} %copy-done.32, ...), custom_call_target="tpu_custom_call" | custom-call | flops 4000000000 | bytes 8388608 | tf_op jit(solution)/shard_map/pair_grad_2/pallas_call | solution.py:265
  91.6 1.2 %away.1 = bf16[512,768]{1,0:T(8,128)(2,1)S(1)} custom-call(s32[1]{0:T(128)} %bitcast.half_ref, bf16[1024,128]{1,0:T(8,128)(2,1)S(1)} %get-tuple-element.107.refs_0_, bf16[1024,128]{1,0:T(8,128)(2,1)S(1)} %get-tuple-element.108.refs_1_, bf16[1024,128]{1,0:T(8,128)(2,1)S(1)} %get-tuple-element.109.refs_2_, bf16[1024,128]{1,0:T(8,128)(2,1)S(1)} %get-tuple-element.110.refs_3_, ...), custom_call_target="tpu_custom_call" | custom-call | flops 1000000000 | bytes 6291456 | tf_op jit(solution)/shard_map/away/pallas_call | solution.py:305
  93.0 1.7 %collective-permute-start.10 = (bf16[144,768]{1,0:T(8,128)(2,1)S(1)}, bf16[144,768]{1,0:T(8,128)(2,1)S(1)}, u32[]{:S(2)}, u32[]{:S(2)}) collective-permute-start(bf16[144,768]{1,0:T(8,128)(2,1)S(1)} %combine.8.held_ref), channel_id=1, source_target_pairs={{0,2},{2,0},{4,6},{6,4},{8,10},{10,8},{12,14},{14,12},{16,18},{18,... | collective-permute-start | bytes 663560 | tf_op jit(solution)/shard_map/ppermute | solution.py:610
  95.2 2.1 %home.1 = bf16[512,768]{1,0:T(8,128)(2,1)} custom-call(s32[1]{0:T(128)} %bitcast.half_ref, f32[512,768]{1,0:T(8,128)S(1)} %get-tuple-element.106.first_ref, bf16[512,768]{1,0:T(8,128)(2,1)S(1)} %collective-permute-done.11.got_ref, bf16[1024,128]{1,0:T(8,128)(2,1)S(1)} %get-tuple-element.107.refs_0_, bf16[1024,128]{1,0:T(8,128)(2,1)S(1)} %get-tuple-element.108.refs_1_, ...), custom_call_target="tpu_custom_call" | custom-call | flops 1000000000 | bytes 6291456 | tf_op jit(solution)/shard_map/home/pallas_call | solution.py:305
  97.3 3.6 %collective-permute-done.10.got_ref = bf16[144,768]{1,0:T(8,128)(2,1)S(1)} collective-permute-done((bf16[144,768]{1,0:T(8,128)(2,1)S(1)}, bf16[144,768]{1,0:T(8,128)(2,1)S(1)}, u32[]{:S(2)}, u32[]{:S(2)}) %collective-permute-start.10) | collective-permute-done | bytes 221216 | tf_op jit(solution)/shard_map/ppermute | solution.py:610
  101.0 1.5 %collective-permute-done.12.got_ref = bf16[144,768]{1,0:T(8,128)(2,1)S(1)} collective-permute-done((bf16[144,768]{1,0:T(8,128)(2,1)S(1)}, bf16[144,768]{1,0:T(8,128)(2,1)S(1)}, u32[]{:S(2)}, u32[]{:S(2)}) %collective-permute-start.12) | collective-permute-done | bytes 221216 | tf_op jit(solution)/shard_map/ppermute | solution.py:563
  (85 shorter events, 10.2 us)
Async XLA Ops:
  0.7 2.6 %collective-permute-start = (bf16[512,768]{1,0:T(8,128)(2,1)}, bf16[512,768]{1,0:T(8,128)(2,1)S(1)}, u32[]{:S(2)}, u32[]{:S(2)}) collective-permute-start(bf16[512,768]{1,0:T(8,128)(2,1)} %x_ref.3), channel_id=1, source_target_pairs={{0,1},{1,0},{2,3},{3,2},{4,5},{5,4},{6,7},{7,6},{8,9},{9,8},{10,11... | collective-permute-start | bytes 2359304 | tf_op jit(solution)/shard_map/ppermute | solution.py:563
  3.3 34.2 %collective-permute-start.3 = (bf16[768,1536]{1,0:T(8,128)(2,1)}, bf16[768,1536]{1,0:T(8,128)(2,1)S(1)}, u32[]{:S(2)}, u32[]{:S(2)}) collective-permute-start(bf16[768,1536]{1,0:T(8,128)(2,1)} %w1_hbm.1), channel_id=1, source_target_pairs={{0,1},{1,0},{2,3},{3,2},{4,5},{5,4},{6,7},{7,6},{8,9},{9,8},{10,11... | collective-permute-start | bytes 7077896 | tf_op jit(solution)/shard_map/ppermute | solution.py:563
  3.7 33.8 %collective-permute-start.4 = (bf16[1536,768]{1,0:T(8,128)(2,1)}, bf16[1536,768]{1,0:T(8,128)(2,1)}, u32[]{:S(2)}, u32[]{:S(2)}) collective-permute-start(bf16[1536,768]{1,0:T(8,128)(2,1)} %w2_hbm.1), channel_id=1, source_target_pairs={{0,1},{1,0},{2,3},{3,2},{4,5},{5,4},{6,7},{7,6},{8,9},{9,8},{10,11... | collective-permute-start | bytes 7077896 | tf_op jit(solution)/shard_map/ppermute | solution.py:563
  10.4 27.1 %collective-permute-start.2 = (bf16[384,768]{1,0:T(8,128)(2,1)S(1)}, bf16[384,768]{1,0:T(8,128)(2,1)S(1)}, u32[]{:S(2)}, u32[]{:S(2)}) collective-permute-start(bf16[384,768]{1,0:T(8,128)(2,1)S(1)} %copy-done.11), channel_id=1, source_target_pairs={{0,1},{1,0},{2,3},{3,2},{4,5},{5,4},{6,7},{7,6},{8,9},{9,8},{10,11... | collective-permute-start | bytes 1769480 | tf_op jit(solution)/shard_map/ppermute | solution.py:563
  10.8 26.7 %copy-start.7 = (bf16[512,768]{1,0:T(8,128)(2,1)S(1)}, bf16[512,768]{1,0:T(8,128)(2,1)}, u32[]{:S(2)}) copy-start(bf16[512,768]{1,0:T(8,128)(2,1)} %x_ref.3) | copy-start | bytes 2359300
  10.8 26.7 %copy-start.8 = (bf16[768,1536]{1,0:T(8,128)(2,1)S(1)}, bf16[768,1536]{1,0:T(8,128)(2,1)}, u32[]{:S(2)}) copy-start(bf16[768,1536]{1,0:T(8,128)(2,1)} %w1_hbm.1) | copy-start | bytes 7077892
  10.9 26.7 %copy-start.9 = (bf16[1536,768]{1,0:T(8,128)(2,1)S(1)}, bf16[1536,768]{1,0:T(8,128)(2,1)}, u32[]{:S(2)}) copy-start(bf16[1536,768]{1,0:T(8,128)(2,1)} %w2_hbm.1) | copy-start | bytes 7077892
  10.9 26.7 %copy-start.10 = (bf16[512,768]{1,0:T(8,128)(2,1)S(1)}, bf16[512,768]{1,0:T(8,128)(2,1)}, u32[]{:S(2)}) copy-start(bf16[512,768]{1,0:T(8,128)(2,1)} %up_ref.1) | copy-start | bytes 2359300
  10.9 26.7 %copy-start.12 = (bf16[768,64]{0,1:T(8,128)(2,1)S(1)}, bf16[768,64]{0,1:T(8,128)(2,1)}, u32[]{:S(2)}) copy-start(bf16[768,64]{0,1:T(8,128)(2,1)} %param.29) | copy-start | bytes 294916
  10.9 26.7 %copy-start.13 = (bf16[64,768]{1,0:T(8,128)(2,1)S(1)}, bf16[64,768]{1,0:T(8,128)(2,1)}, u32[]{:S(2)}) copy-start(bf16[64,768]{1,0:T(8,128)(2,1)} %mu_hbm.1) | copy-start | bytes 294916
  10.9 26.7 %copy-start.14 = (bf16[768,64]{0,1:T(8,128)(2,1)S(1)}, bf16[768,64]{0,1:T(8,128)(2,1)}, u32[]{:S(2)}) copy-start(bf16[768,64]{0,1:T(8,128)(2,1)} %param.33) | copy-start | bytes 294916
  10.9 26.7 %copy-start.15 = (bf16[64,768]{1,0:T(8,128)(2,1)S(1)}, bf16[64,768]{1,0:T(8,128)(2,1)}, u32[]{:S(2)}) copy-start(bf16[64,768]{1,0:T(8,128)(2,1)} %du_hbm.1) | copy-start | bytes 294916
  10.9 26.6 %copy-start.17 = (bf16[768]{0:T(1024)(128)(2,1)S(1)}, bf16[768]{0:T(1024)(128)(2,1)}, u32[]{:S(2)}) copy-start(bf16[768]{0:T(1024)(128)(2,1)} %mub_ref.1) | copy-start | bytes 4612
  10.9 26.6 %copy-start.18 = (bf16[768]{0:T(1024)(128)(2,1)S(1)}, bf16[768]{0:T(1024)(128)(2,1)}, u32[]{:S(2)}) copy-start(bf16[768]{0:T(1024)(128)(2,1)} %dub_ref.1) | copy-start | bytes 4612
  11.0 26.6 %copy-start.19 = (bf16[768]{0:T(1024)(128)(2,1)S(1)}, bf16[768]{0:T(1024)(128)(2,1)}, u32[]{:S(2)}) copy-start(bf16[768]{0:T(1024)(128)(2,1)} %fg_ref.1) | copy-start | bytes 4612
  35.8 1.7 %collective-permute-start.1 = (bf16[512,384]{1,0:T(8,128)(2,1)S(1)}, bf16[512,384]{1,0:T(8,128)(2,1)S(1)}, u32[]{:S(2)}, u32[]{:S(2)}) collective-permute-start(bf16[512,384]{1,0:T(8,128)(2,1)S(1)} %get-tuple-element.72.send_ref), channel_id=1, source_target_pairs={{0,1},{1,0},{2,3},{3,2},{4,5},{5,4},{6,7},{7,6},{8,9},{9,8},{10,11... | collective-permute-start | bytes 1179656 | tf_op jit(solution)/shard_map/ppermute | solution.py:563
  59.4 6.0 %collective-permute-start.5 = (bf16[512,384]{1,0:T(8,128)(2,1)S(1)}, bf16[512,384]{1,0:T(8,128)(2,1)S(1)}, u32[]{:S(2)}, u32[]{:S(2)}) collective-permute-start(bf16[512,384]{1,0:T(8,128)(2,1)S(1)} %get-tuple-element.77), channel_id=1, source_target_pairs={{0,1},{1,0},{2,3},{3,2},{4,5},{5,4},{6,7},{7,6},{8,9},{9,8},{10,11... | collective-permute-start | bytes 1179656 | tf_op jit(solution)/shard_map/ppermute | solution.py:563
  59.6 1.9 %collective-permute-start.6 = (bf16[144,768]{1,0:T(8,128)(2,1)S(1)}, bf16[144,768]{1,0:T(8,128)(2,1)S(1)}, u32[]{:S(2)}, u32[]{:S(2)}) collective-permute-start(bf16[144,768]{1,0:T(8,128)(2,1)S(1)} %get-tuple-element.79), channel_id=1, source_target_pairs={{0,1},{1,0},{2,3},{3,2},{4,5},{5,4},{6,7},{7,6},{8,9},{9,8},{10,11... | collective-permute-start | bytes 663560 | tf_op jit(solution)/shard_map/ppermute | solution.py:563
  61.6 14.8 %collective-permute-start.7 = (bf16[144,768]{1,0:T(8,128)(2,1)S(1)}, bf16[144,768]{1,0:T(8,128)(2,1)S(1)}, u32[]{:S(2)}, u32[]{:S(2)}) collective-permute-start(bf16[144,768]{1,0:T(8,128)(2,1)S(1)} %combine.5.held_ref), channel_id=1, source_target_pairs={{0,16},{2,18},{4,20},{6,22},{8,24},{10,26},{12,28},{14,30},{16,0},... | collective-permute-start | bytes 663560 | tf_op jit(solution)/shard_map/ppermute | solution.py:610
  76.5 7.6 %collective-permute-start.8 = (bf16[144,768]{1,0:T(8,128)(2,1)S(1)}, bf16[144,768]{1,0:T(8,128)(2,1)S(1)}, u32[]{:S(2)}, u32[]{:S(2)}) collective-permute-start(bf16[144,768]{1,0:T(8,128)(2,1)S(1)} %combine.6.held_ref), channel_id=1, source_target_pairs={{0,8},{2,10},{4,12},{6,14},{8,0},{10,2},{12,4},{14,6},{16,24},{18,... | collective-permute-start | bytes 663560 | tf_op jit(solution)/shard_map/ppermute | solution.py:610
  84.2 7.4 %collective-permute-start.9 = (bf16[144,768]{1,0:T(8,128)(2,1)S(1)}, bf16[144,768]{1,0:T(8,128)(2,1)S(1)}, u32[]{:S(2)}, u32[]{:S(2)}) collective-permute-start(bf16[144,768]{1,0:T(8,128)(2,1)S(1)} %combine.7.held_ref), channel_id=1, source_target_pairs={{0,4},{2,6},{4,0},{6,2},{8,12},{10,14},{12,8},{14,10},{16,20},{18,... | collective-permute-start | bytes 663560 | tf_op jit(solution)/shard_map/ppermute | solution.py:610
  92.8 2.4 %collective-permute-start.11 = (bf16[512,768]{1,0:T(8,128)(2,1)S(1)}, bf16[512,768]{1,0:T(8,128)(2,1)S(1)}, u32[]{:S(2)}, u32[]{:S(2)}) collective-permute-start(bf16[512,768]{1,0:T(8,128)(2,1)S(1)} %away.1), channel_id=1, source_target_pairs={{0,1},{1,0},{2,3},{3,2},{4,5},{5,4},{6,7},{7,6},{8,9},{9,8},{10,11... | collective-permute-start | bytes 2359304 | tf_op jit(solution)/shard_map/ppermute | solution.py:563
  93.0 7.9 %collective-permute-start.10 = (bf16[144,768]{1,0:T(8,128)(2,1)S(1)}, bf16[144,768]{1,0:T(8,128)(2,1)S(1)}, u32[]{:S(2)}, u32[]{:S(2)}) collective-permute-start(bf16[144,768]{1,0:T(8,128)(2,1)S(1)} %combine.8.held_ref), channel_id=1, source_target_pairs={{0,2},{2,0},{4,6},{6,4},{8,10},{10,8},{12,14},{14,12},{16,18},{18,... | collective-permute-start | bytes 663560 | tf_op jit(solution)/shard_map/ppermute | solution.py:610
  100.9 1.5 %collective-permute-start.12 = (bf16[144,768]{1,0:T(8,128)(2,1)S(1)}, bf16[144,768]{1,0:T(8,128)(2,1)S(1)}, u32[]{:S(2)}, u32[]{:S(2)}) collective-permute-start(bf16[144,768]{1,0:T(8,128)(2,1)S(1)} %combine.9.held_ref), channel_id=1, source_target_pairs={{0,1},{1,0},{2,3},{3,2},{4,5},{5,4},{6,7},{7,6},{8,9},{9,8},{10,11... | collective-permute-start | bytes 663560 | tf_op jit(solution)/shard_map/ppermute | solution.py:563
  (22 other events, 177.1 us)

commit v4 on v3

--- a/solution.py
+++ b/solution.py
@@ -16,7 +16,10 @@
 LN2 = 0.6931471805599453
 ROOT_HALF = 0.7071067811865476
 ROOT_TWO_PI = 0.3989422804014327
-MASKED = -1e30
+MASKED = -(2.0**100)
+LARGEST = 2.0**100
+SMALLEST = 2.0**-60
+TURNED = 80
 BLOCK = 256
 MIB = 1 << 20
 
@@ -54,10 +57,18 @@
         target[pl.ds((2 * t + 1) * block, block), :] = second[t * block : (t + 1) * block]
 
 
-def fill_columns(row_ref, column_ref):
-    for t in range(row_ref.shape[1] // 128):
-        span = slice(t * 128, (t + 1) * 128)
-        column_ref[span, :] = jnp.broadcast_to(row_ref[0:1, span], (128, 128)).T
+def stack_heads_across(source, target, block):
+    row = lax.broadcasted_iota(jnp.int32, source.shape, 0)
+    zero = jnp.zeros_like(source)
+    first = jnp.where(row < HEAD_DIM, source, zero)
+    second = jnp.where(row < HEAD_DIM, zero, source)
+    for t in range(source.shape[1] // block):
+        target[:, 2 * t * block : (2 * t + 1) * block] = first[:, t * block : (t + 1) * block]
+        target[:, (2 * t + 1) * block : (2 * t + 2) * block] = second[:, t * block : (t + 1) * block]
+
+
+def in_hbm(value):
+    return pltpu.with_memory_space_constraint(value, pltpu.HBM)
 
 
 def start_all(sources, buffers, sems):
@@ -67,101 +78,161 @@
     return copies
 
 
-def write_projection(x, weights, copies, out_ref):
-    width = weights[0].shape[1]
-    for i, weight in enumerate(weights):
-        if copies:
-            copies[i].wait()
-        part = dot(x, weight[...])
-        if i == 0:
-            part = part * (HEAD_DIM**-0.5 * LOG2E)
-        out_ref[:, i * width : (i + 1) * width] = part.astype(BF16)
-
-
-def project_kernel(x_ref, wq_ref, wk_ref, wv_ref, out_ref, x_buf, wq, wk, wv, sems):
+def write_projection(which, x, weights, copies, kv_ref, queries_ref, across_ref, turned_ref):
+    rows, width = x.shape[0], weights[0].shape[1]
+    pairs = width // PAIR
+    if copies:
+        copies[0].wait()
+    queries = (dot(x, weights[0][...]) * (HEAD_DIM**-0.5 * LOG2E)).astype(BF16)
+    for p in range(pairs):
+        pair = queries[:, p * PAIR : (p + 1) * PAIR]
+        stack_heads(pair, queries_ref.at[p, aligned(which, 2 * rows), :], BLOCK)
+        stack_heads_across(pair.T, across_ref.at[p, :, aligned(which, 2 * rows)], BLOCK)
+    if copies:
+        copies[1].wait()
+    kv_ref[aligned(which, rows), :width] = dot(x, weights[1][...]).astype(BF16)
+    if copies:
+        copies[2].wait()
+    values = dot(x, weights[2][...]).astype(BF16)
+    kv_ref[aligned(which, rows), width:] = values
+    ones = jnp.ones((TURNED - HEAD_DIM, rows), BF16)
+    for p in range(pairs):
+        turned = values[:, p * PAIR : (p + 1) * PAIR].T
+        for a in range(2):
+            base = (2 * p + a) * TURNED
+            turned_ref[base : base + HEAD_DIM, aligned(which, rows)] = turned[a * HEAD_DIM : (a + 1) * HEAD_DIM]
+            turned_ref[base + HEAD_DIM : base + TURNED, aligned(which, rows)] = ones
+
+
+def is_shift(lane):
+    return (lane == 63) | (lane == 95) | (lane == 127)
+
+
+def project_kernel(
+    half_ref, ids_ref, seg_ref, x_ref, wq_ref, wk_ref, wv_ref,
+    kv_ref, queries_ref, across_ref, turned_ref, item_ref, hide_ref, rng_ref,
+    x_buf, wq, wk, wv, sems,
+):
     copies = start_all((x_ref, wq_ref, wk_ref, wv_ref), (x_buf, wq, wk, wv), sems)
-    copies[0].wait()
-    write_projection(x_buf[...], (wq, wk, wv), copies[1:], out_ref)
-
-
-def project(x, wq, wk, wv):
-    rows, width = x.shape[0], wq.shape[1]
-    return pl.pallas_call(
-        project_kernel,
-        out_shape=jax.ShapeDtypeStruct((rows, 3 * width), BF16),
-        in_specs=[HB] * 4,
-        out_specs=VM,
-        scratch_shapes=[pltpu.VMEM(v.shape, BF16) for v in (x, wq, wk, wv)] + [pltpu.SemaphoreType.DMA((4,))],
-        compiler_params=pltpu.CompilerParams(vmem_limit_bytes=12 * MIB),
-        cost_estimate=pl.CostEstimate(flops=2 * rows * x.shape[1] * 3 * width, bytes_accessed=5 * MIB, transcendentals=0),
-        name="project",
-    )(x, wq, wk, wv)
-
-
-def attention_kernel(
-    half_ref, ids_ref, seg_ref, own_ref, x_ref, wq_ref, wk_ref, wv_ref,
-    kv_ref, queries_ref, keep_ref, send_ref, factor_ref, rng_ref, *rest,
-):
-    half = own_ref.shape[0]
-    count, width = kv_ref.shape[0], wq_ref.shape[1]
-    pairs, block = width // PAIR, BLOCK
-    share_refs = rest[:pairs]
-    seg_row, seg_col, fresh, turned, bias, peaks, totals, mix, wq, wk, wv, sems = rest[pairs:]
-    here, there = half_ref[0], 1 - half_ref[0]
-    copies = start_all((wq_ref, wk_ref, wv_ref), (wq, wk, wv), sems)
-    seg_row[...] = seg_ref[...].astype(F32)
-    fill_columns(seg_row, seg_col)
-    ids = seg_row[...]
+    count, block = kv_ref.shape[0], BLOCK
+    ids = seg_ref[...].astype(F32)
     for g in range(count // block):
         first = ids_ref[0, g * block].astype(F32)
         last = ids_ref[0, (g + 1) * block - 1].astype(F32)
         rng_ref[0, g] = jnp.sum(jnp.where(ids < first, 1.0, 0.0)).astype(jnp.int32) // block
         rng_ref[1, g] = (jnp.sum(jnp.where(ids <= last, 1.0, 0.0)).astype(jnp.int32) + block - 1) // block
-    write_projection(x_ref[...], (wq, wk, wv), copies, fresh)
-    for source, which in ((own_ref, here), (fresh, there)):
-        kv_ref[aligned(which, half), :] = source[:, width:]
-        for p in range(pairs):
-            cols = slice(p * PAIR, (p + 1) * PAIR)
-            stack_heads(source[:, cols], queries_ref.at[p, aligned(which, 2 * half), :], block)
-            turned[cols, aligned(which, half)] = source[:, 2 * width + p * PAIR : 2 * width + (p + 1) * PAIR].T
+    lane = lax.broadcasted_iota(jnp.int32, (128, 128), 1)
+    for t in range(count // 128):
+        same = jnp.broadcast_to(ids[:, t * 128 : (t + 1) * 128], (128, 128)).T == lane.astype(F32)
+        item_ref[t * 128 : (t + 1) * 128, :] = jnp.where(same | is_shift(lane), 1.0, 0.0).astype(BF16)
+    row = lax.broadcasted_iota(jnp.int32, (128, block), 0)
+    for t in range(count // block):
+        same = row.astype(F32) == ids[:, t * block : (t + 1) * block]
+        hide = jnp.where(same | is_shift(row), 0.0, MASKED).astype(BF16)
+        for a in range(2):
+            hide_ref[:, (2 * t + a) * block : (2 * t + a + 1) * block] = hide
+    copies[0].wait()
+    write_projection(half_ref[0], x_buf[...], (wq, wk, wv), copies[1:], kv_ref, queries_ref, across_ref, turned_ref)
+
+
+def project(half_index, seg, x, wq, wk, wv):
+    rows, width = x.shape[0], wq.shape[1]
+    count, pairs = 2 * rows, width // PAIR
+    return pl.pallas_call(
+        project_kernel,
+        out_shape=(
+            jax.ShapeDtypeStruct((count, 2 * width), BF16),
+            jax.ShapeDtypeStruct((pairs, 2 * count, PAIR), BF16),
+            jax.ShapeDtypeStruct((pairs, PAIR, 2 * count), BF16),
+            jax.ShapeDtypeStruct((2 * pairs * TURNED, count), BF16),
+            jax.ShapeDtypeStruct((count, 128), BF16),
+            jax.ShapeDtypeStruct((128, 2 * count), BF16),
+            jax.ShapeDtypeStruct((2, count // BLOCK), jnp.int32),
+        ),
+        in_specs=[SM, SM, VM] + [HB] * 4,
+        out_specs=(VM,) * 6 + (SM,),
+        scratch_shapes=[pltpu.VMEM(v.shape, BF16) for v in (x, wq, wk, wv)] + [pltpu.SemaphoreType.DMA((4,))],
+        compiler_params=pltpu.CompilerParams(vmem_limit_bytes=16 * MIB),
+        cost_estimate=pl.CostEstimate(flops=2 * rows * x.shape[1] * 3 * width, bytes_accessed=5 * MIB, transcendentals=0),
+        name="project",
+    )(half_index, seg, seg, *map(in_hbm, (x, wq, wk, wv)))
+
+
+def attention_kernel(
+    half_ref, rng_ref, x_ref, item_ref, hide_ref, wq_ref, wk_ref, wv_ref, kv_in, queries_in, across_in, turned_in,
+    kv_ref, queries_ref, keep_ref, send_ref, inverse_ref, *rest,
+):
+    half = x_ref.shape[0]
+    count, width = kv_ref.shape[0], wq_ref.shape[1]
+    pairs, block = width // PAIR, BLOCK
+    share_refs = rest[:pairs]
+    across, turned, mix, shifted, peaks = rest[pairs:]
+    here, there = half_ref[0], 1 - half_ref[0]
+    turned[:, aligned(here, half)] = turned_in[:, aligned(here, half)]
+    across[:, :, aligned(here, 2 * half)] = across_in[:, :, aligned(here, 2 * half)]
+    kv_ref[aligned(here, half), :] = kv_in[aligned(here, half), :]
+    queries_ref[:, aligned(here, 2 * half), :] = queries_in[:, aligned(here, 2 * half), :]
+    write_projection(there, x_ref[...], (wq_ref, wk_ref, wv_ref), (), kv_ref, queries_ref, across, turned)
+
+    def scores(p, span, both, hide):
+        keys = jnp.concatenate([kv_ref[span, p * PAIR : (p + 1) * PAIR], item_ref[span, :]], 1)
+        return dot(keys, jnp.concatenate([across[p, :, both], hide], 0))
 
     def query_block(g, carry):
         rows, both = aligned(g, block), aligned(g, 2 * block)
-        peaks[...] = jnp.full(peaks.shape, MASKED, F32)
-        totals[...] = jnp.zeros(totals.shape, F32)
-        mix[...] = jnp.zeros(mix.shape, F32)
-        factor_ref[:, :, both] = jnp.full((pairs, 8, 2 * block), MASKED, F32)
-
-        def key_block(j, c):
-            span = aligned(j, block)
-            bias[...] = jnp.where(seg_col[span, 0:1] == seg_row[0:1, rows], 0.0, MASKED)
+        low, high = rng_ref[0, g], rng_ref[1, g]
+
+        def mix_all(hide_of):
+            mix[...] = jnp.zeros(mix.shape, F32)
+
+            def key_block(j, c):
+                span = aligned(j, block)
+                for p in range(pairs):
+                    e = jnp.exp2(scores(p, span, both, hide_of(p))).astype(BF16)
+                    share_refs[p][span, both] = e
+                    for a in range(2):
+                        head = slice((2 * p + a) * TURNED, (2 * p + a + 1) * TURNED)
+                        mix[head, :] += dot(turned[head, span], e[:, a * block : (a + 1) * block])
+                return c
+
+            lax.fori_loop(low, high, key_block, 0)
+
+        mix_all(lambda p: hide_ref[:, both])
+        total_rows = [h * TURNED + HEAD_DIM for h in range(2 * pairs)]
+        sums = jnp.concatenate([mix[r : r + 8, :] for r in total_rows], 0)
+        fine = jnp.where((sums <= LARGEST) & (sums >= SMALLEST), 0.0, 1.0)
+
+        @pl.when(jnp.max(fine) > 0.0)
+        def _():
+            peaks[...] = jnp.full(peaks.shape, MASKED, F32)
+
+            def peak_block(j, c):
+                for p in range(pairs):
+                    s = scores(p, aligned(j, block), both, hide_ref[:, both])
+                    peaks[p] = jnp.maximum(peaks[p], jnp.max(s, 0, keepdims=True))
+                return c
+
+            lax.fori_loop(low, high, peak_block, 0)
+            row = lax.broadcasted_iota(jnp.int32, (128, 2 * block), 0)
+            hide = hide_ref[:, both].astype(F32)
             for p in range(pairs):
-                s = dot_nt(kv_ref[span, p * PAIR : (p + 1) * PAIR], queries_ref[p, both, :])
-                hide = bias[...]
-                s = s + jnp.concatenate([hide, hide], 1)
-                old = peaks[p]
-                top = jnp.maximum(old, jnp.max(s, 0, keepdims=True))
-                e = jnp.exp2(s - top)
-                drop = jnp.exp2(old - top)
-                peaks[p] = top
-                totals[p] = totals[p] * drop + jnp.sum(e, 0, keepdims=True)
-                factor_ref[p, pl.ds(j, 1), both] = top
-                e = e.astype(BF16)
-                share_refs[p][span, both] = e
-                for a in range(2):
-                    side = slice(a * block, (a + 1) * block)
-                    head = slice(p * PAIR + a * HEAD_DIM, p * PAIR + (a + 1) * HEAD_DIM)
-                    mix[head, :] = mix[head, :] * drop[:, side] + dot(turned[head, span], e[:, side])
-            return c
-
-        lax.fori_loop(rng_ref[0, g], rng_ref[1, g], key_block, 0)
+                peak = peaks[p]
+                first = peak.astype(BF16).astype(F32)
+                second = (peak - first).astype(BF16).astype(F32)
+                third = peak - first - second
+                parts = jnp.where(row < 64, first, jnp.where(row < 96, second, third))
+                shifted[p] = jnp.where(is_shift(row), -parts, hide).astype(BF16)
+            mix_all(lambda p: shifted[p])
+
         outs = []
         for p in range(pairs):
-            inverse = 1.0 / totals[p]
-            factor_ref[p, :, both] = jnp.exp2(factor_ref[p, :, both] - peaks[p]) * inverse
+            scales = []
             for a in range(2):
-                head = slice(p * PAIR + a * HEAD_DIM, p * PAIR + (a + 1) * HEAD_DIM)
-                outs.append((mix[head, :] * inverse[:, a * block : (a + 1) * block]).astype(BF16))
+                base = (2 * p + a) * TURNED
+                scale = jnp.broadcast_to(1.0 / mix[base + HEAD_DIM : base + HEAD_DIM + 1, :], (HEAD_DIM, block))
+                outs.append((mix[base : base + HEAD_DIM, :] * scale).astype(BF16))
+                scales.append(scale)
+            inverse_ref[rows, p * PAIR : (p + 1) * PAIR] = jnp.concatenate(scales, 0).T
         result = jnp.concatenate(outs, 0).T
         per_half = half // block
 
@@ -178,44 +249,39 @@
     lax.fori_loop(0, count // block, query_block, 0)
 
 
-def attention(half_index, seg, own, x, wq, wk, wv):
-    half, width = own.shape[0], wq.shape[1]
+def attention(half_index, rng, x, item, hide, wq, wk, wv, kv, queries, across, turned):
+    half, width = x.shape[0], wq.shape[1]
     count, pairs = 2 * half, width // PAIR
+    like = lambda v: jax.ShapeDtypeStruct(v.shape, v.dtype)
     return pl.pallas_call(
         attention_kernel,
         out_shape=(
-            jax.ShapeDtypeStruct((count, 2 * width), BF16),
-            jax.ShapeDtypeStruct((pairs, 2 * count, PAIR), BF16),
+            like(kv),
+            like(queries),
             jax.ShapeDtypeStruct((half, width), BF16),
             jax.ShapeDtypeStruct((half, width), BF16),
-            jax.ShapeDtypeStruct((pairs, 8, 2 * count), F32),
-            jax.ShapeDtypeStruct((2, count // BLOCK), jnp.int32),
+            jax.ShapeDtypeStruct((count, width), F32),
         )
         + (jax.ShapeDtypeStruct((count, 2 * count), BF16),) * pairs,
-        in_specs=[SM, SM] + [VM] * 3 + [HB] * 3,
-        out_specs=(VM,) * 5 + (SM,) + (VM,) * pairs,
+        in_specs=[SM, SM] + [VM] * 10,
+        out_specs=(VM,) * (5 + pairs),
         scratch_shapes=[
-            pltpu.VMEM((1, count), F32),
-            pltpu.VMEM((count, 128), F32),
-            pltpu.VMEM((half, 3 * width), BF16),
-            pltpu.VMEM((width, count), BF16),
-            pltpu.VMEM((BLOCK, BLOCK), F32),
+            pltpu.VMEM(across.shape, BF16),
+            pltpu.VMEM(turned.shape, BF16),
+            pltpu.VMEM((2 * pairs * TURNED, BLOCK), F32),
+            pltpu.VMEM((pairs, 128, 2 * BLOCK), BF16),
             pltpu.VMEM((pairs, 1, 2 * BLOCK), F32),
-            pltpu.VMEM((pairs, 1, 2 * BLOCK), F32),
-            pltpu.VMEM((width, BLOCK), F32),
-        ]
-        + [pltpu.VMEM(wq.shape, BF16)] * 3
-        + [pltpu.SemaphoreType.DMA((3,))],
-        compiler_params=pltpu.CompilerParams(vmem_limit_bytes=16 * MIB),
+        ],
+        compiler_params=pltpu.CompilerParams(vmem_limit_bytes=12 * MIB),
         cost_estimate=pl.CostEstimate(flops=10**10, bytes_accessed=8 * MIB, transcendentals=10**6),
         name="attention",
-    )(half_index, seg, seg, own, x, wq, wk, wv)
+    )(half_index, rng, x, item, hide, wq, wk, wv, kv, queries, across, turned)
 
 
 def pair_grad_kernel(
-    p, half_ref, rng_ref, kv_ref, queries_ref, keep_ref, send_ref, own_ref, other_ref, factor_ref, share_ref,
+    p, half_ref, rng_ref, kv_ref, queries_ref, keep_ref, send_ref, own_ref, other_ref, inverse_ref, share_ref,
     dq_ref, dk_ref, dv_ref,
-    grads, turned, delta, dq, dk, dv,
+    grads, across, turned, delta, dq, dk, dv,
 ):
     half, width = keep_ref.shape
     count, block = kv_ref.shape[0], BLOCK
@@ -225,11 +291,13 @@
     column = lax.broadcasted_iota(jnp.int32, (8, PAIR), 1)
     pick = jnp.where(column // HEAD_DIM == row, 1.0, 0.0).astype(BF16)
     for which, mixed_ref, up_ref in ((here, keep_ref, own_ref), (there, send_ref, other_ref)):
-        product = mixed_ref[:, cols].astype(F32) * up_ref[:, cols].astype(F32)
+        scaled = (up_ref[:, cols].astype(F32) * inverse_ref[aligned(which, half), cols]).astype(BF16)
+        product = mixed_ref[:, cols].astype(F32) * scaled.astype(F32)
         high = product.astype(BF16)
         low = (product - high.astype(F32)).astype(BF16)
         delta[:, aligned(which, half)] = dot_nt(pick, high) + dot_nt(pick, low)
-        stack_heads(up_ref[:, cols], grads.at[aligned(which, 2 * half), :], block)
+        stack_heads(scaled, grads.at[aligned(which, 2 * half), :], block)
+        stack_heads_across(scaled.T, across.at[:, aligned(which, 2 * half)], block)
     turned[...] = kv_ref[:, cols].T
     dk[...] = jnp.zeros(dk.shape, F32)
     dv[...] = jnp.zeros(dv.shape, F32)
@@ -237,14 +305,14 @@
     def query_block(g, carry):
         rows, both = aligned(g, block), aligned(g, 2 * block)
         dq[...] = jnp.zeros(dq.shape, F32)
+        level = jnp.concatenate([delta[0:1, rows], delta[1:2, rows]], 1)
 
         def key_block(j, c):
             span = aligned(j, block)
-            d = dot_nt(kv_ref[span, width + p * PAIR : width + (p + 1) * PAIR], grads[both, :])
-            shares = share_ref[span, both].astype(F32) * factor_ref[p, pl.ds(j, 1), both]
-            level = jnp.concatenate([delta[0:1, rows], delta[1:2, rows]], 1)
-            slopes = (shares * (d - level)).astype(BF16)
-            dv[span, :] += dot(shares.astype(BF16), grads[both, :])
+            d = dot(kv_ref[span, width + p * PAIR : width + (p + 1) * PAIR], across[:, both])
+            shares = share_ref[span, both]
+            slopes = (shares.astype(F32) * (d - level)).astype(BF16)
+            dv[span, :] += dot(shares, grads[both, :])
             dk[span, :] += dot(slopes, queries_ref[p, both, :])
             for a in range(2):
                 head = slice(a * HEAD_DIM, (a + 1) * HEAD_DIM)
@@ -260,7 +328,7 @@
     dv_ref[...] = dv[...].astype(BF16)
 
 
-def pair_grad(p, half_index, rng, kv, queries, keep, send, own, other, factor, shares):
+def pair_grad(p, half_index, rng, kv, queries, keep, send, own, other, inverse, shares):
     count = kv.shape[0]
     return pl.pallas_call(
         functools.partial(pair_grad_kernel, p),
@@ -269,6 +337,7 @@
         out_specs=(VM,) * 3,
         scratch_shapes=[
             pltpu.VMEM((2 * count, PAIR), BF16),
+            pltpu.VMEM((PAIR, 2 * count), BF16),
             pltpu.VMEM((PAIR, count), BF16),
             pltpu.VMEM((8, count), F32),
             pltpu.VMEM((PAIR, BLOCK), F32),
@@ -278,7 +347,7 @@
         compiler_params=pltpu.CompilerParams(vmem_limit_bytes=12 * MIB),
         cost_estimate=pl.CostEstimate(flops=4 * 10**9, bytes_accessed=8 * MIB, transcendentals=0),
         name=f"pair_grad_{p}",
-    )(half_index, rng, kv, queries, keep, send, own, other, factor, shares)
+    )(half_index, rng, kv, queries, keep, send, own, other, inverse, shares)
 
 
 def input_part(half_ref, flip, pieces, weights, half):
@@ -489,10 +558,10 @@
             pltpu.SemaphoreType.DMA((10,)),
             pltpu.SemaphoreType.DMA,
         ],
-        compiler_params=pltpu.CompilerParams(vmem_limit_bytes=40 * MIB),
+        compiler_params=pltpu.CompilerParams(vmem_limit_bytes=36 * MIB),
         cost_estimate=pl.CostEstimate(flops=2 * 10**10, bytes_accessed=16 * MIB, transcendentals=10**6),
         name="middle",
-    )(half_index, x, keep, got, up, *vectors, *matrices)
+    )(half_index, x, keep, got, up, *vectors, *map(in_hbm, matrices))
 
 
 def combine_kernel(held_ref, got_ref, out_ref):
@@ -576,13 +645,15 @@
     devices = lax.axis_size("dp")
     adapt = mixer_down.shape[1]
     other_tokens = swap_cores(tokens)
-    own = project(tokens, query_weight, key_weight, value_weight)
+    kv, queries, across, turned, item, hide, rng = project(
+        half_index, segment_ids, tokens, query_weight, key_weight, value_weight
+    )
     other_tokens, output_late, inner_late, outer_late = tie(other_tokens, output_weight, inner_weight, outer_weight)
     other_output = swap_cores(output_late)
     other_inner = swap_cores(inner_late)
     other_outer = swap_cores(outer_late)
-    kv, queries, keep, send, factor, rng, *shares = attention(
-        half_index, segment_ids, own, other_tokens, query_weight, key_weight, value_weight
+    kv, queries, keep, send, inverse, *shares = attention(
+        half_index, rng, other_tokens, item, hide, query_weight, key_weight, value_weight, kv, queries, across, turned
     )
     got = swap_cores(send)
     vectors = (
@@ -610,7 +681,7 @@
         arriving = lax.ppermute(packed, "dp", [(i, i ^ step) for i in range(devices)])
         if n < pairs:
             got_grad, packed = tie(got_grad, packed)
-            parts = pair_grad(n, half_index, rng, kv, queries, keep, send, own_grad, got_grad, factor, shares[n])
+            parts = pair_grad(n, half_index, rng, kv, queries, keep, send, own_grad, got_grad, inverse, shares[n])
             arriving, *parts = tie(arriving, *parts)
             grads.append(parts)
         elif n == pairs:

time: 106 us -> 94.1 us (0.89)
  local copies, waits for them, and re-layouts: 17.5 us -> 4.42 us
  waiting for transfers between devices: 10.8 us -> 17.2 us
  Pallas kernels: 64.9 us -> 62.4 us
  starting transfers between devices: 10.9 us -> 8.97 us
    unnamed x66 -> x36, local copies, waits for them, and re-layouts: 15.8 us -> 2.75 us
    ppermute x4, waiting for transfers between devices: 3.56 us -> 8.95 us  [per_device(): lax.ppermute(packed, 'dp', [(i, i ^ step) for i in range(devices)])]
    ppermute x4, starting transfers between devices: 8.59 us -> 6.64 us  [per_device(): lax.ppermute(packed, 'dp', [(i, i ^ step) for i in range(devices)])]
    pallas_call x2, Pallas kernels: 20.6 us -> 18.7 us  [the longest x1 14.6 us: attention(): pl.pallas_call(attention_kernel, out_shape=(like(kv), like(queries), jax....]
  transfers between devices with their start and end apart: 13 -> 13, of which waited for: 6 -> 8; matrix products, arithmetic and copies ran while one was open for 0% -> 0% of each run, Pallas kernels for 39% -> 41%
where the time goes in v4:
time: 94.1 us; the launch traced here: 93.9 us
  Pallas kernels  62.4 us (66%)
  waiting for transfers between devices  17.2 us (18%)
  starting transfers between devices  8.97 us (10%)
  local copies, waits for them, and re-layouts  4.42 us (5%)
  between operations  0.95 us (1%)
    pallas_call x1, Pallas kernels, middle(): pl.pallas_call(middle_kernel, out_shape=(jax.ShapeDtypeStruct((rows, feat...  21.6 us
    pallas_call x3, Pallas kernels, pair_grad(): pl.pallas_call(functools.partial(pair_grad_kernel, p), out_shape=(jax.Sha...  17.4 us
    pallas_call x1, Pallas kernels, attention(): pl.pallas_call(attention_kernel, out_shape=(like(kv), like(queries), jax....  14.6 us
    ppermute x4, waiting for transfers between devices, per_device(): lax.ppermute(packed, 'dp', [(i, i ^ step) for i in range(devices)])  8.95 us
    ppermute x9, waiting for transfers between devices, swap_cores(): return lax.ppermute(value, 'mp', [(0, 1), (1, 0)])  8.26 us
    ppermute x4, starting transfers between devices, per_device(): lax.ppermute(packed, 'dp', [(i, i ^ step) for i in range(devices)])  6.64 us
    pallas_call x1, Pallas kernels, project(): pl.pallas_call(project_kernel, out_shape=(jax.ShapeDtypeStruct((count, 2...  4.11 us
    pallas_call x2, Pallas kernels, input_call(): pl.pallas_call(kernel, out_shape=jax.ShapeDtypeStruct((half, features), B...  3.41 us
  transfers between devices with their start and end apart: 13, of which 8 were waited for; matrix products, arithmetic and copies ran while one was open for 0% of the time, Pallas kernels for 41%

profile of v4, /device:TPU:0, one launch (start us, length us, event | category | flops | bytes accessed | tf_op | source)
XLA Modules:
  0.0 93.9 jit_solution(1552381539908201406)
XLA Ops:
  1.2 2.1 %collective-permute-done.x_ref = bf16[512,768]{1,0:T(8,128)(2,1)S(1)} collective-permute-done((bf16[512,768]{1,0:T(8,128)(2,1)}, bf16[512,768]{1,0:T(8,128)(2,1)S(1)}, u32[]{:S(2)}, u32[]{:S(2)}) %collective-permute-start) | collective-permute-done | bytes 786464 | tf_op jit(solution)/shard_map/ppermute | solution.py:632
  3.8 0.7 copy-done.5
  4.5 4.1 %project.1 = (bf16[1024,768]{1,0:T(8,128)(2,1)S(1)}, bf16[3,2048,128]{2,1,0:T(8,128)(2,1)S(1)}, bf16[3,128,2048]{2,1,0:T(8,128)(2,1)S(1)}, bf16[480,1024]{1,0:T(...) custom-call(s32[1]{0:T(128)} %bitcast.half_ref, ...), custom_call_target="tpu_custom_call" | custom-call | flops 905969664 | bytes 5242880 | tf_op jit(solution)/shard_map/project/pallas_call | solution.py:141
  9.2 14.6 %attention.1 = (bf16[1024,768]{1,0:T(8,128)(2,1)S(1)}, bf16[3,2048,128]{2,1,0:T(8,128)(2,1)S(1)}, bf16[512,384]{1,0:T(8,128)(2,1)S(1)}, bf16[512,384]{1,0:T(8,12...) custom-call(s32[1]{0:T(128)} %bitcast.half_ref, ...), custom_call_target="tpu_custom_call" | custom-call | flops 10000000000 | bytes 8388608 | tf_op jit(solution)/shard_map/attention/pallas_call | solution.py:256
  23.8 1.2 %copy-done.14 = f32[1024,384]{1,0:T(8,128)} copy-done((f32[1024,384]{1,0:T(8,128)}, f32[1024,384]{1,0:T(8,128)S(1)}, u32[]{:S(2)}) %copy-start.14) | copy-done | bytes 1572888
  25.2 1.6 %collective-permute-done.1.got_ref = bf16[512,384]{1,0:T(8,128)(2,1)S(1)} collective-permute-done((bf16[512,384]{1,0:T(8,128)(2,1)S(1)}, bf16[512,384]{1,0:T(8,128)(2,1)S(1)}, u32[]{:S(2)}, u32[]{:S(2)}) %collective-permute-start.1) | collective-permute-done | bytes 393248 | tf_op jit(solution)/shard_map/ppermute | solution.py:632
  26.8 0.8 copy-done.17
  27.6 21.6 %middle.1 = (bf16[512,768]{1,0:T(8,128)(2,1)}, f32[512,768]{1,0:T(8,128)S(1)}, bf16[512,384]{1,0:T(8,128)(2,1)S(1)}, bf16[512,384]{1,0:T(8,128)(2,1)S(1)}, bf16[...) custom-call(s32[1]{0:T(128)} %bitcast.half_ref, bf16[512,768]{1,0:T(8,128)(2,1)S(1)} %copy-done.3, ...), custom_call_target="tpu_custom_call" | custom-call | flops 20000000000 | bytes 16777216 | tf_op jit(solution)/shard_map/middle/pallas_call | solution.py:538
  49.8 1.5 %collective-permute-done.6.got_ref = bf16[144,768]{1,0:T(8,128)(2,1)S(1)} collective-permute-done((bf16[144,768]{1,0:T(8,128)(2,1)S(1)}, bf16[144,768]{1,0:T(8,128)(2,1)S(1)}, u32[]{:S(2)}, u32[]{:S(2)}) %collective-permute-start.6) | collective-permute-done | bytes 221216 | tf_op jit(solution)/shard_map/ppermute | solution.py:632
  51.4 3.8 %collective-permute-start.7 = (bf16[144,768]{1,0:T(8,128)(2,1)S(1)}, bf16[144,768]{1,0:T(8,128)(2,1)S(1)}, u32[]{:S(2)}, u32[]{:S(2)}) collective-permute-start(bf16[144,768]{1,0:T(8,128)(2,1)S(1)} %combine.5.held_ref), channel_id=1, source_target_pairs={{0,16},{2,18},{4,20},{6,22},{8,24},{10,26},{12,28},{14,30},{16,0},... | collective-permute-start | bytes 663560 | tf_op jit(solution)/shard_map/ppermute | solution.py:681
  55.2 5.8 %pair_grad_0.1 = (bf16[1024,128]{1,0:T(8,128)(2,1)S(1)}, bf16[1024,128]{1,0:T(8,128)(2,1)S(1)}, bf16[1024,128]{1,0:T(8,128)(2,1)S(1)}) custom-call(s32[1]{0:T(128)} %bitcast.half_ref, s32[2,4]{1,0:T(2,128)S(1)} %get-tuple-element.76.rng_ref, bf16[1024,768]{1,0:T(8,128)(2,1)S(1)} %get-tuple-element.95.kv_ref, ...), custom_call_target="tpu_custom_call" | custom-call | flops 4000000000 | bytes 8388608 | tf_op jit(solution)/shard_map/pair_grad_0/pallas_call | solution.py:333
  61.0 4.9 %collective-permute-done.7.got_ref = bf16[144,768]{1,0:T(8,128)(2,1)S(1)} collective-permute-done((bf16[144,768]{1,0:T(8,128)(2,1)S(1)}, bf16[144,768]{1,0:T(8,128)(2,1)S(1)}, u32[]{:S(2)}, u32[]{:S(2)}) %collective-permute-start.7) | collective-permute-done | bytes 221216 | tf_op jit(solution)/shard_map/ppermute | solution.py:681
  66.0 0.8 collective-permute-start.8
  66.8 5.8 %pair_grad_1.1 = (bf16[1024,128]{1,0:T(8,128)(2,1)S(1)}, bf16[1024,128]{1,0:T(8,128)(2,1)S(1)}, bf16[1024,128]{1,0:T(8,128)(2,1)S(1)}) custom-call(s32[1]{0:T(128)} %bitcast.half_ref, s32[2,4]{1,0:T(2,128)S(1)} %get-tuple-element.76.rng_ref, bf16[1024,768]{1,0:T(8,128)(2,1)S(1)} %get-tuple-element.95.kv_ref, ...), custom_call_target="tpu_custom_call" | custom-call | flops 4000000000 | bytes 8388608 | tf_op jit(solution)/shard_map/pair_grad_1/pallas_call | solution.py:333
  73.2 1.4 %collective-permute-start.9 = (bf16[144,768]{1,0:T(8,128)(2,1)S(1)}, bf16[144,768]{1,0:T(8,128)(2,1)S(1)}, u32[]{:S(2)}, u32[]{:S(2)}) collective-permute-start(bf16[144,768]{1,0:T(8,128)(2,1)S(1)} %combine.7.held_ref), channel_id=1, source_target_pairs={{0,4},{2,6},{4,0},{6,2},{8,12},{10,14},{12,8},{14,10},{16,20},{18,... | collective-permute-start | bytes 663560 | tf_op jit(solution)/shard_map/ppermute | solution.py:681
  74.6 5.8 %pair_grad_2.1 = (bf16[1024,128]{1,0:T(8,128)(2,1)S(1)}, bf16[1024,128]{1,0:T(8,128)(2,1)S(1)}, bf16[1024,128]{1,0:T(8,128)(2,1)S(1)}) custom-call(s32[1]{0:T(128)} %bitcast.half_ref, s32[2,4]{1,0:T(2,128)S(1)} %get-tuple-element.76.rng_ref, bf16[1024,768]{1,0:T(8,128)(2,1)S(1)} %get-tuple-element.95.kv_ref, ...), custom_call_target="tpu_custom_call" | custom-call | flops 4000000000 | bytes 8388608 | tf_op jit(solution)/shard_map/pair_grad_2/pallas_call | solution.py:333
  80.5 1.2 %away.1 = bf16[512,768]{1,0:T(8,128)(2,1)S(1)} custom-call(s32[1]{0:T(128)} %bitcast.half_ref, bf16[1024,128]{1,0:T(8,128)(2,1)S(1)} %get-tuple-element.119.refs_0_, bf16[1024,128]{1,0:T(8,128)(2,1)S(1)} %get-tuple-element.120.refs_1_, bf16[1024,128]{1,0:T(8,128)(2,1)S(1)} %get-tuple-element.121.refs_2_, bf16[1024,128]{1,0:T(8,128)(2,1)S(1)} %get-tuple-element.122.refs_3_, ...), custom_call_target="tpu_custom_call" | custom-call | flops 1000000000 | bytes 6291456 | tf_op jit(solution)/shard_map/away/pallas_call | solution.py:374
  81.8 0.6 collective-permute-start.10
  82.5 1.6 %collective-permute-done.11.got_ref = bf16[512,768]{1,0:T(8,128)(2,1)S(1)} collective-permute-done((bf16[512,768]{1,0:T(8,128)(2,1)S(1)}, bf16[512,768]{1,0:T(8,128)(2,1)S(1)}, u32[]{:S(2)}, u32[]{:S(2)}) %collective-permute-start.11) | collective-permute-done | bytes 786464 | tf_op jit(solution)/shard_map/ppermute | solution.py:632
  84.0 2.2 %home.1 = bf16[512,768]{1,0:T(8,128)(2,1)} custom-call(s32[1]{0:T(128)} %bitcast.half_ref, f32[512,768]{1,0:T(8,128)S(1)} %get-tuple-element.118.first_ref, bf16[512,768]{1,0:T(8,128)(2,1)S(1)} %collective-permute-done.11.got_ref, bf16[1024,128]{1,0:T(8,128)(2,1)S(1)} %get-tuple-element.119.refs_0_, bf16[1024,128]{1,0:T(8,128)(2,1)S(1)} %get-tuple-element.120.refs_1_, ...), custom_call_target="tpu_custom_call" | custom-call | flops 1000000000 | bytes 6291456 | tf_op jit(solution)/shard_map/home/pallas_call | solution.py:374
  86.2 3.5 %collective-permute-done.10.got_ref = bf16[144,768]{1,0:T(8,128)(2,1)S(1)} collective-permute-done((bf16[144,768]{1,0:T(8,128)(2,1)S(1)}, bf16[144,768]{1,0:T(8,128)(2,1)S(1)}, u32[]{:S(2)}, u32[]{:S(2)}) %collective-permute-start.10) | collective-permute-done | bytes 221216 | tf_op jit(solution)/shard_map/ppermute | solution.py:681
  89.9 1.5 %collective-permute-done.12.got_ref = bf16[144,768]{1,0:T(8,128)(2,1)S(1)} collective-permute-done((bf16[144,768]{1,0:T(8,128)(2,1)S(1)}, bf16[144,768]{1,0:T(8,128)(2,1)S(1)}, u32[]{:S(2)}, u32[]{:S(2)}) %collective-permute-start.12) | collective-permute-done | bytes 221216 | tf_op jit(solution)/shard_map/ppermute | solution.py:632
  91.3 0.9 finish.1
  92.3 0.6 slice_reduce_fusion
  (55 shorter events, 4.3 us)
Async XLA Ops:
  0.7 2.6 %collective-permute-start = (bf16[512,768]{1,0:T(8,128)(2,1)}, bf16[512,768]{1,0:T(8,128)(2,1)S(1)}, u32[]{:S(2)}, u32[]{:S(2)}) collective-permute-start(bf16[512,768]{1,0:T(8,128)(2,1)} %x_ref.3), channel_id=1, source_target_pairs={{0,1},{1,0},{2,3},{3,2},{4,5},{5,4},{6,7},{7,6},{8,9},{9,8},{10,11... | collective-permute-start | bytes 2359304 | tf_op jit(solution)/shard_map/ppermute | solution.py:632
  3.3 23.4 %collective-permute-start.3 = (bf16[768,1536]{1,0:T(8,128)(2,1)}, bf16[768,1536]{1,0:T(8,128)(2,1)}, u32[]{:S(2)}, u32[]{:S(2)}) collective-permute-start(bf16[768,1536]{1,0:T(8,128)(2,1)} %w1_hbm.1), channel_id=1, source_target_pairs={{0,1},{1,0},{2,3},{3,2},{4,5},{5,4},{6,7},{7,6},{8,9},{9,8},{10,11... | collective-permute-start | bytes 7077896 | tf_op jit(solution)/shard_map/ppermute | solution.py:632
  3.7 23.1 %collective-permute-start.4 = (bf16[1536,768]{1,0:T(8,128)(2,1)}, bf16[1536,768]{1,0:T(8,128)(2,1)}, u32[]{:S(2)}, u32[]{:S(2)}) collective-permute-start(bf16[1536,768]{1,0:T(8,128)(2,1)} %w2_hbm.1), channel_id=1, source_target_pairs={{0,1},{1,0},{2,3},{3,2},{4,5},{5,4},{6,7},{7,6},{8,9},{9,8},{10,11... | collective-permute-start | bytes 7077896 | tf_op jit(solution)/shard_map/ppermute | solution.py:632
  8.6 18.1 %collective-permute-start.2 = (bf16[384,768]{1,0:T(8,128)(2,1)S(1)}, bf16[384,768]{1,0:T(8,128)(2,1)S(1)}, u32[]{:S(2)}, u32[]{:S(2)}) collective-permute-start(bf16[384,768]{1,0:T(8,128)(2,1)S(1)} %copy-done.16), channel_id=1, source_target_pairs={{0,1},{1,0},{2,3},{3,2},{4,5},{5,4},{6,7},{7,6},{8,9},{9,8},{10,11... | collective-permute-start | bytes 1769480 | tf_op jit(solution)/shard_map/ppermute | solution.py:632
  9.1 18.5 %copy-start.3 = (bf16[512,768]{1,0:T(8,128)(2,1)S(1)}, bf16[512,768]{1,0:T(8,128)(2,1)}, u32[]{:S(2)}) copy-start(bf16[512,768]{1,0:T(8,128)(2,1)} %x_ref.3) | copy-start | bytes 2359300
  9.1 18.5 %copy-start.4 = (bf16[512,768]{1,0:T(8,128)(2,1)S(1)}, bf16[512,768]{1,0:T(8,128)(2,1)}, u32[]{:S(2)}) copy-start(bf16[512,768]{1,0:T(8,128)(2,1)} %up_ref.1) | copy-start | bytes 2359300
  9.1 18.5 %copy-start.6 = (bf16[768]{0:T(1024)(128)(2,1)S(1)}, bf16[768]{0:T(1024)(128)(2,1)}, u32[]{:S(2)}) copy-start(bf16[768]{0:T(1024)(128)(2,1)} %mub_ref.1) | copy-start | bytes 4612
  9.1 18.4 %copy-start.7 = (bf16[768]{0:T(1024)(128)(2,1)S(1)}, bf16[768]{0:T(1024)(128)(2,1)}, u32[]{:S(2)}) copy-start(bf16[768]{0:T(1024)(128)(2,1)} %dub_ref.1) | copy-start | bytes 4612
  9.1 18.4 %copy-start.8 = (bf16[768]{0:T(1024)(128)(2,1)S(1)}, bf16[768]{0:T(1024)(128)(2,1)}, u32[]{:S(2)}) copy-start(bf16[768]{0:T(1024)(128)(2,1)} %fg_ref.1) | copy-start | bytes 4612
  9.1 18.4 %copy-start.9 = (bf16[768]{0:T(1024)(128)(2,1)S(1)}, bf16[768]{0:T(1024)(128)(2,1)}, u32[]{:S(2)}) copy-start(bf16[768]{0:T(1024)(128)(2,1)} %fs_ref.1) | copy-start | bytes 4612
  9.2 18.4 %copy-start.10 = (bf16[768]{0:T(1024)(128)(2,1)S(1)}, bf16[768]{0:T(1024)(128)(2,1)}, u32[]{:S(2)}) copy-start(bf16[768]{0:T(1024)(128)(2,1)} %sg_ref.1) | copy-start | bytes 4612
  9.2 18.4 %copy-start.11 = (bf16[768]{0:T(1024)(128)(2,1)S(1)}, bf16[768]{0:T(1024)(128)(2,1)}, u32[]{:S(2)}) copy-start(bf16[768]{0:T(1024)(128)(2,1)} %ss_ref.1) | copy-start | bytes 4612
  9.2 18.4 %copy-start.12 = (bf16[64]{0:T(256)(128)(2,1)S(1)}, bf16[64]{0:T(256)(128)(2,1)}, u32[]{:S(2)}) copy-start(bf16[64]{0:T(256)(128)(2,1)} %mdb_ref.1) | copy-start | bytes 388
  9.2 18.4 %copy-start.13 = (bf16[64]{0:T(256)(128)(2,1)S(1)}, bf16[64]{0:T(256)(128)(2,1)}, u32[]{:S(2)}) copy-start(bf16[64]{0:T(256)(128)(2,1)} %ddb_ref.1) | copy-start | bytes 388
  25.0 1.7 %collective-permute-start.1 = (bf16[512,384]{1,0:T(8,128)(2,1)S(1)}, bf16[512,384]{1,0:T(8,128)(2,1)S(1)}, u32[]{:S(2)}, u32[]{:S(2)}) collective-permute-start(bf16[512,384]{1,0:T(8,128)(2,1)S(1)} %get-tuple-element.85.send_ref), channel_id=1, source_target_pairs={{0,1},{1,0},{2,3},{3,2},{4,5},{5,4},{6,7},{7,6},{8,9},{9,8},{10,11... | collective-permute-start | bytes 1179656 | tf_op jit(solution)/shard_map/ppermute | solution.py:632
  27.6 27.6 %copy-start.15 = (f32[1024,384]{1,0:T(8,128)S(1)}, f32[1024,384]{1,0:T(8,128)}, u32[]{:S(2)}) copy-start(f32[1024,384]{1,0:T(8,128)} %copy-done.14) | copy-start | bytes 4718596
  49.2 6.0 %collective-permute-start.5 = (bf16[512,384]{1,0:T(8,128)(2,1)S(1)}, bf16[512,384]{1,0:T(8,128)(2,1)S(1)}, u32[]{:S(2)}, u32[]{:S(2)}) collective-permute-start(bf16[512,384]{1,0:T(8,128)(2,1)S(1)} %get-tuple-element.90), channel_id=1, source_target_pairs={{0,1},{1,0},{2,3},{3,2},{4,5},{5,4},{6,7},{7,6},{8,9},{9,8},{10,11... | collective-permute-start | bytes 1179656 | tf_op jit(solution)/shard_map/ppermute | solution.py:632
  49.5 1.9 %collective-permute-start.6 = (bf16[144,768]{1,0:T(8,128)(2,1)S(1)}, bf16[144,768]{1,0:T(8,128)(2,1)S(1)}, u32[]{:S(2)}, u32[]{:S(2)}) collective-permute-start(bf16[144,768]{1,0:T(8,128)(2,1)S(1)} %get-tuple-element.92), channel_id=1, source_target_pairs={{0,1},{1,0},{2,3},{3,2},{4,5},{5,4},{6,7},{7,6},{8,9},{9,8},{10,11... | collective-permute-start | bytes 663560 | tf_op jit(solution)/shard_map/ppermute | solution.py:632
  51.4 14.5 %collective-permute-start.7 = (bf16[144,768]{1,0:T(8,128)(2,1)S(1)}, bf16[144,768]{1,0:T(8,128)(2,1)S(1)}, u32[]{:S(2)}, u32[]{:S(2)}) collective-permute-start(bf16[144,768]{1,0:T(8,128)(2,1)S(1)} %combine.5.held_ref), channel_id=1, source_target_pairs={{0,16},{2,18},{4,20},{6,22},{8,24},{10,26},{12,28},{14,30},{16,0},... | collective-permute-start | bytes 663560 | tf_op jit(solution)/shard_map/ppermute | solution.py:681
  66.0 7.2 %collective-permute-start.8 = (bf16[144,768]{1,0:T(8,128)(2,1)S(1)}, bf16[144,768]{1,0:T(8,128)(2,1)S(1)}, u32[]{:S(2)}, u32[]{:S(2)}) collective-permute-start(bf16[144,768]{1,0:T(8,128)(2,1)S(1)} %combine.6.held_ref), channel_id=1, source_target_pairs={{0,8},{2,10},{4,12},{6,14},{8,0},{10,2},{12,4},{14,6},{16,24},{18,... | collective-permute-start | bytes 663560 | tf_op jit(solution)/shard_map/ppermute | solution.py:681
  73.2 7.2 %collective-permute-start.9 = (bf16[144,768]{1,0:T(8,128)(2,1)S(1)}, bf16[144,768]{1,0:T(8,128)(2,1)S(1)}, u32[]{:S(2)}, u32[]{:S(2)}) collective-permute-start(bf16[144,768]{1,0:T(8,128)(2,1)S(1)} %combine.7.held_ref), channel_id=1, source_target_pairs={{0,4},{2,6},{4,0},{6,2},{8,12},{10,14},{12,8},{14,10},{16,20},{18,... | collective-permute-start | bytes 663560 | tf_op jit(solution)/shard_map/ppermute | solution.py:681
  81.7 2.4 %collective-permute-start.11 = (bf16[512,768]{1,0:T(8,128)(2,1)S(1)}, bf16[512,768]{1,0:T(8,128)(2,1)S(1)}, u32[]{:S(2)}, u32[]{:S(2)}) collective-permute-start(bf16[512,768]{1,0:T(8,128)(2,1)S(1)} %away.1), channel_id=1, source_target_pairs={{0,1},{1,0},{2,3},{3,2},{4,5},{5,4},{6,7},{7,6},{8,9},{9,8},{10,11... | collective-permute-start | bytes 2359304 | tf_op jit(solution)/shard_map/ppermute | solution.py:632
  81.8 7.9 %collective-permute-start.10 = (bf16[144,768]{1,0:T(8,128)(2,1)S(1)}, bf16[144,768]{1,0:T(8,128)(2,1)S(1)}, u32[]{:S(2)}, u32[]{:S(2)}) collective-permute-start(bf16[144,768]{1,0:T(8,128)(2,1)S(1)} %combine.8.held_ref), channel_id=1, source_target_pairs={{0,2},{2,0},{4,6},{6,4},{8,10},{10,8},{12,14},{14,12},{16,18},{18,... | collective-permute-start | bytes 663560 | tf_op jit(solution)/shard_map/ppermute | solution.py:681
  89.8 1.5 %collective-permute-start.12 = (bf16[144,768]{1,0:T(8,128)(2,1)S(1)}, bf16[144,768]{1,0:T(8,128)(2,1)S(1)}, u32[]{:S(2)}, u32[]{:S(2)}) collective-permute-start(bf16[144,768]{1,0:T(8,128)(2,1)S(1)} %combine.9.held_ref), channel_id=1, source_target_pairs={{0,1},{1,0},{2,3},{3,2},{4,5},{5,4},{6,7},{7,6},{8,9},{9,8},{10,11... | collective-permute-start | bytes 663560 | tf_op jit(solution)/shard_map/ppermute | solution.py:632
  (7 other events, 32.1 us)

commit v5 on v4

--- a/solution.py
+++ b/solution.py
@@ -187,8 +187,12 @@
 
             def key_block(j, c):
                 span = aligned(j, block)
+                ahead = scores(0, span, both, hide_of(0))
                 for p in range(pairs):
-                    e = jnp.exp2(scores(p, span, both, hide_of(p))).astype(BF16)
+                    s = ahead
+                    if p + 1 < pairs:
+                        ahead = scores(p + 1, span, both, hide_of(p + 1))
+                    e = jnp.exp2(s).astype(BF16)
                     share_refs[p][span, both] = e
                     for a in range(2):
                         head = slice((2 * p + a) * TURNED, (2 * p + a + 1) * TURNED)
@@ -558,7 +562,7 @@
             pltpu.SemaphoreType.DMA((10,)),
             pltpu.SemaphoreType.DMA,
         ],
-        compiler_params=pltpu.CompilerParams(vmem_limit_bytes=36 * MIB),
+        compiler_params=pltpu.CompilerParams(vmem_limit_bytes=32 * MIB),
         cost_estimate=pl.CostEstimate(flops=2 * 10**10, bytes_accessed=16 * MIB, transcendentals=10**6),
         name="middle",
     )(half_index, x, keep, got, up, *vectors, *map(in_hbm, matrices))
@@ -582,7 +586,8 @@
     )(held, got)
 
 
-def finish_kernel(half_ref, held_ref, got_ref, md_ref, mu_ref, dd_ref, du_ref, vec_ref, bias_ref, ratio_ref):
+def finish_kernel(half_ref, held_ref, got_ref, md_ref, mdb_ref, mu_ref, mub_ref, dd_ref, ddb_ref, du_ref, dub_ref,
+                  fg_ref, fs_ref, sg_ref, ss_ref, ratio_ref):
     adapt = md_ref.shape[0]
 
     def write(first_ref, second_ref):
@@ -590,6 +595,16 @@
         mu_ref[...] = first_ref[adapt : 2 * adapt, :].astype(F32)
         dd_ref[...] = second_ref[:adapt, :].astype(F32)
         du_ref[...] = second_ref[adapt : 2 * adapt, :].astype(F32)
+        vectors = vectors_of(first_ref[2 * adapt :, :])
+        for row, out_ref in enumerate((mub_ref, dub_ref, fg_ref, fs_ref, sg_ref, ss_ref)):
+            out_ref[...] = vectors[row, :]
+        last = vectors[6:7, :]
+        mdb_ref[...] = last[0, :adapt]
+        ddb_ref[...] = last[0, adapt : 2 * adapt]
+        squares = last[:, 2 * adapt : 2 * adapt + 128]
+        lane = lax.broadcasted_iota(jnp.int32, (1, 128), 1)
+        base = jnp.sum(jnp.where(lane == 2, squares, 0.0), -1, keepdims=True)
+        ratio_ref[...] = jnp.sqrt(squares / base)[0, :2]
 
     @pl.when(half_ref[0] == 0)
     def _():
@@ -599,30 +614,16 @@
     def _():
         write(got_ref, held_ref)
 
-    vectors = vectors_of(held_ref[2 * adapt :, :])
-    vec_ref[...] = vectors
-    last = vectors[6:7, :]
-    bias_ref[0:1, :] = last[:, :adapt]
-    bias_ref[1:2, :] = last[:, adapt : 2 * adapt]
-    squares = last[:, 2 * adapt : 2 * adapt + 128]
-    lane = lax.broadcasted_iota(jnp.int32, (1, 128), 1)
-    base = jnp.sum(jnp.where(lane == 2, squares, 0.0), -1, keepdims=True)
-    ratio_ref[...] = jnp.sqrt(squares / base)
-
 
 def finish(half_index, held, got, adapt):
     features = held.shape[1]
     matrix = jax.ShapeDtypeStruct((adapt, features), F32)
+    short, vector = jax.ShapeDtypeStruct((adapt,), F32), jax.ShapeDtypeStruct((features,), F32)
     return pl.pallas_call(
         finish_kernel,
-        out_shape=(matrix,) * 4
-        + (
-            jax.ShapeDtypeStruct((8, features), F32),
-            jax.ShapeDtypeStruct((2, adapt), F32),
-            jax.ShapeDtypeStruct((1, 128), F32),
-        ),
+        out_shape=(matrix, short, matrix, vector) * 2 + (vector,) * 4 + (jax.ShapeDtypeStruct((2,), F32),),
         in_specs=[SM, VM, VM],
-        out_specs=(VM,) * 7,
+        out_specs=(VM,) * 13,
         compiler_params=pltpu.CompilerParams(vmem_limit_bytes=4 * MIB),
         name="finish",
     )(half_index, held, got)
@@ -648,7 +649,9 @@
     kv, queries, across, turned, item, hide, rng = project(
         half_index, segment_ids, tokens, query_weight, key_weight, value_weight
     )
-    other_tokens, output_late, inner_late, outer_late = tie(other_tokens, output_weight, inner_weight, outer_weight)
+    kv, other_tokens, output_late, inner_late, outer_late = tie(
+        kv, other_tokens, output_weight, inner_weight, outer_weight
+    )
     other_output = swap_cores(output_late)
     other_inner = swap_cores(inner_late)
     other_outer = swap_cores(outer_late)
@@ -673,12 +676,14 @@
     while 2 ** len(steps) < devices:
         steps.append(2 ** len(steps))
     steps.reverse()
+    turn = len(steps) // 2
     pairs = len(shares)
     grads = []
-    away = None
     weights = (query_weight, key_weight, value_weight)
     for n, step in enumerate(steps):
-        arriving = lax.ppermute(packed, "dp", [(i, i ^ step) for i in range(devices)])
+        other_step = steps[(n + turn) % len(steps)]
+        exchange = [(2 * i + c, 2 * (i ^ s) + c) for i in range(devices) for c, s in enumerate((step, other_step))]
+        arriving = lax.ppermute(packed, ("dp", "mp"), exchange)
         if n < pairs:
             got_grad, packed = tie(got_grad, packed)
             parts = pair_grad(n, half_index, rng, kv, queries, keep, send, own_grad, got_grad, inverse, shares[n])
@@ -690,10 +695,8 @@
             input_grad = input_call(home_kernel, half_index, (first_grad, away), pieces, weights, "home")
             arriving, input_grad = tie(arriving, input_grad)
         packed = combine(packed, arriving)
-    md, mu, dd, du, vec, bias, ratio = finish(half_index, packed, swap_cores(packed), adapt)
-    return (
-        result, input_grad, md.T, bias[0], mu, vec[0], dd.T, bias[1], du, vec[1], vec[2], vec[3], vec[4], vec[5], ratio[0, :2],
-    )
+    md, mdb, mu, mub, dd, ddb, du, dub, *rest = finish(half_index, packed, swap_cores(packed), adapt)
+    return (result, input_grad, md.T, mdb, mu, mub, dd.T, ddb, du, dub, *rest)
 
 
 def solution(mesh):

time: 94.1 us -> 81.6 us (0.87)
  waiting for transfers between devices: 17.2 us -> 8.15 us
  Pallas kernels: 62.4 us -> 59.4 us
  local copies, waits for them, and re-layouts: 4.42 us -> 3.1 us
    ppermute x4, waiting for transfers between devices: 8.95 us -> 2.07 us  [per_device(): arriving = lax.ppermute(packed, ('dp', 'mp'), exchange)]
    pallas_call x1, Pallas kernels: 14.6 us -> 11.7 us  [attention(): pl.pallas_call(attention_kernel, out_shape=(like(kv), like(queries), jax....]
    ppermute x9, waiting for transfers between devices: 8.26 us -> 6.07 us  [swap_cores(): return lax.ppermute(value, 'mp', [(0, 1), (1, 0)])]
    squeeze x2 -> x0, local copies, waits for them, and re-layouts: 1.03 us -> none  [the longest x1 0.52 us: per_device(): bias[1]]
  transfers between devices with their start and end apart: 13 -> 13, of which waited for: 8 -> 6; matrix products, arithmetic and copies ran while one was open for 0% -> 0% of each run, Pallas kernels for 41% -> 44%
where the time goes in v5:
time: 81.6 us; the launch traced here: 81.4 us
  Pallas kernels  59.4 us (73%)
  starting transfers between devices  9.68 us (12%)
  waiting for transfers between devices  8.15 us (10%)
  local copies, waits for them, and re-layouts  3.1 us (4%)
  between operations  1.04 us (1%)
    pallas_call x1, Pallas kernels, middle(): pl.pallas_call(middle_kernel, out_shape=(jax.ShapeDtypeStruct((rows, feat...  21.5 us
    pallas_call x3, Pallas kernels, pair_grad(): pl.pallas_call(functools.partial(pair_grad_kernel, p), out_shape=(jax.Sha...  17.5 us
    pallas_call x1, Pallas kernels, attention(): pl.pallas_call(attention_kernel, out_shape=(like(kv), like(queries), jax....  11.7 us
    ppermute x4, starting transfers between devices, per_device(): arriving = lax.ppermute(packed, ('dp', 'mp'), exchange)  7.28 us
    ppermute x9, waiting for transfers between devices, swap_cores(): return lax.ppermute(value, 'mp', [(0, 1), (1, 0)])  6.07 us
    pallas_call x1, Pallas kernels, project(): pl.pallas_call(project_kernel, out_shape=(jax.ShapeDtypeStruct((count, 2...  4.11 us
    pallas_call x2, Pallas kernels, input_call(): pl.pallas_call(kernel, out_shape=jax.ShapeDtypeStruct((half, features), B...  3.41 us
    unnamed x36, local copies, waits for them, and re-layouts  3.1 us
  transfers between devices with their start and end apart: 13, of which 6 were waited for; matrix products, arithmetic and copies ran while one was open for 0% of the time, Pallas kernels for 44%

profile of v5, /device:TPU:0, one launch (start us, length us, event | category | flops | bytes accessed | tf_op | source)
XLA Modules:
  0.0 81.4 jit_solution(2263991426943179901)
XLA Ops:
  0.7 0.5 collective-permute-start
  1.2 0.7 copy-done.5
  1.9 4.1 %project.1 = (bf16[1024,768]{1,0:T(8,128)(2,1)S(1)}, bf16[3,2048,128]{2,1,0:T(8,128)(2,1)S(1)}, bf16[3,128,2048]{2,1,0:T(8,128)(2,1)S(1)}, bf16[480,1024]{1,0:T(...) custom-call(s32[1]{0:T(128)} %bitcast.half_ref, ...), custom_call_target="tpu_custom_call" | custom-call | flops 905969664 | bytes 5242880 | tf_op jit(solution)/shard_map/project/pallas_call | solution.py:141
  6.9 11.7 %attention.1 = (bf16[1024,768]{1,0:T(8,128)(2,1)S(1)}, bf16[3,2048,128]{2,1,0:T(8,128)(2,1)S(1)}, bf16[512,384]{1,0:T(8,128)(2,1)S(1)}, bf16[512,384]{1,0:T(8,12...) custom-call(s32[1]{0:T(128)} %bitcast.half_ref, ...), custom_call_target="tpu_custom_call" | custom-call | flops 10000000000 | bytes 8388608 | tf_op jit(solution)/shard_map/attention/pallas_call | solution.py:260
  19.0 1.4 %collective-permute-done.1.got_ref = bf16[512,384]{1,0:T(8,128)(2,1)S(1)} collective-permute-done((bf16[512,384]{1,0:T(8,128)(2,1)S(1)}, bf16[512,384]{1,0:T(8,128)(2,1)S(1)}, u32[]{:S(2)}, u32[]{:S(2)}) %collective-permute-start.1) | collective-permute-done | bytes 393248 | tf_op jit(solution)/shard_map/ppermute | solution.py:633
  20.4 1.4 %copy-done.14 = bf16[768,1536]{1,0:T(8,128)(2,1)} copy-done((bf16[768,1536]{1,0:T(8,128)(2,1)}, bf16[768,1536]{1,0:T(8,128)(2,1)S(1)}, u32[]{:S(2)}) %copy-start.14) | copy-done | bytes 2359320
  21.8 0.8 copy-done.15
  22.8 21.5 %middle.1 = (bf16[512,768]{1,0:T(8,128)(2,1)}, f32[512,768]{1,0:T(8,128)S(1)}, bf16[512,384]{1,0:T(8,128)(2,1)S(1)}, bf16[512,384]{1,0:T(8,128)(2,1)S(1)}, bf16[...) custom-call(s32[1]{0:T(128)} %bitcast.half_ref, bf16[512,768]{1,0:T(8,128)(2,1)S(1)} %copy-done.3, ...), custom_call_target="tpu_custom_call" | custom-call | flops 20000000000 | bytes 16777216 | tf_op jit(solution)/shard_map/middle/pallas_call | solution.py:542
  44.3 0.4 collective-permute-start.5
  44.8 1.5 %collective-permute-done.6.got_ref = bf16[144,768]{1,0:T(8,128)(2,1)S(1)} collective-permute-done((bf16[144,768]{1,0:T(8,128)(2,1)S(1)}, bf16[144,768]{1,0:T(8,128)(2,1)S(1)}, u32[]{:S(2)}, u32[]{:S(2)}) %collective-permute-start.6) | collective-permute-done | bytes 221216 | tf_op jit(solution)/shard_map/ppermute | solution.py:633
  46.4 4.0 %collective-permute-start.7 = (bf16[144,768]{1,0:T(8,128)(2,1)S(1)}, bf16[144,768]{1,0:T(8,128)(2,1)S(1)}, u32[]{:S(2)}, u32[]{:S(2)}) collective-permute-start(bf16[144,768]{1,0:T(8,128)(2,1)S(1)} %combine.5.held_ref), channel_id=1, source_target_pairs={{0,16},{1,5},{2,18},{3,7},{4,20},{5,1},{6,22},{7,3},{8,24},{9,13},... | collective-permute-start | bytes 663560 | tf_op jit(solution)/shard_map/ppermute | solution.py:686
  50.5 5.8 %pair_grad_0.1 = (bf16[1024,128]{1,0:T(8,128)(2,1)S(1)}, bf16[1024,128]{1,0:T(8,128)(2,1)S(1)}, bf16[1024,128]{1,0:T(8,128)(2,1)S(1)}) custom-call(s32[1]{0:T(128)} %bitcast.half_ref, s32[2,4]{1,0:T(2,128)S(1)} %get-tuple-element.83.rng_ref, bf16[1024,768]{1,0:T(8,128)(2,1)S(1)} %get-tuple-element.103.kv_ref, ...), custom_call_target="tpu_custom_call" | custom-call | flops 4000000000 | bytes 8388608 | tf_op jit(solution)/shard_map/pair_grad_0/pallas_call | solution.py:337
  56.3 0.5 collective-permute-done.7.got_ref
  56.8 1.2 %collective-permute-start.8 = (bf16[144,768]{1,0:T(8,128)(2,1)S(1)}, bf16[144,768]{1,0:T(8,128)(2,1)S(1)}, u32[]{:S(2)}, u32[]{:S(2)}) collective-permute-start(bf16[144,768]{1,0:T(8,128)(2,1)S(1)} %combine.6.held_ref), channel_id=1, source_target_pairs={{0,8},{1,3},{2,10},{3,1},{4,12},{5,7},{6,14},{7,5},{8,0},{9,11},{1... | collective-permute-start | bytes 663560 | tf_op jit(solution)/shard_map/ppermute | solution.py:686
  58.0 5.8 %pair_grad_1.1 = (bf16[1024,128]{1,0:T(8,128)(2,1)S(1)}, bf16[1024,128]{1,0:T(8,128)(2,1)S(1)}, bf16[1024,128]{1,0:T(8,128)(2,1)S(1)}) custom-call(s32[1]{0:T(128)} %bitcast.half_ref, s32[2,4]{1,0:T(2,128)S(1)} %get-tuple-element.83.rng_ref, bf16[1024,768]{1,0:T(8,128)(2,1)S(1)} %get-tuple-element.103.kv_ref, ...), custom_call_target="tpu_custom_call" | custom-call | flops 4000000000 | bytes 8388608 | tf_op jit(solution)/shard_map/pair_grad_1/pallas_call | solution.py:337
  63.9 1.6 %collective-permute-start.9 = (bf16[144,768]{1,0:T(8,128)(2,1)S(1)}, bf16[144,768]{1,0:T(8,128)(2,1)S(1)}, u32[]{:S(2)}, u32[]{:S(2)}) collective-permute-start(bf16[144,768]{1,0:T(8,128)(2,1)S(1)} %combine.7.held_ref), channel_id=1, source_target_pairs={{0,4},{1,17},{2,6},{3,19},{4,0},{5,21},{6,2},{7,23},{8,12},{9,25},... | collective-permute-start | bytes 663560 | tf_op jit(solution)/shard_map/ppermute | solution.py:686
  65.5 5.8 %pair_grad_2.1 = (bf16[1024,128]{1,0:T(8,128)(2,1)S(1)}, bf16[1024,128]{1,0:T(8,128)(2,1)S(1)}, bf16[1024,128]{1,0:T(8,128)(2,1)S(1)}) custom-call(s32[1]{0:T(128)} %bitcast.half_ref, s32[2,4]{1,0:T(2,128)S(1)} %get-tuple-element.83.rng_ref, bf16[1024,768]{1,0:T(8,128)(2,1)S(1)} %get-tuple-element.103.kv_ref, ...), custom_call_target="tpu_custom_call" | custom-call | flops 4000000000 | bytes 8388608 | tf_op jit(solution)/shard_map/pair_grad_2/pallas_call | solution.py:337
  71.3 1.2 %away.1 = bf16[512,768]{1,0:T(8,128)(2,1)S(1)} custom-call(s32[1]{0:T(128)} %bitcast.half_ref, bf16[1024,128]{1,0:T(8,128)(2,1)S(1)} %get-tuple-element.127.refs_0_, bf16[1024,128]{1,0:T(8,128)(2,1)S(1)} %get-tuple-element.128.refs_1_, bf16[1024,128]{1,0:T(8,128)(2,1)S(1)} %get-tuple-element.129.refs_2_, bf16[1024,128]{1,0:T(8,128)(2,1)S(1)} %get-tuple-element.130.refs_3_, ...), custom_call_target="tpu_custom_call" | custom-call | flops 1000000000 | bytes 6291456 | tf_op jit(solution)/shard_map/away/pallas_call | solution.py:378
  72.7 0.5 collective-permute-start.10
  73.2 1.7 %collective-permute-done.11.got_ref = bf16[512,768]{1,0:T(8,128)(2,1)S(1)} collective-permute-done((bf16[512,768]{1,0:T(8,128)(2,1)S(1)}, bf16[512,768]{1,0:T(8,128)(2,1)S(1)}, u32[]{:S(2)}, u32[]{:S(2)}) %collective-permute-start.11) | collective-permute-done | bytes 786464 | tf_op jit(solution)/shard_map/ppermute | solution.py:633
  74.9 2.2 %home.1 = bf16[512,768]{1,0:T(8,128)(2,1)} custom-call(s32[1]{0:T(128)} %bitcast.half_ref, f32[512,768]{1,0:T(8,128)S(1)} %get-tuple-element.126.first_ref, bf16[512,768]{1,0:T(8,128)(2,1)S(1)} %collective-permute-done.11.got_ref, bf16[1024,128]{1,0:T(8,128)(2,1)S(1)} %get-tuple-element.127.refs_0_, bf16[1024,128]{1,0:T(8,128)(2,1)S(1)} %get-tuple-element.128.refs_1_, ...), custom_call_target="tpu_custom_call" | custom-call | flops 1000000000 | bytes 6291456 | tf_op jit(solution)/shard_map/home/pallas_call | solution.py:378
  77.1 1.6 %collective-permute-done.10.got_ref = bf16[144,768]{1,0:T(8,128)(2,1)S(1)} collective-permute-done((bf16[144,768]{1,0:T(8,128)(2,1)S(1)}, bf16[144,768]{1,0:T(8,128)(2,1)S(1)}, u32[]{:S(2)}, u32[]{:S(2)}) %collective-permute-start.10) | collective-permute-done | bytes 221216 | tf_op jit(solution)/shard_map/ppermute | solution.py:686
  78.9 1.5 %collective-permute-done.12.got_ref = bf16[144,768]{1,0:T(8,128)(2,1)S(1)} collective-permute-done((bf16[144,768]{1,0:T(8,128)(2,1)S(1)}, bf16[144,768]{1,0:T(8,128)(2,1)S(1)}, u32[]{:S(2)}, u32[]{:S(2)}) %collective-permute-start.12) | collective-permute-done | bytes 221216 | tf_op jit(solution)/shard_map/ppermute | solution.py:633
  80.3 1.0 %finish.1 = (f32[64,768]{1,0:T(8,128)}, f32[64]{0:T(128)}, f32[64,768]{1,0:T(8,128)}, f32[768]{0:T(1024)}, f32[64,768]{1,0:T(8,128)}, /*index=5*/f32[64]{0:T(128...) custom-call(s32[1]{0:T(128)} %bitcast.half_ref, ...), custom_call_target="tpu_custom_call" | custom-call | tf_op jit(solution)/shard_map/finish/pallas_call | solution.py:622
  (52 shorter events, 2.0 us)
Async XLA Ops:
  0.6 6.1 %copy-start = (bf16[768,384]{1,0:T(8,128)(2,1)S(1)}, bf16[768,384]{1,0:T(8,128)(2,1)}, u32[]{:S(2)}) copy-start(bf16[768,384]{1,0:T(8,128)(2,1)} %refs_9_.3) | copy-start | bytes 1769476
  0.7 5.3 %collective-permute-start = (bf16[512,768]{1,0:T(8,128)(2,1)}, bf16[512,768]{1,0:T(8,128)(2,1)S(1)}, u32[]{:S(2)}, u32[]{:S(2)}) collective-permute-start(bf16[512,768]{1,0:T(8,128)(2,1)} %x_ref.3), channel_id=1, source_target_pairs={{0,1},{1,0},{2,3},{3,2},{4,5},{5,4},{6,7},{7,6},{8,9},{9,8},{10,11... | collective-permute-start | bytes 2359304 | tf_op jit(solution)/shard_map/ppermute | solution.py:633
  6.0 14.3 %collective-permute-start.3 = (bf16[768,1536]{1,0:T(8,128)(2,1)}, bf16[768,1536]{1,0:T(8,128)(2,1)S(1)}, u32[]{:S(2)}, u32[]{:S(2)}) collective-permute-start(bf16[768,1536]{1,0:T(8,128)(2,1)} %w1_hbm.1), channel_id=1, source_target_pairs={{0,1},{1,0},{2,3},{3,2},{4,5},{5,4},{6,7},{7,6},{8,9},{9,8},{10,11... | collective-permute-start | bytes 7077896 | tf_op jit(solution)/shard_map/ppermute | solution.py:633
  6.2 14.1 %collective-permute-start.4 = (bf16[1536,768]{1,0:T(8,128)(2,1)}, bf16[1536,768]{1,0:T(8,128)(2,1)S(1)}, u32[]{:S(2)}, u32[]{:S(2)}) collective-permute-start(bf16[1536,768]{1,0:T(8,128)(2,1)} %w2_hbm.1), channel_id=1, source_target_pairs={{0,1},{1,0},{2,3},{3,2},{4,5},{5,4},{6,7},{7,6},{8,9},{9,8},{10,11... | collective-permute-start | bytes 7077896 | tf_op jit(solution)/shard_map/ppermute | solution.py:633
  6.6 13.8 %collective-permute-start.2 = (bf16[384,768]{1,0:T(8,128)(2,1)S(1)}, bf16[384,768]{1,0:T(8,128)(2,1)S(1)}, u32[]{:S(2)}, u32[]{:S(2)}) collective-permute-start(bf16[384,768]{1,0:T(8,128)(2,1)S(1)} %copy-done.16), channel_id=1, source_target_pairs={{0,1},{1,0},{2,3},{3,2},{4,5},{5,4},{6,7},{7,6},{8,9},{9,8},{10,11... | collective-permute-start | bytes 1769480 | tf_op jit(solution)/shard_map/ppermute | solution.py:633
  6.8 16.0 %copy-start.3 = (bf16[512,768]{1,0:T(8,128)(2,1)S(1)}, bf16[512,768]{1,0:T(8,128)(2,1)}, u32[]{:S(2)}) copy-start(bf16[512,768]{1,0:T(8,128)(2,1)} %x_ref.3) | copy-start | bytes 2359300
  6.8 16.0 %copy-start.4 = (bf16[512,768]{1,0:T(8,128)(2,1)S(1)}, bf16[512,768]{1,0:T(8,128)(2,1)}, u32[]{:S(2)}) copy-start(bf16[512,768]{1,0:T(8,128)(2,1)} %up_ref.1) | copy-start | bytes 2359300
  6.8 15.9 %copy-start.6 = (bf16[768]{0:T(1024)(128)(2,1)S(1)}, bf16[768]{0:T(1024)(128)(2,1)}, u32[]{:S(2)}) copy-start(bf16[768]{0:T(1024)(128)(2,1)} %mub_ref.1) | copy-start | bytes 4612
  6.8 15.9 %copy-start.7 = (bf16[768]{0:T(1024)(128)(2,1)S(1)}, bf16[768]{0:T(1024)(128)(2,1)}, u32[]{:S(2)}) copy-start(bf16[768]{0:T(1024)(128)(2,1)} %dub_ref.1) | copy-start | bytes 4612
  6.8 15.9 %copy-start.8 = (bf16[768]{0:T(1024)(128)(2,1)S(1)}, bf16[768]{0:T(1024)(128)(2,1)}, u32[]{:S(2)}) copy-start(bf16[768]{0:T(1024)(128)(2,1)} %fg_ref.1) | copy-start | bytes 4612
  6.8 15.9 %copy-start.9 = (bf16[768]{0:T(1024)(128)(2,1)S(1)}, bf16[768]{0:T(1024)(128)(2,1)}, u32[]{:S(2)}) copy-start(bf16[768]{0:T(1024)(128)(2,1)} %fs_ref.1) | copy-start | bytes 4612
  6.8 15.9 %copy-start.10 = (bf16[768]{0:T(1024)(128)(2,1)S(1)}, bf16[768]{0:T(1024)(128)(2,1)}, u32[]{:S(2)}) copy-start(bf16[768]{0:T(1024)(128)(2,1)} %sg_ref.1) | copy-start | bytes 4612
  6.8 15.9 %copy-start.11 = (bf16[768]{0:T(1024)(128)(2,1)S(1)}, bf16[768]{0:T(1024)(128)(2,1)}, u32[]{:S(2)}) copy-start(bf16[768]{0:T(1024)(128)(2,1)} %ss_ref.1) | copy-start | bytes 4612
  6.9 15.9 %copy-start.12 = (bf16[64]{0:T(256)(128)(2,1)S(1)}, bf16[64]{0:T(256)(128)(2,1)}, u32[]{:S(2)}) copy-start(bf16[64]{0:T(256)(128)(2,1)} %mdb_ref.1) | copy-start | bytes 388
  6.9 15.9 %copy-start.13 = (bf16[64]{0:T(256)(128)(2,1)S(1)}, bf16[64]{0:T(256)(128)(2,1)}, u32[]{:S(2)}) copy-start(bf16[64]{0:T(256)(128)(2,1)} %ddb_ref.1) | copy-start | bytes 388
  18.6 1.8 %collective-permute-start.1 = (bf16[512,384]{1,0:T(8,128)(2,1)S(1)}, bf16[512,384]{1,0:T(8,128)(2,1)S(1)}, u32[]{:S(2)}, u32[]{:S(2)}) collective-permute-start(bf16[512,384]{1,0:T(8,128)(2,1)S(1)} %get-tuple-element.93.send_ref), channel_id=1, source_target_pairs={{0,1},{1,0},{2,3},{3,2},{4,5},{5,4},{6,7},{7,6},{8,9},{9,8},{10,11... | collective-permute-start | bytes 1179656 | tf_op jit(solution)/shard_map/ppermute | solution.py:633
  44.3 6.2 %collective-permute-start.5 = (bf16[512,384]{1,0:T(8,128)(2,1)S(1)}, bf16[512,384]{1,0:T(8,128)(2,1)S(1)}, u32[]{:S(2)}, u32[]{:S(2)}) collective-permute-start(bf16[512,384]{1,0:T(8,128)(2,1)S(1)} %get-tuple-element.98), channel_id=1, source_target_pairs={{0,1},{1,0},{2,3},{3,2},{4,5},{5,4},{6,7},{7,6},{8,9},{9,8},{10,11... | collective-permute-start | bytes 1179656 | tf_op jit(solution)/shard_map/ppermute | solution.py:633
  44.7 1.7 %collective-permute-start.6 = (bf16[144,768]{1,0:T(8,128)(2,1)S(1)}, bf16[144,768]{1,0:T(8,128)(2,1)S(1)}, u32[]{:S(2)}, u32[]{:S(2)}) collective-permute-start(bf16[144,768]{1,0:T(8,128)(2,1)S(1)} %get-tuple-element.100), channel_id=1, source_target_pairs={{0,1},{1,0},{2,3},{3,2},{4,5},{5,4},{6,7},{7,6},{8,9},{9,8},{10,11... | collective-permute-start | bytes 663560 | tf_op jit(solution)/shard_map/ppermute | solution.py:633
  46.4 10.3 %collective-permute-start.7 = (bf16[144,768]{1,0:T(8,128)(2,1)S(1)}, bf16[144,768]{1,0:T(8,128)(2,1)S(1)}, u32[]{:S(2)}, u32[]{:S(2)}) collective-permute-start(bf16[144,768]{1,0:T(8,128)(2,1)S(1)} %combine.5.held_ref), channel_id=1, source_target_pairs={{0,16},{1,5},{2,18},{3,7},{4,20},{5,1},{6,22},{7,3},{8,24},{9,13},... | collective-permute-start | bytes 663560 | tf_op jit(solution)/shard_map/ppermute | solution.py:686
  56.8 7.0 %collective-permute-start.8 = (bf16[144,768]{1,0:T(8,128)(2,1)S(1)}, bf16[144,768]{1,0:T(8,128)(2,1)S(1)}, u32[]{:S(2)}, u32[]{:S(2)}) collective-permute-start(bf16[144,768]{1,0:T(8,128)(2,1)S(1)} %combine.6.held_ref), channel_id=1, source_target_pairs={{0,8},{1,3},{2,10},{3,1},{4,12},{5,7},{6,14},{7,5},{8,0},{9,11},{1... | collective-permute-start | bytes 663560 | tf_op jit(solution)/shard_map/ppermute | solution.py:686
  63.9 7.4 %collective-permute-start.9 = (bf16[144,768]{1,0:T(8,128)(2,1)S(1)}, bf16[144,768]{1,0:T(8,128)(2,1)S(1)}, u32[]{:S(2)}, u32[]{:S(2)}) collective-permute-start(bf16[144,768]{1,0:T(8,128)(2,1)S(1)} %combine.7.held_ref), channel_id=1, source_target_pairs={{0,4},{1,17},{2,6},{3,19},{4,0},{5,21},{6,2},{7,23},{8,12},{9,25},... | collective-permute-start | bytes 663560 | tf_op jit(solution)/shard_map/ppermute | solution.py:686
  72.6 2.4 %collective-permute-start.11 = (bf16[512,768]{1,0:T(8,128)(2,1)S(1)}, bf16[512,768]{1,0:T(8,128)(2,1)S(1)}, u32[]{:S(2)}, u32[]{:S(2)}) collective-permute-start(bf16[512,768]{1,0:T(8,128)(2,1)S(1)} %away.1), channel_id=1, source_target_pairs={{0,1},{1,0},{2,3},{3,2},{4,5},{5,4},{6,7},{7,6},{8,9},{9,8},{10,11... | collective-permute-start | bytes 2359304 | tf_op jit(solution)/shard_map/ppermute | solution.py:633
  72.7 6.0 %collective-permute-start.10 = (bf16[144,768]{1,0:T(8,128)(2,1)S(1)}, bf16[144,768]{1,0:T(8,128)(2,1)S(1)}, u32[]{:S(2)}, u32[]{:S(2)}) collective-permute-start(bf16[144,768]{1,0:T(8,128)(2,1)S(1)} %combine.8.held_ref), channel_id=1, source_target_pairs={{0,2},{1,9},{2,0},{3,11},{4,6},{5,13},{6,4},{7,15},{8,10},{9,1},{1... | collective-permute-start | bytes 663560 | tf_op jit(solution)/shard_map/ppermute | solution.py:686
  78.8 1.5 %collective-permute-start.12 = (bf16[144,768]{1,0:T(8,128)(2,1)S(1)}, bf16[144,768]{1,0:T(8,128)(2,1)S(1)}, u32[]{:S(2)}, u32[]{:S(2)}) collective-permute-start(bf16[144,768]{1,0:T(8,128)(2,1)S(1)} %combine.9.held_ref), channel_id=1, source_target_pairs={{0,1},{1,0},{2,3},{3,2},{4,5},{5,4},{6,7},{7,6},{8,9},{9,8},{10,11... | collective-permute-start | bytes 663560 | tf_op jit(solution)/shard_map/ppermute | solution.py:633
  (7 other events, 23.6 us)

commit v6 on v5

--- a/solution.py
+++ b/solution.py
@@ -21,6 +21,7 @@
 SMALLEST = 2.0**-60
 TURNED = 80
 BLOCK = 256
+STEP = 128
 MIB = 1 << 20
 
 VM = pl.BlockSpec(memory_space=pltpu.VMEM)
@@ -104,23 +105,39 @@
             turned_ref[base + HEAD_DIM : base + TURNED, aligned(which, rows)] = ones
 
 
+def over_keys(low, high, visit):
+    def whole(t, c):
+        visit(pl.ds(pl.multiple_of(low * STEP + t * BLOCK, STEP), BLOCK), BLOCK)
+        return c
+
+    lax.fori_loop(0, (high - low) // 2, whole, 0)
+
+    @pl.when((high - low) % 2 == 1)
+    def _():
+        visit(pl.ds(pl.multiple_of((high - 1) * STEP, STEP), STEP), STEP)
+
+
 def is_shift(lane):
     return (lane == 63) | (lane == 95) | (lane == 127)
 
 
 def project_kernel(
-    half_ref, ids_ref, seg_ref, x_ref, wq_ref, wk_ref, wv_ref,
+    seg_hbm, x_ref, wq_ref, wk_ref, wv_ref,
     kv_ref, queries_ref, across_ref, turned_ref, item_ref, hide_ref, rng_ref,
-    x_buf, wq, wk, wv, sems,
+    seg_ref, x_buf, wq, wk, wv, sems,
 ):
-    copies = start_all((x_ref, wq_ref, wk_ref, wv_ref), (x_buf, wq, wk, wv), sems)
+    sources, buffers = (seg_hbm, x_ref, wq_ref, wk_ref, wv_ref), (seg_ref, x_buf, wq, wk, wv)
+    seg_copy, *copies = start_all(sources, buffers, sems)
     count, block = kv_ref.shape[0], BLOCK
+    seg_copy.wait()
     ids = seg_ref[...].astype(F32)
+    position = lax.broadcasted_iota(jnp.int32, ids.shape, 1)
     for g in range(count // block):
-        first = ids_ref[0, g * block].astype(F32)
-        last = ids_ref[0, (g + 1) * block - 1].astype(F32)
-        rng_ref[0, g] = jnp.sum(jnp.where(ids < first, 1.0, 0.0)).astype(jnp.int32) // block
-        rng_ref[1, g] = (jnp.sum(jnp.where(ids <= last, 1.0, 0.0)).astype(jnp.int32) + block - 1) // block
+        first, last = (
+            jnp.sum(jnp.where(position == at, ids, 0.0), -1, keepdims=True) for at in (g * block, (g + 1) * block - 1)
+        )
+        rng_ref[0, g] = jnp.sum(jnp.where(ids < first, 1.0, 0.0)).astype(jnp.int32) // STEP
+        rng_ref[1, g] = (jnp.sum(jnp.where(ids <= last, 1.0, 0.0)).astype(jnp.int32) + STEP - 1) // STEP
     lane = lax.broadcasted_iota(jnp.int32, (128, 128), 1)
     for t in range(count // 128):
         same = jnp.broadcast_to(ids[:, t * 128 : (t + 1) * 128], (128, 128)).T == lane.astype(F32)
@@ -132,10 +149,10 @@
         for a in range(2):
             hide_ref[:, (2 * t + a) * block : (2 * t + a + 1) * block] = hide
     copies[0].wait()
-    write_projection(half_ref[0], x_buf[...], (wq, wk, wv), copies[1:], kv_ref, queries_ref, across_ref, turned_ref)
-
-
-def project(half_index, seg, x, wq, wk, wv):
+    write_projection(lax.axis_index("mp"), x_buf[...], (wq, wk, wv), copies[1:], kv_ref, queries_ref, across_ref, turned_ref)
+
+
+def project(seg, x, wq, wk, wv):
     rows, width = x.shape[0], wq.shape[1]
     count, pairs = 2 * rows, width // PAIR
     return pl.pallas_call(
@@ -149,17 +166,17 @@
             jax.ShapeDtypeStruct((128, 2 * count), BF16),
             jax.ShapeDtypeStruct((2, count // BLOCK), jnp.int32),
         ),
-        in_specs=[SM, SM, VM] + [HB] * 4,
+        in_specs=[HB] * 5,
         out_specs=(VM,) * 6 + (SM,),
-        scratch_shapes=[pltpu.VMEM(v.shape, BF16) for v in (x, wq, wk, wv)] + [pltpu.SemaphoreType.DMA((4,))],
+        scratch_shapes=[pltpu.VMEM(v.shape, v.dtype) for v in (seg, x, wq, wk, wv)] + [pltpu.SemaphoreType.DMA((5,))],
         compiler_params=pltpu.CompilerParams(vmem_limit_bytes=16 * MIB),
         cost_estimate=pl.CostEstimate(flops=2 * rows * x.shape[1] * 3 * width, bytes_accessed=5 * MIB, transcendentals=0),
         name="project",
-    )(half_index, seg, seg, *map(in_hbm, (x, wq, wk, wv)))
+    )(*map(in_hbm, (seg, x, wq, wk, wv)))
 
 
 def attention_kernel(
-    half_ref, rng_ref, x_ref, item_ref, hide_ref, wq_ref, wk_ref, wv_ref, kv_in, queries_in, across_in, turned_in,
+    rng_ref, x_ref, item_ref, hide_ref, wq_ref, wk_ref, wv_ref, kv_in, queries_in, across_in, turned_in,
     kv_ref, queries_ref, keep_ref, send_ref, inverse_ref, *rest,
 ):
     half = x_ref.shape[0]
@@ -167,7 +184,7 @@
     pairs, block = width // PAIR, BLOCK
     share_refs = rest[:pairs]
     across, turned, mix, shifted, peaks = rest[pairs:]
-    here, there = half_ref[0], 1 - half_ref[0]
+    here, there = lax.axis_index("mp"), 1 - lax.axis_index("mp")
     turned[:, aligned(here, half)] = turned_in[:, aligned(here, half)]
     across[:, :, aligned(here, 2 * half)] = across_in[:, :, aligned(here, 2 * half)]
     kv_ref[aligned(here, half), :] = kv_in[aligned(here, half), :]
@@ -185,8 +202,7 @@
         def mix_all(hide_of):
             mix[...] = jnp.zeros(mix.shape, F32)
 
-            def key_block(j, c):
-                span = aligned(j, block)
+            def visit(span, size):
                 ahead = scores(0, span, both, hide_of(0))
                 for p in range(pairs):
                     s = ahead
@@ -197,9 +213,8 @@
                     for a in range(2):
                         head = slice((2 * p + a) * TURNED, (2 * p + a + 1) * TURNED)
                         mix[head, :] += dot(turned[head, span], e[:, a * block : (a + 1) * block])
-                return c
-
-            lax.fori_loop(low, high, key_block, 0)
+
+            over_keys(low, high, visit)
 
         mix_all(lambda p: hide_ref[:, both])
         total_rows = [h * TURNED + HEAD_DIM for h in range(2 * pairs)]
@@ -210,13 +225,12 @@
         def _():
             peaks[...] = jnp.full(peaks.shape, MASKED, F32)
 
-            def peak_block(j, c):
+            def visit(span, size):
                 for p in range(pairs):
-                    s = scores(p, aligned(j, block), both, hide_ref[:, both])
+                    s = scores(p, span, both, hide_ref[:, both])
                     peaks[p] = jnp.maximum(peaks[p], jnp.max(s, 0, keepdims=True))
-                return c
-
-            lax.fori_loop(low, high, peak_block, 0)
+
+            over_keys(low, high, visit)
             row = lax.broadcasted_iota(jnp.int32, (128, 2 * block), 0)
             hide = hide_ref[:, both].astype(F32)
             for p in range(pairs):
@@ -253,7 +267,7 @@
     lax.fori_loop(0, count // block, query_block, 0)
 
 
-def attention(half_index, rng, x, item, hide, wq, wk, wv, kv, queries, across, turned):
+def attention(rng, x, item, hide, wq, wk, wv, kv, queries, across, turned):
     half, width = x.shape[0], wq.shape[1]
     count, pairs = 2 * half, width // PAIR
     like = lambda v: jax.ShapeDtypeStruct(v.shape, v.dtype)
@@ -267,7 +281,7 @@
             jax.ShapeDtypeStruct((count, width), F32),
         )
         + (jax.ShapeDtypeStruct((count, 2 * count), BF16),) * pairs,
-        in_specs=[SM, SM] + [VM] * 10,
+        in_specs=[SM] + [VM] * 10,
         out_specs=(VM,) * (5 + pairs),
         scratch_shapes=[
             pltpu.VMEM(across.shape, BF16),
@@ -279,18 +293,18 @@
         compiler_params=pltpu.CompilerParams(vmem_limit_bytes=12 * MIB),
         cost_estimate=pl.CostEstimate(flops=10**10, bytes_accessed=8 * MIB, transcendentals=10**6),
         name="attention",
-    )(half_index, rng, x, item, hide, wq, wk, wv, kv, queries, across, turned)
+    )(rng, x, item, hide, wq, wk, wv, kv, queries, across, turned)
 
 
 def pair_grad_kernel(
-    p, half_ref, rng_ref, kv_ref, queries_ref, keep_ref, send_ref, own_ref, other_ref, inverse_ref, share_ref,
+    p, rng_ref, kv_ref, queries_ref, keep_ref, send_ref, own_ref, other_ref, inverse_ref, share_ref,
     dq_ref, dk_ref, dv_ref,
     grads, across, turned, delta, dq, dk, dv,
 ):
     half, width = keep_ref.shape
     count, block = kv_ref.shape[0], BLOCK
     cols = slice(p * PAIR, (p + 1) * PAIR)
-    here, there = half_ref[0], 1 - half_ref[0]
+    here, there = lax.axis_index("mp"), 1 - lax.axis_index("mp")
     row = lax.broadcasted_iota(jnp.int32, (8, PAIR), 0)
     column = lax.broadcasted_iota(jnp.int32, (8, PAIR), 1)
     pick = jnp.where(column // HEAD_DIM == row, 1.0, 0.0).astype(BF16)
@@ -311,8 +325,7 @@
         dq[...] = jnp.zeros(dq.shape, F32)
         level = jnp.concatenate([delta[0:1, rows], delta[1:2, rows]], 1)
 
-        def key_block(j, c):
-            span = aligned(j, block)
+        def visit(span, size):
             d = dot(kv_ref[span, width + p * PAIR : width + (p + 1) * PAIR], across[:, both])
             shares = share_ref[span, both]
             slopes = (shares.astype(F32) * (d - level)).astype(BF16)
@@ -321,9 +334,8 @@
             for a in range(2):
                 head = slice(a * HEAD_DIM, (a + 1) * HEAD_DIM)
                 dq[head, :] += dot(turned[head, span], slopes[:, a * block : (a + 1) * block])
-            return c
-
-        lax.fori_loop(rng_ref[0, g], rng_ref[1, g], key_block, 0)
+
+        over_keys(rng_ref[0, g], rng_ref[1, g], visit)
         dq_ref[rows, :] = (dq[...] * HEAD_DIM**-0.5).astype(BF16).T
         return carry
 
@@ -332,12 +344,12 @@
     dv_ref[...] = dv[...].astype(BF16)
 
 
-def pair_grad(p, half_index, rng, kv, queries, keep, send, own, other, inverse, shares):
+def pair_grad(p, rng, kv, queries, keep, send, own, other, inverse, shares):
     count = kv.shape[0]
     return pl.pallas_call(
         functools.partial(pair_grad_kernel, p),
         out_shape=(jax.ShapeDtypeStruct((count, PAIR), BF16),) * 3,
-        in_specs=[SM, SM] + [VM] * 8,
+        in_specs=[SM] + [VM] * 8,
         out_specs=(VM,) * 3,
         scratch_shapes=[
             pltpu.VMEM((2 * count, PAIR), BF16),
@@ -351,39 +363,52 @@
         compiler_params=pltpu.CompilerParams(vmem_limit_bytes=12 * MIB),
         cost_estimate=pl.CostEstimate(flops=4 * 10**9, bytes_accessed=8 * MIB, transcendentals=0),
         name=f"pair_grad_{p}",
-    )(half_index, rng, kv, queries, keep, send, own, other, inverse, shares)
-
-
-def input_part(half_ref, flip, pieces, weights, half):
-    which = 1 - half_ref[0] if flip else half_ref[0]
+    )(rng, kv, queries, keep, send, own, other, inverse, shares)
+
+
+def input_part(flip, pieces, weights, half):
+    which = 1 - lax.axis_index("mp") if flip else lax.axis_index("mp")
     rows = aligned(which, half)
     left = jnp.concatenate([piece[rows, :] for piece in pieces], 1)
     right = jnp.concatenate([weight[...] for weight in weights], 1)
     return dot_nt(left, right)
 
 
-def away_kernel(half_ref, *refs):
+def away_kernel(*refs):
     out_ref = refs[-1]
-    out_ref[...] = input_part(half_ref, True, refs[:-4], refs[-4:-1], out_ref.shape[0]).astype(BF16)
-
-
-def home_kernel(half_ref, first_ref, got_ref, *refs):
-    out_ref = refs[-1]
-    part = input_part(half_ref, False, refs[:-4], refs[-4:-1], out_ref.shape[0])
-    out_ref[...] = (part + first_ref[...] + got_ref[...].astype(F32)).astype(BF16)
-
-
-def input_call(kernel, half_index, extra, pieces, weights, name):
+    out_ref[...] = input_part(True, refs[:-4], refs[-4:-1], out_ref.shape[0]).astype(BF16)
+
+
+def home_kernel(first_ref, got_ref, *refs):
+    *pieces, wq_ref, wk_ref, wv_ref, out_hbm, out_ref, sems = refs
+    half = out_ref.shape[0]
+    parts = 2
+    size = half // parts
+    right = jnp.concatenate([wq_ref[...], wk_ref[...], wv_ref[...]], 1)
+    copies = []
+    for t in range(parts):
+        part = slice(t * size, (t + 1) * size)
+        rows = aligned(lax.axis_index("mp") * parts + t, size)
+        total = dot_nt(jnp.concatenate([piece[rows, :] for piece in pieces], 1), right)
+        out_ref[part, :] = (total + first_ref[part, :] + got_ref[part, :].astype(F32)).astype(BF16)
+        copies.append(pltpu.make_async_copy(out_ref.at[part, :], out_hbm.at[part, :], sems.at[t]))
+        copies[-1].start()
+    for copy in copies:
+        copy.wait()
+
+
+def input_call(kernel, extra, pieces, weights, name):
     half, features = pieces[0].shape[0] // 2, weights[0].shape[0]
     return pl.pallas_call(
         kernel,
         out_shape=jax.ShapeDtypeStruct((half, features), BF16),
-        in_specs=[SM] + [VM] * (len(extra) + len(pieces) + len(weights)),
-        out_specs=VM,
+        in_specs=[VM] * (len(extra) + len(pieces) + len(weights)),
+        out_specs=HB if extra else VM,
+        scratch_shapes=[pltpu.VMEM((half, features), BF16), pltpu.SemaphoreType.DMA((2,))] if extra else [],
         compiler_params=pltpu.CompilerParams(vmem_limit_bytes=16 * MIB),
         cost_estimate=pl.CostEstimate(flops=10**9, bytes_accessed=6 * MIB, transcendentals=0),
         name=name,
-    )(half_index, *extra, *pieces, *weights)
+    )(*extra, *pieces, *weights)
 
 
 def gelu_both(v):
@@ -411,22 +436,22 @@
 
 
 def middle_kernel(
-    half_ref, x_ref, keep_ref, got_ref, up_ref,
+    x_ref, keep_ref, got_ref, up_ref,
     mdb_ref, mub_ref, ddb_ref, dub_ref, fg_ref, fs_ref, sg_ref, ss_ref,
-    wo_hbm, wo2_hbm, md_hbm, mu_hbm, w1_hbm, w12_hbm, w2_hbm, w22_hbm, dd_hbm, du_hbm,
+    wo2_ref, w12_ref, w22_ref, wo_hbm, md_hbm, mu_hbm, w1_hbm, w2_hbm, dd_hbm, du_hbm,
     act_hbm, first_ref, own_ref, away_ref, mine_ref, theirs_ref,
-    wo_ref, wo2_ref, md_ref, mu_ref, w1_ref, w12_ref, w2_ref, w22_ref, dd_ref, du_ref,
+    wo_ref, md_ref, mu_ref, w1_ref, w2_ref, dd_ref, du_ref,
     slope_ref, hidden_ref, normed_ref, act_ref, big_ref, small_ref, sems, act_sem,
 ):
     rows, features = x_ref.shape
     adapt = md_ref.shape[0]
-    names = ("wo", "wo2", "md", "mu", "w1", "w2", "w12", "w22", "dd", "du")
+    names = ("wo", "md", "mu", "w1", "w2", "dd", "du")
     waits = dict(
         zip(
             names,
             start_all(
-                (wo_hbm, wo2_hbm, md_hbm, mu_hbm, w1_hbm, w2_hbm, w12_hbm, w22_hbm, dd_hbm, du_hbm),
-                (wo_ref, wo2_ref, md_ref, mu_ref, w1_ref, w2_ref, w12_ref, w22_ref, dd_ref, du_ref),
+                (wo_hbm, md_hbm, mu_hbm, w1_hbm, w2_hbm, dd_hbm, du_hbm),
+                (wo_ref, md_ref, mu_ref, w1_ref, w2_ref, dd_ref, du_ref),
                 sems,
             ),
         )
@@ -438,7 +463,6 @@
     x = x_ref[...].astype(F32)
     waits["wo"].wait()
     attended = dot(keep_ref[...], wo_ref[...])
-    waits["wo2"].wait()
     attended = attended + dot(got_ref[...], wo2_ref[...])
     attended_low = attended.astype(BF16)
     waits["md"].wait()
@@ -454,11 +478,12 @@
     hidden_low = hidden.astype(BF16)
     chunk = 512
     units = w1_ref.shape[1]
-    sides = ((w1_ref, w2_ref, "w1", "w2"), (w12_ref, w22_ref, "w12", "w22"))
+    sides = ((w1_ref, w2_ref, "w1", "w2"), (w12_ref, w22_ref, None, None))
     dense_in = jnp.zeros((rows, features), F32)
     for s, (win, wout, first, second) in enumerate(sides):
-        waits[first].wait()
-        waits[second].wait()
+        for name in (first, second):
+            if name:
+                waits[name].wait()
         for c in range(units // chunk):
             span = slice(c * chunk, (c + 1) * chunk)
             value, slope = gelu_both(dot(hidden_low, win[:, span]))
@@ -517,7 +542,7 @@
     small_ref[7:8, :] = jnp.zeros((1, features), F32)
     tail = tail_of(small_ref[...])
     share = 2 * adapt
-    for out_ref, which in ((mine_ref, half_ref[0]), (theirs_ref, 1 - half_ref[0])):
+    for out_ref, which in ((mine_ref, lax.axis_index("mp")), (theirs_ref, 1 - lax.axis_index("mp"))):
         out_ref[:share, :] = big_ref[aligned(which, share), :]
         out_ref[share:, :] = tail
     act_copy.wait()
@@ -533,11 +558,11 @@
     return wide[:8] + wide[8:]
 
 
-def middle(half_index, x, keep, got, up, vectors, matrices):
+def middle(x, keep, got, up, vectors, swapped, matrices):
     rows, features = x.shape
     width = keep.shape[1]
-    adapt = matrices[2].shape[0]
-    units = matrices[4].shape[1]
+    adapt = matrices[1].shape[0]
+    units = matrices[3].shape[1]
     packed = jax.ShapeDtypeStruct((2 * adapt + 16, features), BF16)
     return pl.pallas_call(
         middle_kernel,
@@ -549,7 +574,7 @@
             packed,
             packed,
         ),
-        in_specs=[SM] + [VM] * 12 + [HB] * 10,
+        in_specs=[VM] * 15 + [HB] * 7,
         out_specs=(HB,) + (VM,) * 5,
         scratch_shapes=[pltpu.VMEM(m.shape, BF16) for m in matrices]
         + [
@@ -559,13 +584,13 @@
             pltpu.VMEM((rows, features), BF16),
             pltpu.VMEM((4 * adapt, features), BF16),
             pltpu.VMEM((8, features), F32),
-            pltpu.SemaphoreType.DMA((10,)),
+            pltpu.SemaphoreType.DMA((7,)),
             pltpu.SemaphoreType.DMA,
         ],
-        compiler_params=pltpu.CompilerParams(vmem_limit_bytes=32 * MIB),
+        compiler_params=pltpu.CompilerParams(vmem_limit_bytes=26 * MIB),
         cost_estimate=pl.CostEstimate(flops=2 * 10**10, bytes_accessed=16 * MIB, transcendentals=10**6),
         name="middle",
-    )(half_index, x, keep, got, up, *vectors, *map(in_hbm, matrices))
+    )(x, keep, got, up, *vectors, *swapped, *map(in_hbm, matrices))
 
 
 def combine_kernel(held_ref, got_ref, out_ref):
@@ -586,7 +611,7 @@
     )(held, got)
 
 
-def finish_kernel(half_ref, held_ref, got_ref, md_ref, mdb_ref, mu_ref, mub_ref, dd_ref, ddb_ref, du_ref, dub_ref,
+def finish_kernel(held_ref, got_ref, md_ref, mdb_ref, mu_ref, mub_ref, dd_ref, ddb_ref, du_ref, dub_ref,
                   fg_ref, fs_ref, sg_ref, ss_ref, ratio_ref):
     adapt = md_ref.shape[0]
 
@@ -606,27 +631,27 @@
         base = jnp.sum(jnp.where(lane == 2, squares, 0.0), -1, keepdims=True)
         ratio_ref[...] = jnp.sqrt(squares / base)[0, :2]
 
-    @pl.when(half_ref[0] == 0)
+    @pl.when(lax.axis_index("mp") == 0)
     def _():
         write(held_ref, got_ref)
 
-    @pl.when(half_ref[0] != 0)
+    @pl.when(lax.axis_index("mp") != 0)
     def _():
         write(got_ref, held_ref)
 
 
-def finish(half_index, held, got, adapt):
+def finish(held, got, adapt):
     features = held.shape[1]
     matrix = jax.ShapeDtypeStruct((adapt, features), F32)
     short, vector = jax.ShapeDtypeStruct((adapt,), F32), jax.ShapeDtypeStruct((features,), F32)
     return pl.pallas_call(
         finish_kernel,
         out_shape=(matrix, short, matrix, vector) * 2 + (vector,) * 4 + (jax.ShapeDtypeStruct((2,), F32),),
-        in_specs=[SM, VM, VM],
+        in_specs=[VM, VM],
         out_specs=(VM,) * 13,
         compiler_params=pltpu.CompilerParams(vmem_limit_bytes=4 * MIB),
         name="finish",
-    )(half_index, held, got)
+    )(held, got)
 
 
 def swap_cores(value):
@@ -642,12 +667,11 @@
     mixer_down, mixer_down_bias, mixer_up, mixer_up_bias, dense_down, dense_down_bias, dense_up, dense_up_bias,
     first_gain, first_shift, second_gain, second_shift, output_grad,
 ):
-    half_index = lax.axis_index("mp").astype(jnp.int32).reshape(1)
     devices = lax.axis_size("dp")
     adapt = mixer_down.shape[1]
     other_tokens = swap_cores(tokens)
     kv, queries, across, turned, item, hide, rng = project(
-        half_index, segment_ids, tokens, query_weight, key_weight, value_weight
+        segment_ids, tokens, query_weight, key_weight, value_weight
     )
     kv, other_tokens, output_late, inner_late, outer_late = tie(
         kv, other_tokens, output_weight, inner_weight, outer_weight
@@ -656,18 +680,16 @@
     other_inner = swap_cores(inner_late)
     other_outer = swap_cores(outer_late)
     kv, queries, keep, send, inverse, *shares = attention(
-        half_index, rng, other_tokens, item, hide, query_weight, key_weight, value_weight, kv, queries, across, turned
+        rng, other_tokens, item, hide, query_weight, key_weight, value_weight, kv, queries, across, turned
     )
     got = swap_cores(send)
     vectors = (
         mixer_down_bias, mixer_up_bias, dense_down_bias, dense_up_bias, first_gain, first_shift, second_gain, second_shift,
     )
-    matrices = (
-        output_weight, other_output, mixer_down.T, mixer_up,
-        inner_weight, other_inner, outer_weight, other_outer, dense_down.T, dense_up,
-    )
+    swapped = (other_output, other_inner, other_outer)
+    matrices = (output_weight, mixer_down.T, mixer_up, inner_weight, outer_weight, dense_down.T, dense_up)
     result, first_grad, own_grad, away_grad, mine, theirs = middle(
-        half_index, tokens, keep, got, output_grad, vectors, matrices
+        tokens, keep, got, output_grad, vectors, swapped, matrices
     )
     got_grad = swap_cores(away_grad)
     packed = combine(mine, swap_cores(theirs))
@@ -686,16 +708,16 @@
         arriving = lax.ppermute(packed, ("dp", "mp"), exchange)
         if n < pairs:
             got_grad, packed = tie(got_grad, packed)
-            parts = pair_grad(n, half_index, rng, kv, queries, keep, send, own_grad, got_grad, inverse, shares[n])
+            parts = pair_grad(n, rng, kv, queries, keep, send, own_grad, got_grad, inverse, shares[n])
             arriving, *parts = tie(arriving, *parts)
             grads.append(parts)
         elif n == pairs:
             pieces = [grads[p][i] for i in range(3) for p in range(pairs)]
-            away = swap_cores(input_call(away_kernel, half_index, (), pieces, weights, "away"))
-            input_grad = input_call(home_kernel, half_index, (first_grad, away), pieces, weights, "home")
+            away = swap_cores(input_call(away_kernel, (), pieces, weights, "away"))
+            input_grad = input_call(home_kernel, (first_grad, away), pieces, weights, "home")
             arriving, input_grad = tie(arriving, input_grad)
         packed = combine(packed, arriving)
-    md, mdb, mu, mub, dd, ddb, du, dub, *rest = finish(half_index, packed, swap_cores(packed), adapt)
+    md, mdb, mu, mub, dd, ddb, du, dub, *rest = finish(packed, swap_cores(packed), adapt)
     return (result, input_grad, md.T, mdb, mu, mub, dd.T, ddb, du, dub, *rest)
 
 

time: 81.6 us -> 76.6 us (0.939)
  Pallas kernels: 59.4 us -> 56.2 us
  local copies, waits for them, and re-layouts: 3.1 us -> 0.08 us
    unnamed x36 -> x28, local copies, waits for them, and re-layouts: 3.1 us -> 0.08 us
    pallas_call x3, Pallas kernels: 17.5 us -> 16.1 us  [pair_grad(): pl.pallas_call(functools.partial(pair_grad_kernel, p), out_shape=(jax.Sha...]
  transfers between devices with their start and end apart: 13 -> 13, of which waited for: 6 -> 6; matrix products, arithmetic and copies ran while one was open for 0% -> 0% of each run, Pallas kernels for 44% -> 43%
where the time goes in v6:
time: 76.6 us; the launch traced here: 76.1 us
  Pallas kernels  56.2 us (73%)
  starting transfers between devices  10 us (13%)
  waiting for transfers between devices  8.75 us (11%)
  between operations  1.05 us (1%)
    pallas_call x1, Pallas kernels, middle(): pl.pallas_call(middle_kernel, out_shape=(jax.ShapeDtypeStruct((rows, feat...  21.2 us
    pallas_call x3, Pallas kernels, pair_grad(): pl.pallas_call(functools.partial(pair_grad_kernel, p), out_shape=(jax.Sha...  16.1 us
    pallas_call x1, Pallas kernels, attention(): pl.pallas_call(attention_kernel, out_shape=(like(kv), like(queries), jax....  10.9 us
    ppermute x4, starting transfers between devices, per_device(): arriving = lax.ppermute(packed, ('dp', 'mp'), exchange)  7.62 us
    ppermute x9, waiting for transfers between devices, swap_cores(): return lax.ppermute(value, 'mp', [(0, 1), (1, 0)])  6.08 us
    pallas_call x1, Pallas kernels, project(): pl.pallas_call(project_kernel, out_shape=(jax.ShapeDtypeStruct((count, 2...  3.47 us
    pallas_call x2, Pallas kernels, input_call(): pl.pallas_call(kernel, out_shape=jax.ShapeDtypeStruct((half, features), B...  3.27 us
    ppermute x4, waiting for transfers between devices, per_device(): arriving = lax.ppermute(packed, ('dp', 'mp'), exchange)  2.66 us
  transfers between devices with their start and end apart: 13, of which 6 were waited for; matrix products, arithmetic and copies ran while one was open for 0% of the time, Pallas kernels for 43%

profile of v6, /device:TPU:0, one launch (start us, length us, event | category | flops | bytes accessed | tf_op | source)
XLA Modules:
  0.0 76.1 jit_solution(14650875314737092417)
XLA Ops:
  0.7 0.5 collective-permute-start
  1.2 3.5 %project.1 = (bf16[1024,768]{1,0:T(8,128)(2,1)S(1)}, bf16[3,2048,128]{2,1,0:T(8,128)(2,1)S(1)}, bf16[3,128,2048]{2,1,0:T(8,128)(2,1)S(1)}, bf16[480,1024]{1,0:T(...) custom-call(s32[1,1024]{1,0:T(1,128)} %seg_hbm.1, ...), custom_call_target="tpu_custom_call" | custom-call | flops 905969664 | bytes 5242880 | tf_op jit(solution)/shard_map/project/pallas_call | solution.py:158
  4.8 0.4 collective-permute-start.4
  5.5 10.9 %attention.1 = (bf16[1024,768]{1,0:T(8,128)(2,1)S(1)}, bf16[3,2048,128]{2,1,0:T(8,128)(2,1)S(1)}, bf16[512,384]{1,0:T(8,128)(2,1)S(1)}, bf16[512,384]{1,0:T(8,12...) custom-call(s32[2,4]{1,0:T(2,128)S(1)} %get-tuple-element.83.rng_ref, ...), custom_call_target="tpu_custom_call" | custom-call | flops 10000000000 | bytes 8388608 | tf_op jit(solution)/shard_map/attention/pallas_call | solution.py:274
  16.4 0.5 collective-permute-start.1
  16.9 1.3 %collective-permute-done.1.got_ref = bf16[512,384]{1,0:T(8,128)(2,1)S(1)} collective-permute-done((bf16[512,384]{1,0:T(8,128)(2,1)S(1)}, bf16[512,384]{1,0:T(8,128)(2,1)S(1)}, u32[]{:S(2)}, u32[]{:S(2)}) %collective-permute-start.1) | collective-permute-done | bytes 393248 | tf_op jit(solution)/shard_map/ppermute | solution.py:658
  18.3 21.2 %middle.1 = (bf16[512,768]{1,0:T(8,128)(2,1)}, f32[512,768]{1,0:T(8,128)S(1)}, bf16[512,384]{1,0:T(8,128)(2,1)S(1)}, bf16[512,384]{1,0:T(8,128)(2,1)S(1)}, bf16[...) custom-call(bf16[512,768]{1,0:T(8,128)(2,1)S(1)} %copy-done.3, bf16[512,384]{1,0:T(8,128)(2,1)S(1)} %get-tuple-element.92.keep_ref, ...), custom_call_target="tpu_custom_call" | custom-call | flops 20000000000 | bytes 16777216 | tf_op jit(solution)/shard_map/middle/pallas_call | solution.py:567
  39.5 0.4 collective-permute-start.5
  40.0 0.1 collective-permute-start.6
  40.1 1.5 %collective-permute-done.6.got_ref = bf16[144,768]{1,0:T(8,128)(2,1)S(1)} collective-permute-done((bf16[144,768]{1,0:T(8,128)(2,1)S(1)}, bf16[144,768]{1,0:T(8,128)(2,1)S(1)}, u32[]{:S(2)}, u32[]{:S(2)}) %collective-permute-start.6) | collective-permute-done | bytes 221216 | tf_op jit(solution)/shard_map/ppermute | solution.py:658
  41.7 4.0 %collective-permute-start.7 = (bf16[144,768]{1,0:T(8,128)(2,1)S(1)}, bf16[144,768]{1,0:T(8,128)(2,1)S(1)}, u32[]{:S(2)}, u32[]{:S(2)}) collective-permute-start(bf16[144,768]{1,0:T(8,128)(2,1)S(1)} %combine.5.held_ref), channel_id=1, source_target_pairs={{0,16},{1,5},{2,18},{3,7},{4,20},{5,1},{6,22},{7,3},{8,24},{9,13},... | collective-permute-start | bytes 663560 | tf_op jit(solution)/shard_map/ppermute | solution.py:708
  45.7 5.4 %pair_grad_0.1 = (bf16[1024,128]{1,0:T(8,128)(2,1)S(1)}, bf16[1024,128]{1,0:T(8,128)(2,1)S(1)}, bf16[1024,128]{1,0:T(8,128)(2,1)S(1)}) custom-call(s32[2,4]{1,0:T(2,128)S(1)} %get-tuple-element.83.rng_ref, bf16[1024,768]{1,0:T(8,128)(2,1)S(1)} %get-tuple-element.103.kv_ref, bf16[3,2048,128]{2,1,0:T(8,128)(2,1)S(1)} %get-tuple-element.104.queries_ref, ...), custom_call_target="tpu_custom_call" | custom-call | flops 4000000000 | bytes 8388608 | tf_op jit(solution)/shard_map/pair_grad_0/pallas_call | solution.py:349
  51.1 0.9 %collective-permute-done.7.got_ref = bf16[144,768]{1,0:T(8,128)(2,1)S(1)} collective-permute-done((bf16[144,768]{1,0:T(8,128)(2,1)S(1)}, bf16[144,768]{1,0:T(8,128)(2,1)S(1)}, u32[]{:S(2)}, u32[]{:S(2)}) %collective-permute-start.7) | collective-permute-done | bytes 221216 | tf_op jit(solution)/shard_map/ppermute | solution.py:708
  52.1 1.2 %collective-permute-start.8 = (bf16[144,768]{1,0:T(8,128)(2,1)S(1)}, bf16[144,768]{1,0:T(8,128)(2,1)S(1)}, u32[]{:S(2)}, u32[]{:S(2)}) collective-permute-start(bf16[144,768]{1,0:T(8,128)(2,1)S(1)} %combine.6.held_ref), channel_id=1, source_target_pairs={{0,8},{1,3},{2,10},{3,1},{4,12},{5,7},{6,14},{7,5},{8,0},{9,11},{1... | collective-permute-start | bytes 663560 | tf_op jit(solution)/shard_map/ppermute | solution.py:708
  53.3 5.4 %pair_grad_1.1 = (bf16[1024,128]{1,0:T(8,128)(2,1)S(1)}, bf16[1024,128]{1,0:T(8,128)(2,1)S(1)}, bf16[1024,128]{1,0:T(8,128)(2,1)S(1)}) custom-call(s32[2,4]{1,0:T(2,128)S(1)} %get-tuple-element.83.rng_ref, bf16[1024,768]{1,0:T(8,128)(2,1)S(1)} %get-tuple-element.103.kv_ref, bf16[3,2048,128]{2,1,0:T(8,128)(2,1)S(1)} %get-tuple-element.104.queries_ref, ...), custom_call_target="tpu_custom_call" | custom-call | flops 4000000000 | bytes 8388608 | tf_op jit(solution)/shard_map/pair_grad_1/pallas_call | solution.py:349
  58.7 1.9 %collective-permute-start.9 = (bf16[144,768]{1,0:T(8,128)(2,1)S(1)}, bf16[144,768]{1,0:T(8,128)(2,1)S(1)}, u32[]{:S(2)}, u32[]{:S(2)}) collective-permute-start(bf16[144,768]{1,0:T(8,128)(2,1)S(1)} %combine.7.held_ref), channel_id=1, source_target_pairs={{0,4},{1,17},{2,6},{3,19},{4,0},{5,21},{6,2},{7,23},{8,12},{9,25},... | collective-permute-start | bytes 663560 | tf_op jit(solution)/shard_map/ppermute | solution.py:708
  60.7 5.4 %pair_grad_2.1 = (bf16[1024,128]{1,0:T(8,128)(2,1)S(1)}, bf16[1024,128]{1,0:T(8,128)(2,1)S(1)}, bf16[1024,128]{1,0:T(8,128)(2,1)S(1)}) custom-call(s32[2,4]{1,0:T(2,128)S(1)} %get-tuple-element.83.rng_ref, bf16[1024,768]{1,0:T(8,128)(2,1)S(1)} %get-tuple-element.103.kv_ref, bf16[3,2048,128]{2,1,0:T(8,128)(2,1)S(1)} %get-tuple-element.104.queries_ref, ...), custom_call_target="tpu_custom_call" | custom-call | flops 4000000000 | bytes 8388608 | tf_op jit(solution)/shard_map/pair_grad_2/pallas_call | solution.py:349
  66.0 1.2 %away.1 = bf16[512,768]{1,0:T(8,128)(2,1)S(1)} custom-call(bf16[1024,128]{1,0:T(8,128)(2,1)S(1)} %get-tuple-element.127.refs_0_, bf16[1024,128]{1,0:T(8,128)(2,1)S(1)} %get-tuple-element.128.refs_1_, bf16[1024,128]{1,0:T(8,128)(2,1)S(1)} %get-tuple-element.129.refs_2_, bf16[1024,128]{1,0:T(8,128)(2,1)S(1)} %get-tuple-element.130.refs_3_, ...), custom_call_target="tpu_custom_call" | custom-call | flops 1000000000 | bytes 6291456 | tf_op jit(solution)/shard_map/away/pallas_call | solution.py:402
  67.4 0.5 collective-permute-start.10
  67.9 1.7 %collective-permute-done.11.got_ref = bf16[512,768]{1,0:T(8,128)(2,1)S(1)} collective-permute-done((bf16[512,768]{1,0:T(8,128)(2,1)S(1)}, bf16[512,768]{1,0:T(8,128)(2,1)S(1)}, u32[]{:S(2)}, u32[]{:S(2)}) %collective-permute-start.11) | collective-permute-done | bytes 786464 | tf_op jit(solution)/shard_map/ppermute | solution.py:658
  69.6 2.0 %home.1 = bf16[512,768]{1,0:T(8,128)(2,1)} custom-call(f32[512,768]{1,0:T(8,128)S(1)} %get-tuple-element.126.first_ref, bf16[512,768]{1,0:T(8,128)(2,1)S(1)} %collective-permute-done.11.got_ref, bf16[1024,128]{1,0:T(8,128)(2,1)S(1)} %get-tuple-element.127.refs_0_, bf16[1024,128]{1,0:T(8,128)(2,1)S(1)} %get-tuple-element.128.refs_1_, ...), custom_call_target="tpu_custom_call" | custom-call | flops 1000000000 | bytes 6291456 | tf_op jit(solution)/shard_map/home/pallas_call | solution.py:402
  71.7 1.7 %collective-permute-done.10.got_ref = bf16[144,768]{1,0:T(8,128)(2,1)S(1)} collective-permute-done((bf16[144,768]{1,0:T(8,128)(2,1)S(1)}, bf16[144,768]{1,0:T(8,128)(2,1)S(1)}, u32[]{:S(2)}, u32[]{:S(2)}) %collective-permute-start.10) | collective-permute-done | bytes 221216 | tf_op jit(solution)/shard_map/ppermute | solution.py:708
  73.6 1.5 %collective-permute-done.12.got_ref = bf16[144,768]{1,0:T(8,128)(2,1)S(1)} collective-permute-done((bf16[144,768]{1,0:T(8,128)(2,1)S(1)}, bf16[144,768]{1,0:T(8,128)(2,1)S(1)}, u32[]{:S(2)}, u32[]{:S(2)}) %collective-permute-start.12) | collective-permute-done | bytes 221216 | tf_op jit(solution)/shard_map/ppermute | solution.py:658
  75.0 1.0 %finish.1 = (f32[64,768]{1,0:T(8,128)}, f32[64]{0:T(128)}, f32[64,768]{1,0:T(8,128)}, f32[768]{0:T(1024)}, f32[64,768]{1,0:T(8,128)}, /*index=5*/f32[64]{0:T(128...) custom-call(bf16[144,768]{1,0:T(8,128)(2,1)S(1)} %combine.9.held_ref, ...), custom_call_target="tpu_custom_call" | custom-call | tf_op jit(solution)/shard_map/finish/pallas_call | solution.py:647
  (44 shorter events, 0.8 us)
Async XLA Ops:
  0.6 4.7 %copy-start = (bf16[768,384]{1,0:T(8,128)(2,1)S(1)}, bf16[768,384]{1,0:T(8,128)(2,1)}, u32[]{:S(2)}) copy-start(bf16[768,384]{1,0:T(8,128)(2,1)} %refs_9_.3) | copy-start | bytes 1769476
  0.7 4.0 %collective-permute-start = (bf16[512,768]{1,0:T(8,128)(2,1)}, bf16[512,768]{1,0:T(8,128)(2,1)S(1)}, u32[]{:S(2)}, u32[]{:S(2)}) collective-permute-start(bf16[512,768]{1,0:T(8,128)(2,1)} %x_ref.3), channel_id=1, source_target_pairs={{0,1},{1,0},{2,3},{3,2},{4,5},{5,4},{6,7},{7,6},{8,9},{9,8},{10,11... | collective-permute-start | bytes 2359304 | tf_op jit(solution)/shard_map/ppermute | solution.py:658
  4.7 13.5 %collective-permute-start.3 = (bf16[768,1536]{1,0:T(8,128)(2,1)}, bf16[768,1536]{1,0:T(8,128)(2,1)S(1)}, u32[]{:S(2)}, u32[]{:S(2)}) collective-permute-start(bf16[768,1536]{1,0:T(8,128)(2,1)} %w1_hbm.1), channel_id=1, source_target_pairs={{0,1},{1,0},{2,3},{3,2},{4,5},{5,4},{6,7},{7,6},{8,9},{9,8},{10,11... | collective-permute-start | bytes 7077896 | tf_op jit(solution)/shard_map/ppermute | solution.py:658
  4.8 13.4 %collective-permute-start.4 = (bf16[1536,768]{1,0:T(8,128)(2,1)}, bf16[1536,768]{1,0:T(8,128)(2,1)S(1)}, u32[]{:S(2)}, u32[]{:S(2)}) collective-permute-start(bf16[1536,768]{1,0:T(8,128)(2,1)} %w2_hbm.1), channel_id=1, source_target_pairs={{0,1},{1,0},{2,3},{3,2},{4,5},{5,4},{6,7},{7,6},{8,9},{9,8},{10,11... | collective-permute-start | bytes 7077896 | tf_op jit(solution)/shard_map/ppermute | solution.py:658
  5.3 13.0 %collective-permute-start.2 = (bf16[384,768]{1,0:T(8,128)(2,1)S(1)}, bf16[384,768]{1,0:T(8,128)(2,1)S(1)}, u32[]{:S(2)}, u32[]{:S(2)}) collective-permute-start(bf16[384,768]{1,0:T(8,128)(2,1)S(1)} %copy-done.13), channel_id=1, source_target_pairs={{0,1},{1,0},{2,3},{3,2},{4,5},{5,4},{6,7},{7,6},{8,9},{9,8},{10,11... | collective-permute-start | bytes 1769480 | tf_op jit(solution)/shard_map/ppermute | solution.py:658
  5.4 12.9 %copy-start.3 = (bf16[512,768]{1,0:T(8,128)(2,1)S(1)}, bf16[512,768]{1,0:T(8,128)(2,1)}, u32[]{:S(2)}) copy-start(bf16[512,768]{1,0:T(8,128)(2,1)} %x_ref.3) | copy-start | bytes 2359300
  5.4 12.9 %copy-start.4 = (bf16[512,768]{1,0:T(8,128)(2,1)S(1)}, bf16[512,768]{1,0:T(8,128)(2,1)}, u32[]{:S(2)}) copy-start(bf16[512,768]{1,0:T(8,128)(2,1)} %up_ref.1) | copy-start | bytes 2359300
  5.4 12.9 %copy-start.5 = (bf16[768]{0:T(1024)(128)(2,1)S(1)}, bf16[768]{0:T(1024)(128)(2,1)}, u32[]{:S(2)}) copy-start(bf16[768]{0:T(1024)(128)(2,1)} %mub_ref.1) | copy-start | bytes 4612
  5.4 12.9 %copy-start.6 = (bf16[768]{0:T(1024)(128)(2,1)S(1)}, bf16[768]{0:T(1024)(128)(2,1)}, u32[]{:S(2)}) copy-start(bf16[768]{0:T(1024)(128)(2,1)} %dub_ref.1) | copy-start | bytes 4612
  5.4 12.9 %copy-start.7 = (bf16[768]{0:T(1024)(128)(2,1)S(1)}, bf16[768]{0:T(1024)(128)(2,1)}, u32[]{:S(2)}) copy-start(bf16[768]{0:T(1024)(128)(2,1)} %fg_ref.1) | copy-start | bytes 4612
  5.4 12.9 %copy-start.8 = (bf16[768]{0:T(1024)(128)(2,1)S(1)}, bf16[768]{0:T(1024)(128)(2,1)}, u32[]{:S(2)}) copy-start(bf16[768]{0:T(1024)(128)(2,1)} %fs_ref.1) | copy-start | bytes 4612
  5.4 12.9 %copy-start.9 = (bf16[768]{0:T(1024)(128)(2,1)S(1)}, bf16[768]{0:T(1024)(128)(2,1)}, u32[]{:S(2)}) copy-start(bf16[768]{0:T(1024)(128)(2,1)} %sg_ref.1) | copy-start | bytes 4612
  5.4 12.9 %copy-start.10 = (bf16[768]{0:T(1024)(128)(2,1)S(1)}, bf16[768]{0:T(1024)(128)(2,1)}, u32[]{:S(2)}) copy-start(bf16[768]{0:T(1024)(128)(2,1)} %ss_ref.1) | copy-start | bytes 4612
  5.5 12.9 %copy-start.11 = (bf16[64]{0:T(256)(128)(2,1)S(1)}, bf16[64]{0:T(256)(128)(2,1)}, u32[]{:S(2)}) copy-start(bf16[64]{0:T(256)(128)(2,1)} %mdb_ref.1) | copy-start | bytes 388
  5.5 12.9 %copy-start.12 = (bf16[64]{0:T(256)(128)(2,1)S(1)}, bf16[64]{0:T(256)(128)(2,1)}, u32[]{:S(2)}) copy-start(bf16[64]{0:T(256)(128)(2,1)} %ddb_ref.1) | copy-start | bytes 388
  16.4 1.8 %collective-permute-start.1 = (bf16[512,384]{1,0:T(8,128)(2,1)S(1)}, bf16[512,384]{1,0:T(8,128)(2,1)S(1)}, u32[]{:S(2)}, u32[]{:S(2)}) collective-permute-start(bf16[512,384]{1,0:T(8,128)(2,1)S(1)} %get-tuple-element.93.send_ref), channel_id=1, source_target_pairs={{0,1},{1,0},{2,3},{3,2},{4,5},{5,4},{6,7},{7,6},{8,9},{9,8},{10,11... | collective-permute-start | bytes 1179656 | tf_op jit(solution)/shard_map/ppermute | solution.py:658
  39.5 6.2 %collective-permute-start.5 = (bf16[512,384]{1,0:T(8,128)(2,1)S(1)}, bf16[512,384]{1,0:T(8,128)(2,1)S(1)}, u32[]{:S(2)}, u32[]{:S(2)}) collective-permute-start(bf16[512,384]{1,0:T(8,128)(2,1)S(1)} %get-tuple-element.98), channel_id=1, source_target_pairs={{0,1},{1,0},{2,3},{3,2},{4,5},{5,4},{6,7},{7,6},{8,9},{9,8},{10,11... | collective-permute-start | bytes 1179656 | tf_op jit(solution)/shard_map/ppermute | solution.py:658
  40.0 1.7 %collective-permute-start.6 = (bf16[144,768]{1,0:T(8,128)(2,1)S(1)}, bf16[144,768]{1,0:T(8,128)(2,1)S(1)}, u32[]{:S(2)}, u32[]{:S(2)}) collective-permute-start(bf16[144,768]{1,0:T(8,128)(2,1)S(1)} %get-tuple-element.100), channel_id=1, source_target_pairs={{0,1},{1,0},{2,3},{3,2},{4,5},{5,4},{6,7},{7,6},{8,9},{9,8},{10,11... | collective-permute-start | bytes 663560 | tf_op jit(solution)/shard_map/ppermute | solution.py:658
  41.7 10.3 %collective-permute-start.7 = (bf16[144,768]{1,0:T(8,128)(2,1)S(1)}, bf16[144,768]{1,0:T(8,128)(2,1)S(1)}, u32[]{:S(2)}, u32[]{:S(2)}) collective-permute-start(bf16[144,768]{1,0:T(8,128)(2,1)S(1)} %combine.5.held_ref), channel_id=1, source_target_pairs={{0,16},{1,5},{2,18},{3,7},{4,20},{5,1},{6,22},{7,3},{8,24},{9,13},... | collective-permute-start | bytes 663560 | tf_op jit(solution)/shard_map/ppermute | solution.py:708
  52.1 6.6 %collective-permute-start.8 = (bf16[144,768]{1,0:T(8,128)(2,1)S(1)}, bf16[144,768]{1,0:T(8,128)(2,1)S(1)}, u32[]{:S(2)}, u32[]{:S(2)}) collective-permute-start(bf16[144,768]{1,0:T(8,128)(2,1)S(1)} %combine.6.held_ref), channel_id=1, source_target_pairs={{0,8},{1,3},{2,10},{3,1},{4,12},{5,7},{6,14},{7,5},{8,0},{9,11},{1... | collective-permute-start | bytes 663560 | tf_op jit(solution)/shard_map/ppermute | solution.py:708
  58.7 7.3 %collective-permute-start.9 = (bf16[144,768]{1,0:T(8,128)(2,1)S(1)}, bf16[144,768]{1,0:T(8,128)(2,1)S(1)}, u32[]{:S(2)}, u32[]{:S(2)}) collective-permute-start(bf16[144,768]{1,0:T(8,128)(2,1)S(1)} %combine.7.held_ref), channel_id=1, source_target_pairs={{0,4},{1,17},{2,6},{3,19},{4,0},{5,21},{6,2},{7,23},{8,12},{9,25},... | collective-permute-start | bytes 663560 | tf_op jit(solution)/shard_map/ppermute | solution.py:708
  67.3 2.4 %collective-permute-start.11 = (bf16[512,768]{1,0:T(8,128)(2,1)S(1)}, bf16[512,768]{1,0:T(8,128)(2,1)S(1)}, u32[]{:S(2)}, u32[]{:S(2)}) collective-permute-start(bf16[512,768]{1,0:T(8,128)(2,1)S(1)} %away.1), channel_id=1, source_target_pairs={{0,1},{1,0},{2,3},{3,2},{4,5},{5,4},{6,7},{7,6},{8,9},{9,8},{10,11... | collective-permute-start | bytes 2359304 | tf_op jit(solution)/shard_map/ppermute | solution.py:658
  67.4 6.0 %collective-permute-start.10 = (bf16[144,768]{1,0:T(8,128)(2,1)S(1)}, bf16[144,768]{1,0:T(8,128)(2,1)S(1)}, u32[]{:S(2)}, u32[]{:S(2)}) collective-permute-start(bf16[144,768]{1,0:T(8,128)(2,1)S(1)} %combine.8.held_ref), channel_id=1, source_target_pairs={{0,2},{1,9},{2,0},{3,11},{4,6},{5,13},{6,4},{7,15},{8,10},{9,1},{1... | collective-permute-start | bytes 663560 | tf_op jit(solution)/shard_map/ppermute | solution.py:708
  73.5 1.5 %collective-permute-start.12 = (bf16[144,768]{1,0:T(8,128)(2,1)S(1)}, bf16[144,768]{1,0:T(8,128)(2,1)S(1)}, u32[]{:S(2)}, u32[]{:S(2)}) collective-permute-start(bf16[144,768]{1,0:T(8,128)(2,1)S(1)} %combine.9.held_ref), channel_id=1, source_target_pairs={{0,1},{1,0},{2,3},{3,2},{4,5},{5,4},{6,7},{7,6},{8,9},{9,8},{10,11... | collective-permute-start | bytes 663560 | tf_op jit(solution)/shard_map/ppermute | solution.py:658
  (3 other events, 14.0 us)

commit v7 on v6

--- a/solution.py
+++ b/solution.py
@@ -435,13 +435,29 @@
     return jnp.sum(values, 0, keepdims=True)
 
 
+def eight_rows(values):
+    return jnp.sum(values.reshape(-1, 8, values.shape[1]), 0)
+
+
+def interleave(first, second):
+    done = 0
+    for i, step in enumerate(first):
+        step()
+        while done < len(second) and (done + 1) * len(first) <= (i + 1) * len(second):
+            second[done]()
+            done += 1
+    for step in second[done:]:
+        step()
+
+
 def middle_kernel(
     x_ref, keep_ref, got_ref, up_ref,
     mdb_ref, mub_ref, ddb_ref, dub_ref, fg_ref, fs_ref, sg_ref, ss_ref,
     wo2_ref, w12_ref, w22_ref, wo_hbm, md_hbm, mu_hbm, w1_hbm, w2_hbm, dd_hbm, du_hbm,
     act_hbm, first_ref, own_ref, away_ref, mine_ref, theirs_ref,
     wo_ref, md_ref, mu_ref, w1_ref, w2_ref, dd_ref, du_ref,
-    slope_ref, hidden_ref, normed_ref, act_ref, big_ref, small_ref, sems, act_sem,
+    slope_ref, wide_ref, out_ref, hidden_ref, normed_ref, low_ref, hidden_low_ref, act_ref, top_ref,
+    big_ref, small_ref, sems, act_sem,
 ):
     rows, features = x_ref.shape
     adapt = md_ref.shape[0]
@@ -456,96 +472,234 @@
             ),
         )
     )
+    waited = set()
+
+    def need(*wanted):
+        for name in wanted:
+            if name not in waited:
+                waited.add(name)
+                waits[name].wait()
 
     def vector(ref):
         return ref[...].astype(F32).reshape(1, -1)
 
-    x = x_ref[...].astype(F32)
-    waits["wo"].wait()
-    attended = dot(keep_ref[...], wo_ref[...])
-    attended = attended + dot(got_ref[...], wo2_ref[...])
-    attended_low = attended.astype(BF16)
-    waits["md"].wait()
-    waits["mu"].wait()
-    mixer_active, mixer_slope = gelu_both(dot_nt(attended_low, md_ref[...]) + vector(mdb_ref))
-    mixer_active = mixer_active.astype(BF16)
-    mixer_out = dot(mixer_active, mu_ref[...]) + vector(mub_ref)
-    hidden, normed_one, reciprocal_one = norm(x + attended + mixer_out, vector(fg_ref), vector(fs_ref))
-    normed_ref[...] = normed_one
-    hidden_ref[...] = hidden
-    mixer_square = jnp.sum(column_sum(mixer_out * mixer_out), -1, keepdims=True)
-    input_square = jnp.sum(column_sum(x * x), -1, keepdims=True)
-    hidden_low = hidden.astype(BF16)
-    chunk = 512
     units = w1_ref.shape[1]
-    sides = ((w1_ref, w2_ref, "w1", "w2"), (w12_ref, w22_ref, None, None))
-    dense_in = jnp.zeros((rows, features), F32)
-    for s, (win, wout, first, second) in enumerate(sides):
-        for name in (first, second):
-            if name:
-                waits[name].wait()
-        for c in range(units // chunk):
-            span = slice(c * chunk, (c + 1) * chunk)
-            value, slope = gelu_both(dot(hidden_low, win[:, span]))
-            slope_ref[:, s * units + c * chunk : s * units + (c + 1) * chunk] = slope.astype(BF16)
-            dense_in = dense_in + dot(value.astype(BF16), wout[span, :])
-    dense_low = dense_in.astype(BF16)
-    waits["dd"].wait()
-    waits["du"].wait()
-    dense_active, dense_slope = gelu_both(dot_nt(dense_low, dd_ref[...]) + vector(ddb_ref))
-    dense_active = dense_active.astype(BF16)
-    dense_out = dot(dense_active, du_ref[...]) + vector(dub_ref)
-    second_gain = vector(sg_ref)
-    result, normed_two, reciprocal_two = norm(hidden_ref[...] + dense_in + dense_out, second_gain, vector(ss_ref))
-    act_ref[...] = result.astype(BF16)
-    act_copy = pltpu.make_async_copy(act_ref, act_hbm, act_sem)
-    act_copy.start()
-    dense_square = jnp.sum(column_sum(dense_out * dense_out), -1, keepdims=True)
-
-    upstream = up_ref[...].astype(F32)
-    small_ref[4:5, :] = column_sum(upstream * normed_two)
-    small_ref[5:6, :] = column_sum(upstream)
-    second_grad = norm_grad(upstream, normed_two, reciprocal_two, second_gain)
-    dense_top = second_grad.astype(BF16)
-    big_ref[3 * adapt : 4 * adapt, :] = dot_tn(dense_active, dense_top).astype(BF16)
-    small_ref[1:2, :] = column_sum(dense_top.astype(F32))
-    dense_mid = (dot_nt(dense_top, du_ref[...]) * dense_slope).astype(BF16)
-    big_ref[2 * adapt : 3 * adapt, :] = dot_tn(dense_mid, dense_low).astype(BF16)
-    dense_mid_sum = column_sum(dense_mid.astype(F32))
-    dense_in_grad = (second_grad + dot(dense_mid, dd_ref[...])).astype(BF16)
-    hidden_grad = second_grad
-    for s, (win, wout, _, _) in enumerate(sides):
-        for c in range(units // chunk):
-            span = slice(c * chunk, (c + 1) * chunk)
-            slope = slope_ref[:, s * units + c * chunk : s * units + (c + 1) * chunk].astype(F32)
-            inner_grad = (dot_nt(dense_in_grad, wout[span, :]) * slope).astype(BF16)
-            hidden_grad = hidden_grad + dot_nt(inner_grad, win[:, span])
-    normed_one = normed_ref[...]
-    small_ref[2:3, :] = column_sum(hidden_grad * normed_one)
-    small_ref[3:4, :] = column_sum(hidden_grad)
-    first_grad = norm_grad(hidden_grad, normed_one, reciprocal_one, vector(fg_ref))
-    first_ref[...] = first_grad
-    mixer_top = first_grad.astype(BF16)
-    big_ref[adapt : 2 * adapt, :] = dot_tn(mixer_active, mixer_top).astype(BF16)
-    small_ref[0:1, :] = column_sum(mixer_top.astype(F32))
-    mixer_mid = (dot_nt(mixer_top, mu_ref[...]) * mixer_slope).astype(BF16)
-    big_ref[0:adapt, :] = dot_tn(mixer_mid, attended_low).astype(BF16)
-    mixer_mid_sum = column_sum(mixer_mid.astype(F32))
-    attended_grad = (first_grad + dot(mixer_mid, md_ref[...])).astype(BF16)
-    own_ref[...] = dot_nt(attended_grad, wo_ref[...]).astype(BF16)
-    away_ref[...] = dot_nt(attended_grad, wo2_ref[...]).astype(BF16)
+    chunk, piece_rows = 512, 64
+    sides = ((w1_ref, w2_ref, ("w1", "w2")), (w12_ref, w22_ref, ()))
+    pieces = [(side, slice(c * chunk, (c + 1) * chunk)) for side in sides for c in range(units // chunk)]
+    kept = {}
+    sums = {}
+
+    def add(name, value):
+        sums[name] = sums[name] + value if name in sums else value
+
+    def parts(half):
+        return [slice(r, r + piece_rows) for r in range(half.start, half.stop, piece_rows)]
+
+    def attend(half):
+        def first():
+            need("wo")
+            attended = dot(keep_ref[half, :], wo_ref[...]) + dot(got_ref[half, :], wo2_ref[...])
+            wide_ref[half, :] = attended
+            low_ref[half, :] = attended.astype(BF16)
+
+        def second():
+            need("md", "mu")
+            active, slope = gelu_both(dot_nt(low_ref[half, :], md_ref[...]) + vector(mdb_ref))
+            kept["mixer", half.start] = (active.astype(BF16), slope)
+
+        def third():
+            out_ref[half, :] = dot(kept["mixer", half.start][0], mu_ref[...]) + vector(mub_ref)
+
+        return [first, second, third]
+
+    def norm_one(half):
+        def one(part):
+            x, mixer_out = x_ref[part, :].astype(F32), out_ref[part, :]
+            add("mixer_square", eight_rows(mixer_out * mixer_out))
+            add("input_square", eight_rows(x * x))
+            hidden, normed, reciprocal = norm(x + wide_ref[part, :] + mixer_out, vector(fg_ref), vector(fs_ref))
+            normed_ref[part, :] = normed
+            hidden_ref[part, :] = hidden
+            hidden_low_ref[part, :] = hidden.astype(BF16)
+            kept["reciprocal", part.start] = reciprocal
+
+        return [functools.partial(one, part) for part in parts(half)]
+
+    def feed_forward(half):
+        state = {}
+
+        def start():
+            need("w1", "w2")
+            side, span = pieces[0]
+            state["ahead"] = dot(hidden_low_ref[half, :], side[0][:, span])
+
+        def one(n):
+            side, span = pieces[n]
+            inner = state["ahead"]
+            if n + 1 < len(pieces):
+                after, after_span = pieces[n + 1]
+                state["ahead"] = dot(hidden_low_ref[half, :], after[0][:, after_span])
+            value, slope = gelu_both(inner)
+            slope_ref[half, n * chunk : (n + 1) * chunk] = slope.astype(BF16)
+            state["value"] = value.astype(BF16)
+
+        def two(n):
+            side, span = pieces[n]
+            total = dot(state["value"], side[1][span, :])
+            state["total"] = state["total"] + total if n else total
+            if n + 1 == len(pieces):
+                wide_ref[half, :] = state["total"]
+
+        steps = [start]
+        for n in range(len(pieces)):
+            steps += [functools.partial(one, n), functools.partial(two, n)]
+        return steps
+
+    def dense(half):
+        def first():
+            need("dd", "du")
+            dense_low = wide_ref[half, :].astype(BF16)
+            active, slope = gelu_both(dot_nt(dense_low, dd_ref[...]) + vector(ddb_ref))
+            kept["dense", half.start] = (active.astype(BF16), slope, dense_low)
+
+        def second():
+            out_ref[half, :] = dot(kept["dense", half.start][0], du_ref[...]) + vector(dub_ref)
+
+        return [first, second]
+
+    def norm_two(half):
+        def one(part):
+            dense_out = out_ref[part, :]
+            add("dense_square", eight_rows(dense_out * dense_out))
+            gain = vector(sg_ref)
+            result, normed, reciprocal = norm(hidden_ref[part, :] + wide_ref[part, :] + dense_out, gain, vector(ss_ref))
+            act_ref[part, :] = result.astype(BF16)
+            upstream = up_ref[part, :].astype(F32)
+            add(4, eight_rows(upstream * normed))
+            add(5, eight_rows(upstream))
+            second_grad = norm_grad(upstream, normed, reciprocal, gain)
+            hidden_ref[part, :] = second_grad
+            top = second_grad.astype(BF16)
+            top_ref[part, :] = top
+            add(1, eight_rows(top.astype(F32)))
+
+        return [functools.partial(one, part) for part in parts(half)]
+
+    def dense_back(half):
+        def first():
+            active, slope, dense_low = kept["dense", half.start]
+            top = top_ref[half, :]
+            add("dense_up", dot_tn(active, top))
+            mid = (dot_nt(top, du_ref[...]) * slope).astype(BF16)
+            kept["dense_mid", half.start] = mid
+            add("dense_mid", eight_rows(mid.astype(F32)))
+
+        def second():
+            mid = kept["dense_mid", half.start]
+            add("dense_down", dot_tn(mid, kept["dense", half.start][2]))
+            hidden_low_ref[half, :] = (hidden_ref[half, :] + dot(mid, dd_ref[...])).astype(BF16)
+
+        return [first, second]
+
+    def feed_back(half):
+        state = {}
+
+        def start():
+            side, span = pieces[0]
+            state["ahead"] = dot_nt(hidden_low_ref[half, :], side[1][span, :])
+
+        def one(n):
+            back = state["ahead"]
+            if n + 1 < len(pieces):
+                after, after_span = pieces[n + 1]
+                state["ahead"] = dot_nt(hidden_low_ref[half, :], after[1][after_span, :])
+            slope = slope_ref[half, n * chunk : (n + 1) * chunk].astype(F32)
+            state["value"] = (back * slope).astype(BF16)
+
+        def two(n):
+            side, span = pieces[n]
+            total = dot_nt(state["value"], side[0][:, span])
+            state["total"] = state["total"] + total if n else total
+            if n + 1 == len(pieces):
+                hidden_ref[half, :] = hidden_ref[half, :] + state["total"]
+
+        steps = [start]
+        for n in range(len(pieces)):
+            steps += [functools.partial(one, n), functools.partial(two, n)]
+        return steps
+
+    def norm_one_back(half):
+        def one(part):
+            hidden_grad, normed = hidden_ref[part, :], normed_ref[part, :]
+            add(2, eight_rows(hidden_grad * normed))
+            add(3, eight_rows(hidden_grad))
+            first_grad = norm_grad(hidden_grad, normed, kept["reciprocal", part.start], vector(fg_ref))
+            first_ref[part, :] = first_grad
+            top = first_grad.astype(BF16)
+            top_ref[part, :] = top
+            add(0, eight_rows(top.astype(F32)))
+
+        return [functools.partial(one, part) for part in parts(half)]
+
+    def attend_back(half):
+        def first():
+            active, slope = kept["mixer", half.start]
+            top = top_ref[half, :]
+            add("mixer_up", dot_tn(active, top))
+            mid = (dot_nt(top, mu_ref[...]) * slope).astype(BF16)
+            kept["mixer_mid", half.start] = mid
+            add("mixer_mid", eight_rows(mid.astype(F32)))
+
+        def second():
+            mid = kept["mixer_mid", half.start]
+            add("mixer_down", dot_tn(mid, low_ref[half, :]))
+            kept["attended", half.start] = (first_ref[half, :] + dot(mid, md_ref[...])).astype(BF16)
+
+        def third():
+            own_ref[half, :] = dot_nt(kept["attended", half.start], wo_ref[...]).astype(BF16)
+
+        def fourth():
+            away_ref[half, :] = dot_nt(kept["attended", half.start], wo2_ref[...]).astype(BF16)
+
+        return [first, second, third, fourth]
+
+    def send_result(half, index):
+        copy = pltpu.make_async_copy(act_ref.at[half, :], act_hbm.at[half, :], act_sem.at[index])
+        copy.start()
+        return copy
+
+    one, two = slice(0, rows // 2), slice(rows // 2, rows)
+    interleave(attend(one), [])
+    interleave(norm_one(one), attend(two))
+    interleave(feed_forward(one), norm_one(two))
+    interleave(feed_forward(two), dense(one) + norm_two(one) + dense_back(one))
+    copies = [send_result(one, 0)]
+    interleave(feed_back(one), dense(two) + norm_two(two) + dense_back(two))
+    copies.append(send_result(two, 1))
+    interleave(feed_back(two), norm_one_back(one) + attend_back(one))
+    interleave(norm_one_back(two), [])
+    interleave(attend_back(two), [])
+
+    for n, name in enumerate(("mixer_down", "mixer_up", "dense_down", "dense_up")):
+        big_ref[n * adapt : (n + 1) * adapt, :] = sums[name].astype(BF16)
+    for row in range(6):
+        small_ref[row : row + 1, :] = column_sum(sums[row])
     lane = lax.broadcasted_iota(jnp.int32, (1, 128), 1)
-    squares = jnp.where(lane == 0, mixer_square, jnp.where(lane == 1, dense_square, jnp.where(lane == 2, input_square, 0.0)))
+    squares = jnp.zeros((1, 128), F32)
+    for n, name in enumerate(("mixer_square", "dense_square", "input_square")):
+        squares = jnp.where(lane == n, jnp.sum(column_sum(sums[name]), -1, keepdims=True), squares)
     small_ref[6:7, :] = jnp.concatenate(
-        [mixer_mid_sum, dense_mid_sum, squares, jnp.zeros((1, features - 2 * adapt - 128), F32)], 1
+        [column_sum(sums["mixer_mid"]), column_sum(sums["dense_mid"]), squares, jnp.zeros((1, features - 2 * adapt - 128), F32)], 1
     )
     small_ref[7:8, :] = jnp.zeros((1, features), F32)
     tail = tail_of(small_ref[...])
     share = 2 * adapt
-    for out_ref, which in ((mine_ref, lax.axis_index("mp")), (theirs_ref, 1 - lax.axis_index("mp"))):
-        out_ref[:share, :] = big_ref[aligned(which, share), :]
-        out_ref[share:, :] = tail
-    act_copy.wait()
+    for pack_ref, which in ((mine_ref, lax.axis_index("mp")), (theirs_ref, 1 - lax.axis_index("mp"))):
+        pack_ref[:share, :] = big_ref[aligned(which, share), :]
+        pack_ref[share:, :] = tail
+    for copy in copies:
+        copy.wait()
 
 
 def tail_of(vectors):
@@ -577,17 +731,16 @@
         in_specs=[VM] * 15 + [HB] * 7,
         out_specs=(HB,) + (VM,) * 5,
         scratch_shapes=[pltpu.VMEM(m.shape, BF16) for m in matrices]
+        + [pltpu.VMEM((rows, 2 * units), BF16)]
+        + [pltpu.VMEM((rows, features), F32)] * 4
+        + [pltpu.VMEM((rows, features), BF16)] * 4
         + [
-            pltpu.VMEM((rows, 2 * units), BF16),
-            pltpu.VMEM((rows, features), F32),
-            pltpu.VMEM((rows, features), F32),
-            pltpu.VMEM((rows, features), BF16),
             pltpu.VMEM((4 * adapt, features), BF16),
             pltpu.VMEM((8, features), F32),
             pltpu.SemaphoreType.DMA((7,)),
-            pltpu.SemaphoreType.DMA,
+            pltpu.SemaphoreType.DMA((2,)),
         ],
-        compiler_params=pltpu.CompilerParams(vmem_limit_bytes=26 * MIB),
+        compiler_params=pltpu.CompilerParams(vmem_limit_bytes=28 * MIB),
         cost_estimate=pl.CostEstimate(flops=2 * 10**10, bytes_accessed=16 * MIB, transcendentals=10**6),
         name="middle",
     )(x, keep, got, up, *vectors, *swapped, *map(in_hbm, matrices))

time: 76.6 us -> 73.8 us (0.963)
  Pallas kernels: 56.2 us -> 48.6 us
  starting transfers between devices: 10 us -> 14.1 us
    ppermute x4, starting transfers between devices: 7.62 us -> 11.3 us  [per_device(): arriving = lax.ppermute(packed, ('dp', 'mp'), exchange)]
    pallas_call x3, Pallas kernels: 16.1 us -> 12.8 us  [pair_grad(): pl.pallas_call(functools.partial(pair_grad_kernel, p), out_shape=(jax.Sha...]
    pallas_call x1, Pallas kernels: 21.2 us -> 18.8 us  [middle(): pl.pallas_call(middle_kernel, out_shape=(jax.ShapeDtypeStruct((rows, feat...]
    ppermute x4, waiting for transfers between devices: 2.66 us -> 4.73 us  [per_device(): arriving = lax.ppermute(packed, ('dp', 'mp'), exchange)]
    pallas_call x1, Pallas kernels: 10.9 us -> 9.01 us  [attention(): pl.pallas_call(attention_kernel, out_shape=(like(kv), like(queries), jax....]
    ppermute x9, waiting for transfers between devices: 6.08 us -> 4.36 us  [swap_cores(): return lax.ppermute(value, 'mp', [(0, 1), (1, 0)])]
  transfers between devices with their start and end apart: 13 -> 13, of which waited for: 6 -> 6; matrix products, arithmetic and copies ran while one was open for 0% -> 0% of each run, Pallas kernels for 43% -> 38%
where the time goes in v7:
time: 73.8 us; the launch traced here: 72.9 us
  Pallas kernels  48.6 us (66%)
  starting transfers between devices  14.1 us (19%)
  waiting for transfers between devices  9.08 us (12%)
  between operations  1.03 us (1%)
    pallas_call x1, Pallas kernels, middle(): pl.pallas_call(middle_kernel, out_shape=(jax.ShapeDtypeStruct((rows, feat...  18.8 us
    pallas_call x3, Pallas kernels, pair_grad(): pl.pallas_call(functools.partial(pair_grad_kernel, p), out_shape=(jax.Sha...  12.8 us
    ppermute x4, starting transfers between devices, per_device(): arriving = lax.ppermute(packed, ('dp', 'mp'), exchange)  11.3 us
    pallas_call x1, Pallas kernels, attention(): pl.pallas_call(attention_kernel, out_shape=(like(kv), like(queries), jax....  9.01 us
    ppermute x4, waiting for transfers between devices, per_device(): arriving = lax.ppermute(packed, ('dp', 'mp'), exchange)  4.73 us
    ppermute x9, waiting for transfers between devices, swap_cores(): return lax.ppermute(value, 'mp', [(0, 1), (1, 0)])  4.36 us
    pallas_call x1, Pallas kernels, project(): pl.pallas_call(project_kernel, out_shape=(jax.ShapeDtypeStruct((count, 2...  3.46 us
    pallas_call x2, Pallas kernels, input_call(): pl.pallas_call(kernel, out_shape=jax.ShapeDtypeStruct((half, features), B...  3.26 us
  transfers between devices with their start and end apart: 13, of which 6 were waited for; matrix products, arithmetic and copies ran while one was open for 0% of the time, Pallas kernels for 38%

profile of v7, /device:TPU:0, one launch (start us, length us, event | category | flops | bytes accessed | tf_op | source)
XLA Modules:
  0.0 72.9 jit_solution(14575714831857588763)
XLA Ops:
  0.7 0.5 collective-permute-start
  1.2 3.5 %project.1 = (bf16[1024,768]{1,0:T(8,128)(2,1)S(1)}, bf16[3,2048,128]{2,1,0:T(8,128)(2,1)S(1)}, bf16[3,128,2048]{2,1,0:T(8,128)(2,1)S(1)}, bf16[480,1024]{1,0:T(...) custom-call(s32[1,1024]{1,0:T(1,128)} %seg_hbm.1, ...), custom_call_target="tpu_custom_call" | custom-call | flops 905969664 | bytes 5242880 | tf_op jit(solution)/shard_map/project/pallas_call | solution.py:158
  4.8 0.4 collective-permute-start.4
  5.5 9.0 %attention.1 = (bf16[1024,768]{1,0:T(8,128)(2,1)S(1)}, bf16[3,2048,128]{2,1,0:T(8,128)(2,1)S(1)}, bf16[512,384]{1,0:T(8,128)(2,1)S(1)}, bf16[512,384]{1,0:T(8,12...) custom-call(s32[2,4]{1,0:T(2,128)S(1)} %get-tuple-element.83.rng_ref, ...), custom_call_target="tpu_custom_call" | custom-call | flops 10000000000 | bytes 8388608 | tf_op jit(solution)/shard_map/attention/pallas_call | solution.py:274
  14.5 0.5 collective-permute-start.1
  15.0 1.3 %collective-permute-done.1.got_ref = bf16[512,384]{1,0:T(8,128)(2,1)S(1)} collective-permute-done((bf16[512,384]{1,0:T(8,128)(2,1)S(1)}, bf16[512,384]{1,0:T(8,128)(2,1)S(1)}, u32[]{:S(2)}, u32[]{:S(2)}) %collective-permute-start.1) | collective-permute-done | bytes 393248 | tf_op jit(solution)/shard_map/ppermute | solution.py:811
  16.4 18.8 %middle.1 = (bf16[512,768]{1,0:T(8,128)(2,1)}, f32[512,768]{1,0:T(8,128)S(1)}, bf16[512,384]{1,0:T(8,128)(2,1)S(1)}, bf16[512,384]{1,0:T(8,128)(2,1)S(1)}, bf16[...) custom-call(bf16[512,768]{1,0:T(8,128)(2,1)S(1)} %copy-done.3, bf16[512,384]{1,0:T(8,128)(2,1)S(1)} %get-tuple-element.92.keep_ref, ...), custom_call_target="tpu_custom_call" | custom-call | flops 20000000000 | bytes 16777216 | tf_op jit(solution)/shard_map/middle/pallas_call | solution.py:721
  35.2 0.4 collective-permute-start.5
  35.8 1.5 %collective-permute-done.6.got_ref = bf16[144,768]{1,0:T(8,128)(2,1)S(1)} collective-permute-done((bf16[144,768]{1,0:T(8,128)(2,1)S(1)}, bf16[144,768]{1,0:T(8,128)(2,1)S(1)}, u32[]{:S(2)}, u32[]{:S(2)}) %collective-permute-start.6) | collective-permute-done | bytes 221216 | tf_op jit(solution)/shard_map/ppermute | solution.py:811
  37.4 5.9 %collective-permute-start.7 = (bf16[144,768]{1,0:T(8,128)(2,1)S(1)}, bf16[144,768]{1,0:T(8,128)(2,1)S(1)}, u32[]{:S(2)}, u32[]{:S(2)}) collective-permute-start(bf16[144,768]{1,0:T(8,128)(2,1)S(1)} %combine.5.held_ref), channel_id=1, source_target_pairs={{0,16},{1,5},{2,18},{3,7},{4,20},{5,1},{6,22},{7,3},{8,24},{9,13},... | collective-permute-start | bytes 663560 | tf_op jit(solution)/shard_map/ppermute | solution.py:861
  43.3 4.3 %pair_grad_0.1 = (bf16[1024,128]{1,0:T(8,128)(2,1)S(1)}, bf16[1024,128]{1,0:T(8,128)(2,1)S(1)}, bf16[1024,128]{1,0:T(8,128)(2,1)S(1)}) custom-call(s32[2,4]{1,0:T(2,128)S(1)} %get-tuple-element.83.rng_ref, bf16[1024,768]{1,0:T(8,128)(2,1)S(1)} %get-tuple-element.103.kv_ref, bf16[3,2048,128]{2,1,0:T(8,128)(2,1)S(1)} %get-tuple-element.104.queries_ref, ...), custom_call_target="tpu_custom_call" | custom-call | flops 4000000000 | bytes 8388608 | tf_op jit(solution)/shard_map/pair_grad_0/pallas_call | solution.py:349
  47.6 2.0 %collective-permute-done.7.got_ref = bf16[144,768]{1,0:T(8,128)(2,1)S(1)} collective-permute-done((bf16[144,768]{1,0:T(8,128)(2,1)S(1)}, bf16[144,768]{1,0:T(8,128)(2,1)S(1)}, u32[]{:S(2)}, u32[]{:S(2)}) %collective-permute-start.7) | collective-permute-done | bytes 221216 | tf_op jit(solution)/shard_map/ppermute | solution.py:861
  49.7 1.1 %collective-permute-start.8 = (bf16[144,768]{1,0:T(8,128)(2,1)S(1)}, bf16[144,768]{1,0:T(8,128)(2,1)S(1)}, u32[]{:S(2)}, u32[]{:S(2)}) collective-permute-start(bf16[144,768]{1,0:T(8,128)(2,1)S(1)} %combine.6.held_ref), channel_id=1, source_target_pairs={{0,8},{1,3},{2,10},{3,1},{4,12},{5,7},{6,14},{7,5},{8,0},{9,11},{1... | collective-permute-start | bytes 663560 | tf_op jit(solution)/shard_map/ppermute | solution.py:861
  50.7 4.3 %pair_grad_1.1 = (bf16[1024,128]{1,0:T(8,128)(2,1)S(1)}, bf16[1024,128]{1,0:T(8,128)(2,1)S(1)}, bf16[1024,128]{1,0:T(8,128)(2,1)S(1)}) custom-call(s32[2,4]{1,0:T(2,128)S(1)} %get-tuple-element.83.rng_ref, bf16[1024,768]{1,0:T(8,128)(2,1)S(1)} %get-tuple-element.103.kv_ref, bf16[3,2048,128]{2,1,0:T(8,128)(2,1)S(1)} %get-tuple-element.104.queries_ref, ...), custom_call_target="tpu_custom_call" | custom-call | flops 4000000000 | bytes 8388608 | tf_op jit(solution)/shard_map/pair_grad_1/pallas_call | solution.py:349
  55.0 0.7 collective-permute-done.8.got_ref
  55.7 2.4 %collective-permute-start.9 = (bf16[144,768]{1,0:T(8,128)(2,1)S(1)}, bf16[144,768]{1,0:T(8,128)(2,1)S(1)}, u32[]{:S(2)}, u32[]{:S(2)}) collective-permute-start(bf16[144,768]{1,0:T(8,128)(2,1)S(1)} %combine.7.held_ref), channel_id=1, source_target_pairs={{0,4},{1,17},{2,6},{3,19},{4,0},{5,21},{6,2},{7,23},{8,12},{9,25},... | collective-permute-start | bytes 663560 | tf_op jit(solution)/shard_map/ppermute | solution.py:861
  58.1 4.3 %pair_grad_2.1 = (bf16[1024,128]{1,0:T(8,128)(2,1)S(1)}, bf16[1024,128]{1,0:T(8,128)(2,1)S(1)}, bf16[1024,128]{1,0:T(8,128)(2,1)S(1)}) custom-call(s32[2,4]{1,0:T(2,128)S(1)} %get-tuple-element.83.rng_ref, bf16[1024,768]{1,0:T(8,128)(2,1)S(1)} %get-tuple-element.103.kv_ref, bf16[3,2048,128]{2,1,0:T(8,128)(2,1)S(1)} %get-tuple-element.104.queries_ref, ...), custom_call_target="tpu_custom_call" | custom-call | flops 4000000000 | bytes 8388608 | tf_op jit(solution)/shard_map/pair_grad_2/pallas_call | solution.py:349
  62.4 1.2 %away.1 = bf16[512,768]{1,0:T(8,128)(2,1)S(1)} custom-call(bf16[1024,128]{1,0:T(8,128)(2,1)S(1)} %get-tuple-element.127.refs_0_, bf16[1024,128]{1,0:T(8,128)(2,1)S(1)} %get-tuple-element.128.refs_1_, bf16[1024,128]{1,0:T(8,128)(2,1)S(1)} %get-tuple-element.129.refs_2_, bf16[1024,128]{1,0:T(8,128)(2,1)S(1)} %get-tuple-element.130.refs_3_, ...), custom_call_target="tpu_custom_call" | custom-call | flops 1000000000 | bytes 6291456 | tf_op jit(solution)/shard_map/away/pallas_call | solution.py:402
  63.6 0.6 collective-permute-start.11
  64.2 1.9 %collective-permute-start.10 = (bf16[144,768]{1,0:T(8,128)(2,1)S(1)}, bf16[144,768]{1,0:T(8,128)(2,1)S(1)}, u32[]{:S(2)}, u32[]{:S(2)}) collective-permute-start(bf16[144,768]{1,0:T(8,128)(2,1)S(1)} %combine.8.held_ref), channel_id=1, source_target_pairs={{0,2},{1,9},{2,0},{3,11},{4,6},{5,13},{6,4},{7,15},{8,10},{9,1},{1... | collective-permute-start | bytes 663560 | tf_op jit(solution)/shard_map/ppermute | solution.py:861
  66.1 2.0 %home.1 = bf16[512,768]{1,0:T(8,128)(2,1)} custom-call(f32[512,768]{1,0:T(8,128)S(1)} %get-tuple-element.126.first_ref, bf16[512,768]{1,0:T(8,128)(2,1)S(1)} %collective-permute-done.11.got_ref, bf16[1024,128]{1,0:T(8,128)(2,1)S(1)} %get-tuple-element.127.refs_0_, bf16[1024,128]{1,0:T(8,128)(2,1)S(1)} %get-tuple-element.128.refs_1_, ...), custom_call_target="tpu_custom_call" | custom-call | flops 1000000000 | bytes 6291456 | tf_op jit(solution)/shard_map/home/pallas_call | solution.py:402
  68.2 2.1 %collective-permute-done.10.got_ref = bf16[144,768]{1,0:T(8,128)(2,1)S(1)} collective-permute-done((bf16[144,768]{1,0:T(8,128)(2,1)S(1)}, bf16[144,768]{1,0:T(8,128)(2,1)S(1)}, u32[]{:S(2)}, u32[]{:S(2)}) %collective-permute-start.10) | collective-permute-done | bytes 221216 | tf_op jit(solution)/shard_map/ppermute | solution.py:861
  70.4 1.5 %collective-permute-done.12.got_ref = bf16[144,768]{1,0:T(8,128)(2,1)S(1)} collective-permute-done((bf16[144,768]{1,0:T(8,128)(2,1)S(1)}, bf16[144,768]{1,0:T(8,128)(2,1)S(1)}, u32[]{:S(2)}, u32[]{:S(2)}) %collective-permute-start.12) | collective-permute-done | bytes 221216 | tf_op jit(solution)/shard_map/ppermute | solution.py:811
  71.8 1.0 %finish.1 = (f32[64,768]{1,0:T(8,128)}, f32[64]{0:T(128)}, f32[64,768]{1,0:T(8,128)}, f32[768]{0:T(1024)}, f32[64,768]{1,0:T(8,128)}, /*index=5*/f32[64]{0:T(128...) custom-call(bf16[144,768]{1,0:T(8,128)(2,1)S(1)} %combine.9.held_ref, ...), custom_call_target="tpu_custom_call" | custom-call | tf_op jit(solution)/shard_map/finish/pallas_call | solution.py:800
  (44 shorter events, 0.8 us)
Async XLA Ops:
  0.6 4.7 %copy-start = (bf16[768,384]{1,0:T(8,128)(2,1)S(1)}, bf16[768,384]{1,0:T(8,128)(2,1)}, u32[]{:S(2)}) copy-start(bf16[768,384]{1,0:T(8,128)(2,1)} %refs_9_.3) | copy-start | bytes 1769476
  0.7 4.0 %collective-permute-start = (bf16[512,768]{1,0:T(8,128)(2,1)}, bf16[512,768]{1,0:T(8,128)(2,1)S(1)}, u32[]{:S(2)}, u32[]{:S(2)}) collective-permute-start(bf16[512,768]{1,0:T(8,128)(2,1)} %x_ref.3), channel_id=1, source_target_pairs={{0,1},{1,0},{2,3},{3,2},{4,5},{5,4},{6,7},{7,6},{8,9},{9,8},{10,11... | collective-permute-start | bytes 2359304 | tf_op jit(solution)/shard_map/ppermute | solution.py:811
  4.7 11.7 %collective-permute-start.3 = (bf16[768,1536]{1,0:T(8,128)(2,1)}, bf16[768,1536]{1,0:T(8,128)(2,1)S(1)}, u32[]{:S(2)}, u32[]{:S(2)}) collective-permute-start(bf16[768,1536]{1,0:T(8,128)(2,1)} %w1_hbm.1), channel_id=1, source_target_pairs={{0,1},{1,0},{2,3},{3,2},{4,5},{5,4},{6,7},{7,6},{8,9},{9,8},{10,11... | collective-permute-start | bytes 7077896 | tf_op jit(solution)/shard_map/ppermute | solution.py:811
  4.8 11.5 %collective-permute-start.4 = (bf16[1536,768]{1,0:T(8,128)(2,1)}, bf16[1536,768]{1,0:T(8,128)(2,1)S(1)}, u32[]{:S(2)}, u32[]{:S(2)}) collective-permute-start(bf16[1536,768]{1,0:T(8,128)(2,1)} %w2_hbm.1), channel_id=1, source_target_pairs={{0,1},{1,0},{2,3},{3,2},{4,5},{5,4},{6,7},{7,6},{8,9},{9,8},{10,11... | collective-permute-start | bytes 7077896 | tf_op jit(solution)/shard_map/ppermute | solution.py:811
  5.3 11.1 %collective-permute-start.2 = (bf16[384,768]{1,0:T(8,128)(2,1)S(1)}, bf16[384,768]{1,0:T(8,128)(2,1)S(1)}, u32[]{:S(2)}, u32[]{:S(2)}) collective-permute-start(bf16[384,768]{1,0:T(8,128)(2,1)S(1)} %copy-done.13), channel_id=1, source_target_pairs={{0,1},{1,0},{2,3},{3,2},{4,5},{5,4},{6,7},{7,6},{8,9},{9,8},{10,11... | collective-permute-start | bytes 1769480 | tf_op jit(solution)/shard_map/ppermute | solution.py:811
  5.4 11.0 %copy-start.3 = (bf16[512,768]{1,0:T(8,128)(2,1)S(1)}, bf16[512,768]{1,0:T(8,128)(2,1)}, u32[]{:S(2)}) copy-start(bf16[512,768]{1,0:T(8,128)(2,1)} %x_ref.3) | copy-start | bytes 2359300
  5.4 11.0 %copy-start.4 = (bf16[512,768]{1,0:T(8,128)(2,1)S(1)}, bf16[512,768]{1,0:T(8,128)(2,1)}, u32[]{:S(2)}) copy-start(bf16[512,768]{1,0:T(8,128)(2,1)} %up_ref.1) | copy-start | bytes 2359300
  5.4 11.0 %copy-start.5 = (bf16[768]{0:T(1024)(128)(2,1)S(1)}, bf16[768]{0:T(1024)(128)(2,1)}, u32[]{:S(2)}) copy-start(bf16[768]{0:T(1024)(128)(2,1)} %mub_ref.1) | copy-start | bytes 4612
  5.4 11.0 %copy-start.6 = (bf16[768]{0:T(1024)(128)(2,1)S(1)}, bf16[768]{0:T(1024)(128)(2,1)}, u32[]{:S(2)}) copy-start(bf16[768]{0:T(1024)(128)(2,1)} %dub_ref.1) | copy-start | bytes 4612
  5.4 11.0 %copy-start.7 = (bf16[768]{0:T(1024)(128)(2,1)S(1)}, bf16[768]{0:T(1024)(128)(2,1)}, u32[]{:S(2)}) copy-start(bf16[768]{0:T(1024)(128)(2,1)} %fg_ref.1) | copy-start | bytes 4612
  5.4 11.0 %copy-start.8 = (bf16[768]{0:T(1024)(128)(2,1)S(1)}, bf16[768]{0:T(1024)(128)(2,1)}, u32[]{:S(2)}) copy-start(bf16[768]{0:T(1024)(128)(2,1)} %fs_ref.1) | copy-start | bytes 4612
  5.4 11.0 %copy-start.9 = (bf16[768]{0:T(1024)(128)(2,1)S(1)}, bf16[768]{0:T(1024)(128)(2,1)}, u32[]{:S(2)}) copy-start(bf16[768]{0:T(1024)(128)(2,1)} %sg_ref.1) | copy-start | bytes 4612
  5.4 11.0 %copy-start.10 = (bf16[768]{0:T(1024)(128)(2,1)S(1)}, bf16[768]{0:T(1024)(128)(2,1)}, u32[]{:S(2)}) copy-start(bf16[768]{0:T(1024)(128)(2,1)} %ss_ref.1) | copy-start | bytes 4612
  5.4 11.0 %copy-start.11 = (bf16[64]{0:T(256)(128)(2,1)S(1)}, bf16[64]{0:T(256)(128)(2,1)}, u32[]{:S(2)}) copy-start(bf16[64]{0:T(256)(128)(2,1)} %mdb_ref.1) | copy-start | bytes 388
  5.5 11.0 %copy-start.12 = (bf16[64]{0:T(256)(128)(2,1)S(1)}, bf16[64]{0:T(256)(128)(2,1)}, u32[]{:S(2)}) copy-start(bf16[64]{0:T(256)(128)(2,1)} %ddb_ref.1) | copy-start | bytes 388
  14.5 1.8 %collective-permute-start.1 = (bf16[512,384]{1,0:T(8,128)(2,1)S(1)}, bf16[512,384]{1,0:T(8,128)(2,1)S(1)}, u32[]{:S(2)}, u32[]{:S(2)}) collective-permute-start(bf16[512,384]{1,0:T(8,128)(2,1)S(1)} %get-tuple-element.93.send_ref), channel_id=1, source_target_pairs={{0,1},{1,0},{2,3},{3,2},{4,5},{5,4},{6,7},{7,6},{8,9},{9,8},{10,11... | collective-permute-start | bytes 1179656 | tf_op jit(solution)/shard_map/ppermute | solution.py:811
  35.2 8.1 %collective-permute-start.5 = (bf16[512,384]{1,0:T(8,128)(2,1)S(1)}, bf16[512,384]{1,0:T(8,128)(2,1)S(1)}, u32[]{:S(2)}, u32[]{:S(2)}) collective-permute-start(bf16[512,384]{1,0:T(8,128)(2,1)S(1)} %get-tuple-element.98), channel_id=1, source_target_pairs={{0,1},{1,0},{2,3},{3,2},{4,5},{5,4},{6,7},{7,6},{8,9},{9,8},{10,11... | collective-permute-start | bytes 1179656 | tf_op jit(solution)/shard_map/ppermute | solution.py:811
  35.7 1.7 %collective-permute-start.6 = (bf16[144,768]{1,0:T(8,128)(2,1)S(1)}, bf16[144,768]{1,0:T(8,128)(2,1)S(1)}, u32[]{:S(2)}, u32[]{:S(2)}) collective-permute-start(bf16[144,768]{1,0:T(8,128)(2,1)S(1)} %get-tuple-element.100), channel_id=1, source_target_pairs={{0,1},{1,0},{2,3},{3,2},{4,5},{5,4},{6,7},{7,6},{8,9},{9,8},{10,11... | collective-permute-start | bytes 663560 | tf_op jit(solution)/shard_map/ppermute | solution.py:811
  37.4 12.2 %collective-permute-start.7 = (bf16[144,768]{1,0:T(8,128)(2,1)S(1)}, bf16[144,768]{1,0:T(8,128)(2,1)S(1)}, u32[]{:S(2)}, u32[]{:S(2)}) collective-permute-start(bf16[144,768]{1,0:T(8,128)(2,1)S(1)} %combine.5.held_ref), channel_id=1, source_target_pairs={{0,16},{1,5},{2,18},{3,7},{4,20},{5,1},{6,22},{7,3},{8,24},{9,13},... | collective-permute-start | bytes 663560 | tf_op jit(solution)/shard_map/ppermute | solution.py:861
  49.7 6.0 %collective-permute-start.8 = (bf16[144,768]{1,0:T(8,128)(2,1)S(1)}, bf16[144,768]{1,0:T(8,128)(2,1)S(1)}, u32[]{:S(2)}, u32[]{:S(2)}) collective-permute-start(bf16[144,768]{1,0:T(8,128)(2,1)S(1)} %combine.6.held_ref), channel_id=1, source_target_pairs={{0,8},{1,3},{2,10},{3,1},{4,12},{5,7},{6,14},{7,5},{8,0},{9,11},{1... | collective-permute-start | bytes 663560 | tf_op jit(solution)/shard_map/ppermute | solution.py:861
  55.7 6.6 %collective-permute-start.9 = (bf16[144,768]{1,0:T(8,128)(2,1)S(1)}, bf16[144,768]{1,0:T(8,128)(2,1)S(1)}, u32[]{:S(2)}, u32[]{:S(2)}) collective-permute-start(bf16[144,768]{1,0:T(8,128)(2,1)S(1)} %combine.7.held_ref), channel_id=1, source_target_pairs={{0,4},{1,17},{2,6},{3,19},{4,0},{5,21},{6,2},{7,23},{8,12},{9,25},... | collective-permute-start | bytes 663560 | tf_op jit(solution)/shard_map/ppermute | solution.py:861
  63.6 2.5 %collective-permute-start.11 = (bf16[512,768]{1,0:T(8,128)(2,1)S(1)}, bf16[512,768]{1,0:T(8,128)(2,1)S(1)}, u32[]{:S(2)}, u32[]{:S(2)}) collective-permute-start(bf16[512,768]{1,0:T(8,128)(2,1)S(1)} %away.1), channel_id=1, source_target_pairs={{0,1},{1,0},{2,3},{3,2},{4,5},{5,4},{6,7},{7,6},{8,9},{9,8},{10,11... | collective-permute-start | bytes 2359304 | tf_op jit(solution)/shard_map/ppermute | solution.py:811
  64.2 6.0 %collective-permute-start.10 = (bf16[144,768]{1,0:T(8,128)(2,1)S(1)}, bf16[144,768]{1,0:T(8,128)(2,1)S(1)}, u32[]{:S(2)}, u32[]{:S(2)}) collective-permute-start(bf16[144,768]{1,0:T(8,128)(2,1)S(1)} %combine.8.held_ref), channel_id=1, source_target_pairs={{0,2},{1,9},{2,0},{3,11},{4,6},{5,13},{6,4},{7,15},{8,10},{9,1},{1... | collective-permute-start | bytes 663560 | tf_op jit(solution)/shard_map/ppermute | solution.py:861
  70.3 1.5 %collective-permute-start.12 = (bf16[144,768]{1,0:T(8,128)(2,1)S(1)}, bf16[144,768]{1,0:T(8,128)(2,1)S(1)}, u32[]{:S(2)}, u32[]{:S(2)}) collective-permute-start(bf16[144,768]{1,0:T(8,128)(2,1)S(1)} %combine.9.held_ref), channel_id=1, source_target_pairs={{0,1},{1,0},{2,3},{3,2},{4,5},{5,4},{6,7},{7,6},{8,9},{9,8},{10,11... | collective-permute-start | bytes 663560 | tf_op jit(solution)/shard_map/ppermute | solution.py:811
  (3 other events, 14.0 us)

commit v8 on v7

--- a/solution.py
+++ b/solution.py
@@ -23,6 +23,7 @@
 BLOCK = 256
 STEP = 128
 MIB = 1 << 20
+SHORT = pl.CostEstimate(flops=10**4, bytes_accessed=10**3, transcendentals=0)
 
 VM = pl.BlockSpec(memory_space=pltpu.VMEM)
 SM = pl.BlockSpec(memory_space=pltpu.SMEM)
@@ -79,12 +80,14 @@
     return copies
 
 
-def write_projection(which, x, weights, copies, kv_ref, queries_ref, across_ref, turned_ref):
+def write_projection(which, x, weights, copies, kv_ref, queries_ref, across_ref, turned_ref, between=None):
     rows, width = x.shape[0], weights[0].shape[1]
     pairs = width // PAIR
     if copies:
         copies[0].wait()
     queries = (dot(x, weights[0][...]) * (HEAD_DIM**-0.5 * LOG2E)).astype(BF16)
+    if between is not None:
+        between()
     for p in range(pairs):
         pair = queries[:, p * PAIR : (p + 1) * PAIR]
         stack_heads(pair, queries_ref.at[p, aligned(which, 2 * rows), :], BLOCK)
@@ -129,27 +132,32 @@
     sources, buffers = (seg_hbm, x_ref, wq_ref, wk_ref, wv_ref), (seg_ref, x_buf, wq, wk, wv)
     seg_copy, *copies = start_all(sources, buffers, sems)
     count, block = kv_ref.shape[0], BLOCK
+
+    def items():
+        ids = seg_ref[...].astype(F32)
+        position = lax.broadcasted_iota(jnp.int32, ids.shape, 1)
+        for g in range(count // block):
+            first, last = (
+                jnp.sum(jnp.where(position == at, ids, 0.0), -1, keepdims=True) for at in (g * block, (g + 1) * block - 1)
+            )
+            rng_ref[0, g] = jnp.sum(jnp.where(ids < first, 1.0, 0.0)).astype(jnp.int32) // STEP
+            rng_ref[1, g] = (jnp.sum(jnp.where(ids <= last, 1.0, 0.0)).astype(jnp.int32) + STEP - 1) // STEP
+        lane = lax.broadcasted_iota(jnp.int32, (128, 128), 1)
+        for t in range(count // 128):
+            same = jnp.broadcast_to(ids[:, t * 128 : (t + 1) * 128], (128, 128)).T == lane.astype(F32)
+            item_ref[t * 128 : (t + 1) * 128, :] = jnp.where(same | is_shift(lane), 1.0, 0.0).astype(BF16)
+        row = lax.broadcasted_iota(jnp.int32, (128, block), 0)
+        for t in range(count // block):
+            same = row.astype(F32) == ids[:, t * block : (t + 1) * block]
+            hide = jnp.where(same | is_shift(row), 0.0, MASKED).astype(BF16)
+            for a in range(2):
+                hide_ref[:, (2 * t + a) * block : (2 * t + a + 1) * block] = hide
+
     seg_copy.wait()
-    ids = seg_ref[...].astype(F32)
-    position = lax.broadcasted_iota(jnp.int32, ids.shape, 1)
-    for g in range(count // block):
-        first, last = (
-            jnp.sum(jnp.where(position == at, ids, 0.0), -1, keepdims=True) for at in (g * block, (g + 1) * block - 1)
-        )
-        rng_ref[0, g] = jnp.sum(jnp.where(ids < first, 1.0, 0.0)).astype(jnp.int32) // STEP
-        rng_ref[1, g] = (jnp.sum(jnp.where(ids <= last, 1.0, 0.0)).astype(jnp.int32) + STEP - 1) // STEP
-    lane = lax.broadcasted_iota(jnp.int32, (128, 128), 1)
-    for t in range(count // 128):
-        same = jnp.broadcast_to(ids[:, t * 128 : (t + 1) * 128], (128, 128)).T == lane.astype(F32)
-        item_ref[t * 128 : (t + 1) * 128, :] = jnp.where(same | is_shift(lane), 1.0, 0.0).astype(BF16)
-    row = lax.broadcasted_iota(jnp.int32, (128, block), 0)
-    for t in range(count // block):
-        same = row.astype(F32) == ids[:, t * block : (t + 1) * block]
-        hide = jnp.where(same | is_shift(row), 0.0, MASKED).astype(BF16)
-        for a in range(2):
-            hide_ref[:, (2 * t + a) * block : (2 * t + a + 1) * block] = hide
     copies[0].wait()
-    write_projection(lax.axis_index("mp"), x_buf[...], (wq, wk, wv), copies[1:], kv_ref, queries_ref, across_ref, turned_ref)
+    write_projection(
+        lax.axis_index("mp"), x_buf[...], (wq, wk, wv), copies[1:], kv_ref, queries_ref, across_ref, turned_ref, items
+    )
 
 
 def project(seg, x, wq, wk, wv):
@@ -298,7 +306,7 @@
 
 def pair_grad_kernel(
     p, rng_ref, kv_ref, queries_ref, keep_ref, send_ref, own_ref, other_ref, inverse_ref, share_ref,
-    dq_ref, dk_ref, dv_ref,
+    home_ref, away_ref,
     grads, across, turned, delta, dq, dk, dv,
 ):
     half, width = keep_ref.shape
@@ -336,21 +344,33 @@
                 dq[head, :] += dot(turned[head, span], slopes[:, a * block : (a + 1) * block])
 
         over_keys(rng_ref[0, g], rng_ref[1, g], visit)
-        dq_ref[rows, :] = (dq[...] * HEAD_DIM**-0.5).astype(BF16).T
+        result = (dq[...] * HEAD_DIM**-0.5).astype(BF16).T
+        per_half = half // block
+
+        @pl.when(g // per_half == here)
+        def _():
+            home_ref[aligned(g % per_half, block), :PAIR] = result
+
+        @pl.when(g // per_half != here)
+        def _():
+            away_ref[aligned(g % per_half, block), :PAIR] = result
+
         return carry
 
     lax.fori_loop(0, count // block, query_block, 0)
-    dk_ref[...] = (dk[...] * LN2).astype(BF16)
-    dv_ref[...] = dv[...].astype(BF16)
+    for which, out_ref in ((here, home_ref), (there, away_ref)):
+        rows = aligned(which, half)
+        out_ref[:, PAIR : 2 * PAIR] = (dk[rows, :] * LN2).astype(BF16)
+        out_ref[:, 2 * PAIR :] = dv[rows, :].astype(BF16)
 
 
 def pair_grad(p, rng, kv, queries, keep, send, own, other, inverse, shares):
     count = kv.shape[0]
     return pl.pallas_call(
         functools.partial(pair_grad_kernel, p),
-        out_shape=(jax.ShapeDtypeStruct((count, PAIR), BF16),) * 3,
+        out_shape=(jax.ShapeDtypeStruct((count // 2, 3 * PAIR), BF16),) * 2,
         in_specs=[SM] + [VM] * 8,
-        out_specs=(VM,) * 3,
+        out_specs=(VM,) * 2,
         scratch_shapes=[
             pltpu.VMEM((2 * count, PAIR), BF16),
             pltpu.VMEM((PAIR, 2 * count), BF16),
@@ -366,49 +386,36 @@
     )(rng, kv, queries, keep, send, own, other, inverse, shares)
 
 
-def input_part(flip, pieces, weights, half):
-    which = 1 - lax.axis_index("mp") if flip else lax.axis_index("mp")
-    rows = aligned(which, half)
-    left = jnp.concatenate([piece[rows, :] for piece in pieces], 1)
-    right = jnp.concatenate([weight[...] for weight in weights], 1)
-    return dot_nt(left, right)
-
-
-def away_kernel(*refs):
-    out_ref = refs[-1]
-    out_ref[...] = input_part(True, refs[:-4], refs[-4:-1], out_ref.shape[0]).astype(BF16)
-
-
-def home_kernel(first_ref, got_ref, *refs):
-    *pieces, wq_ref, wk_ref, wv_ref, out_hbm, out_ref, sems = refs
-    half = out_ref.shape[0]
-    parts = 2
-    size = half // parts
-    right = jnp.concatenate([wq_ref[...], wk_ref[...], wv_ref[...]], 1)
+def input_kernel(pairs, first_ref, *refs):
+    *refs, out_hbm, out_ref, sems = refs
+    pieces, weights = refs[: 2 * pairs], refs[2 * pairs :]
+    spans = [slice(p * PAIR, (p + 1) * PAIR) for p in range(pairs)]
+    right = jnp.concatenate(
+        [weight[:, span] for side in (weights[:3], weights[3:]) for span in spans for weight in side], 1
+    )
+    size = out_ref.shape[0] // 2
     copies = []
-    for t in range(parts):
+    for t in range(2):
         part = slice(t * size, (t + 1) * size)
-        rows = aligned(lax.axis_index("mp") * parts + t, size)
-        total = dot_nt(jnp.concatenate([piece[rows, :] for piece in pieces], 1), right)
-        out_ref[part, :] = (total + first_ref[part, :] + got_ref[part, :].astype(F32)).astype(BF16)
+        left = jnp.concatenate([piece[part, :] for piece in pieces], 1)
+        out_ref[part, :] = (dot_nt(left, right) + first_ref[part, :]).astype(BF16)
         copies.append(pltpu.make_async_copy(out_ref.at[part, :], out_hbm.at[part, :], sems.at[t]))
         copies[-1].start()
     for copy in copies:
         copy.wait()
 
 
-def input_call(kernel, extra, pieces, weights, name):
-    half, features = pieces[0].shape[0] // 2, weights[0].shape[0]
+def input_gradient(first_grad, pieces, weights):
     return pl.pallas_call(
-        kernel,
-        out_shape=jax.ShapeDtypeStruct((half, features), BF16),
-        in_specs=[VM] * (len(extra) + len(pieces) + len(weights)),
-        out_specs=HB if extra else VM,
-        scratch_shapes=[pltpu.VMEM((half, features), BF16), pltpu.SemaphoreType.DMA((2,))] if extra else [],
+        functools.partial(input_kernel, len(pieces) // 2),
+        out_shape=jax.ShapeDtypeStruct(first_grad.shape, BF16),
+        in_specs=[VM] * (1 + len(pieces) + len(weights)),
+        out_specs=HB,
+        scratch_shapes=[pltpu.VMEM(first_grad.shape, BF16), pltpu.SemaphoreType.DMA((2,))],
         compiler_params=pltpu.CompilerParams(vmem_limit_bytes=16 * MIB),
-        cost_estimate=pl.CostEstimate(flops=10**9, bytes_accessed=6 * MIB, transcendentals=0),
-        name=name,
-    )(*extra, *pieces, *weights)
+        cost_estimate=pl.CostEstimate(flops=2 * 10**9, bytes_accessed=8 * MIB, transcendentals=0),
+        name="input_gradient",
+    )(first_grad, *pieces, *weights)
 
 
 def gelu_both(v):
@@ -454,7 +461,7 @@
     x_ref, keep_ref, got_ref, up_ref,
     mdb_ref, mub_ref, ddb_ref, dub_ref, fg_ref, fs_ref, sg_ref, ss_ref,
     wo2_ref, w12_ref, w22_ref, wo_hbm, md_hbm, mu_hbm, w1_hbm, w2_hbm, dd_hbm, du_hbm,
-    act_hbm, first_ref, own_ref, away_ref, mine_ref, theirs_ref,
+    act_hbm, first_ref, attended_ref, mine_ref, theirs_ref,
     wo_ref, md_ref, mu_ref, w1_ref, w2_ref, dd_ref, du_ref,
     slope_ref, wide_ref, out_ref, hidden_ref, normed_ref, low_ref, hidden_low_ref, act_ref, top_ref,
     big_ref, small_ref, sems, act_sem,
@@ -654,15 +661,9 @@
         def second():
             mid = kept["mixer_mid", half.start]
             add("mixer_down", dot_tn(mid, low_ref[half, :]))
-            kept["attended", half.start] = (first_ref[half, :] + dot(mid, md_ref[...])).astype(BF16)
-
-        def third():
-            own_ref[half, :] = dot_nt(kept["attended", half.start], wo_ref[...]).astype(BF16)
-
-        def fourth():
-            away_ref[half, :] = dot_nt(kept["attended", half.start], wo2_ref[...]).astype(BF16)
-
-        return [first, second, third, fourth]
+            attended_ref[half, :] = (first_ref[half, :] + dot(mid, md_ref[...])).astype(BF16)
+
+        return [first, second]
 
     def send_result(half, index):
         copy = pltpu.make_async_copy(act_ref.at[half, :], act_hbm.at[half, :], act_sem.at[index])
@@ -714,7 +715,6 @@
 
 def middle(x, keep, got, up, vectors, swapped, matrices):
     rows, features = x.shape
-    width = keep.shape[1]
     adapt = matrices[1].shape[0]
     units = matrices[3].shape[1]
     packed = jax.ShapeDtypeStruct((2 * adapt + 16, features), BF16)
@@ -723,13 +723,12 @@
         out_shape=(
             jax.ShapeDtypeStruct((rows, features), BF16),
             jax.ShapeDtypeStruct((rows, features), F32),
-            jax.ShapeDtypeStruct((rows, width), BF16),
-            jax.ShapeDtypeStruct((rows, width), BF16),
+            jax.ShapeDtypeStruct((rows, features), BF16),
             packed,
             packed,
         ),
         in_specs=[VM] * 15 + [HB] * 7,
-        out_specs=(HB,) + (VM,) * 5,
+        out_specs=(HB,) + (VM,) * 4,
         scratch_shapes=[pltpu.VMEM(m.shape, BF16) for m in matrices]
         + [pltpu.VMEM((rows, 2 * units), BF16)]
         + [pltpu.VMEM((rows, features), F32)] * 4
@@ -740,10 +739,29 @@
             pltpu.SemaphoreType.DMA((7,)),
             pltpu.SemaphoreType.DMA((2,)),
         ],
-        compiler_params=pltpu.CompilerParams(vmem_limit_bytes=28 * MIB),
+        compiler_params=pltpu.CompilerParams(vmem_limit_bytes=25 * MIB),
         cost_estimate=pl.CostEstimate(flops=2 * 10**10, bytes_accessed=16 * MIB, transcendentals=10**6),
         name="middle",
     )(x, keep, got, up, *vectors, *swapped, *map(in_hbm, matrices))
+
+
+def spread_kernel(attended_ref, wo_ref, wo2_ref, own_ref, away_ref):
+    attended = attended_ref[...]
+    away_ref[...] = dot_nt(attended, wo2_ref[...]).astype(BF16)
+    own_ref[...] = dot_nt(attended, wo_ref[...]).astype(BF16)
+
+
+def spread(attended, wo, wo2):
+    rows, width = attended.shape[0], wo.shape[0]
+    return pl.pallas_call(
+        spread_kernel,
+        out_shape=(jax.ShapeDtypeStruct((rows, width), BF16),) * 2,
+        in_specs=[VM] * 3,
+        out_specs=(VM,) * 2,
+        compiler_params=pltpu.CompilerParams(vmem_limit_bytes=8 * MIB),
+        cost_estimate=SHORT,
+        name="spread",
+    )(attended, wo, wo2)
 
 
 def combine_kernel(held_ref, got_ref, out_ref):
@@ -841,11 +859,19 @@
     )
     swapped = (other_output, other_inner, other_outer)
     matrices = (output_weight, mixer_down.T, mixer_up, inner_weight, outer_weight, dense_down.T, dense_up)
-    result, first_grad, own_grad, away_grad, mine, theirs = middle(
+    got, *late = tie(got, query_weight, key_weight, value_weight)
+    late = [swap_cores(weight) for weight in late]
+    result, first_grad, attended, mine, theirs = middle(
         tokens, keep, got, output_grad, vectors, swapped, matrices
     )
+    theirs, *late = tie(theirs, *late)
+    weights = (query_weight, key_weight, value_weight, *late)
+    arriving = swap_cores(theirs)
+    own_grad, away_grad = spread(attended, output_weight, other_output)
+    arriving, own_grad = tie(arriving, own_grad)
+    packed = combine(mine, arriving)
+    away_grad, packed = tie(away_grad, packed)
     got_grad = swap_cores(away_grad)
-    packed = combine(mine, swap_cores(theirs))
 
     steps = []
     while 2 ** len(steps) < devices:
@@ -853,24 +879,35 @@
     steps.reverse()
     turn = len(steps) // 2
     pairs = len(shares)
-    grads = []
-    weights = (query_weight, key_weight, value_weight)
-    for n, step in enumerate(steps):
-        other_step = steps[(n + turn) % len(steps)]
-        exchange = [(2 * i + c, 2 * (i ^ s) + c) for i in range(devices) for c, s in enumerate((step, other_step))]
-        arriving = lax.ppermute(packed, ("dp", "mp"), exchange)
+    home, away = [], []
+    input_grad = None
+    for n in range(max(len(steps), pairs + 1)):
+        arriving = None
+        if n < len(steps):
+            both = (steps[n], steps[(n + turn) % len(steps)])
+            exchange = [(2 * i + c, 2 * (i ^ s) + c) for i in range(devices) for c, s in enumerate(both)]
+            arriving = lax.ppermute(packed, ("dp", "mp"), exchange)
+        work = None
         if n < pairs:
             got_grad, packed = tie(got_grad, packed)
-            parts = pair_grad(n, rng, kv, queries, keep, send, own_grad, got_grad, inverse, shares[n])
-            arriving, *parts = tie(arriving, *parts)
-            grads.append(parts)
+            work = pair_grad(n, rng, kv, queries, keep, send, own_grad, got_grad, inverse, shares[n])
         elif n == pairs:
-            pieces = [grads[p][i] for i in range(3) for p in range(pairs)]
-            away = swap_cores(input_call(away_kernel, (), pieces, weights, "away"))
-            input_grad = input_call(home_kernel, (first_grad, away), pieces, weights, "home")
-            arriving, input_grad = tie(arriving, input_grad)
-        packed = combine(packed, arriving)
-    md, mdb, mu, mub, dd, ddb, du, dub, *rest = finish(packed, swap_cores(packed), adapt)
+            away[-1], packed = tie(away[-1], packed)
+            work = (input_gradient(first_grad, home + away, weights),)
+        if work is not None and arriving is not None:
+            early = away[-1:] if n < pairs else []
+            arriving, *work = tie(arriving, *work, *early)
+            if early:
+                away[-1] = work.pop()
+        if n < pairs:
+            home.append(work[0])
+            away.append(swap_cores(work[1]))
+        elif n == pairs:
+            input_grad = work[0]
+        if arriving is not None:
+            packed = combine(packed, arriving)
+    last = swap_cores(packed)
+    md, mdb, mu, mub, dd, ddb, du, dub, *rest = finish(packed, last, adapt)
     return (result, input_grad, md.T, mdb, mu, mub, dd.T, ddb, du, dub, *rest)
 
 

time: 73.8 us -> 75 us (1.016); the launches traced: 72.9 us -> 75.1 us
  Pallas kernels: 48.6 us -> 54.4 us
  waiting for transfers between devices: 9.08 us -> 5.04 us
    pallas_call x3, Pallas kernels: 12.8 us -> 16.5 us  [pair_grad(): pl.pallas_call(functools.partial(pair_grad_kernel, p), out_shape=(jax.Sha...]
    ppermute x4, waiting for transfers between devices: 4.73 us -> 1.85 us  [per_device(): arriving = lax.ppermute(packed, ('dp', 'mp'), exchange)]
    ppermute x9 -> x14, starting transfers between devices: 2.87 us -> 5.39 us  [swap_cores(): return lax.ppermute(value, 'mp', [(0, 1), (1, 0)])]
    ppermute x4, starting transfers between devices: 11.3 us -> 9.1 us  [per_device(): arriving = lax.ppermute(packed, ('dp', 'mp'), exchange)]
    pallas_call x1, Pallas kernels: 9.01 us -> 10.9 us  [attention(): pl.pallas_call(attention_kernel, out_shape=(like(kv), like(queries), jax....]
    ppermute x9 -> x14, waiting for transfers between devices: 4.36 us -> 3.19 us  [swap_cores(): return lax.ppermute(value, 'mp', [(0, 1), (1, 0)])]
  transfers between devices with their start and end apart: 13 -> 18, of which waited for: 6 -> 5; matrix products, arithmetic and copies ran while one was open for 0% -> 0% of each run, Pallas kernels for 38% -> 71%
where the time goes in v8:
time: 75 us; the launch traced here: 75.1 us
  Pallas kernels  54.4 us (73%)
  starting transfers between devices  14.5 us (19%)
  waiting for transfers between devices  5.04 us (7%)
  between operations  1.08 us (1%)
    pallas_call x1, Pallas kernels, middle(): pl.pallas_call(middle_kernel, out_shape=(jax.ShapeDtypeStruct((rows, feat...  18.4 us
    pallas_call x3, Pallas kernels, pair_grad(): pl.pallas_call(functools.partial(pair_grad_kernel, p), out_shape=(jax.Sha...  16.5 us
    pallas_call x1, Pallas kernels, attention(): pl.pallas_call(attention_kernel, out_shape=(like(kv), like(queries), jax....  10.9 us
    ppermute x4, starting transfers between devices, per_device(): arriving = lax.ppermute(packed, ('dp', 'mp'), exchange)  9.1 us
    ppermute x14, starting transfers between devices, swap_cores(): return lax.ppermute(value, 'mp', [(0, 1), (1, 0)])  5.39 us
    pallas_call x1, Pallas kernels, project(): pl.pallas_call(project_kernel, out_shape=(jax.ShapeDtypeStruct((count, 2...  3.51 us
    ppermute x14, waiting for transfers between devices, swap_cores(): return lax.ppermute(value, 'mp', [(0, 1), (1, 0)])  3.19 us
    pallas_call x1, Pallas kernels, input_gradient(): pl.pallas_call(functools.partial(input_kernel, len(pieces) // 2), out_sha...  2.83 us
  transfers between devices with their start and end apart: 18, of which 5 were waited for; matrix products, arithmetic and copies ran while one was open for 0% of the time, Pallas kernels for 71%

profile of v8, /device:TPU:0, one launch (start us, length us, event | category | flops | bytes accessed | tf_op | source)
XLA Modules:
  0.0 75.1 jit_solution(2945772049887791044)
XLA Ops:
  0.7 0.5 collective-permute-start
  1.2 3.5 %project.1 = (bf16[1024,768]{1,0:T(8,128)(2,1)S(1)}, bf16[3,2048,128]{2,1,0:T(8,128)(2,1)S(1)}, bf16[3,128,2048]{2,1,0:T(8,128)(2,1)S(1)}, bf16[480,1024]{1,0:T(...) custom-call(s32[1,1024]{1,0:T(1,128)} %seg_hbm.1, ...), custom_call_target="tpu_custom_call" | custom-call | flops 905969664 | bytes 5242880 | tf_op jit(solution)/shard_map/project/pallas_call | solution.py:166
  4.9 0.4 collective-permute-start.4
  5.5 10.9 %attention.1 = (bf16[1024,768]{1,0:T(8,128)(2,1)S(1)}, bf16[3,2048,128]{2,1,0:T(8,128)(2,1)S(1)}, bf16[512,384]{1,0:T(8,128)(2,1)S(1)}, bf16[512,384]{1,0:T(8,12...) custom-call(s32[2,4]{1,0:T(2,128)S(1)} %get-tuple-element.94.rng_ref, ...), custom_call_target="tpu_custom_call" | custom-call | flops 10000000000 | bytes 8388608 | tf_op jit(solution)/shard_map/attention/pallas_call | solution.py:282
  16.4 0.5 collective-permute-start.1
  16.9 1.3 %collective-permute-done.1.got_ref = bf16[512,384]{1,0:T(8,128)(2,1)S(1)} collective-permute-done((bf16[512,384]{1,0:T(8,128)(2,1)S(1)}, bf16[512,384]{1,0:T(8,128)(2,1)S(1)}, u32[]{:S(2)}, u32[]{:S(2)}) %collective-permute-start.1) | collective-permute-done | bytes 393248 | tf_op jit(solution)/shard_map/ppermute | solution.py:829
  18.3 0.4 collective-permute-start.5
  18.8 0.4 collective-permute-start.7
  19.3 18.4 %middle.1 = (bf16[512,768]{1,0:T(8,128)(2,1)}, f32[512,768]{1,0:T(8,128)S(1)}, bf16[512,768]{1,0:T(8,128)(2,1)S(1)}, bf16[144,768]{1,0:T(8,128)(2,1)S(1)}, bf16[144,768]{1,0:T(8,128)(2,1)S(1)}) custom-call(bf16[512,768]{1,0:T(8,128)(2,1)S(1)} %copy-done.5, bf16[512,384]{1,0:T(8,128)(2,1)S(1)} %get-tuple-element.103.keep_ref, ...), custom_call_target="tpu_custom_call" | custom-call | flops 20000000000 | bytes 16777216 | tf_op jit(solution)/shard_map/middle/pallas_call | solution.py:721
  37.9 1.0 %spread.1 = (bf16[512,384]{1,0:T(8,128)(2,1)S(1)}, bf16[512,384]{1,0:T(8,128)(2,1)S(1)}) custom-call(bf16[512,768]{1,0:T(8,128)(2,1)S(1)} %get-tuple-element.110.attended_ref, bf16[384,768]{1,0:T(8,128)(2,1)S(1)} %copy-done.4, bf16[384,768]{1,0:T(8,128)(2,1)S(1)} %collective-permute-done.2.wo2_ref), custom_call_target="tpu_custom_call" | custom-call | flops 10000 | bytes 1000 | tf_op jit(solution)/shard_map/spread/pallas_call | solution.py:756
  39.5 3.9 %collective-permute-start.10 = (bf16[144,768]{1,0:T(8,128)(2,1)S(1)}, bf16[144,768]{1,0:T(8,128)(2,1)S(1)}, u32[]{:S(2)}, u32[]{:S(2)}) collective-permute-start(bf16[144,768]{1,0:T(8,128)(2,1)S(1)} %combine.5.held_ref), channel_id=1, source_target_pairs={{0,16},{1,5},{2,18},{3,7},{4,20},{5,1},{6,22},{7,3},{8,24},{9,13},... | collective-permute-start | bytes 663560 | tf_op jit(solution)/shard_map/ppermute | solution.py:889
  43.4 5.5 %pair_grad_0.1 = (bf16[512,384]{1,0:T(8,128)(2,1)S(1)}, bf16[512,384]{1,0:T(8,128)(2,1)S(1)}) custom-call(s32[2,4]{1,0:T(2,128)S(1)} %get-tuple-element.94.rng_ref, bf16[1024,768]{1,0:T(8,128)(2,1)S(1)} %get-tuple-element.124.kv_ref, bf16[3,2048,128]{2,1,0:T(8,128)(2,1)S(1)} %get-tuple-element.125.queries_ref, ...), custom_call_target="tpu_custom_call" | custom-call | flops 4000000000 | bytes 8388608 | tf_op jit(solution)/shard_map/pair_grad_0/pallas_call | solution.py:369
  48.9 0.8 %collective-permute-done.10.got_ref = bf16[144,768]{1,0:T(8,128)(2,1)S(1)} collective-permute-done((bf16[144,768]{1,0:T(8,128)(2,1)S(1)}, bf16[144,768]{1,0:T(8,128)(2,1)S(1)}, u32[]{:S(2)}, u32[]{:S(2)}) %collective-permute-start.10) | collective-permute-done | bytes 221216 | tf_op jit(solution)/shard_map/ppermute | solution.py:889
  49.7 1.4 %collective-permute-start.11 = (bf16[144,768]{1,0:T(8,128)(2,1)S(1)}, bf16[144,768]{1,0:T(8,128)(2,1)S(1)}, u32[]{:S(2)}, u32[]{:S(2)}) collective-permute-start(bf16[144,768]{1,0:T(8,128)(2,1)S(1)} %combine.6.held_ref), channel_id=1, source_target_pairs={{0,8},{1,3},{2,10},{3,1},{4,12},{5,7},{6,14},{7,5},{8,0},{9,11},{1... | collective-permute-start | bytes 663560 | tf_op jit(solution)/shard_map/ppermute | solution.py:889
  51.2 5.5 %pair_grad_1.1 = (bf16[512,384]{1,0:T(8,128)(2,1)S(1)}, bf16[512,384]{1,0:T(8,128)(2,1)S(1)}) custom-call(s32[2,4]{1,0:T(2,128)S(1)} %get-tuple-element.94.rng_ref, bf16[1024,768]{1,0:T(8,128)(2,1)S(1)} %get-tuple-element.124.kv_ref, bf16[3,2048,128]{2,1,0:T(8,128)(2,1)S(1)} %get-tuple-element.125.queries_ref, ...), custom_call_target="tpu_custom_call" | custom-call | flops 4000000000 | bytes 8388608 | tf_op jit(solution)/shard_map/pair_grad_1/pallas_call | solution.py:369
  56.7 1.3 %collective-permute-start.14 = (bf16[512,384]{1,0:T(8,128)(2,1)S(1)}, bf16[512,384]{1,0:T(8,128)(2,1)S(1)}, u32[]{:S(2)}, u32[]{:S(2)}) collective-permute-start(bf16[512,384]{1,0:T(8,128)(2,1)S(1)} %get-tuple-element.144), channel_id=1, source_target_pairs={{0,1},{1,0},{2,3},{3,2},{4,5},{5,4},{6,7},{7,6},{8,9},{9,8},{10,11... | collective-permute-start | bytes 1179656 | tf_op jit(solution)/shard_map/ppermute | solution.py:829
  58.0 1.5 %collective-permute-start.13 = (bf16[144,768]{1,0:T(8,128)(2,1)S(1)}, bf16[144,768]{1,0:T(8,128)(2,1)S(1)}, u32[]{:S(2)}, u32[]{:S(2)}) collective-permute-start(bf16[144,768]{1,0:T(8,128)(2,1)S(1)} %combine.7.held_ref), channel_id=1, source_target_pairs={{0,4},{1,17},{2,6},{3,19},{4,0},{5,21},{6,2},{7,23},{8,12},{9,25},... | collective-permute-start | bytes 663560 | tf_op jit(solution)/shard_map/ppermute | solution.py:889
  59.6 5.5 %pair_grad_2.1 = (bf16[512,384]{1,0:T(8,128)(2,1)S(1)}, bf16[512,384]{1,0:T(8,128)(2,1)S(1)}) custom-call(s32[2,4]{1,0:T(2,128)S(1)} %get-tuple-element.94.rng_ref, bf16[1024,768]{1,0:T(8,128)(2,1)S(1)} %get-tuple-element.124.kv_ref, bf16[3,2048,128]{2,1,0:T(8,128)(2,1)S(1)} %get-tuple-element.125.queries_ref, ...), custom_call_target="tpu_custom_call" | custom-call | flops 4000000000 | bytes 8388608 | tf_op jit(solution)/shard_map/pair_grad_2/pallas_call | solution.py:369
  65.1 1.1 %collective-permute-start.16 = (bf16[512,384]{1,0:T(8,128)(2,1)S(1)}, bf16[512,384]{1,0:T(8,128)(2,1)S(1)}, u32[]{:S(2)}, u32[]{:S(2)}) collective-permute-start(bf16[512,384]{1,0:T(8,128)(2,1)S(1)} %get-tuple-element.152), channel_id=1, source_target_pairs={{0,1},{1,0},{2,3},{3,2},{4,5},{5,4},{6,7},{7,6},{8,9},{9,8},{10,11... | collective-permute-start | bytes 1179656 | tf_op jit(solution)/shard_map/ppermute | solution.py:829
  66.2 2.2 %collective-permute-start.15 = (bf16[144,768]{1,0:T(8,128)(2,1)S(1)}, bf16[144,768]{1,0:T(8,128)(2,1)S(1)}, u32[]{:S(2)}, u32[]{:S(2)}) collective-permute-start(bf16[144,768]{1,0:T(8,128)(2,1)S(1)} %combine.8.held_ref), channel_id=1, source_target_pairs={{0,2},{1,9},{2,0},{3,11},{4,6},{5,13},{6,4},{7,15},{8,10},{9,1},{1... | collective-permute-start | bytes 663560 | tf_op jit(solution)/shard_map/ppermute | solution.py:889
  68.5 2.8 %input_gradient.1 = bf16[512,768]{1,0:T(8,128)(2,1)} custom-call(f32[512,768]{1,0:T(8,128)S(1)} %get-tuple-element.146.first_ref, bf16[512,384]{1,0:T(8,128)(2,1)S(1)} %get-tuple-element.147.refs_0_, bf16[512,384]{1,0:T(8,128)(2,1)S(1)} %get-tuple-element.148.refs_1_, bf16[512,384]{1,0:T(8,128)(2,1)S(1)} %get-tuple-element.149.refs_2_, ...), custom_call_target="tpu_custom_call" | custom-call | flops 2000000000 | bytes 8388608 | tf_op jit(solution)/shard_map/input_gradient/pallas_call | solution.py:409
  71.3 1.1 %collective-permute-done.15.got_ref = bf16[144,768]{1,0:T(8,128)(2,1)S(1)} collective-permute-done((bf16[144,768]{1,0:T(8,128)(2,1)S(1)}, bf16[144,768]{1,0:T(8,128)(2,1)S(1)}, u32[]{:S(2)}, u32[]{:S(2)}) %collective-permute-start.15) | collective-permute-done | bytes 221216 | tf_op jit(solution)/shard_map/ppermute | solution.py:889
  72.5 1.5 %collective-permute-done.17.got_ref = bf16[144,768]{1,0:T(8,128)(2,1)S(1)} collective-permute-done((bf16[144,768]{1,0:T(8,128)(2,1)S(1)}, bf16[144,768]{1,0:T(8,128)(2,1)S(1)}, u32[]{:S(2)}, u32[]{:S(2)}) %collective-permute-start.17) | collective-permute-done | bytes 221216 | tf_op jit(solution)/shard_map/ppermute | solution.py:829
  74.0 1.0 %finish.1 = (f32[64,768]{1,0:T(8,128)}, f32[64]{0:T(128)}, f32[64,768]{1,0:T(8,128)}, f32[768]{0:T(1024)}, f32[64,768]{1,0:T(8,128)}, /*index=5*/f32[64]{0:T(128...) custom-call(bf16[144,768]{1,0:T(8,128)(2,1)S(1)} %combine.9.held_ref, ...), custom_call_target="tpu_custom_call" | custom-call | tf_op jit(solution)/shard_map/finish/pallas_call | solution.py:818
  (56 shorter events, 1.6 us)
Async XLA Ops:
  0.7 4.0 %collective-permute-start = (bf16[512,768]{1,0:T(8,128)(2,1)}, bf16[512,768]{1,0:T(8,128)(2,1)S(1)}, u32[]{:S(2)}, u32[]{:S(2)}) collective-permute-start(bf16[512,768]{1,0:T(8,128)(2,1)} %x_ref.3), channel_id=1, source_target_pairs={{0,1},{1,0},{2,3},{3,2},{4,5},{5,4},{6,7},{7,6},{8,9},{9,8},{10,11... | collective-permute-start | bytes 2359304 | tf_op jit(solution)/shard_map/ppermute | solution.py:829
  4.7 14.4 %collective-permute-start.3 = (bf16[768,1536]{1,0:T(8,128)(2,1)}, bf16[768,1536]{1,0:T(8,128)(2,1)S(1)}, u32[]{:S(2)}, u32[]{:S(2)}) collective-permute-start(bf16[768,1536]{1,0:T(8,128)(2,1)} %w1_hbm.1), channel_id=1, source_target_pairs={{0,1},{1,0},{2,3},{3,2},{4,5},{5,4},{6,7},{7,6},{8,9},{9,8},{10,11... | collective-permute-start | bytes 7077896 | tf_op jit(solution)/shard_map/ppermute | solution.py:829
  4.9 14.3 %collective-permute-start.4 = (bf16[1536,768]{1,0:T(8,128)(2,1)}, bf16[1536,768]{1,0:T(8,128)(2,1)S(1)}, u32[]{:S(2)}, u32[]{:S(2)}) collective-permute-start(bf16[1536,768]{1,0:T(8,128)(2,1)} %w2_hbm.1), channel_id=1, source_target_pairs={{0,1},{1,0},{2,3},{3,2},{4,5},{5,4},{6,7},{7,6},{8,9},{9,8},{10,11... | collective-permute-start | bytes 7077896 | tf_op jit(solution)/shard_map/ppermute | solution.py:829
  5.3 13.5 %collective-permute-start.2 = (bf16[384,768]{1,0:T(8,128)(2,1)S(1)}, bf16[384,768]{1,0:T(8,128)(2,1)S(1)}, u32[]{:S(2)}, u32[]{:S(2)}) collective-permute-start(bf16[384,768]{1,0:T(8,128)(2,1)S(1)} %copy-done.3), channel_id=1, source_target_pairs={{0,1},{1,0},{2,3},{3,2},{4,5},{5,4},{6,7},{7,6},{8,9},{9,8},{10,11... | collective-permute-start | bytes 1769480 | tf_op jit(solution)/shard_map/ppermute | solution.py:829
  5.4 13.8 %copy-start.5 = (bf16[512,768]{1,0:T(8,128)(2,1)S(1)}, bf16[512,768]{1,0:T(8,128)(2,1)}, u32[]{:S(2)}) copy-start(bf16[512,768]{1,0:T(8,128)(2,1)} %x_ref.3) | copy-start | bytes 2359300
  5.4 13.8 %copy-start.6 = (bf16[512,768]{1,0:T(8,128)(2,1)S(1)}, bf16[512,768]{1,0:T(8,128)(2,1)}, u32[]{:S(2)}) copy-start(bf16[512,768]{1,0:T(8,128)(2,1)} %up_ref.1) | copy-start | bytes 2359300
  5.4 13.8 %copy-start.7 = (bf16[768]{0:T(1024)(128)(2,1)S(1)}, bf16[768]{0:T(1024)(128)(2,1)}, u32[]{:S(2)}) copy-start(bf16[768]{0:T(1024)(128)(2,1)} %mub_ref.1) | copy-start | bytes 4612
  5.4 13.8 %copy-start.8 = (bf16[768]{0:T(1024)(128)(2,1)S(1)}, bf16[768]{0:T(1024)(128)(2,1)}, u32[]{:S(2)}) copy-start(bf16[768]{0:T(1024)(128)(2,1)} %dub_ref.1) | copy-start | bytes 4612
  5.4 13.8 %copy-start.9 = (bf16[768]{0:T(1024)(128)(2,1)S(1)}, bf16[768]{0:T(1024)(128)(2,1)}, u32[]{:S(2)}) copy-start(bf16[768]{0:T(1024)(128)(2,1)} %fg_ref.1) | copy-start | bytes 4612
  16.4 1.8 %collective-permute-start.1 = (bf16[512,384]{1,0:T(8,128)(2,1)S(1)}, bf16[512,384]{1,0:T(8,128)(2,1)S(1)}, u32[]{:S(2)}, u32[]{:S(2)}) collective-permute-start(bf16[512,384]{1,0:T(8,128)(2,1)S(1)} %get-tuple-element.104.send_ref), channel_id=1, source_target_pairs={{0,1},{1,0},{2,3},{3,2},{4,5},{5,4},{6,7},{7,6},{8,9},{9,8},{10,11... | collective-permute-start | bytes 1179656 | tf_op jit(solution)/shard_map/ppermute | solution.py:829
  18.3 19.4 %collective-permute-start.5 = (bf16[768,384]{1,0:T(8,128)(2,1)S(1)}, bf16[768,384]{1,0:T(8,128)(2,1)S(1)}, u32[]{:S(2)}, u32[]{:S(2)}) collective-permute-start(bf16[768,384]{1,0:T(8,128)(2,1)S(1)} %copy-done), channel_id=1, source_target_pairs={{0,1},{1,0},{2,3},{3,2},{4,5},{5,4},{6,7},{7,6},{8,9},{9,8},{10,11... | collective-permute-start | bytes 1769480 | tf_op jit(solution)/shard_map/ppermute | solution.py:829
  18.6 19.0 %collective-permute-start.6 = (bf16[768,384]{1,0:T(8,128)(2,1)S(1)}, bf16[768,384]{1,0:T(8,128)(2,1)S(1)}, u32[]{:S(2)}, u32[]{:S(2)}) collective-permute-start(bf16[768,384]{1,0:T(8,128)(2,1)S(1)} %copy-done.1), channel_id=1, source_target_pairs={{0,1},{1,0},{2,3},{3,2},{4,5},{5,4},{6,7},{7,6},{8,9},{9,8},{10,11... | collective-permute-start | bytes 1769480 | tf_op jit(solution)/shard_map/ppermute | solution.py:829
  18.8 18.9 %collective-permute-start.7 = (bf16[768,384]{1,0:T(8,128)(2,1)S(1)}, bf16[768,384]{1,0:T(8,128)(2,1)S(1)}, u32[]{:S(2)}, u32[]{:S(2)}) collective-permute-start(bf16[768,384]{1,0:T(8,128)(2,1)S(1)} %copy-done.2), channel_id=1, source_target_pairs={{0,1},{1,0},{2,3},{3,2},{4,5},{5,4},{6,7},{7,6},{8,9},{9,8},{10,11... | collective-permute-start | bytes 1769480 | tf_op jit(solution)/shard_map/ppermute | solution.py:829
  19.3 18.6 %copy-start.4 = (bf16[384,768]{1,0:T(8,128)(2,1)S(1)}, bf16[384,768]{1,0:T(8,128)(2,1)}, u32[]{:S(2)}) copy-start(bf16[384,768]{1,0:T(8,128)(2,1)} %wo_ref.1) | copy-start | bytes 1769476
  37.7 1.5 %collective-permute-start.8 = (bf16[144,768]{1,0:T(8,128)(2,1)S(1)}, bf16[144,768]{1,0:T(8,128)(2,1)S(1)}, u32[]{:S(2)}, u32[]{:S(2)}) collective-permute-start(bf16[144,768]{1,0:T(8,128)(2,1)S(1)} %get-tuple-element.117), channel_id=1, source_target_pairs={{0,1},{1,0},{2,3},{3,2},{4,5},{5,4},{6,7},{7,6},{8,9},{9,8},{10,11... | collective-permute-start | bytes 663560 | tf_op jit(solution)/shard_map/ppermute | solution.py:829
  39.3 4.1 %collective-permute-start.9 = (bf16[512,384]{1,0:T(8,128)(2,1)S(1)}, bf16[512,384]{1,0:T(8,128)(2,1)S(1)}, u32[]{:S(2)}, u32[]{:S(2)}) collective-permute-start(bf16[512,384]{1,0:T(8,128)(2,1)S(1)} %get-tuple-element.120), channel_id=1, source_target_pairs={{0,1},{1,0},{2,3},{3,2},{4,5},{5,4},{6,7},{7,6},{8,9},{9,8},{10,11... | collective-permute-start | bytes 1179656 | tf_op jit(solution)/shard_map/ppermute | solution.py:829
  39.5 10.2 %collective-permute-start.10 = (bf16[144,768]{1,0:T(8,128)(2,1)S(1)}, bf16[144,768]{1,0:T(8,128)(2,1)S(1)}, u32[]{:S(2)}, u32[]{:S(2)}) collective-permute-start(bf16[144,768]{1,0:T(8,128)(2,1)S(1)} %combine.5.held_ref), channel_id=1, source_target_pairs={{0,16},{1,5},{2,18},{3,7},{4,20},{5,1},{6,22},{7,3},{8,24},{9,13},... | collective-permute-start | bytes 663560 | tf_op jit(solution)/shard_map/ppermute | solution.py:889
  49.7 7.0 %collective-permute-start.12 = (bf16[512,384]{1,0:T(8,128)(2,1)S(1)}, bf16[512,384]{1,0:T(8,128)(2,1)S(1)}, u32[]{:S(2)}, u32[]{:S(2)}) collective-permute-start(bf16[512,384]{1,0:T(8,128)(2,1)S(1)} %get-tuple-element.137), channel_id=1, source_target_pairs={{0,1},{1,0},{2,3},{3,2},{4,5},{5,4},{6,7},{7,6},{8,9},{9,8},{10,11... | collective-permute-start | bytes 1179656 | tf_op jit(solution)/shard_map/ppermute | solution.py:829
  49.7 6.9 %collective-permute-start.11 = (bf16[144,768]{1,0:T(8,128)(2,1)S(1)}, bf16[144,768]{1,0:T(8,128)(2,1)S(1)}, u32[]{:S(2)}, u32[]{:S(2)}) collective-permute-start(bf16[144,768]{1,0:T(8,128)(2,1)S(1)} %combine.6.held_ref), channel_id=1, source_target_pairs={{0,8},{1,3},{2,10},{3,1},{4,12},{5,7},{6,14},{7,5},{8,0},{9,11},{1... | collective-permute-start | bytes 663560 | tf_op jit(solution)/shard_map/ppermute | solution.py:889
  56.7 8.4 %collective-permute-start.14 = (bf16[512,384]{1,0:T(8,128)(2,1)S(1)}, bf16[512,384]{1,0:T(8,128)(2,1)S(1)}, u32[]{:S(2)}, u32[]{:S(2)}) collective-permute-start(bf16[512,384]{1,0:T(8,128)(2,1)S(1)} %get-tuple-element.144), channel_id=1, source_target_pairs={{0,1},{1,0},{2,3},{3,2},{4,5},{5,4},{6,7},{7,6},{8,9},{9,8},{10,11... | collective-permute-start | bytes 1179656 | tf_op jit(solution)/shard_map/ppermute | solution.py:829
  58.0 7.0 %collective-permute-start.13 = (bf16[144,768]{1,0:T(8,128)(2,1)S(1)}, bf16[144,768]{1,0:T(8,128)(2,1)S(1)}, u32[]{:S(2)}, u32[]{:S(2)}) collective-permute-start(bf16[144,768]{1,0:T(8,128)(2,1)S(1)} %combine.7.held_ref), channel_id=1, source_target_pairs={{0,4},{1,17},{2,6},{3,19},{4,0},{5,21},{6,2},{7,23},{8,12},{9,25},... | collective-permute-start | bytes 663560 | tf_op jit(solution)/shard_map/ppermute | solution.py:889
  65.1 3.4 %collective-permute-start.16 = (bf16[512,384]{1,0:T(8,128)(2,1)S(1)}, bf16[512,384]{1,0:T(8,128)(2,1)S(1)}, u32[]{:S(2)}, u32[]{:S(2)}) collective-permute-start(bf16[512,384]{1,0:T(8,128)(2,1)S(1)} %get-tuple-element.152), channel_id=1, source_target_pairs={{0,1},{1,0},{2,3},{3,2},{4,5},{5,4},{6,7},{7,6},{8,9},{9,8},{10,11... | collective-permute-start | bytes 1179656 | tf_op jit(solution)/shard_map/ppermute | solution.py:829
  66.2 6.1 %collective-permute-start.15 = (bf16[144,768]{1,0:T(8,128)(2,1)S(1)}, bf16[144,768]{1,0:T(8,128)(2,1)S(1)}, u32[]{:S(2)}, u32[]{:S(2)}) collective-permute-start(bf16[144,768]{1,0:T(8,128)(2,1)S(1)} %combine.8.held_ref), channel_id=1, source_target_pairs={{0,2},{1,9},{2,0},{3,11},{4,6},{5,13},{6,4},{7,15},{8,10},{9,1},{1... | collective-permute-start | bytes 663560 | tf_op jit(solution)/shard_map/ppermute | solution.py:889
  72.4 1.5 %collective-permute-start.17 = (bf16[144,768]{1,0:T(8,128)(2,1)S(1)}, bf16[144,768]{1,0:T(8,128)(2,1)S(1)}, u32[]{:S(2)}, u32[]{:S(2)}) collective-permute-start(bf16[144,768]{1,0:T(8,128)(2,1)S(1)} %combine.9.held_ref), channel_id=1, source_target_pairs={{0,1},{1,0},{2,3},{3,2},{4,5},{5,4},{6,7},{7,6},{8,9},{9,8},{10,11... | collective-permute-start | bytes 663560 | tf_op jit(solution)/shard_map/ppermute | solution.py:829
  (9 other events, 87.6 us)

commit v9 on v7

--- a/solution.py
+++ b/solution.py
@@ -79,12 +79,14 @@
     return copies
 
 
-def write_projection(which, x, weights, copies, kv_ref, queries_ref, across_ref, turned_ref):
+def write_projection(which, x, weights, copies, kv_ref, queries_ref, across_ref, turned_ref, between=None):
     rows, width = x.shape[0], weights[0].shape[1]
     pairs = width // PAIR
     if copies:
         copies[0].wait()
     queries = (dot(x, weights[0][...]) * (HEAD_DIM**-0.5 * LOG2E)).astype(BF16)
+    if between is not None:
+        between()
     for p in range(pairs):
         pair = queries[:, p * PAIR : (p + 1) * PAIR]
         stack_heads(pair, queries_ref.at[p, aligned(which, 2 * rows), :], BLOCK)
@@ -129,27 +131,32 @@
     sources, buffers = (seg_hbm, x_ref, wq_ref, wk_ref, wv_ref), (seg_ref, x_buf, wq, wk, wv)
     seg_copy, *copies = start_all(sources, buffers, sems)
     count, block = kv_ref.shape[0], BLOCK
+
+    def items():
+        ids = seg_ref[...].astype(F32)
+        position = lax.broadcasted_iota(jnp.int32, ids.shape, 1)
+        for g in range(count // block):
+            first, last = (
+                jnp.sum(jnp.where(position == at, ids, 0.0), -1, keepdims=True) for at in (g * block, (g + 1) * block - 1)
+            )
+            rng_ref[0, g] = jnp.sum(jnp.where(ids < first, 1.0, 0.0)).astype(jnp.int32) // STEP
+            rng_ref[1, g] = (jnp.sum(jnp.where(ids <= last, 1.0, 0.0)).astype(jnp.int32) + STEP - 1) // STEP
+        lane = lax.broadcasted_iota(jnp.int32, (128, 128), 1)
+        for t in range(count // 128):
+            same = jnp.broadcast_to(ids[:, t * 128 : (t + 1) * 128], (128, 128)).T == lane.astype(F32)
+            item_ref[t * 128 : (t + 1) * 128, :] = jnp.where(same | is_shift(lane), 1.0, 0.0).astype(BF16)
+        row = lax.broadcasted_iota(jnp.int32, (128, block), 0)
+        for t in range(count // block):
+            same = row.astype(F32) == ids[:, t * block : (t + 1) * block]
+            hide = jnp.where(same | is_shift(row), 0.0, MASKED).astype(BF16)
+            for a in range(2):
+                hide_ref[:, (2 * t + a) * block : (2 * t + a + 1) * block] = hide
+
     seg_copy.wait()
-    ids = seg_ref[...].astype(F32)
-    position = lax.broadcasted_iota(jnp.int32, ids.shape, 1)
-    for g in range(count // block):
-        first, last = (
-            jnp.sum(jnp.where(position == at, ids, 0.0), -1, keepdims=True) for at in (g * block, (g + 1) * block - 1)
-        )
-        rng_ref[0, g] = jnp.sum(jnp.where(ids < first, 1.0, 0.0)).astype(jnp.int32) // STEP
-        rng_ref[1, g] = (jnp.sum(jnp.where(ids <= last, 1.0, 0.0)).astype(jnp.int32) + STEP - 1) // STEP
-    lane = lax.broadcasted_iota(jnp.int32, (128, 128), 1)
-    for t in range(count // 128):
-        same = jnp.broadcast_to(ids[:, t * 128 : (t + 1) * 128], (128, 128)).T == lane.astype(F32)
-        item_ref[t * 128 : (t + 1) * 128, :] = jnp.where(same | is_shift(lane), 1.0, 0.0).astype(BF16)
-    row = lax.broadcasted_iota(jnp.int32, (128, block), 0)
-    for t in range(count // block):
-        same = row.astype(F32) == ids[:, t * block : (t + 1) * block]
-        hide = jnp.where(same | is_shift(row), 0.0, MASKED).astype(BF16)
-        for a in range(2):
-            hide_ref[:, (2 * t + a) * block : (2 * t + a + 1) * block] = hide
     copies[0].wait()
-    write_projection(lax.axis_index("mp"), x_buf[...], (wq, wk, wv), copies[1:], kv_ref, queries_ref, across_ref, turned_ref)
+    write_projection(
+        lax.axis_index("mp"), x_buf[...], (wq, wk, wv), copies[1:], kv_ref, queries_ref, across_ref, turned_ref, items
+    )
 
 
 def project(seg, x, wq, wk, wv):
@@ -175,28 +182,17 @@
     )(*map(in_hbm, (seg, x, wq, wk, wv)))
 
 
-def attention_kernel(
-    rng_ref, x_ref, item_ref, hide_ref, wq_ref, wk_ref, wv_ref, kv_in, queries_in, across_in, turned_in,
-    kv_ref, queries_ref, keep_ref, send_ref, inverse_ref, *rest,
-):
-    half = x_ref.shape[0]
-    count, width = kv_ref.shape[0], wq_ref.shape[1]
-    pairs, block = width // PAIR, BLOCK
-    share_refs = rest[:pairs]
-    across, turned, mix, shifted, peaks = rest[pairs:]
-    here, there = lax.axis_index("mp"), 1 - lax.axis_index("mp")
-    turned[:, aligned(here, half)] = turned_in[:, aligned(here, half)]
-    across[:, :, aligned(here, 2 * half)] = across_in[:, :, aligned(here, 2 * half)]
-    kv_ref[aligned(here, half), :] = kv_in[aligned(here, half), :]
-    queries_ref[:, aligned(here, 2 * half), :] = queries_in[:, aligned(here, 2 * half), :]
-    write_projection(there, x_ref[...], (wq_ref, wk_ref, wv_ref), (), kv_ref, queries_ref, across, turned)
+def attend_queries(which, rng_ref, item_ref, hide_ref, kv_ref, across, turned, out_ref, inverse_ref, share_refs, mix, shifted, peaks):
+    pairs, block = len(share_refs), BLOCK
+    per_half = out_ref.shape[0] // block
 
     def scores(p, span, both, hide):
         keys = jnp.concatenate([kv_ref[span, p * PAIR : (p + 1) * PAIR], item_ref[span, :]], 1)
         return dot(keys, jnp.concatenate([across[p, :, both], hide], 0))
 
-    def query_block(g, carry):
-        rows, both = aligned(g, block), aligned(g, 2 * block)
+    def query_block(i, carry):
+        g = which * per_half + i
+        both, here = aligned(g, 2 * block), aligned(i, 2 * block)
         low, high = rng_ref[0, g], rng_ref[1, g]
 
         def mix_all(hide_of):
@@ -209,7 +205,7 @@
                     if p + 1 < pairs:
                         ahead = scores(p + 1, span, both, hide_of(p + 1))
                     e = jnp.exp2(s).astype(BF16)
-                    share_refs[p][span, both] = e
+                    share_refs[p][span, here] = e
                     for a in range(2):
                         head = slice((2 * p + a) * TURNED, (2 * p + a + 1) * TURNED)
                         mix[head, :] += dot(turned[head, span], e[:, a * block : (a + 1) * block])
@@ -242,6 +238,7 @@
                 shifted[p] = jnp.where(is_shift(row), -parts, hide).astype(BF16)
             mix_all(lambda p: shifted[p])
 
+        rows = aligned(i, block)
         outs = []
         for p in range(pairs):
             scales = []
@@ -251,53 +248,57 @@
                 outs.append((mix[base : base + HEAD_DIM, :] * scale).astype(BF16))
                 scales.append(scale)
             inverse_ref[rows, p * PAIR : (p + 1) * PAIR] = jnp.concatenate(scales, 0).T
-        result = jnp.concatenate(outs, 0).T
-        per_half = half // block
-
-        @pl.when(g // per_half == here)
-        def _():
-            keep_ref[aligned(g % per_half, block), :] = result
-
-        @pl.when(g // per_half != here)
-        def _():
-            send_ref[aligned(g % per_half, block), :] = result
-
+        out_ref[rows, :] = jnp.concatenate(outs, 0).T
         return carry
 
-    lax.fori_loop(0, count // block, query_block, 0)
-
-
-def attention(rng, x, item, hide, wq, wk, wv, kv, queries, across, turned):
-    half, width = x.shape[0], wq.shape[1]
-    count, pairs = 2 * half, width // PAIR
-    like = lambda v: jax.ShapeDtypeStruct(v.shape, v.dtype)
+    lax.fori_loop(0, per_half, query_block, 0)
+
+
+def attention_kernel(
+    rng_ref, x_ref, item_ref, hide_ref, wq_ref, wk_ref, wv_ref, kv_in, queries_in, across_in, turned_in,
+    kv_ref, queries_ref, across, turned, out_ref, inverse_ref, *rest,
+):
+    half = x_ref.shape[0]
+    *share_refs, mix, shifted, peaks = rest
+    here, there = lax.axis_index("mp"), 1 - lax.axis_index("mp")
+    turned[:, aligned(here, half)] = turned_in[:, aligned(here, half)]
+    across[:, :, aligned(here, 2 * half)] = across_in[:, :, aligned(here, 2 * half)]
+    kv_ref[aligned(here, half), :] = kv_in[aligned(here, half), :]
+    queries_ref[:, aligned(here, 2 * half), :] = queries_in[:, aligned(here, 2 * half), :]
+    write_projection(there, x_ref[...], (wq_ref, wk_ref, wv_ref), (), kv_ref, queries_ref, across, turned)
+    attend_queries(there, rng_ref, item_ref, hide_ref, kv_ref, across, turned, out_ref, inverse_ref, share_refs, mix, shifted, peaks)
+
+
+def own_attention_kernel(rng_ref, item_ref, hide_ref, kv_ref, across, turned, out_ref, inverse_ref, *rest):
+    *share_refs, mix, shifted, peaks = rest
+    here = lax.axis_index("mp")
+    attend_queries(here, rng_ref, item_ref, hide_ref, kv_ref, across, turned, out_ref, inverse_ref, share_refs, mix, shifted, peaks)
+
+
+def attention_call(kernel, name, kept, half, operands):
+    kv = operands[7] if kept else operands[3]
+    count, width = kv.shape[0], kv.shape[1] // 2
+    pairs = width // PAIR
     return pl.pallas_call(
-        attention_kernel,
-        out_shape=(
-            like(kv),
-            like(queries),
-            jax.ShapeDtypeStruct((half, width), BF16),
-            jax.ShapeDtypeStruct((half, width), BF16),
-            jax.ShapeDtypeStruct((count, width), F32),
-        )
-        + (jax.ShapeDtypeStruct((count, 2 * count), BF16),) * pairs,
-        in_specs=[SM] + [VM] * 10,
-        out_specs=(VM,) * (5 + pairs),
+        kernel,
+        out_shape=tuple(jax.ShapeDtypeStruct(v.shape, v.dtype) for v in kept)
+        + (jax.ShapeDtypeStruct((half, width), BF16), jax.ShapeDtypeStruct((half, width), F32))
+        + (jax.ShapeDtypeStruct((count, 2 * half), BF16),) * pairs,
+        in_specs=[SM] + [VM] * (len(operands) - 1),
+        out_specs=(VM,) * (len(kept) + 2 + pairs),
         scratch_shapes=[
-            pltpu.VMEM(across.shape, BF16),
-            pltpu.VMEM(turned.shape, BF16),
             pltpu.VMEM((2 * pairs * TURNED, BLOCK), F32),
             pltpu.VMEM((pairs, 128, 2 * BLOCK), BF16),
             pltpu.VMEM((pairs, 1, 2 * BLOCK), F32),
         ],
-        compiler_params=pltpu.CompilerParams(vmem_limit_bytes=12 * MIB),
-        cost_estimate=pl.CostEstimate(flops=10**10, bytes_accessed=8 * MIB, transcendentals=10**6),
-        name="attention",
-    )(rng, x, item, hide, wq, wk, wv, kv, queries, across, turned)
+        compiler_params=pltpu.CompilerParams(vmem_limit_bytes=10 * MIB),
+        cost_estimate=pl.CostEstimate(flops=5 * 10**9, bytes_accessed=8 * MIB, transcendentals=10**6),
+        name=name,
+    )(*operands)
 
 
 def pair_grad_kernel(
-    p, rng_ref, kv_ref, queries_ref, keep_ref, send_ref, own_ref, other_ref, inverse_ref, share_ref,
+    p, rng_ref, kv_ref, queries_ref, keep_ref, send_ref, own_ref, other_ref, inverse_ref, inverse2_ref, share_ref, share2_ref,
     dq_ref, dk_ref, dv_ref,
     grads, across, turned, delta, dq, dk, dv,
 ):
@@ -308,8 +309,9 @@
     row = lax.broadcasted_iota(jnp.int32, (8, PAIR), 0)
     column = lax.broadcasted_iota(jnp.int32, (8, PAIR), 1)
     pick = jnp.where(column // HEAD_DIM == row, 1.0, 0.0).astype(BF16)
-    for which, mixed_ref, up_ref in ((here, keep_ref, own_ref), (there, send_ref, other_ref)):
-        scaled = (up_ref[:, cols].astype(F32) * inverse_ref[aligned(which, half), cols]).astype(BF16)
+    sides = ((here, keep_ref, own_ref, inverse_ref), (there, send_ref, other_ref, inverse2_ref))
+    for which, mixed_ref, up_ref, scale_ref in sides:
+        scaled = (up_ref[:, cols].astype(F32) * scale_ref[:, cols]).astype(BF16)
         product = mixed_ref[:, cols].astype(F32) * scaled.astype(F32)
         high = product.astype(BF16)
         low = (product - high.astype(F32)).astype(BF16)
@@ -320,14 +322,15 @@
     dk[...] = jnp.zeros(dk.shape, F32)
     dv[...] = jnp.zeros(dv.shape, F32)
 
-    def query_block(g, carry):
+    def query_block(which, shares_ref, i, carry):
+        g = which * (half // block) + i
         rows, both = aligned(g, block), aligned(g, 2 * block)
         dq[...] = jnp.zeros(dq.shape, F32)
         level = jnp.concatenate([delta[0:1, rows], delta[1:2, rows]], 1)
 
         def visit(span, size):
             d = dot(kv_ref[span, width + p * PAIR : width + (p + 1) * PAIR], across[:, both])
-            shares = share_ref[span, both]
+            shares = shares_ref[span, aligned(i, 2 * block)]
             slopes = (shares.astype(F32) * (d - level)).astype(BF16)
             dv[span, :] += dot(shares, grads[both, :])
             dk[span, :] += dot(slopes, queries_ref[p, both, :])
@@ -339,17 +342,18 @@
         dq_ref[rows, :] = (dq[...] * HEAD_DIM**-0.5).astype(BF16).T
         return carry
 
-    lax.fori_loop(0, count // block, query_block, 0)
+    for which, shares_ref in ((here, share_ref), (there, share2_ref)):
+        lax.fori_loop(0, half // block, functools.partial(query_block, which, shares_ref), 0)
     dk_ref[...] = (dk[...] * LN2).astype(BF16)
     dv_ref[...] = dv[...].astype(BF16)
 
 
-def pair_grad(p, rng, kv, queries, keep, send, own, other, inverse, shares):
+def pair_grad(p, rng, kv, queries, keep, send, own, other, *per_half):
     count = kv.shape[0]
     return pl.pallas_call(
         functools.partial(pair_grad_kernel, p),
         out_shape=(jax.ShapeDtypeStruct((count, PAIR), BF16),) * 3,
-        in_specs=[SM] + [VM] * 8,
+        in_specs=[SM] + [VM] * 10,
         out_specs=(VM,) * 3,
         scratch_shapes=[
             pltpu.VMEM((2 * count, PAIR), BF16),
@@ -363,7 +367,7 @@
         compiler_params=pltpu.CompilerParams(vmem_limit_bytes=12 * MIB),
         cost_estimate=pl.CostEstimate(flops=4 * 10**9, bytes_accessed=8 * MIB, transcendentals=0),
         name=f"pair_grad_{p}",
-    )(rng, kv, queries, keep, send, own, other, inverse, shares)
+    )(rng, kv, queries, keep, send, own, other, *per_half)
 
 
 def input_part(flip, pieces, weights, half):
@@ -454,7 +458,7 @@
     x_ref, keep_ref, got_ref, up_ref,
     mdb_ref, mub_ref, ddb_ref, dub_ref, fg_ref, fs_ref, sg_ref, ss_ref,
     wo2_ref, w12_ref, w22_ref, wo_hbm, md_hbm, mu_hbm, w1_hbm, w2_hbm, dd_hbm, du_hbm,
-    act_hbm, first_ref, own_ref, away_ref, mine_ref, theirs_ref,
+    act_hbm, first_ref, attended_ref, mine_ref, theirs_ref,
     wo_ref, md_ref, mu_ref, w1_ref, w2_ref, dd_ref, du_ref,
     slope_ref, wide_ref, out_ref, hidden_ref, normed_ref, low_ref, hidden_low_ref, act_ref, top_ref,
     big_ref, small_ref, sems, act_sem,
@@ -654,15 +658,9 @@
         def second():
             mid = kept["mixer_mid", half.start]
             add("mixer_down", dot_tn(mid, low_ref[half, :]))
-            kept["attended", half.start] = (first_ref[half, :] + dot(mid, md_ref[...])).astype(BF16)
-
-        def third():
-            own_ref[half, :] = dot_nt(kept["attended", half.start], wo_ref[...]).astype(BF16)
-
-        def fourth():
-            away_ref[half, :] = dot_nt(kept["attended", half.start], wo2_ref[...]).astype(BF16)
-
-        return [first, second, third, fourth]
+            attended_ref[half, :] = (first_ref[half, :] + dot(mid, md_ref[...])).astype(BF16)
+
+        return [first, second]
 
     def send_result(half, index):
         copy = pltpu.make_async_copy(act_ref.at[half, :], act_hbm.at[half, :], act_sem.at[index])
@@ -714,7 +712,6 @@
 
 def middle(x, keep, got, up, vectors, swapped, matrices):
     rows, features = x.shape
-    width = keep.shape[1]
     adapt = matrices[1].shape[0]
     units = matrices[3].shape[1]
     packed = jax.ShapeDtypeStruct((2 * adapt + 16, features), BF16)
@@ -723,13 +720,12 @@
         out_shape=(
             jax.ShapeDtypeStruct((rows, features), BF16),
             jax.ShapeDtypeStruct((rows, features), F32),
-            jax.ShapeDtypeStruct((rows, width), BF16),
-            jax.ShapeDtypeStruct((rows, width), BF16),
+            jax.ShapeDtypeStruct((rows, features), BF16),
             packed,
             packed,
         ),
         in_specs=[VM] * 15 + [HB] * 7,
-        out_specs=(HB,) + (VM,) * 5,
+        out_specs=(HB,) + (VM,) * 4,
         scratch_shapes=[pltpu.VMEM(m.shape, BF16) for m in matrices]
         + [pltpu.VMEM((rows, 2 * units), BF16)]
         + [pltpu.VMEM((rows, features), F32)] * 4
@@ -740,10 +736,29 @@
             pltpu.SemaphoreType.DMA((7,)),
             pltpu.SemaphoreType.DMA((2,)),
         ],
-        compiler_params=pltpu.CompilerParams(vmem_limit_bytes=28 * MIB),
+        compiler_params=pltpu.CompilerParams(vmem_limit_bytes=25 * MIB),
         cost_estimate=pl.CostEstimate(flops=2 * 10**10, bytes_accessed=16 * MIB, transcendentals=10**6),
         name="middle",
     )(x, keep, got, up, *vectors, *swapped, *map(in_hbm, matrices))
+
+
+def spread_kernel(attended_ref, wo_ref, wo2_ref, own_ref, away_ref):
+    attended = attended_ref[...]
+    away_ref[...] = dot_nt(attended, wo2_ref[...]).astype(BF16)
+    own_ref[...] = dot_nt(attended, wo_ref[...]).astype(BF16)
+
+
+def spread(attended, wo, wo2):
+    rows, width = attended.shape[0], wo.shape[0]
+    return pl.pallas_call(
+        spread_kernel,
+        out_shape=(jax.ShapeDtypeStruct((rows, width), BF16),) * 2,
+        in_specs=[VM] * 3,
+        out_specs=(VM,) * 2,
+        compiler_params=pltpu.CompilerParams(vmem_limit_bytes=8 * MIB),
+        cost_estimate=pl.CostEstimate(flops=4 * rows * attended.shape[1] * width, bytes_accessed=3 * MIB, transcendentals=0),
+        name="spread",
+    )(attended, wo, wo2)
 
 
 def combine_kernel(held_ref, got_ref, out_ref):
@@ -832,20 +847,31 @@
     other_output = swap_cores(output_late)
     other_inner = swap_cores(inner_late)
     other_outer = swap_cores(outer_late)
-    kv, queries, keep, send, inverse, *shares = attention(
-        rng, other_tokens, item, hide, query_weight, key_weight, value_weight, kv, queries, across, turned
+    half = tokens.shape[0]
+    written = (kv, queries, across, turned)
+    kv, queries, across, turned, send, inverse2, *shares2 = attention_call(
+        attention_kernel, "attention", written, half,
+        (rng, other_tokens, item, hide, query_weight, key_weight, value_weight, *written),
     )
     got = swap_cores(send)
+    keep, inverse, *shares = attention_call(
+        own_attention_kernel, "own_attention", (), half, (rng, item, hide, kv, across, turned)
+    )
+    got, keep = tie(got, keep)
     vectors = (
         mixer_down_bias, mixer_up_bias, dense_down_bias, dense_up_bias, first_gain, first_shift, second_gain, second_shift,
     )
     swapped = (other_output, other_inner, other_outer)
     matrices = (output_weight, mixer_down.T, mixer_up, inner_weight, outer_weight, dense_down.T, dense_up)
-    result, first_grad, own_grad, away_grad, mine, theirs = middle(
+    result, first_grad, attended, mine, theirs = middle(
         tokens, keep, got, output_grad, vectors, swapped, matrices
     )
+    arriving = swap_cores(theirs)
+    own_grad, away_grad = spread(attended, output_weight, other_output)
+    arriving, own_grad = tie(arriving, own_grad)
+    packed = combine(mine, arriving)
+    away_grad, packed = tie(away_grad, packed)
     got_grad = swap_cores(away_grad)
-    packed = combine(mine, swap_cores(theirs))
 
     steps = []
     while 2 ** len(steps) < devices:
@@ -861,7 +887,7 @@
         arriving = lax.ppermute(packed, ("dp", "mp"), exchange)
         if n < pairs:
             got_grad, packed = tie(got_grad, packed)
-            parts = pair_grad(n, rng, kv, queries, keep, send, own_grad, got_grad, inverse, shares[n])
+            parts = pair_grad(n, rng, kv, queries, keep, send, own_grad, got_grad, inverse, inverse2, shares[n], shares2[n])
             arriving, *parts = tie(arriving, *parts)
             grads.append(parts)
         elif n == pairs:

time: 73.8 us -> 72.4 us (0.981)
  Pallas kernels: 48.6 us -> 54.9 us
  waiting for transfers between devices: 9.08 us -> 4.51 us
  starting transfers between devices: 14.1 us -> 11.5 us
    pallas_call x3, Pallas kernels: 12.8 us -> 16.3 us  [pair_grad(): pl.pallas_call(functools.partial(pair_grad_kernel, p), out_shape=(jax.Sha...]
    pallas_call x1 -> x3, Pallas kernels: 9.01 us -> 12.4 us  [the longest x2 11.4 us: attention_call(): pl.pallas_call(kernel, out_shape=tuple((jax.ShapeDtypeStruct(v.shape, v.d...]
    ppermute x4, starting transfers between devices: 11.3 us -> 8.02 us  [per_device(): arriving = lax.ppermute(packed, ('dp', 'mp'), exchange)]
    ppermute x9, waiting for transfers between devices: 4.36 us -> 1.6 us  [swap_cores(): return lax.ppermute(value, 'mp', [(0, 1), (1, 0)])]
    ppermute x4, waiting for transfers between devices: 4.73 us -> 2.91 us  [per_device(): arriving = lax.ppermute(packed, ('dp', 'mp'), exchange)]
  transfers between devices with their start and end apart: 13 -> 13, of which waited for: 6 -> 4; matrix products, arithmetic and copies ran while one was open for 0% -> 0% of each run, Pallas kernels for 38% -> 48%
where the time goes in v9:
time: 72.4 us; the launch traced here: 72.1 us
  Pallas kernels  54.9 us (76%)
  starting transfers between devices  11.5 us (16%)
  waiting for transfers between devices  4.51 us (6%)
  between operations  1.1 us (2%)
    pallas_call x1, Pallas kernels, middle(): pl.pallas_call(middle_kernel, out_shape=(jax.ShapeDtypeStruct((rows, feat...  18.1 us
    pallas_call x3, Pallas kernels, pair_grad(): pl.pallas_call(functools.partial(pair_grad_kernel, p), out_shape=(jax.Sha...  16.3 us
    pallas_call x2, Pallas kernels, attention_call(): pl.pallas_call(kernel, out_shape=tuple((jax.ShapeDtypeStruct(v.shape, v.d...  11.4 us
    ppermute x4, starting transfers between devices, per_device(): arriving = lax.ppermute(packed, ('dp', 'mp'), exchange)  8.02 us
    ppermute x9, starting transfers between devices, swap_cores(): return lax.ppermute(value, 'mp', [(0, 1), (1, 0)])  3.51 us
    pallas_call x1, Pallas kernels, project(): pl.pallas_call(project_kernel, out_shape=(jax.ShapeDtypeStruct((count, 2...  3.51 us
    pallas_call x2, Pallas kernels, input_call(): pl.pallas_call(kernel, out_shape=jax.ShapeDtypeStruct((half, features), B...  3.25 us
    ppermute x4, waiting for transfers between devices, per_device(): arriving = lax.ppermute(packed, ('dp', 'mp'), exchange)  2.91 us
  transfers between devices with their start and end apart: 13, of which 4 were waited for; matrix products, arithmetic and copies ran while one was open for 0% of the time, Pallas kernels for 48%

profile of v9, /device:TPU:0, one launch (start us, length us, event | category | flops | bytes accessed | tf_op | source)
XLA Modules:
  0.0 72.1 jit_solution(1361462782820530966)
XLA Ops:
  0.7 0.5 collective-permute-start
  1.2 3.5 %project.1 = (bf16[1024,768]{1,0:T(8,128)(2,1)S(1)}, bf16[3,2048,128]{2,1,0:T(8,128)(2,1)S(1)}, bf16[3,128,2048]{2,1,0:T(8,128)(2,1)S(1)}, bf16[480,1024]{1,0:T(...) custom-call(s32[1,1024]{1,0:T(1,128)} %seg_hbm.1, ...), custom_call_target="tpu_custom_call" | custom-call | flops 905969664 | bytes 5242880 | tf_op jit(solution)/shard_map/project/pallas_call | solution.py:165
  4.7 0.1 collective-permute-start.3
  4.9 0.4 collective-permute-start.4
  5.4 6.7 %attention.1 = (bf16[1024,768]{1,0:T(8,128)(2,1)S(1)}, bf16[3,2048,128]{2,1,0:T(8,128)(2,1)S(1)}, bf16[3,128,2048]{2,1,0:T(8,128)(2,1)S(1)}, bf16[480,1024]{1,0:...) custom-call(s32[2,4]{1,0:T(2,128)S(1)} %get-tuple-element.96.rng_ref, ...), custom_call_target="tpu_custom_call" | custom-call | flops 5000000000 | bytes 8388608 | tf_op jit(solution)/shard_map/attention/pallas_call | solution.py:282
  12.3 4.7 %own_attention.1 = (bf16[512,384]{1,0:T(8,128)(2,1)S(1)}, f32[512,384]{1,0:T(8,128)S(1)}, bf16[1024,1024]{1,0:T(8,128)(2,1)S(1)}, bf16[1024,1024]{1,0:T(8,128)(2,1)S(1)}, bf16[1024,1024]{1,0:T(8,128)(2,1)S(1)}) custom-call(s32[2,4]{1,0:T(2,128)S(1)} %get-tuple-element.96.rng_ref, bf16[1024,128]{1,0:T(8,128)(2,1)S(1)} %get-tuple-element.99.item_ref, ...), custom_call_target="tpu_custom_call" | custom-call | flops 5000000000 | bytes 8388608 | tf_op jit(solution)/shard_map/own_attention/pallas_call | solution.py:282
  17.2 18.1 %middle.1 = (bf16[512,768]{1,0:T(8,128)(2,1)}, f32[512,768]{1,0:T(8,128)S(1)}, bf16[512,768]{1,0:T(8,128)(2,1)S(1)}, bf16[144,768]{1,0:T(8,128)(2,1)S(1)}, bf16[144,768]{1,0:T(8,128)(2,1)S(1)}) custom-call(bf16[512,768]{1,0:T(8,128)(2,1)S(1)} %copy-done.3, bf16[512,384]{1,0:T(8,128)(2,1)S(1)} %get-tuple-element.110.keep_ref, ...), custom_call_target="tpu_custom_call" | custom-call | flops 20000000000 | bytes 16777216 | tf_op jit(solution)/shard_map/middle/pallas_call | solution.py:718
  35.3 1.2 %collective-permute-start.5 = (bf16[144,768]{1,0:T(8,128)(2,1)S(1)}, bf16[144,768]{1,0:T(8,128)(2,1)S(1)}, u32[]{:S(2)}, u32[]{:S(2)}) collective-permute-start(bf16[144,768]{1,0:T(8,128)(2,1)S(1)} %get-tuple-element.119), channel_id=1, source_target_pairs={{0,1},{1,0},{2,3},{3,2},{4,5},{5,4},{6,7},{7,6},{8,9},{9,8},{10,11... | collective-permute-start | bytes 663560 | tf_op jit(solution)/shard_map/ppermute | solution.py:826
  36.5 1.0 %spread.1 = (bf16[512,384]{1,0:T(8,128)(2,1)S(1)}, bf16[512,384]{1,0:T(8,128)(2,1)S(1)}) custom-call(bf16[512,768]{1,0:T(8,128)(2,1)S(1)} %get-tuple-element.116.attended_ref, bf16[384,768]{1,0:T(8,128)(2,1)S(1)} %copy-done.6, bf16[384,768]{1,0:T(8,128)(2,1)S(1)} %collective-permute-done.2.wo2_ref), custom_call_target="tpu_custom_call" | custom-call | flops 603979776 | bytes 3145728 | tf_op jit(solution)/shard_map/spread/pallas_call | solution.py:753
  37.6 0.4 collective-permute-start.6
  38.1 3.9 %collective-permute-start.7 = (bf16[144,768]{1,0:T(8,128)(2,1)S(1)}, bf16[144,768]{1,0:T(8,128)(2,1)S(1)}, u32[]{:S(2)}, u32[]{:S(2)}) collective-permute-start(bf16[144,768]{1,0:T(8,128)(2,1)S(1)} %combine.5.held_ref), channel_id=1, source_target_pairs={{0,16},{1,5},{2,18},{3,7},{4,20},{5,1},{6,22},{7,3},{8,24},{9,13},... | collective-permute-start | bytes 663560 | tf_op jit(solution)/shard_map/ppermute | solution.py:887
  41.9 5.4 %pair_grad_0.1 = (bf16[1024,128]{1,0:T(8,128)(2,1)S(1)}, bf16[1024,128]{1,0:T(8,128)(2,1)S(1)}, bf16[1024,128]{1,0:T(8,128)(2,1)S(1)}) custom-call(s32[2,4]{1,0:T(2,128)S(1)} %get-tuple-element.96.rng_ref, bf16[1024,768]{1,0:T(8,128)(2,1)S(1)} %get-tuple-element.106.kv_ref, bf16[3,2048,128]{2,1,0:T(8,128)(2,1)S(1)} %get-tuple-element.126.queries_ref, ...), custom_call_target="tpu_custom_call" | custom-call | flops 4000000000 | bytes 8388608 | tf_op jit(solution)/shard_map/pair_grad_0/pallas_call | solution.py:353
  47.4 0.8 %collective-permute-done.7.got_ref = bf16[144,768]{1,0:T(8,128)(2,1)S(1)} collective-permute-done((bf16[144,768]{1,0:T(8,128)(2,1)S(1)}, bf16[144,768]{1,0:T(8,128)(2,1)S(1)}, u32[]{:S(2)}, u32[]{:S(2)}) %collective-permute-start.7) | collective-permute-done | bytes 221216 | tf_op jit(solution)/shard_map/ppermute | solution.py:887
  48.3 1.1 %collective-permute-start.8 = (bf16[144,768]{1,0:T(8,128)(2,1)S(1)}, bf16[144,768]{1,0:T(8,128)(2,1)S(1)}, u32[]{:S(2)}, u32[]{:S(2)}) collective-permute-start(bf16[144,768]{1,0:T(8,128)(2,1)S(1)} %combine.6.held_ref), channel_id=1, source_target_pairs={{0,8},{1,3},{2,10},{3,1},{4,12},{5,7},{6,14},{7,5},{8,0},{9,11},{1... | collective-permute-start | bytes 663560 | tf_op jit(solution)/shard_map/ppermute | solution.py:887
  49.4 5.4 %pair_grad_1.1 = (bf16[1024,128]{1,0:T(8,128)(2,1)S(1)}, bf16[1024,128]{1,0:T(8,128)(2,1)S(1)}, bf16[1024,128]{1,0:T(8,128)(2,1)S(1)}) custom-call(s32[2,4]{1,0:T(2,128)S(1)} %get-tuple-element.96.rng_ref, bf16[1024,768]{1,0:T(8,128)(2,1)S(1)} %get-tuple-element.106.kv_ref, bf16[3,2048,128]{2,1,0:T(8,128)(2,1)S(1)} %get-tuple-element.126.queries_ref, ...), custom_call_target="tpu_custom_call" | custom-call | flops 4000000000 | bytes 8388608 | tf_op jit(solution)/shard_map/pair_grad_1/pallas_call | solution.py:353
  54.9 1.2 %collective-permute-start.9 = (bf16[144,768]{1,0:T(8,128)(2,1)S(1)}, bf16[144,768]{1,0:T(8,128)(2,1)S(1)}, u32[]{:S(2)}, u32[]{:S(2)}) collective-permute-start(bf16[144,768]{1,0:T(8,128)(2,1)S(1)} %combine.7.held_ref), channel_id=1, source_target_pairs={{0,4},{1,17},{2,6},{3,19},{4,0},{5,21},{6,2},{7,23},{8,12},{9,25},... | collective-permute-start | bytes 663560 | tf_op jit(solution)/shard_map/ppermute | solution.py:887
  56.1 5.4 %pair_grad_2.1 = (bf16[1024,128]{1,0:T(8,128)(2,1)S(1)}, bf16[1024,128]{1,0:T(8,128)(2,1)S(1)}, bf16[1024,128]{1,0:T(8,128)(2,1)S(1)}) custom-call(s32[2,4]{1,0:T(2,128)S(1)} %get-tuple-element.96.rng_ref, bf16[1024,768]{1,0:T(8,128)(2,1)S(1)} %get-tuple-element.106.kv_ref, bf16[3,2048,128]{2,1,0:T(8,128)(2,1)S(1)} %get-tuple-element.126.queries_ref, ...), custom_call_target="tpu_custom_call" | custom-call | flops 4000000000 | bytes 8388608 | tf_op jit(solution)/shard_map/pair_grad_2/pallas_call | solution.py:353
  61.5 1.2 %away.1 = bf16[512,768]{1,0:T(8,128)(2,1)S(1)} custom-call(bf16[1024,128]{1,0:T(8,128)(2,1)S(1)} %get-tuple-element.153.refs_0_, bf16[1024,128]{1,0:T(8,128)(2,1)S(1)} %get-tuple-element.154.refs_1_, bf16[1024,128]{1,0:T(8,128)(2,1)S(1)} %get-tuple-element.155.refs_2_, bf16[1024,128]{1,0:T(8,128)(2,1)S(1)} %get-tuple-element.156.refs_3_, ...), custom_call_target="tpu_custom_call" | custom-call | flops 1000000000 | bytes 6291456 | tf_op jit(solution)/shard_map/away/pallas_call | solution.py:406
  62.8 0.6 collective-permute-start.11
  63.4 1.9 %collective-permute-start.10 = (bf16[144,768]{1,0:T(8,128)(2,1)S(1)}, bf16[144,768]{1,0:T(8,128)(2,1)S(1)}, u32[]{:S(2)}, u32[]{:S(2)}) collective-permute-start(bf16[144,768]{1,0:T(8,128)(2,1)S(1)} %combine.8.held_ref), channel_id=1, source_target_pairs={{0,2},{1,9},{2,0},{3,11},{4,6},{5,13},{6,4},{7,15},{8,10},{9,1},{1... | collective-permute-start | bytes 663560 | tf_op jit(solution)/shard_map/ppermute | solution.py:887
  65.3 2.0 %home.1 = bf16[512,768]{1,0:T(8,128)(2,1)} custom-call(f32[512,768]{1,0:T(8,128)S(1)} %get-tuple-element.152.first_ref, bf16[512,768]{1,0:T(8,128)(2,1)S(1)} %collective-permute-done.11.got_ref, bf16[1024,128]{1,0:T(8,128)(2,1)S(1)} %get-tuple-element.153.refs_0_, bf16[1024,128]{1,0:T(8,128)(2,1)S(1)} %get-tuple-element.154.refs_1_, ...), custom_call_target="tpu_custom_call" | custom-call | flops 1000000000 | bytes 6291456 | tf_op jit(solution)/shard_map/home/pallas_call | solution.py:406
  67.4 2.1 %collective-permute-done.10.got_ref = bf16[144,768]{1,0:T(8,128)(2,1)S(1)} collective-permute-done((bf16[144,768]{1,0:T(8,128)(2,1)S(1)}, bf16[144,768]{1,0:T(8,128)(2,1)S(1)}, u32[]{:S(2)}, u32[]{:S(2)}) %collective-permute-start.10) | collective-permute-done | bytes 221216 | tf_op jit(solution)/shard_map/ppermute | solution.py:887
  69.6 1.5 %collective-permute-done.12.got_ref = bf16[144,768]{1,0:T(8,128)(2,1)S(1)} collective-permute-done((bf16[144,768]{1,0:T(8,128)(2,1)S(1)}, bf16[144,768]{1,0:T(8,128)(2,1)S(1)}, u32[]{:S(2)}, u32[]{:S(2)}) %collective-permute-start.12) | collective-permute-done | bytes 221216 | tf_op jit(solution)/shard_map/ppermute | solution.py:826
  71.0 1.0 %finish.1 = (f32[64,768]{1,0:T(8,128)}, f32[64]{0:T(128)}, f32[64,768]{1,0:T(8,128)}, f32[768]{0:T(1024)}, f32[64,768]{1,0:T(8,128)}, /*index=5*/f32[64]{0:T(128...) custom-call(bf16[144,768]{1,0:T(8,128)(2,1)S(1)} %combine.9.held_ref, ...), custom_call_target="tpu_custom_call" | custom-call | tf_op jit(solution)/shard_map/finish/pallas_call | solution.py:815
  (48 shorter events, 0.8 us)
Async XLA Ops:
  0.7 4.0 %collective-permute-start = (bf16[512,768]{1,0:T(8,128)(2,1)}, bf16[512,768]{1,0:T(8,128)(2,1)S(1)}, u32[]{:S(2)}, u32[]{:S(2)}) collective-permute-start(bf16[512,768]{1,0:T(8,128)(2,1)} %x_ref.3), channel_id=1, source_target_pairs={{0,1},{1,0},{2,3},{3,2},{4,5},{5,4},{6,7},{7,6},{8,9},{9,8},{10,11... | collective-permute-start | bytes 2359304 | tf_op jit(solution)/shard_map/ppermute | solution.py:826
  4.7 12.3 %collective-permute-start.3 = (bf16[768,1536]{1,0:T(8,128)(2,1)}, bf16[768,1536]{1,0:T(8,128)(2,1)S(1)}, u32[]{:S(2)}, u32[]{:S(2)}) collective-permute-start(bf16[768,1536]{1,0:T(8,128)(2,1)} %w1_hbm.1), channel_id=1, source_target_pairs={{0,1},{1,0},{2,3},{3,2},{4,5},{5,4},{6,7},{7,6},{8,9},{9,8},{10,11... | collective-permute-start | bytes 7077896 | tf_op jit(solution)/shard_map/ppermute | solution.py:826
  4.9 12.2 %collective-permute-start.4 = (bf16[1536,768]{1,0:T(8,128)(2,1)}, bf16[1536,768]{1,0:T(8,128)(2,1)S(1)}, u32[]{:S(2)}, u32[]{:S(2)}) collective-permute-start(bf16[1536,768]{1,0:T(8,128)(2,1)} %w2_hbm.1), channel_id=1, source_target_pairs={{0,1},{1,0},{2,3},{3,2},{4,5},{5,4},{6,7},{7,6},{8,9},{9,8},{10,11... | collective-permute-start | bytes 7077896 | tf_op jit(solution)/shard_map/ppermute | solution.py:826
  5.3 11.7 %collective-permute-start.2 = (bf16[384,768]{1,0:T(8,128)(2,1)S(1)}, bf16[384,768]{1,0:T(8,128)(2,1)S(1)}, u32[]{:S(2)}, u32[]{:S(2)}) collective-permute-start(bf16[384,768]{1,0:T(8,128)(2,1)S(1)} %copy-done.5), channel_id=1, source_target_pairs={{0,1},{1,0},{2,3},{3,2},{4,5},{5,4},{6,7},{7,6},{8,9},{9,8},{10,11... | collective-permute-start | bytes 1769480 | tf_op jit(solution)/shard_map/ppermute | solution.py:826
  12.1 4.9 %collective-permute-start.1 = (bf16[512,384]{1,0:T(8,128)(2,1)S(1)}, bf16[512,384]{1,0:T(8,128)(2,1)S(1)}, u32[]{:S(2)}, u32[]{:S(2)}) collective-permute-start(bf16[512,384]{1,0:T(8,128)(2,1)S(1)} %get-tuple-element.105.send_ref), channel_id=1, source_target_pairs={{0,1},{1,0},{2,3},{3,2},{4,5},{5,4},{6,7},{7,6},{8,9},{9,8},{10,11... | collective-permute-start | bytes 1179656 | tf_op jit(solution)/shard_map/ppermute | solution.py:826
  12.2 4.8 %copy-start.3 = (bf16[512,768]{1,0:T(8,128)(2,1)S(1)}, bf16[512,768]{1,0:T(8,128)(2,1)}, u32[]{:S(2)}) copy-start(bf16[512,768]{1,0:T(8,128)(2,1)} %x_ref.3) | copy-start | bytes 2359300
  12.2 4.8 %copy-start.4 = (bf16[512,768]{1,0:T(8,128)(2,1)S(1)}, bf16[512,768]{1,0:T(8,128)(2,1)}, u32[]{:S(2)}) copy-start(bf16[512,768]{1,0:T(8,128)(2,1)} %up_ref.1) | copy-start | bytes 2359300
  12.2 4.8 %copy-start.7 = (bf16[768]{0:T(1024)(128)(2,1)S(1)}, bf16[768]{0:T(1024)(128)(2,1)}, u32[]{:S(2)}) copy-start(bf16[768]{0:T(1024)(128)(2,1)} %mub_ref.1) | copy-start | bytes 4612
  12.3 4.8 %copy-start.8 = (bf16[768]{0:T(1024)(128)(2,1)S(1)}, bf16[768]{0:T(1024)(128)(2,1)}, u32[]{:S(2)}) copy-start(bf16[768]{0:T(1024)(128)(2,1)} %dub_ref.1) | copy-start | bytes 4612
  12.3 4.8 %copy-start.9 = (bf16[768]{0:T(1024)(128)(2,1)S(1)}, bf16[768]{0:T(1024)(128)(2,1)}, u32[]{:S(2)}) copy-start(bf16[768]{0:T(1024)(128)(2,1)} %fg_ref.1) | copy-start | bytes 4612
  12.3 4.8 %copy-start.10 = (bf16[768]{0:T(1024)(128)(2,1)S(1)}, bf16[768]{0:T(1024)(128)(2,1)}, u32[]{:S(2)}) copy-start(bf16[768]{0:T(1024)(128)(2,1)} %fs_ref.1) | copy-start | bytes 4612
  12.3 4.8 %copy-start.11 = (bf16[768]{0:T(1024)(128)(2,1)S(1)}, bf16[768]{0:T(1024)(128)(2,1)}, u32[]{:S(2)}) copy-start(bf16[768]{0:T(1024)(128)(2,1)} %sg_ref.1) | copy-start | bytes 4612
  12.3 4.8 %copy-start.12 = (bf16[768]{0:T(1024)(128)(2,1)S(1)}, bf16[768]{0:T(1024)(128)(2,1)}, u32[]{:S(2)}) copy-start(bf16[768]{0:T(1024)(128)(2,1)} %ss_ref.1) | copy-start | bytes 4612
  12.3 4.8 %copy-start.13 = (bf16[64]{0:T(256)(128)(2,1)S(1)}, bf16[64]{0:T(256)(128)(2,1)}, u32[]{:S(2)}) copy-start(bf16[64]{0:T(256)(128)(2,1)} %mdb_ref.1) | copy-start | bytes 388
  12.3 4.8 %copy-start.14 = (bf16[64]{0:T(256)(128)(2,1)S(1)}, bf16[64]{0:T(256)(128)(2,1)}, u32[]{:S(2)}) copy-start(bf16[64]{0:T(256)(128)(2,1)} %ddb_ref.1) | copy-start | bytes 388
  17.2 19.3 %copy-start.6 = (bf16[384,768]{1,0:T(8,128)(2,1)S(1)}, bf16[384,768]{1,0:T(8,128)(2,1)}, u32[]{:S(2)}) copy-start(bf16[384,768]{1,0:T(8,128)(2,1)} %wo_ref.1) | copy-start | bytes 1769476
  35.3 2.3 %collective-permute-start.5 = (bf16[144,768]{1,0:T(8,128)(2,1)S(1)}, bf16[144,768]{1,0:T(8,128)(2,1)S(1)}, u32[]{:S(2)}, u32[]{:S(2)}) collective-permute-start(bf16[144,768]{1,0:T(8,128)(2,1)S(1)} %get-tuple-element.119), channel_id=1, source_target_pairs={{0,1},{1,0},{2,3},{3,2},{4,5},{5,4},{6,7},{7,6},{8,9},{9,8},{10,11... | collective-permute-start | bytes 663560 | tf_op jit(solution)/shard_map/ppermute | solution.py:826
  37.6 4.3 %collective-permute-start.6 = (bf16[512,384]{1,0:T(8,128)(2,1)S(1)}, bf16[512,384]{1,0:T(8,128)(2,1)S(1)}, u32[]{:S(2)}, u32[]{:S(2)}) collective-permute-start(bf16[512,384]{1,0:T(8,128)(2,1)S(1)} %get-tuple-element.122), channel_id=1, source_target_pairs={{0,1},{1,0},{2,3},{3,2},{4,5},{5,4},{6,7},{7,6},{8,9},{9,8},{10,11... | collective-permute-start | bytes 1179656 | tf_op jit(solution)/shard_map/ppermute | solution.py:826
  38.1 10.1 %collective-permute-start.7 = (bf16[144,768]{1,0:T(8,128)(2,1)S(1)}, bf16[144,768]{1,0:T(8,128)(2,1)S(1)}, u32[]{:S(2)}, u32[]{:S(2)}) collective-permute-start(bf16[144,768]{1,0:T(8,128)(2,1)S(1)} %combine.5.held_ref), channel_id=1, source_target_pairs={{0,16},{1,5},{2,18},{3,7},{4,20},{5,1},{6,22},{7,3},{8,24},{9,13},... | collective-permute-start | bytes 663560 | tf_op jit(solution)/shard_map/ppermute | solution.py:887
  48.3 6.5 %collective-permute-start.8 = (bf16[144,768]{1,0:T(8,128)(2,1)S(1)}, bf16[144,768]{1,0:T(8,128)(2,1)S(1)}, u32[]{:S(2)}, u32[]{:S(2)}) collective-permute-start(bf16[144,768]{1,0:T(8,128)(2,1)S(1)} %combine.6.held_ref), channel_id=1, source_target_pairs={{0,8},{1,3},{2,10},{3,1},{4,12},{5,7},{6,14},{7,5},{8,0},{9,11},{1... | collective-permute-start | bytes 663560 | tf_op jit(solution)/shard_map/ppermute | solution.py:887
  54.9 6.7 %collective-permute-start.9 = (bf16[144,768]{1,0:T(8,128)(2,1)S(1)}, bf16[144,768]{1,0:T(8,128)(2,1)S(1)}, u32[]{:S(2)}, u32[]{:S(2)}) collective-permute-start(bf16[144,768]{1,0:T(8,128)(2,1)S(1)} %combine.7.held_ref), channel_id=1, source_target_pairs={{0,4},{1,17},{2,6},{3,19},{4,0},{5,21},{6,2},{7,23},{8,12},{9,25},... | collective-permute-start | bytes 663560 | tf_op jit(solution)/shard_map/ppermute | solution.py:887
  62.8 2.6 %collective-permute-start.11 = (bf16[512,768]{1,0:T(8,128)(2,1)S(1)}, bf16[512,768]{1,0:T(8,128)(2,1)S(1)}, u32[]{:S(2)}, u32[]{:S(2)}) collective-permute-start(bf16[512,768]{1,0:T(8,128)(2,1)S(1)} %away.1), channel_id=1, source_target_pairs={{0,1},{1,0},{2,3},{3,2},{4,5},{5,4},{6,7},{7,6},{8,9},{9,8},{10,11... | collective-permute-start | bytes 2359304 | tf_op jit(solution)/shard_map/ppermute | solution.py:826
  63.4 6.0 %collective-permute-start.10 = (bf16[144,768]{1,0:T(8,128)(2,1)S(1)}, bf16[144,768]{1,0:T(8,128)(2,1)S(1)}, u32[]{:S(2)}, u32[]{:S(2)}) collective-permute-start(bf16[144,768]{1,0:T(8,128)(2,1)S(1)} %combine.8.held_ref), channel_id=1, source_target_pairs={{0,2},{1,9},{2,0},{3,11},{4,6},{5,13},{6,4},{7,15},{8,10},{9,1},{1... | collective-permute-start | bytes 663560 | tf_op jit(solution)/shard_map/ppermute | solution.py:887
  69.5 1.5 %collective-permute-start.12 = (bf16[144,768]{1,0:T(8,128)(2,1)S(1)}, bf16[144,768]{1,0:T(8,128)(2,1)S(1)}, u32[]{:S(2)}, u32[]{:S(2)}) collective-permute-start(bf16[144,768]{1,0:T(8,128)(2,1)S(1)} %combine.9.held_ref), channel_id=1, source_target_pairs={{0,1},{1,0},{2,3},{3,2},{4,5},{5,4},{6,7},{7,6},{8,9},{9,8},{10,11... | collective-permute-start | bytes 663560 | tf_op jit(solution)/shard_map/ppermute | solution.py:826
  (4 other events, 18.9 us)

commit v10 on v9

--- a/solution.py
+++ b/solution.py
@@ -108,15 +108,18 @@
 
 
 def over_keys(low, high, visit):
+    odd = (high - low) % 2
+
     def whole(t, c):
         visit(pl.ds(pl.multiple_of(low * STEP + t * BLOCK, STEP), BLOCK), BLOCK)
         return c
 
-    lax.fori_loop(0, (high - low) // 2, whole, 0)
-
-    @pl.when((high - low) % 2 == 1)
+    lax.fori_loop(0, (high - low) // 2 - odd, whole, 0)
+
+    @pl.when(odd == 1)
     def _():
-        visit(pl.ds(pl.multiple_of((high - 1) * STEP, STEP), STEP), STEP)
+        size = BLOCK + STEP
+        visit(pl.ds(pl.multiple_of(high * STEP - size, STEP), size), size)
 
 
 def is_shift(lane):
@@ -457,21 +460,21 @@
 def middle_kernel(
     x_ref, keep_ref, got_ref, up_ref,
     mdb_ref, mub_ref, ddb_ref, dub_ref, fg_ref, fs_ref, sg_ref, ss_ref,
-    wo2_ref, w12_ref, w22_ref, wo_hbm, md_hbm, mu_hbm, w1_hbm, w2_hbm, dd_hbm, du_hbm,
+    wo_ref, wo2_ref, w12_ref, w22_ref, md_hbm, mu_hbm, w1_hbm, w2_hbm, dd_hbm, du_hbm,
     act_hbm, first_ref, attended_ref, mine_ref, theirs_ref,
-    wo_ref, md_ref, mu_ref, w1_ref, w2_ref, dd_ref, du_ref,
+    md_ref, mu_ref, w1_ref, w2_ref, dd_ref, du_ref,
     slope_ref, wide_ref, out_ref, hidden_ref, normed_ref, low_ref, hidden_low_ref, act_ref, top_ref,
     big_ref, small_ref, sems, act_sem,
 ):
     rows, features = x_ref.shape
     adapt = md_ref.shape[0]
-    names = ("wo", "md", "mu", "w1", "w2", "dd", "du")
+    names = ("md", "mu", "w1", "w2", "dd", "du")
     waits = dict(
         zip(
             names,
             start_all(
-                (wo_hbm, md_hbm, mu_hbm, w1_hbm, w2_hbm, dd_hbm, du_hbm),
-                (wo_ref, md_ref, mu_ref, w1_ref, w2_ref, dd_ref, du_ref),
+                (md_hbm, mu_hbm, w1_hbm, w2_hbm, dd_hbm, du_hbm),
+                (md_ref, mu_ref, w1_ref, w2_ref, dd_ref, du_ref),
                 sems,
             ),
         )
@@ -502,7 +505,6 @@
 
     def attend(half):
         def first():
-            need("wo")
             attended = dot(keep_ref[half, :], wo_ref[...]) + dot(got_ref[half, :], wo2_ref[...])
             wide_ref[half, :] = attended
             low_ref[half, :] = attended.astype(BF16)
@@ -712,8 +714,8 @@
 
 def middle(x, keep, got, up, vectors, swapped, matrices):
     rows, features = x.shape
-    adapt = matrices[1].shape[0]
-    units = matrices[3].shape[1]
+    adapt = matrices[0].shape[0]
+    units = matrices[2].shape[1]
     packed = jax.ShapeDtypeStruct((2 * adapt + 16, features), BF16)
     return pl.pallas_call(
         middle_kernel,
@@ -724,7 +726,7 @@
             packed,
             packed,
         ),
-        in_specs=[VM] * 15 + [HB] * 7,
+        in_specs=[VM] * 16 + [HB] * 6,
         out_specs=(HB,) + (VM,) * 4,
         scratch_shapes=[pltpu.VMEM(m.shape, BF16) for m in matrices]
         + [pltpu.VMEM((rows, 2 * units), BF16)]
@@ -733,7 +735,7 @@
         + [
             pltpu.VMEM((4 * adapt, features), BF16),
             pltpu.VMEM((8, features), F32),
-            pltpu.SemaphoreType.DMA((7,)),
+            pltpu.SemaphoreType.DMA((6,)),
             pltpu.SemaphoreType.DMA((2,)),
         ],
         compiler_params=pltpu.CompilerParams(vmem_limit_bytes=25 * MIB),
@@ -861,8 +863,8 @@
     vectors = (
         mixer_down_bias, mixer_up_bias, dense_down_bias, dense_up_bias, first_gain, first_shift, second_gain, second_shift,
     )
-    swapped = (other_output, other_inner, other_outer)
-    matrices = (output_weight, mixer_down.T, mixer_up, inner_weight, outer_weight, dense_down.T, dense_up)
+    swapped = (output_weight, other_output, other_inner, other_outer)
+    matrices = (mixer_down.T, mixer_up, inner_weight, outer_weight, dense_down.T, dense_up)
     result, first_grad, attended, mine, theirs = middle(
         tokens, keep, got, output_grad, vectors, swapped, matrices
     )

time: 72.4 us -> 69.3 us (0.957)
  Pallas kernels: 54.9 us -> 50 us
  waiting for transfers between devices: 4.51 us -> 7.62 us
  starting transfers between devices: 11.5 us -> 10.6 us
    pallas_call x3, Pallas kernels: 16.3 us -> 13.8 us  [pair_grad(): pl.pallas_call(functools.partial(pair_grad_kernel, p), out_shape=(jax.Sha...]
    pallas_call x2, Pallas kernels: 11.4 us -> 9.77 us  [attention_call(): pl.pallas_call(kernel, out_shape=tuple((jax.ShapeDtypeStruct(v.shape, v.d...]
    ppermute x4, waiting for transfers between devices: 2.91 us -> 4.51 us  [per_device(): arriving = lax.ppermute(packed, ('dp', 'mp'), exchange)]
    ppermute x9, waiting for transfers between devices: 1.6 us -> 3.11 us  [swap_cores(): return lax.ppermute(value, 'mp', [(0, 1), (1, 0)])]
    ppermute x4, starting transfers between devices: 8.02 us -> 7.19 us  [per_device(): arriving = lax.ppermute(packed, ('dp', 'mp'), exchange)]
    pallas_call x1, Pallas kernels: 18.1 us -> 17.3 us  [middle(): pl.pallas_call(middle_kernel, out_shape=(jax.ShapeDtypeStruct((rows, feat...]
  transfers between devices with their start and end apart: 13 -> 13, of which waited for: 4 -> 6; matrix products, arithmetic and copies ran while one was open for 0% -> 0% of each run, Pallas kernels for 48% -> 44%
where the time goes in v10:
time: 69.3 us
  Pallas kernels  50 us (72%)
  starting transfers between devices  10.6 us (15%)
  waiting for transfers between devices  7.62 us (11%)
  between operations  1.06 us (2%)
    pallas_call x1, Pallas kernels, middle(): pl.pallas_call(middle_kernel, out_shape=(jax.ShapeDtypeStruct((rows, feat...  17.3 us
    pallas_call x3, Pallas kernels, pair_grad(): pl.pallas_call(functools.partial(pair_grad_kernel, p), out_shape=(jax.Sha...  13.8 us
    pallas_call x2, Pallas kernels, attention_call(): pl.pallas_call(kernel, out_shape=tuple((jax.ShapeDtypeStruct(v.shape, v.d...  9.77 us
    ppermute x4, starting transfers between devices, per_device(): arriving = lax.ppermute(packed, ('dp', 'mp'), exchange)  7.19 us
    ppermute x4, waiting for transfers between devices, per_device(): arriving = lax.ppermute(packed, ('dp', 'mp'), exchange)  4.51 us
    pallas_call x1, Pallas kernels, project(): pl.pallas_call(project_kernel, out_shape=(jax.ShapeDtypeStruct((count, 2...  3.51 us
    ppermute x9, starting transfers between devices, swap_cores(): return lax.ppermute(value, 'mp', [(0, 1), (1, 0)])  3.37 us
    pallas_call x2, Pallas kernels, input_call(): pl.pallas_call(kernel, out_shape=jax.ShapeDtypeStruct((half, features), B...  3.25 us
  transfers between devices with their start and end apart: 13, of which 6 were waited for; matrix products, arithmetic and copies ran while one was open for 0% of the time, Pallas kernels for 44%

profile of v10, /device:TPU:0, one launch (start us, length us, event | category | flops | bytes accessed | tf_op | source)
XLA Modules:
  0.0 69.3 jit_solution(13071967361019332644)
XLA Ops:
  0.7 0.5 collective-permute-start
  1.2 3.5 %project.1 = (bf16[1024,768]{1,0:T(8,128)(2,1)S(1)}, bf16[3,2048,128]{2,1,0:T(8,128)(2,1)S(1)}, bf16[3,128,2048]{2,1,0:T(8,128)(2,1)S(1)}, bf16[480,1024]{1,0:T(...) custom-call(s32[1,1024]{1,0:T(1,128)} %seg_hbm.1, ...), custom_call_target="tpu_custom_call" | custom-call | flops 905969664 | bytes 5242880 | tf_op jit(solution)/shard_map/project/pallas_call | solution.py:168
  4.9 0.4 collective-permute-start.4
  5.4 5.0 %attention.1 = (bf16[1024,768]{1,0:T(8,128)(2,1)S(1)}, bf16[3,2048,128]{2,1,0:T(8,128)(2,1)S(1)}, bf16[3,128,2048]{2,1,0:T(8,128)(2,1)S(1)}, bf16[480,1024]{1,0:...) custom-call(s32[2,4]{1,0:T(2,128)S(1)} %get-tuple-element.96.rng_ref, ...), custom_call_target="tpu_custom_call" | custom-call | flops 5000000000 | bytes 8388608 | tf_op jit(solution)/shard_map/attention/pallas_call | solution.py:285
  10.4 1.8 %collective-permute-start.1 = (bf16[512,384]{1,0:T(8,128)(2,1)S(1)}, bf16[512,384]{1,0:T(8,128)(2,1)S(1)}, u32[]{:S(2)}, u32[]{:S(2)}) collective-permute-start(bf16[512,384]{1,0:T(8,128)(2,1)S(1)} %get-tuple-element.105.send_ref), channel_id=1, source_target_pairs={{0,1},{1,0},{2,3},{3,2},{4,5},{5,4},{6,7},{7,6},{8,9},{9,8},{10,11... | collective-permute-start | bytes 1179656 | tf_op jit(solution)/shard_map/ppermute | solution.py:828
  12.2 4.8 %own_attention.1 = (bf16[512,384]{1,0:T(8,128)(2,1)S(1)}, f32[512,384]{1,0:T(8,128)S(1)}, bf16[1024,1024]{1,0:T(8,128)(2,1)S(1)}, bf16[1024,1024]{1,0:T(8,128)(2,1)S(1)}, bf16[1024,1024]{1,0:T(8,128)(2,1)S(1)}) custom-call(s32[2,4]{1,0:T(2,128)S(1)} %get-tuple-element.96.rng_ref, bf16[1024,128]{1,0:T(8,128)(2,1)S(1)} %get-tuple-element.99.item_ref, ...), custom_call_target="tpu_custom_call" | custom-call | flops 5000000000 | bytes 8388608 | tf_op jit(solution)/shard_map/own_attention/pallas_call | solution.py:285
  17.2 17.3 %middle.1 = (bf16[512,768]{1,0:T(8,128)(2,1)}, f32[512,768]{1,0:T(8,128)S(1)}, bf16[512,768]{1,0:T(8,128)(2,1)S(1)}, bf16[144,768]{1,0:T(8,128)(2,1)S(1)}, bf16[144,768]{1,0:T(8,128)(2,1)S(1)}) custom-call(bf16[512,768]{1,0:T(8,128)(2,1)S(1)} %copy-done.3, bf16[512,384]{1,0:T(8,128)(2,1)S(1)} %get-tuple-element.110.keep_ref, ...), custom_call_target="tpu_custom_call" | custom-call | flops 20000000000 | bytes 16777216 | tf_op jit(solution)/shard_map/middle/pallas_call | solution.py:720
  34.6 1.0 %spread.1 = (bf16[512,384]{1,0:T(8,128)(2,1)S(1)}, bf16[512,384]{1,0:T(8,128)(2,1)S(1)}) custom-call(bf16[512,768]{1,0:T(8,128)(2,1)S(1)} %get-tuple-element.116.attended_ref, bf16[384,768]{1,0:T(8,128)(2,1)S(1)} %copy-done.5, bf16[384,768]{1,0:T(8,128)(2,1)S(1)} %collective-permute-done.2.wo2_ref), custom_call_target="tpu_custom_call" | custom-call | flops 603979776 | bytes 3145728 | tf_op jit(solution)/shard_map/spread/pallas_call | solution.py:755
  35.6 0.5 collective-permute-done.5.got_ref
  36.3 2.5 %collective-permute-start.7 = (bf16[144,768]{1,0:T(8,128)(2,1)S(1)}, bf16[144,768]{1,0:T(8,128)(2,1)S(1)}, u32[]{:S(2)}, u32[]{:S(2)}) collective-permute-start(bf16[144,768]{1,0:T(8,128)(2,1)S(1)} %combine.5.held_ref), channel_id=1, source_target_pairs={{0,16},{1,5},{2,18},{3,7},{4,20},{5,1},{6,22},{7,3},{8,24},{9,13},... | collective-permute-start | bytes 663560 | tf_op jit(solution)/shard_map/ppermute | solution.py:889
  38.9 4.6 %pair_grad_0.1 = (bf16[1024,128]{1,0:T(8,128)(2,1)S(1)}, bf16[1024,128]{1,0:T(8,128)(2,1)S(1)}, bf16[1024,128]{1,0:T(8,128)(2,1)S(1)}) custom-call(s32[2,4]{1,0:T(2,128)S(1)} %get-tuple-element.96.rng_ref, bf16[1024,768]{1,0:T(8,128)(2,1)S(1)} %get-tuple-element.106.kv_ref, bf16[3,2048,128]{2,1,0:T(8,128)(2,1)S(1)} %get-tuple-element.126.queries_ref, ...), custom_call_target="tpu_custom_call" | custom-call | flops 4000000000 | bytes 8388608 | tf_op jit(solution)/shard_map/pair_grad_0/pallas_call | solution.py:356
  43.5 2.1 %collective-permute-done.7.got_ref = bf16[144,768]{1,0:T(8,128)(2,1)S(1)} collective-permute-done((bf16[144,768]{1,0:T(8,128)(2,1)S(1)}, bf16[144,768]{1,0:T(8,128)(2,1)S(1)}, u32[]{:S(2)}, u32[]{:S(2)}) %collective-permute-start.7) | collective-permute-done | bytes 221216 | tf_op jit(solution)/shard_map/ppermute | solution.py:889
  45.6 0.7 collective-permute-start.8
  46.3 4.6 %pair_grad_1.1 = (bf16[1024,128]{1,0:T(8,128)(2,1)S(1)}, bf16[1024,128]{1,0:T(8,128)(2,1)S(1)}, bf16[1024,128]{1,0:T(8,128)(2,1)S(1)}) custom-call(s32[2,4]{1,0:T(2,128)S(1)} %get-tuple-element.96.rng_ref, bf16[1024,768]{1,0:T(8,128)(2,1)S(1)} %get-tuple-element.106.kv_ref, bf16[3,2048,128]{2,1,0:T(8,128)(2,1)S(1)} %get-tuple-element.126.queries_ref, ...), custom_call_target="tpu_custom_call" | custom-call | flops 4000000000 | bytes 8388608 | tf_op jit(solution)/shard_map/pair_grad_1/pallas_call | solution.py:356
  50.9 0.7 %collective-permute-done.8.got_ref = bf16[144,768]{1,0:T(8,128)(2,1)S(1)} collective-permute-done((bf16[144,768]{1,0:T(8,128)(2,1)S(1)}, bf16[144,768]{1,0:T(8,128)(2,1)S(1)}, u32[]{:S(2)}, u32[]{:S(2)}) %collective-permute-start.8) | collective-permute-done | bytes 221216 | tf_op jit(solution)/shard_map/ppermute | solution.py:889
  51.7 2.9 %collective-permute-start.9 = (bf16[144,768]{1,0:T(8,128)(2,1)S(1)}, bf16[144,768]{1,0:T(8,128)(2,1)S(1)}, u32[]{:S(2)}, u32[]{:S(2)}) collective-permute-start(bf16[144,768]{1,0:T(8,128)(2,1)S(1)} %combine.7.held_ref), channel_id=1, source_target_pairs={{0,4},{1,17},{2,6},{3,19},{4,0},{5,21},{6,2},{7,23},{8,12},{9,25},... | collective-permute-start | bytes 663560 | tf_op jit(solution)/shard_map/ppermute | solution.py:889
  54.6 4.6 %pair_grad_2.1 = (bf16[1024,128]{1,0:T(8,128)(2,1)S(1)}, bf16[1024,128]{1,0:T(8,128)(2,1)S(1)}, bf16[1024,128]{1,0:T(8,128)(2,1)S(1)}) custom-call(s32[2,4]{1,0:T(2,128)S(1)} %get-tuple-element.96.rng_ref, bf16[1024,768]{1,0:T(8,128)(2,1)S(1)} %get-tuple-element.106.kv_ref, bf16[3,2048,128]{2,1,0:T(8,128)(2,1)S(1)} %get-tuple-element.126.queries_ref, ...), custom_call_target="tpu_custom_call" | custom-call | flops 4000000000 | bytes 8388608 | tf_op jit(solution)/shard_map/pair_grad_2/pallas_call | solution.py:356
  59.3 1.2 %away.1 = bf16[512,768]{1,0:T(8,128)(2,1)S(1)} custom-call(bf16[1024,128]{1,0:T(8,128)(2,1)S(1)} %get-tuple-element.153.refs_0_, bf16[1024,128]{1,0:T(8,128)(2,1)S(1)} %get-tuple-element.154.refs_1_, bf16[1024,128]{1,0:T(8,128)(2,1)S(1)} %get-tuple-element.155.refs_2_, bf16[1024,128]{1,0:T(8,128)(2,1)S(1)} %get-tuple-element.156.refs_3_, ...), custom_call_target="tpu_custom_call" | custom-call | flops 1000000000 | bytes 6291456 | tf_op jit(solution)/shard_map/away/pallas_call | solution.py:409
  60.6 1.0 %collective-permute-start.10 = (bf16[144,768]{1,0:T(8,128)(2,1)S(1)}, bf16[144,768]{1,0:T(8,128)(2,1)S(1)}, u32[]{:S(2)}, u32[]{:S(2)}) collective-permute-start(bf16[144,768]{1,0:T(8,128)(2,1)S(1)} %combine.8.held_ref), channel_id=1, source_target_pairs={{0,2},{1,9},{2,0},{3,11},{4,6},{5,13},{6,4},{7,15},{8,10},{9,1},{1... | collective-permute-start | bytes 663560 | tf_op jit(solution)/shard_map/ppermute | solution.py:889
  61.7 1.2 %collective-permute-done.11.got_ref = bf16[512,768]{1,0:T(8,128)(2,1)S(1)} collective-permute-done((bf16[512,768]{1,0:T(8,128)(2,1)S(1)}, bf16[512,768]{1,0:T(8,128)(2,1)S(1)}, u32[]{:S(2)}, u32[]{:S(2)}) %collective-permute-start.11) | collective-permute-done | bytes 786464 | tf_op jit(solution)/shard_map/ppermute | solution.py:828
  62.8 2.0 %home.1 = bf16[512,768]{1,0:T(8,128)(2,1)} custom-call(f32[512,768]{1,0:T(8,128)S(1)} %get-tuple-element.152.first_ref, bf16[512,768]{1,0:T(8,128)(2,1)S(1)} %collective-permute-done.11.got_ref, bf16[1024,128]{1,0:T(8,128)(2,1)S(1)} %get-tuple-element.153.refs_0_, bf16[1024,128]{1,0:T(8,128)(2,1)S(1)} %get-tuple-element.154.refs_1_, ...), custom_call_target="tpu_custom_call" | custom-call | flops 1000000000 | bytes 6291456 | tf_op jit(solution)/shard_map/home/pallas_call | solution.py:409
  64.9 1.8 %collective-permute-done.10.got_ref = bf16[144,768]{1,0:T(8,128)(2,1)S(1)} collective-permute-done((bf16[144,768]{1,0:T(8,128)(2,1)S(1)}, bf16[144,768]{1,0:T(8,128)(2,1)S(1)}, u32[]{:S(2)}, u32[]{:S(2)}) %collective-permute-start.10) | collective-permute-done | bytes 221216 | tf_op jit(solution)/shard_map/ppermute | solution.py:889
  66.8 1.5 %collective-permute-done.12.got_ref = bf16[144,768]{1,0:T(8,128)(2,1)S(1)} collective-permute-done((bf16[144,768]{1,0:T(8,128)(2,1)S(1)}, bf16[144,768]{1,0:T(8,128)(2,1)S(1)}, u32[]{:S(2)}, u32[]{:S(2)}) %collective-permute-start.12) | collective-permute-done | bytes 221216 | tf_op jit(solution)/shard_map/ppermute | solution.py:828
  68.2 1.0 %finish.1 = (f32[64,768]{1,0:T(8,128)}, f32[64]{0:T(128)}, f32[64,768]{1,0:T(8,128)}, f32[768]{0:T(1024)}, f32[64,768]{1,0:T(8,128)}, /*index=5*/f32[64]{0:T(128...) custom-call(bf16[144,768]{1,0:T(8,128)(2,1)S(1)} %combine.9.held_ref, ...), custom_call_target="tpu_custom_call" | custom-call | tf_op jit(solution)/shard_map/finish/pallas_call | solution.py:817
  (46 shorter events, 1.0 us)
Async XLA Ops:
  0.6 4.7 %copy-start.2 = (bf16[768,384]{1,0:T(8,128)(2,1)S(1)}, bf16[768,384]{1,0:T(8,128)(2,1)}, u32[]{:S(2)}) copy-start(bf16[768,384]{1,0:T(8,128)(2,1)} %refs_11_.3) | copy-start | bytes 1769476
  0.7 4.0 %collective-permute-start = (bf16[512,768]{1,0:T(8,128)(2,1)}, bf16[512,768]{1,0:T(8,128)(2,1)S(1)}, u32[]{:S(2)}, u32[]{:S(2)}) collective-permute-start(bf16[512,768]{1,0:T(8,128)(2,1)} %x_ref.3), channel_id=1, source_target_pairs={{0,1},{1,0},{2,3},{3,2},{4,5},{5,4},{6,7},{7,6},{8,9},{9,8},{10,11... | collective-permute-start | bytes 2359304 | tf_op jit(solution)/shard_map/ppermute | solution.py:828
  4.7 12.3 %collective-permute-start.3 = (bf16[768,1536]{1,0:T(8,128)(2,1)}, bf16[768,1536]{1,0:T(8,128)(2,1)S(1)}, u32[]{:S(2)}, u32[]{:S(2)}) collective-permute-start(bf16[768,1536]{1,0:T(8,128)(2,1)} %w1_hbm.1), channel_id=1, source_target_pairs={{0,1},{1,0},{2,3},{3,2},{4,5},{5,4},{6,7},{7,6},{8,9},{9,8},{10,11... | collective-permute-start | bytes 7077896 | tf_op jit(solution)/shard_map/ppermute | solution.py:828
  4.9 12.2 %collective-permute-start.4 = (bf16[1536,768]{1,0:T(8,128)(2,1)}, bf16[1536,768]{1,0:T(8,128)(2,1)S(1)}, u32[]{:S(2)}, u32[]{:S(2)}) collective-permute-start(bf16[1536,768]{1,0:T(8,128)(2,1)} %w2_hbm.1), channel_id=1, source_target_pairs={{0,1},{1,0},{2,3},{3,2},{4,5},{5,4},{6,7},{7,6},{8,9},{9,8},{10,11... | collective-permute-start | bytes 7077896 | tf_op jit(solution)/shard_map/ppermute | solution.py:828
  5.3 11.7 %collective-permute-start.2 = (bf16[384,768]{1,0:T(8,128)(2,1)S(1)}, bf16[384,768]{1,0:T(8,128)(2,1)S(1)}, u32[]{:S(2)}, u32[]{:S(2)}) collective-permute-start(bf16[384,768]{1,0:T(8,128)(2,1)S(1)} %copy-done.5), channel_id=1, source_target_pairs={{0,1},{1,0},{2,3},{3,2},{4,5},{5,4},{6,7},{7,6},{8,9},{9,8},{10,11... | collective-permute-start | bytes 1769480 | tf_op jit(solution)/shard_map/ppermute | solution.py:828
  10.4 6.7 %collective-permute-start.1 = (bf16[512,384]{1,0:T(8,128)(2,1)S(1)}, bf16[512,384]{1,0:T(8,128)(2,1)S(1)}, u32[]{:S(2)}, u32[]{:S(2)}) collective-permute-start(bf16[512,384]{1,0:T(8,128)(2,1)S(1)} %get-tuple-element.105.send_ref), channel_id=1, source_target_pairs={{0,1},{1,0},{2,3},{3,2},{4,5},{5,4},{6,7},{7,6},{8,9},{9,8},{10,11... | collective-permute-start | bytes 1179656 | tf_op jit(solution)/shard_map/ppermute | solution.py:828
  12.1 4.9 %copy-start.3 = (bf16[512,768]{1,0:T(8,128)(2,1)S(1)}, bf16[512,768]{1,0:T(8,128)(2,1)}, u32[]{:S(2)}) copy-start(bf16[512,768]{1,0:T(8,128)(2,1)} %x_ref.3) | copy-start | bytes 2359300
  12.1 5.0 %copy-start.4 = (bf16[512,768]{1,0:T(8,128)(2,1)S(1)}, bf16[512,768]{1,0:T(8,128)(2,1)}, u32[]{:S(2)}) copy-start(bf16[512,768]{1,0:T(8,128)(2,1)} %up_ref.1) | copy-start | bytes 2359300
  12.1 5.0 %copy-start.6 = (bf16[768]{0:T(1024)(128)(2,1)S(1)}, bf16[768]{0:T(1024)(128)(2,1)}, u32[]{:S(2)}) copy-start(bf16[768]{0:T(1024)(128)(2,1)} %mub_ref.1) | copy-start | bytes 4612
  12.2 5.0 %copy-start.7 = (bf16[768]{0:T(1024)(128)(2,1)S(1)}, bf16[768]{0:T(1024)(128)(2,1)}, u32[]{:S(2)}) copy-start(bf16[768]{0:T(1024)(128)(2,1)} %dub_ref.1) | copy-start | bytes 4612
  12.2 5.0 %copy-start.8 = (bf16[768]{0:T(1024)(128)(2,1)S(1)}, bf16[768]{0:T(1024)(128)(2,1)}, u32[]{:S(2)}) copy-start(bf16[768]{0:T(1024)(128)(2,1)} %fg_ref.1) | copy-start | bytes 4612
  12.2 5.0 %copy-start.9 = (bf16[768]{0:T(1024)(128)(2,1)S(1)}, bf16[768]{0:T(1024)(128)(2,1)}, u32[]{:S(2)}) copy-start(bf16[768]{0:T(1024)(128)(2,1)} %fs_ref.1) | copy-start | bytes 4612
  12.2 5.0 %copy-start.10 = (bf16[768]{0:T(1024)(128)(2,1)S(1)}, bf16[768]{0:T(1024)(128)(2,1)}, u32[]{:S(2)}) copy-start(bf16[768]{0:T(1024)(128)(2,1)} %sg_ref.1) | copy-start | bytes 4612
  12.2 5.0 %copy-start.11 = (bf16[768]{0:T(1024)(128)(2,1)S(1)}, bf16[768]{0:T(1024)(128)(2,1)}, u32[]{:S(2)}) copy-start(bf16[768]{0:T(1024)(128)(2,1)} %ss_ref.1) | copy-start | bytes 4612
  12.2 5.0 %copy-start.12 = (bf16[64]{0:T(256)(128)(2,1)S(1)}, bf16[64]{0:T(256)(128)(2,1)}, u32[]{:S(2)}) copy-start(bf16[64]{0:T(256)(128)(2,1)} %mdb_ref.1) | copy-start | bytes 388
  12.2 5.0 %copy-start.13 = (bf16[64]{0:T(256)(128)(2,1)S(1)}, bf16[64]{0:T(256)(128)(2,1)}, u32[]{:S(2)}) copy-start(bf16[64]{0:T(256)(128)(2,1)} %ddb_ref.1) | copy-start | bytes 388
  34.5 1.5 %collective-permute-start.5 = (bf16[144,768]{1,0:T(8,128)(2,1)S(1)}, bf16[144,768]{1,0:T(8,128)(2,1)S(1)}, u32[]{:S(2)}, u32[]{:S(2)}) collective-permute-start(bf16[144,768]{1,0:T(8,128)(2,1)S(1)} %get-tuple-element.119), channel_id=1, source_target_pairs={{0,1},{1,0},{2,3},{3,2},{4,5},{5,4},{6,7},{7,6},{8,9},{9,8},{10,11... | collective-permute-start | bytes 663560 | tf_op jit(solution)/shard_map/ppermute | solution.py:828
  36.1 2.7 %collective-permute-start.6 = (bf16[512,384]{1,0:T(8,128)(2,1)S(1)}, bf16[512,384]{1,0:T(8,128)(2,1)S(1)}, u32[]{:S(2)}, u32[]{:S(2)}) collective-permute-start(bf16[512,384]{1,0:T(8,128)(2,1)S(1)} %get-tuple-element.122), channel_id=1, source_target_pairs={{0,1},{1,0},{2,3},{3,2},{4,5},{5,4},{6,7},{7,6},{8,9},{9,8},{10,11... | collective-permute-start | bytes 1179656 | tf_op jit(solution)/shard_map/ppermute | solution.py:828
  36.3 9.2 %collective-permute-start.7 = (bf16[144,768]{1,0:T(8,128)(2,1)S(1)}, bf16[144,768]{1,0:T(8,128)(2,1)S(1)}, u32[]{:S(2)}, u32[]{:S(2)}) collective-permute-start(bf16[144,768]{1,0:T(8,128)(2,1)S(1)} %combine.5.held_ref), channel_id=1, source_target_pairs={{0,16},{1,5},{2,18},{3,7},{4,20},{5,1},{6,22},{7,3},{8,24},{9,13},... | collective-permute-start | bytes 663560 | tf_op jit(solution)/shard_map/ppermute | solution.py:889
  45.6 6.0 %collective-permute-start.8 = (bf16[144,768]{1,0:T(8,128)(2,1)S(1)}, bf16[144,768]{1,0:T(8,128)(2,1)S(1)}, u32[]{:S(2)}, u32[]{:S(2)}) collective-permute-start(bf16[144,768]{1,0:T(8,128)(2,1)S(1)} %combine.6.held_ref), channel_id=1, source_target_pairs={{0,8},{1,3},{2,10},{3,1},{4,12},{5,7},{6,14},{7,5},{8,0},{9,11},{1... | collective-permute-start | bytes 663560 | tf_op jit(solution)/shard_map/ppermute | solution.py:889
  51.7 7.6 %collective-permute-start.9 = (bf16[144,768]{1,0:T(8,128)(2,1)S(1)}, bf16[144,768]{1,0:T(8,128)(2,1)S(1)}, u32[]{:S(2)}, u32[]{:S(2)}) collective-permute-start(bf16[144,768]{1,0:T(8,128)(2,1)S(1)} %combine.7.held_ref), channel_id=1, source_target_pairs={{0,4},{1,17},{2,6},{3,19},{4,0},{5,21},{6,2},{7,23},{8,12},{9,25},... | collective-permute-start | bytes 663560 | tf_op jit(solution)/shard_map/ppermute | solution.py:889
  60.5 2.4 %collective-permute-start.11 = (bf16[512,768]{1,0:T(8,128)(2,1)S(1)}, bf16[512,768]{1,0:T(8,128)(2,1)S(1)}, u32[]{:S(2)}, u32[]{:S(2)}) collective-permute-start(bf16[512,768]{1,0:T(8,128)(2,1)S(1)} %away.1), channel_id=1, source_target_pairs={{0,1},{1,0},{2,3},{3,2},{4,5},{5,4},{6,7},{7,6},{8,9},{9,8},{10,11... | collective-permute-start | bytes 2359304 | tf_op jit(solution)/shard_map/ppermute | solution.py:828
  60.6 6.0 %collective-permute-start.10 = (bf16[144,768]{1,0:T(8,128)(2,1)S(1)}, bf16[144,768]{1,0:T(8,128)(2,1)S(1)}, u32[]{:S(2)}, u32[]{:S(2)}) collective-permute-start(bf16[144,768]{1,0:T(8,128)(2,1)S(1)} %combine.8.held_ref), channel_id=1, source_target_pairs={{0,2},{1,9},{2,0},{3,11},{4,6},{5,13},{6,4},{7,15},{8,10},{9,1},{1... | collective-permute-start | bytes 663560 | tf_op jit(solution)/shard_map/ppermute | solution.py:889
  66.7 1.5 %collective-permute-start.12 = (bf16[144,768]{1,0:T(8,128)(2,1)S(1)}, bf16[144,768]{1,0:T(8,128)(2,1)S(1)}, u32[]{:S(2)}, u32[]{:S(2)}) collective-permute-start(bf16[144,768]{1,0:T(8,128)(2,1)S(1)} %combine.9.held_ref), channel_id=1, source_target_pairs={{0,1},{1,0},{2,3},{3,2},{4,5},{5,4},{6,7},{7,6},{8,9},{9,8},{10,11... | collective-permute-start | bytes 663560 | tf_op jit(solution)/shard_map/ppermute | solution.py:828
  (3 other events, 14.1 us)

commit v11 on v10

--- a/solution.py
+++ b/solution.py
@@ -373,49 +373,30 @@
     )(rng, kv, queries, keep, send, own, other, *per_half)
 
 
-def input_part(flip, pieces, weights, half):
-    which = 1 - lax.axis_index("mp") if flip else lax.axis_index("mp")
-    rows = aligned(which, half)
-    left = jnp.concatenate([piece[rows, :] for piece in pieces], 1)
-    right = jnp.concatenate([weight[...] for weight in weights], 1)
-    return dot_nt(left, right)
-
-
-def away_kernel(*refs):
-    out_ref = refs[-1]
-    out_ref[...] = input_part(True, refs[:-4], refs[-4:-1], out_ref.shape[0]).astype(BF16)
-
-
-def home_kernel(first_ref, got_ref, *refs):
-    *pieces, wq_ref, wk_ref, wv_ref, out_hbm, out_ref, sems = refs
-    half = out_ref.shape[0]
-    parts = 2
-    size = half // parts
+def input_kernel(first_ref, *refs):
+    *pieces, wq_ref, wk_ref, wv_ref, away_ref, home_ref = refs
+    half = home_ref.shape[0]
     right = jnp.concatenate([wq_ref[...], wk_ref[...], wv_ref[...]], 1)
-    copies = []
-    for t in range(parts):
-        part = slice(t * size, (t + 1) * size)
-        rows = aligned(lax.axis_index("mp") * parts + t, size)
-        total = dot_nt(jnp.concatenate([piece[rows, :] for piece in pieces], 1), right)
-        out_ref[part, :] = (total + first_ref[part, :] + got_ref[part, :].astype(F32)).astype(BF16)
-        copies.append(pltpu.make_async_copy(out_ref.at[part, :], out_hbm.at[part, :], sems.at[t]))
-        copies[-1].start()
-    for copy in copies:
-        copy.wait()
-
-
-def input_call(kernel, extra, pieces, weights, name):
-    half, features = pieces[0].shape[0] // 2, weights[0].shape[0]
+
+    def part(which):
+        rows = aligned(which, half)
+        return dot_nt(jnp.concatenate([piece[rows, :] for piece in pieces], 1), right)
+
+    away_ref[...] = part(1 - lax.axis_index("mp")).astype(BF16)
+    home_ref[...] = part(lax.axis_index("mp")) + first_ref[...]
+
+
+def input_parts(first_grad, pieces, weights):
+    half, features = first_grad.shape
     return pl.pallas_call(
-        kernel,
-        out_shape=jax.ShapeDtypeStruct((half, features), BF16),
-        in_specs=[VM] * (len(extra) + len(pieces) + len(weights)),
-        out_specs=HB if extra else VM,
-        scratch_shapes=[pltpu.VMEM((half, features), BF16), pltpu.SemaphoreType.DMA((2,))] if extra else [],
+        input_kernel,
+        out_shape=(jax.ShapeDtypeStruct((half, features), BF16), jax.ShapeDtypeStruct((half, features), F32)),
+        in_specs=[VM] * (1 + len(pieces) + len(weights)),
+        out_specs=(VM,) * 2,
         compiler_params=pltpu.CompilerParams(vmem_limit_bytes=16 * MIB),
-        cost_estimate=pl.CostEstimate(flops=10**9, bytes_accessed=6 * MIB, transcendentals=0),
-        name=name,
-    )(*extra, *pieces, *weights)
+        cost_estimate=pl.CostEstimate(flops=2 * 10**9, bytes_accessed=8 * MIB, transcendentals=0),
+        name="input_parts",
+    )(first_grad, *pieces, *weights)
 
 
 def gelu_both(v):
@@ -781,9 +762,19 @@
     )(held, got)
 
 
-def finish_kernel(held_ref, got_ref, md_ref, mdb_ref, mu_ref, mub_ref, dd_ref, ddb_ref, du_ref, dub_ref,
-                  fg_ref, fs_ref, sg_ref, ss_ref, ratio_ref):
+def finish_kernel(
+    held_ref, got_ref, home_ref, away_ref,
+    input_hbm, md_ref, mdb_ref, mu_ref, mub_ref, dd_ref, ddb_ref, du_ref, dub_ref, fg_ref, fs_ref, sg_ref, ss_ref, ratio_ref,
+    input_ref, sems,
+):
     adapt = md_ref.shape[0]
+    size = input_ref.shape[0] // 2
+    copies = []
+    for t in range(2):
+        part = slice(t * size, (t + 1) * size)
+        input_ref[part, :] = (home_ref[part, :] + away_ref[part, :].astype(F32)).astype(BF16)
+        copies.append(pltpu.make_async_copy(input_ref.at[part, :], input_hbm.at[part, :], sems.at[t]))
+        copies[-1].start()
 
     def write(first_ref, second_ref):
         md_ref[...] = first_ref[:adapt, :].astype(F32)
@@ -809,19 +800,26 @@
     def _():
         write(got_ref, held_ref)
 
-
-def finish(held, got, adapt):
+    for copy in copies:
+        copy.wait()
+
+
+def finish(held, got, home, away, adapt):
     features = held.shape[1]
     matrix = jax.ShapeDtypeStruct((adapt, features), F32)
     short, vector = jax.ShapeDtypeStruct((adapt,), F32), jax.ShapeDtypeStruct((features,), F32)
     return pl.pallas_call(
         finish_kernel,
-        out_shape=(matrix, short, matrix, vector) * 2 + (vector,) * 4 + (jax.ShapeDtypeStruct((2,), F32),),
-        in_specs=[VM, VM],
-        out_specs=(VM,) * 13,
-        compiler_params=pltpu.CompilerParams(vmem_limit_bytes=4 * MIB),
+        out_shape=(jax.ShapeDtypeStruct(away.shape, BF16),)
+        + (matrix, short, matrix, vector) * 2
+        + (vector,) * 4
+        + (jax.ShapeDtypeStruct((2,), F32),),
+        in_specs=[VM] * 4,
+        out_specs=(HB,) + (VM,) * 13,
+        scratch_shapes=[pltpu.VMEM(away.shape, BF16), pltpu.SemaphoreType.DMA((2,))],
+        compiler_params=pltpu.CompilerParams(vmem_limit_bytes=8 * MIB),
         name="finish",
-    )(held, got)
+    )(held, got, home, away)
 
 
 def swap_cores(value):
@@ -894,11 +892,11 @@
             grads.append(parts)
         elif n == pairs:
             pieces = [grads[p][i] for i in range(3) for p in range(pairs)]
-            away = swap_cores(input_call(away_kernel, (), pieces, weights, "away"))
-            input_grad = input_call(home_kernel, (first_grad, away), pieces, weights, "home")
-            arriving, input_grad = tie(arriving, input_grad)
+            pieces[0], packed = tie(pieces[0], packed)
+            away, home = input_parts(first_grad, pieces, weights)
+            arriving, away, home = tie(arriving, away, home)
         packed = combine(packed, arriving)
-    md, mdb, mu, mub, dd, ddb, du, dub, *rest = finish(packed, swap_cores(packed), adapt)
+    input_grad, md, mdb, mu, mub, dd, ddb, du, dub, *rest = finish(packed, swap_cores(packed), home, swap_cores(away), adapt)
     return (result, input_grad, md.T, mdb, mu, mub, dd.T, ddb, du, dub, *rest)
 
 

time: 69.3 us -> 69.5 us (level)
  starting transfers between devices: 10.6 us -> 11.5 us
    ppermute x4, starting transfers between devices: 7.19 us -> 8.59 us  [per_device(): arriving = lax.ppermute(packed, ('dp', 'mp'), exchange)]
    ppermute x9, waiting for transfers between devices: 3.11 us -> 2.13 us  [swap_cores(): return lax.ppermute(value, 'mp', [(0, 1), (1, 0)])]
    ppermute x4, waiting for transfers between devices: 4.51 us -> 5.28 us  [per_device(): arriving = lax.ppermute(packed, ('dp', 'mp'), exchange)]
    pallas_call x3 -> x2, Pallas kernels: 4.25 us -> 4.1 us  [the longest x1 2.24 us: input_parts(): pl.pallas_call(input_kernel, out_shape=(jax.ShapeDtypeStruct((half, featu...]
  transfers between devices with their start and end apart: 13 -> 13, of which waited for: 6 -> 5; matrix products, arithmetic and copies ran while one was open for 0% -> 0% of each run, Pallas kernels for 44% -> 44%
where the time goes in v11:
time: 69.5 us; the launch traced here: 69.7 us
  Pallas kernels  49.6 us (71%)
  starting transfers between devices  11.5 us (17%)
  waiting for transfers between devices  7.41 us (11%)
  between operations  1.15 us (2%)
    pallas_call x1, Pallas kernels, middle(): pl.pallas_call(middle_kernel, out_shape=(jax.ShapeDtypeStruct((rows, feat...  17.1 us
    pallas_call x3, Pallas kernels, pair_grad(): pl.pallas_call(functools.partial(pair_grad_kernel, p), out_shape=(jax.Sha...  13.8 us
    pallas_call x2, Pallas kernels, attention_call(): pl.pallas_call(kernel, out_shape=tuple((jax.ShapeDtypeStruct(v.shape, v.d...  9.73 us
    ppermute x4, starting transfers between devices, per_device(): arriving = lax.ppermute(packed, ('dp', 'mp'), exchange)  8.59 us
    ppermute x4, waiting for transfers between devices, per_device(): arriving = lax.ppermute(packed, ('dp', 'mp'), exchange)  5.28 us
    pallas_call x1, Pallas kernels, project(): pl.pallas_call(project_kernel, out_shape=(jax.ShapeDtypeStruct((count, 2...  3.51 us
    ppermute x9, starting transfers between devices, swap_cores(): return lax.ppermute(value, 'mp', [(0, 1), (1, 0)])  2.92 us
    pallas_call x1, Pallas kernels, input_parts(): pl.pallas_call(input_kernel, out_shape=(jax.ShapeDtypeStruct((half, featu...  2.24 us
  transfers between devices with their start and end apart: 13, of which 5 were waited for; matrix products, arithmetic and copies ran while one was open for 0% of the time, Pallas kernels for 44%

profile of v11, /device:TPU:0, one launch (start us, length us, event | category | flops | bytes accessed | tf_op | source)
XLA Modules:
  0.0 69.7 jit_solution(729719844170792858)
XLA Ops:
  0.7 0.5 collective-permute-start
  1.2 3.5 %project.1 = (bf16[1024,768]{1,0:T(8,128)(2,1)S(1)}, bf16[3,2048,128]{2,1,0:T(8,128)(2,1)S(1)}, bf16[3,128,2048]{2,1,0:T(8,128)(2,1)S(1)}, bf16[480,1024]{1,0:T(...) custom-call(s32[1,1024]{1,0:T(1,128)} %seg_hbm.1, ...), custom_call_target="tpu_custom_call" | custom-call | flops 905969664 | bytes 5242880 | tf_op jit(solution)/shard_map/project/pallas_call | solution.py:168
  4.9 0.4 collective-permute-start.4
  5.4 5.6 %attention.1 = (bf16[1024,768]{1,0:T(8,128)(2,1)S(1)}, bf16[3,2048,128]{2,1,0:T(8,128)(2,1)S(1)}, bf16[3,128,2048]{2,1,0:T(8,128)(2,1)S(1)}, bf16[480,1024]{1,0:...) custom-call(s32[2,4]{1,0:T(2,128)S(1)} %get-tuple-element.102.rng_re, ...), custom_call_target="tpu_custom_call" | custom-call | flops 5000000000 | bytes 8388608 | tf_op jit(solution)/shard_map/attention/pallas_call | solution.py:285
  11.0 0.4 collective-permute-start.1
  11.5 4.1 %own_attention.1 = (bf16[512,384]{1,0:T(8,128)(2,1)S(1)}, f32[512,384]{1,0:T(8,128)S(1)}, bf16[1024,1024]{1,0:T(8,128)(2,1)S(1)}, bf16[1024,1024]{1,0:T(8,128)(2,1)S(1)}, bf16[1024,1024]{1,0:T(8,128)(2,1)S(1)}) custom-call(s32[2,4]{1,0:T(2,128)S(1)} %get-tuple-element.102.rng_ref, bf16[1024,128]{1,0:T(8,128)(2,1)S(1)} %get-tuple-element.105.item_ref, ...), custom_call_target="tpu_custom_call" | custom-call | flops 5000000000 | bytes 8388608 | tf_op jit(solution)/shard_map/own_attention/pallas_call | solution.py:285
  15.7 17.1 %middle.1 = (bf16[512,768]{1,0:T(8,128)(2,1)}, f32[512,768]{1,0:T(8,128)S(1)}, bf16[512,768]{1,0:T(8,128)(2,1)S(1)}, bf16[144,768]{1,0:T(8,128)(2,1)S(1)}, bf16[144,768]{1,0:T(8,128)(2,1)S(1)}) custom-call(bf16[512,768]{1,0:T(8,128)(2,1)S(1)} %copy-done, bf16[512,384]{1,0:T(8,128)(2,1)S(1)} %get-tuple-element.116.keep_ref, ...), custom_call_target="tpu_custom_call" | custom-call | flops 20000000000 | bytes 16777216 | tf_op jit(solution)/shard_map/middle/pallas_call | solution.py:701
  32.8 0.4 collective-permute-start.5
  33.2 1.0 %spread.1 = (bf16[512,384]{1,0:T(8,128)(2,1)S(1)}, bf16[512,384]{1,0:T(8,128)(2,1)S(1)}) custom-call(bf16[512,768]{1,0:T(8,128)(2,1)S(1)} %get-tuple-element.122.attended_ref, bf16[384,768]{1,0:T(8,128)(2,1)S(1)} %copy-done.2, bf16[384,768]{1,0:T(8,128)(2,1)S(1)} %collective-permute-done.2.wo2_ref), custom_call_target="tpu_custom_call" | custom-call | flops 603979776 | bytes 3145728 | tf_op jit(solution)/shard_map/spread/pallas_call | solution.py:736
  34.2 0.2 collective-permute-done.5.got_ref
  34.4 0.4 collective-permute-start.7
  34.9 5.2 %collective-permute-start.6 = (bf16[144,768]{1,0:T(8,128)(2,1)S(1)}, bf16[144,768]{1,0:T(8,128)(2,1)S(1)}, u32[]{:S(2)}, u32[]{:S(2)}) collective-permute-start(bf16[144,768]{1,0:T(8,128)(2,1)S(1)} %combine.5.held_ref), channel_id=1, source_target_pairs={{0,16},{1,5},{2,18},{3,7},{4,20},{5,1},{6,22},{7,3},{8,24},{9,13},... | collective-permute-start | bytes 663560 | tf_op jit(solution)/shard_map/ppermute | solution.py:887
  40.0 4.6 %pair_grad_0.1 = (bf16[1024,128]{1,0:T(8,128)(2,1)S(1)}, bf16[1024,128]{1,0:T(8,128)(2,1)S(1)}, bf16[1024,128]{1,0:T(8,128)(2,1)S(1)}) custom-call(s32[2,4]{1,0:T(2,128)S(1)} %get-tuple-element.102.rng_ref, bf16[1024,768]{1,0:T(8,128)(2,1)S(1)} %get-tuple-element.112.kv_ref, bf16[3,2048,128]{2,1,0:T(8,128)(2,1)S(1)} %get-tuple-element.129.queries_ref, ...), custom_call_target="tpu_custom_call" | custom-call | flops 4000000000 | bytes 8388608 | tf_op jit(solution)/shard_map/pair_grad_0/pallas_call | solution.py:356
  44.6 1.7 %collective-permute-done.6.got_ref = bf16[144,768]{1,0:T(8,128)(2,1)S(1)} collective-permute-done((bf16[144,768]{1,0:T(8,128)(2,1)S(1)}, bf16[144,768]{1,0:T(8,128)(2,1)S(1)}, u32[]{:S(2)}, u32[]{:S(2)}) %collective-permute-start.6) | collective-permute-done | bytes 221216 | tf_op jit(solution)/shard_map/ppermute | solution.py:887
  46.5 4.6 %pair_grad_1.1 = (bf16[1024,128]{1,0:T(8,128)(2,1)S(1)}, bf16[1024,128]{1,0:T(8,128)(2,1)S(1)}, bf16[1024,128]{1,0:T(8,128)(2,1)S(1)}) custom-call(s32[2,4]{1,0:T(2,128)S(1)} %get-tuple-element.102.rng_ref, bf16[1024,768]{1,0:T(8,128)(2,1)S(1)} %get-tuple-element.112.kv_ref, bf16[3,2048,128]{2,1,0:T(8,128)(2,1)S(1)} %get-tuple-element.129.queries_ref, ...), custom_call_target="tpu_custom_call" | custom-call | flops 4000000000 | bytes 8388608 | tf_op jit(solution)/shard_map/pair_grad_1/pallas_call | solution.py:356
  51.1 1.3 %collective-permute-done.8.got_ref = bf16[144,768]{1,0:T(8,128)(2,1)S(1)} collective-permute-done((bf16[144,768]{1,0:T(8,128)(2,1)S(1)}, bf16[144,768]{1,0:T(8,128)(2,1)S(1)}, u32[]{:S(2)}, u32[]{:S(2)}) %collective-permute-start.8) | collective-permute-done | bytes 221216 | tf_op jit(solution)/shard_map/ppermute | solution.py:887
  52.4 1.9 %collective-permute-start.9 = (bf16[144,768]{1,0:T(8,128)(2,1)S(1)}, bf16[144,768]{1,0:T(8,128)(2,1)S(1)}, u32[]{:S(2)}, u32[]{:S(2)}) collective-permute-start(bf16[144,768]{1,0:T(8,128)(2,1)S(1)} %combine.7.held_ref), channel_id=1, source_target_pairs={{0,4},{1,17},{2,6},{3,19},{4,0},{5,21},{6,2},{7,23},{8,12},{9,25},... | collective-permute-start | bytes 663560 | tf_op jit(solution)/shard_map/ppermute | solution.py:887
  54.4 4.6 %pair_grad_2.1 = (bf16[1024,128]{1,0:T(8,128)(2,1)S(1)}, bf16[1024,128]{1,0:T(8,128)(2,1)S(1)}, bf16[1024,128]{1,0:T(8,128)(2,1)S(1)}) custom-call(s32[2,4]{1,0:T(2,128)S(1)} %get-tuple-element.102.rng_ref, bf16[1024,768]{1,0:T(8,128)(2,1)S(1)} %get-tuple-element.112.kv_ref, bf16[3,2048,128]{2,1,0:T(8,128)(2,1)S(1)} %get-tuple-element.129.queries_ref, ...), custom_call_target="tpu_custom_call" | custom-call | flops 4000000000 | bytes 8388608 | tf_op jit(solution)/shard_map/pair_grad_2/pallas_call | solution.py:356
  59.1 1.4 %collective-permute-start.10 = (bf16[144,768]{1,0:T(8,128)(2,1)S(1)}, bf16[144,768]{1,0:T(8,128)(2,1)S(1)}, u32[]{:S(2)}, u32[]{:S(2)}) collective-permute-start(bf16[144,768]{1,0:T(8,128)(2,1)S(1)} %combine.8.held_ref), channel_id=1, source_target_pairs={{0,2},{1,9},{2,0},{3,11},{4,6},{5,13},{6,4},{7,15},{8,10},{9,1},{1... | collective-permute-start | bytes 663560 | tf_op jit(solution)/shard_map/ppermute | solution.py:887
  60.5 2.2 %input_parts.1 = (bf16[512,768]{1,0:T(8,128)(2,1)S(1)}, f32[512,768]{1,0:T(8,128)S(1)}) custom-call(f32[512,768]{1,0:T(8,128)S(1)} %get-tuple-element.160.first_ref, bf16[1024,128]{1,0:T(8,128)(2,1)S(1)} %get-tuple-element.161.refs_0_, bf16[1024,128]{1,0:T(8,128)(2,1)S(1)} %get-tuple-element.162.refs_1_, bf16[1024,128]{1,0:T(8,128)(2,1)S(1)} %get-tuple-element.163.refs_2_, ...), custom_call_target="tpu_custom_call" | custom-call | flops 2000000000 | bytes 8388608 | tf_op jit(solution)/shard_map/input_parts/pallas_call | solution.py:391
  62.7 2.3 %collective-permute-done.10.got_ref = bf16[144,768]{1,0:T(8,128)(2,1)S(1)} collective-permute-done((bf16[144,768]{1,0:T(8,128)(2,1)S(1)}, bf16[144,768]{1,0:T(8,128)(2,1)S(1)}, u32[]{:S(2)}, u32[]{:S(2)}) %collective-permute-start.10) | collective-permute-done | bytes 221216 | tf_op jit(solution)/shard_map/ppermute | solution.py:887
  65.1 0.6 collective-permute-start.11
  65.7 2.0 %collective-permute-done.11.got_ref = bf16[144,768]{1,0:T(8,128)(2,1)S(1)} collective-permute-done((bf16[144,768]{1,0:T(8,128)(2,1)S(1)}, bf16[144,768]{1,0:T(8,128)(2,1)S(1)}, u32[]{:S(2)}, u32[]{:S(2)}) %collective-permute-start.11) | collective-permute-done | bytes 221216 | tf_op jit(solution)/shard_map/ppermute | solution.py:826
  67.7 1.9 %finish.1 = (bf16[512,768]{1,0:T(8,128)(2,1)}, f32[64,768]{1,0:T(8,128)}, f32[64]{0:T(128)}, f32[64,768]{1,0:T(8,128)}, f32[768]{0:T(1024)}, /*index=5*/f32[64,7...) custom-call(bf16[144,768]{1,0:T(8,128)(2,1)S(1)} %combine.9.held_ref, ...), custom_call_target="tpu_custom_call" | custom-call | tf_op jit(solution)/shard_map/finish/pallas_call | solution.py:811
  (45 shorter events, 0.7 us)
Async XLA Ops:
  0.6 4.7 %copy-start.5 = (bf16[768,384]{1,0:T(8,128)(2,1)S(1)}, bf16[768,384]{1,0:T(8,128)(2,1)}, u32[]{:S(2)}) copy-start(bf16[768,384]{1,0:T(8,128)(2,1)} %refs_11_.1) | copy-start | bytes 1769476
  0.7 4.7 %copy-start.4 = (bf16[768,384]{1,0:T(8,128)(2,1)S(1)}, bf16[768,384]{1,0:T(8,128)(2,1)}, u32[]{:S(2)}) copy-start(bf16[768,384]{1,0:T(8,128)(2,1)} %refs_10_.1) | copy-start | bytes 1769476
  0.7 4.7 %copy-start.3 = (bf16[768,384]{1,0:T(8,128)(2,1)S(1)}, bf16[768,384]{1,0:T(8,128)(2,1)}, u32[]{:S(2)}) copy-start(bf16[768,384]{1,0:T(8,128)(2,1)} %refs_9_.1) | copy-start | bytes 1769476
  0.7 4.6 %copy-start.2 = (bf16[384,768]{1,0:T(8,128)(2,1)S(1)}, bf16[384,768]{1,0:T(8,128)(2,1)}, u32[]{:S(2)}) copy-start(bf16[384,768]{1,0:T(8,128)(2,1)} %wo_ref.3) | copy-start | bytes 1769476
  0.7 4.0 %collective-permute-start = (bf16[512,768]{1,0:T(8,128)(2,1)}, bf16[512,768]{1,0:T(8,128)(2,1)S(1)}, u32[]{:S(2)}, u32[]{:S(2)}) collective-permute-start(bf16[512,768]{1,0:T(8,128)(2,1)} %x_ref.3), channel_id=1, source_target_pairs={{0,1},{1,0},{2,3},{3,2},{4,5},{5,4},{6,7},{7,6},{8,9},{9,8},{10,11... | collective-permute-start | bytes 2359304 | tf_op jit(solution)/shard_map/ppermute | solution.py:826
  4.7 10.9 %collective-permute-start.3 = (bf16[768,1536]{1,0:T(8,128)(2,1)}, bf16[768,1536]{1,0:T(8,128)(2,1)S(1)}, u32[]{:S(2)}, u32[]{:S(2)}) collective-permute-start(bf16[768,1536]{1,0:T(8,128)(2,1)} %w1_hbm.1), channel_id=1, source_target_pairs={{0,1},{1,0},{2,3},{3,2},{4,5},{5,4},{6,7},{7,6},{8,9},{9,8},{10,11... | collective-permute-start | bytes 7077896 | tf_op jit(solution)/shard_map/ppermute | solution.py:826
  4.9 10.8 %collective-permute-start.4 = (bf16[1536,768]{1,0:T(8,128)(2,1)}, bf16[1536,768]{1,0:T(8,128)(2,1)S(1)}, u32[]{:S(2)}, u32[]{:S(2)}) collective-permute-start(bf16[1536,768]{1,0:T(8,128)(2,1)} %w2_hbm.1), channel_id=1, source_target_pairs={{0,1},{1,0},{2,3},{3,2},{4,5},{5,4},{6,7},{7,6},{8,9},{9,8},{10,11... | collective-permute-start | bytes 7077896 | tf_op jit(solution)/shard_map/ppermute | solution.py:826
  5.3 10.3 %collective-permute-start.2 = (bf16[384,768]{1,0:T(8,128)(2,1)S(1)}, bf16[384,768]{1,0:T(8,128)(2,1)S(1)}, u32[]{:S(2)}, u32[]{:S(2)}) collective-permute-start(bf16[384,768]{1,0:T(8,128)(2,1)S(1)} %copy-done.2), channel_id=1, source_target_pairs={{0,1},{1,0},{2,3},{3,2},{4,5},{5,4},{6,7},{7,6},{8,9},{9,8},{10,11... | collective-permute-start | bytes 1769480 | tf_op jit(solution)/shard_map/ppermute | solution.py:826
  11.0 4.5 %collective-permute-start.1 = (bf16[512,384]{1,0:T(8,128)(2,1)S(1)}, bf16[512,384]{1,0:T(8,128)(2,1)S(1)}, u32[]{:S(2)}, u32[]{:S(2)}) collective-permute-start(bf16[512,384]{1,0:T(8,128)(2,1)S(1)} %get-tuple-element.111.send_ref), channel_id=1, source_target_pairs={{0,1},{1,0},{2,3},{3,2},{4,5},{5,4},{6,7},{7,6},{8,9},{9,8},{10,11... | collective-permute-start | bytes 1179656 | tf_op jit(solution)/shard_map/ppermute | solution.py:826
  11.4 4.2 %copy-start.7 = (bf16[768]{0:T(1024)(128)(2,1)S(1)}, bf16[768]{0:T(1024)(128)(2,1)}, u32[]{:S(2)}) copy-start(bf16[768]{0:T(1024)(128)(2,1)} %dub_ref.1) | copy-start | bytes 4612
  11.4 4.3 %copy-start.8 = (bf16[768]{0:T(1024)(128)(2,1)S(1)}, bf16[768]{0:T(1024)(128)(2,1)}, u32[]{:S(2)}) copy-start(bf16[768]{0:T(1024)(128)(2,1)} %fg_ref.1) | copy-start | bytes 4612
  11.4 4.2 %copy-start.9 = (bf16[768]{0:T(1024)(128)(2,1)S(1)}, bf16[768]{0:T(1024)(128)(2,1)}, u32[]{:S(2)}) copy-start(bf16[768]{0:T(1024)(128)(2,1)} %fs_ref.1) | copy-start | bytes 4612
  11.4 4.2 %copy-start.10 = (bf16[768]{0:T(1024)(128)(2,1)S(1)}, bf16[768]{0:T(1024)(128)(2,1)}, u32[]{:S(2)}) copy-start(bf16[768]{0:T(1024)(128)(2,1)} %sg_ref.1) | copy-start | bytes 4612
  11.5 4.2 %copy-start.11 = (bf16[768]{0:T(1024)(128)(2,1)S(1)}, bf16[768]{0:T(1024)(128)(2,1)}, u32[]{:S(2)}) copy-start(bf16[768]{0:T(1024)(128)(2,1)} %ss_ref.1) | copy-start | bytes 4612
  11.5 4.2 %copy-start.12 = (bf16[64]{0:T(256)(128)(2,1)S(1)}, bf16[64]{0:T(256)(128)(2,1)}, u32[]{:S(2)}) copy-start(bf16[64]{0:T(256)(128)(2,1)} %mdb_ref.1) | copy-start | bytes 388
  11.5 4.2 %copy-start.13 = (bf16[64]{0:T(256)(128)(2,1)S(1)}, bf16[64]{0:T(256)(128)(2,1)}, u32[]{:S(2)}) copy-start(bf16[64]{0:T(256)(128)(2,1)} %ddb_ref.1) | copy-start | bytes 388
  32.8 1.5 %collective-permute-start.5 = (bf16[144,768]{1,0:T(8,128)(2,1)S(1)}, bf16[144,768]{1,0:T(8,128)(2,1)S(1)}, u32[]{:S(2)}, u32[]{:S(2)}) collective-permute-start(bf16[144,768]{1,0:T(8,128)(2,1)S(1)} %get-tuple-element.125), channel_id=1, source_target_pairs={{0,1},{1,0},{2,3},{3,2},{4,5},{5,4},{6,7},{7,6},{8,9},{9,8},{10,11... | collective-permute-start | bytes 663560 | tf_op jit(solution)/shard_map/ppermute | solution.py:826
  34.4 5.6 %collective-permute-start.7 = (bf16[512,384]{1,0:T(8,128)(2,1)S(1)}, bf16[512,384]{1,0:T(8,128)(2,1)S(1)}, u32[]{:S(2)}, u32[]{:S(2)}) collective-permute-start(bf16[512,384]{1,0:T(8,128)(2,1)S(1)} %get-tuple-element.131), channel_id=1, source_target_pairs={{0,1},{1,0},{2,3},{3,2},{4,5},{5,4},{6,7},{7,6},{8,9},{9,8},{10,11... | collective-permute-start | bytes 1179656 | tf_op jit(solution)/shard_map/ppermute | solution.py:826
  34.9 11.5 %collective-permute-start.6 = (bf16[144,768]{1,0:T(8,128)(2,1)S(1)}, bf16[144,768]{1,0:T(8,128)(2,1)S(1)}, u32[]{:S(2)}, u32[]{:S(2)}) collective-permute-start(bf16[144,768]{1,0:T(8,128)(2,1)S(1)} %combine.5.held_ref), channel_id=1, source_target_pairs={{0,16},{1,5},{2,18},{3,7},{4,20},{5,1},{6,22},{7,3},{8,24},{9,13},... | collective-permute-start | bytes 663560 | tf_op jit(solution)/shard_map/ppermute | solution.py:887
  46.4 6.0 %collective-permute-start.8 = (bf16[144,768]{1,0:T(8,128)(2,1)S(1)}, bf16[144,768]{1,0:T(8,128)(2,1)S(1)}, u32[]{:S(2)}, u32[]{:S(2)}) collective-permute-start(bf16[144,768]{1,0:T(8,128)(2,1)S(1)} %combine.6.held_ref), channel_id=1, source_target_pairs={{0,8},{1,3},{2,10},{3,1},{4,12},{5,7},{6,14},{7,5},{8,0},{9,11},{1... | collective-permute-start | bytes 663560 | tf_op jit(solution)/shard_map/ppermute | solution.py:887
  52.4 6.5 %collective-permute-start.9 = (bf16[144,768]{1,0:T(8,128)(2,1)S(1)}, bf16[144,768]{1,0:T(8,128)(2,1)S(1)}, u32[]{:S(2)}, u32[]{:S(2)}) collective-permute-start(bf16[144,768]{1,0:T(8,128)(2,1)S(1)} %combine.7.held_ref), channel_id=1, source_target_pairs={{0,4},{1,17},{2,6},{3,19},{4,0},{5,21},{6,2},{7,23},{8,12},{9,25},... | collective-permute-start | bytes 663560 | tf_op jit(solution)/shard_map/ppermute | solution.py:887
  59.1 6.0 %collective-permute-start.10 = (bf16[144,768]{1,0:T(8,128)(2,1)S(1)}, bf16[144,768]{1,0:T(8,128)(2,1)S(1)}, u32[]{:S(2)}, u32[]{:S(2)}) collective-permute-start(bf16[144,768]{1,0:T(8,128)(2,1)S(1)} %combine.8.held_ref), channel_id=1, source_target_pairs={{0,2},{1,9},{2,0},{3,11},{4,6},{5,13},{6,4},{7,15},{8,10},{9,1},{1... | collective-permute-start | bytes 663560 | tf_op jit(solution)/shard_map/ppermute | solution.py:887
  65.1 2.6 %collective-permute-start.12 = (bf16[512,768]{1,0:T(8,128)(2,1)S(1)}, bf16[512,768]{1,0:T(8,128)(2,1)S(1)}, u32[]{:S(2)}, u32[]{:S(2)}) collective-permute-start(bf16[512,768]{1,0:T(8,128)(2,1)S(1)} %get-tuple-element.174), channel_id=1, source_target_pairs={{0,1},{1,0},{2,3},{3,2},{4,5},{5,4},{6,7},{7,6},{8,9},{9,8},{10,11... | collective-permute-start | bytes 2359304 | tf_op jit(solution)/shard_map/ppermute | solution.py:826
  65.1 2.5 %collective-permute-start.11 = (bf16[144,768]{1,0:T(8,128)(2,1)S(1)}, bf16[144,768]{1,0:T(8,128)(2,1)S(1)}, u32[]{:S(2)}, u32[]{:S(2)}) collective-permute-start(bf16[144,768]{1,0:T(8,128)(2,1)S(1)} %combine.9.held_ref), channel_id=1, source_target_pairs={{0,1},{1,0},{2,3},{3,2},{4,5},{5,4},{6,7},{7,6},{8,9},{9,8},{10,11... | collective-permute-start | bytes 663560 | tf_op jit(solution)/shard_map/ppermute | solution.py:826
  (3 other events, 12.7 us)

commit v12 on v11

--- a/solution.py
+++ b/solution.py
@@ -122,6 +122,36 @@
         visit(pl.ds(pl.multiple_of(high * STEP - size, STEP), size), size)
 
 
+def over_keys_coarse(low, high, visit):
+    steps = high - low
+    doubles = jnp.where(steps % 4 == 0, steps // 4, (steps - 2) // 4)
+
+    def double(t, c):
+        visit(pl.ds(pl.multiple_of(low * STEP + t * 2 * BLOCK, STEP), 2 * BLOCK), 2 * BLOCK)
+        return c
+
+    lax.fori_loop(0, doubles, double, 0)
+    start = low + 4 * doubles
+    left = high - start
+
+    @pl.when((left == 2) | (left == 5))
+    def _():
+        visit(pl.ds(pl.multiple_of(start * STEP, STEP), BLOCK), BLOCK)
+
+    @pl.when((left == 3) | (left == 5))
+    def _():
+        size = BLOCK + STEP
+        visit(pl.ds(pl.multiple_of(high * STEP - size, STEP), size), size)
+
+
+def over_keys_fine(low, high, visit):
+    def one(t, c):
+        visit(pl.ds(pl.multiple_of((low + t) * STEP, STEP), STEP), STEP)
+        return c
+
+    lax.fori_loop(0, high - low, one, 0)
+
+
 def is_shift(lane):
     return (lane == 63) | (lane == 95) | (lane == 127)
 
@@ -198,7 +228,7 @@
         both, here = aligned(g, 2 * block), aligned(i, 2 * block)
         low, high = rng_ref[0, g], rng_ref[1, g]
 
-        def mix_all(hide_of):
+        def mix_all(hide_of, walk):
             mix[...] = jnp.zeros(mix.shape, F32)
 
             def visit(span, size):
@@ -213,9 +243,9 @@
                         head = slice((2 * p + a) * TURNED, (2 * p + a + 1) * TURNED)
                         mix[head, :] += dot(turned[head, span], e[:, a * block : (a + 1) * block])
 
-            over_keys(low, high, visit)
-
-        mix_all(lambda p: hide_ref[:, both])
+            walk(low, high, visit)
+
+        mix_all(lambda p: hide_ref[:, both], over_keys_coarse)
         total_rows = [h * TURNED + HEAD_DIM for h in range(2 * pairs)]
         sums = jnp.concatenate([mix[r : r + 8, :] for r in total_rows], 0)
         fine = jnp.where((sums <= LARGEST) & (sums >= SMALLEST), 0.0, 1.0)
@@ -229,7 +259,7 @@
                     s = scores(p, span, both, hide_ref[:, both])
                     peaks[p] = jnp.maximum(peaks[p], jnp.max(s, 0, keepdims=True))
 
-            over_keys(low, high, visit)
+            over_keys_fine(low, high, visit)
             row = lax.broadcasted_iota(jnp.int32, (128, 2 * block), 0)
             hide = hide_ref[:, both].astype(F32)
             for p in range(pairs):
@@ -239,7 +269,7 @@
                 third = peak - first - second
                 parts = jnp.where(row < 64, first, jnp.where(row < 96, second, third))
                 shifted[p] = jnp.where(is_shift(row), -parts, hide).astype(BF16)
-            mix_all(lambda p: shifted[p])
+            mix_all(lambda p: shifted[p], over_keys_fine)
 
         rows = aligned(i, block)
         outs = []

time: 69.5 us -> 69.3 us (level)
  starting transfers between devices: 11.5 us -> 10.8 us
    ppermute x4, starting transfers between devices: 8.59 us -> 7.55 us  [per_device(): arriving = lax.ppermute(packed, ('dp', 'mp'), exchange)]
    pallas_call x3, Pallas kernels: 13.8 us -> 14.6 us  [pair_grad(): pl.pallas_call(functools.partial(pair_grad_kernel, p), out_shape=(jax.Sha...]
  transfers between devices with their start and end apart: 13 -> 13, of which waited for: 5 -> 5; matrix products, arithmetic and copies ran while one was open for 0% -> 0% of each run, Pallas kernels for 44% -> 45%
where the time goes in v12:
time: 69.3 us; the launch traced here: 69.1 us
  Pallas kernels  50 us (72%)
  starting transfers between devices  10.8 us (16%)
  waiting for transfers between devices  7.06 us (10%)
  between operations  1.17 us (2%)
    pallas_call x1, Pallas kernels, middle(): pl.pallas_call(middle_kernel, out_shape=(jax.ShapeDtypeStruct((rows, feat...  17.1 us
    pallas_call x3, Pallas kernels, pair_grad(): pl.pallas_call(functools.partial(pair_grad_kernel, p), out_shape=(jax.Sha...  14.6 us
    pallas_call x2, Pallas kernels, attention_call(): pl.pallas_call(kernel, out_shape=tuple((jax.ShapeDtypeStruct(v.shape, v.d...  9.45 us
    ppermute x4, starting transfers between devices, per_device(): arriving = lax.ppermute(packed, ('dp', 'mp'), exchange)  7.55 us
    ppermute x4, waiting for transfers between devices, per_device(): arriving = lax.ppermute(packed, ('dp', 'mp'), exchange)  4.97 us
    pallas_call x1, Pallas kernels, project(): pl.pallas_call(project_kernel, out_shape=(jax.ShapeDtypeStruct((count, 2...  3.51 us
    ppermute x9, starting transfers between devices, swap_cores(): return lax.ppermute(value, 'mp', [(0, 1), (1, 0)])  3.21 us
    pallas_call x1, Pallas kernels, input_parts(): pl.pallas_call(input_kernel, out_shape=(jax.ShapeDtypeStruct((half, featu...  2.24 us
  transfers between devices with their start and end apart: 13, of which 5 were waited for; matrix products, arithmetic and copies ran while one was open for 0% of the time, Pallas kernels for 45%

profile of v12, /device:TPU:0, one launch (start us, length us, event | category | flops | bytes accessed | tf_op | source)
XLA Modules:
  0.0 69.1 jit_solution(7176510789398780994)
XLA Ops:
  0.7 0.5 collective-permute-start
  1.2 3.5 %project.1 = (bf16[1024,768]{1,0:T(8,128)(2,1)S(1)}, bf16[3,2048,128]{2,1,0:T(8,128)(2,1)S(1)}, bf16[3,128,2048]{2,1,0:T(8,128)(2,1)S(1)}, bf16[480,1024]{1,0:T(...) custom-call(s32[1,1024]{1,0:T(1,128)} %seg_hbm.1, ...), custom_call_target="tpu_custom_call" | custom-call | flops 905969664 | bytes 5242880 | tf_op jit(solution)/shard_map/project/pallas_call | solution.py:198
  4.7 0.1 collective-permute-start.3
  4.9 0.4 collective-permute-start.4
  5.4 5.6 %attention.1 = (bf16[1024,768]{1,0:T(8,128)(2,1)S(1)}, bf16[3,2048,128]{2,1,0:T(8,128)(2,1)S(1)}, bf16[3,128,2048]{2,1,0:T(8,128)(2,1)S(1)}, bf16[480,1024]{1,0:...) custom-call(s32[2,4]{1,0:T(2,128)S(1)} %get-tuple-element.102.rng_re, ...), custom_call_target="tpu_custom_call" | custom-call | flops 5000000000 | bytes 8388608 | tf_op jit(solution)/shard_map/attention/pallas_call | solution.py:315
  11.2 3.8 %own_attention.1 = (bf16[512,384]{1,0:T(8,128)(2,1)S(1)}, f32[512,384]{1,0:T(8,128)S(1)}, bf16[1024,1024]{1,0:T(8,128)(2,1)S(1)}, bf16[1024,1024]{1,0:T(8,128)(2,1)S(1)}, bf16[1024,1024]{1,0:T(8,128)(2,1)S(1)}) custom-call(s32[2,4]{1,0:T(2,128)S(1)} %get-tuple-element.102.rng_ref, bf16[1024,128]{1,0:T(8,128)(2,1)S(1)} %get-tuple-element.105.item_ref, ...), custom_call_target="tpu_custom_call" | custom-call | flops 5000000000 | bytes 8388608 | tf_op jit(solution)/shard_map/own_attention/pallas_call | solution.py:315
  15.2 17.1 %middle.1 = (bf16[512,768]{1,0:T(8,128)(2,1)}, f32[512,768]{1,0:T(8,128)S(1)}, bf16[512,768]{1,0:T(8,128)(2,1)S(1)}, bf16[144,768]{1,0:T(8,128)(2,1)S(1)}, bf16[144,768]{1,0:T(8,128)(2,1)S(1)}) custom-call(bf16[512,768]{1,0:T(8,128)(2,1)S(1)} %copy-done, bf16[512,384]{1,0:T(8,128)(2,1)S(1)} %get-tuple-element.116.keep_ref, ...), custom_call_target="tpu_custom_call" | custom-call | flops 20000000000 | bytes 16777216 | tf_op jit(solution)/shard_map/middle/pallas_call | solution.py:731
  32.3 0.9 %collective-permute-start.5 = (bf16[144,768]{1,0:T(8,128)(2,1)S(1)}, bf16[144,768]{1,0:T(8,128)(2,1)S(1)}, u32[]{:S(2)}, u32[]{:S(2)}) collective-permute-start(bf16[144,768]{1,0:T(8,128)(2,1)S(1)} %get-tuple-element.125), channel_id=1, source_target_pairs={{0,1},{1,0},{2,3},{3,2},{4,5},{5,4},{6,7},{7,6},{8,9},{9,8},{10,11... | collective-permute-start | bytes 663560 | tf_op jit(solution)/shard_map/ppermute | solution.py:856
  33.3 1.0 %spread.1 = (bf16[512,384]{1,0:T(8,128)(2,1)S(1)}, bf16[512,384]{1,0:T(8,128)(2,1)S(1)}) custom-call(bf16[512,768]{1,0:T(8,128)(2,1)S(1)} %get-tuple-element.122.attended_ref, bf16[384,768]{1,0:T(8,128)(2,1)S(1)} %copy-done.2, bf16[384,768]{1,0:T(8,128)(2,1)S(1)} %collective-permute-done.2.wo2_ref), custom_call_target="tpu_custom_call" | custom-call | flops 603979776 | bytes 3145728 | tf_op jit(solution)/shard_map/spread/pallas_call | solution.py:766
  34.2 0.1 collective-permute-done.5.got_ref
  34.4 0.4 collective-permute-start.7
  34.9 3.7 %collective-permute-start.6 = (bf16[144,768]{1,0:T(8,128)(2,1)S(1)}, bf16[144,768]{1,0:T(8,128)(2,1)S(1)}, u32[]{:S(2)}, u32[]{:S(2)}) collective-permute-start(bf16[144,768]{1,0:T(8,128)(2,1)S(1)} %combine.5.held_ref), channel_id=1, source_target_pairs={{0,16},{1,5},{2,18},{3,7},{4,20},{5,1},{6,22},{7,3},{8,24},{9,13},... | collective-permute-start | bytes 663560 | tf_op jit(solution)/shard_map/ppermute | solution.py:917
  38.6 4.9 %pair_grad_0.1 = (bf16[1024,128]{1,0:T(8,128)(2,1)S(1)}, bf16[1024,128]{1,0:T(8,128)(2,1)S(1)}, bf16[1024,128]{1,0:T(8,128)(2,1)S(1)}) custom-call(s32[2,4]{1,0:T(2,128)S(1)} %get-tuple-element.102.rng_ref, bf16[1024,768]{1,0:T(8,128)(2,1)S(1)} %get-tuple-element.112.kv_ref, bf16[3,2048,128]{2,1,0:T(8,128)(2,1)S(1)} %get-tuple-element.129.queries_ref, ...), custom_call_target="tpu_custom_call" | custom-call | flops 4000000000 | bytes 8388608 | tf_op jit(solution)/shard_map/pair_grad_0/pallas_call | solution.py:386
  43.4 1.4 %collective-permute-done.6.got_ref = bf16[144,768]{1,0:T(8,128)(2,1)S(1)} collective-permute-done((bf16[144,768]{1,0:T(8,128)(2,1)S(1)}, bf16[144,768]{1,0:T(8,128)(2,1)S(1)}, u32[]{:S(2)}, u32[]{:S(2)}) %collective-permute-start.6) | collective-permute-done | bytes 221216 | tf_op jit(solution)/shard_map/ppermute | solution.py:917
  45.0 4.9 %pair_grad_1.1 = (bf16[1024,128]{1,0:T(8,128)(2,1)S(1)}, bf16[1024,128]{1,0:T(8,128)(2,1)S(1)}, bf16[1024,128]{1,0:T(8,128)(2,1)S(1)}) custom-call(s32[2,4]{1,0:T(2,128)S(1)} %get-tuple-element.102.rng_ref, bf16[1024,768]{1,0:T(8,128)(2,1)S(1)} %get-tuple-element.112.kv_ref, bf16[3,2048,128]{2,1,0:T(8,128)(2,1)S(1)} %get-tuple-element.129.queries_ref, ...), custom_call_target="tpu_custom_call" | custom-call | flops 4000000000 | bytes 8388608 | tf_op jit(solution)/shard_map/pair_grad_1/pallas_call | solution.py:386
  49.9 1.0 %collective-permute-done.8.got_ref = bf16[144,768]{1,0:T(8,128)(2,1)S(1)} collective-permute-done((bf16[144,768]{1,0:T(8,128)(2,1)S(1)}, bf16[144,768]{1,0:T(8,128)(2,1)S(1)}, u32[]{:S(2)}, u32[]{:S(2)}) %collective-permute-start.8) | collective-permute-done | bytes 221216 | tf_op jit(solution)/shard_map/ppermute | solution.py:917
  51.0 2.5 %collective-permute-start.9 = (bf16[144,768]{1,0:T(8,128)(2,1)S(1)}, bf16[144,768]{1,0:T(8,128)(2,1)S(1)}, u32[]{:S(2)}, u32[]{:S(2)}) collective-permute-start(bf16[144,768]{1,0:T(8,128)(2,1)S(1)} %combine.7.held_ref), channel_id=1, source_target_pairs={{0,4},{1,17},{2,6},{3,19},{4,0},{5,21},{6,2},{7,23},{8,12},{9,25},... | collective-permute-start | bytes 663560 | tf_op jit(solution)/shard_map/ppermute | solution.py:917
  53.5 4.9 %pair_grad_2.1 = (bf16[1024,128]{1,0:T(8,128)(2,1)S(1)}, bf16[1024,128]{1,0:T(8,128)(2,1)S(1)}, bf16[1024,128]{1,0:T(8,128)(2,1)S(1)}) custom-call(s32[2,4]{1,0:T(2,128)S(1)} %get-tuple-element.102.rng_ref, bf16[1024,768]{1,0:T(8,128)(2,1)S(1)} %get-tuple-element.112.kv_ref, bf16[3,2048,128]{2,1,0:T(8,128)(2,1)S(1)} %get-tuple-element.129.queries_ref, ...), custom_call_target="tpu_custom_call" | custom-call | flops 4000000000 | bytes 8388608 | tf_op jit(solution)/shard_map/pair_grad_2/pallas_call | solution.py:386
  58.5 1.2 %collective-permute-start.10 = (bf16[144,768]{1,0:T(8,128)(2,1)S(1)}, bf16[144,768]{1,0:T(8,128)(2,1)S(1)}, u32[]{:S(2)}, u32[]{:S(2)}) collective-permute-start(bf16[144,768]{1,0:T(8,128)(2,1)S(1)} %combine.8.held_ref), channel_id=1, source_target_pairs={{0,2},{1,9},{2,0},{3,11},{4,6},{5,13},{6,4},{7,15},{8,10},{9,1},{1... | collective-permute-start | bytes 663560 | tf_op jit(solution)/shard_map/ppermute | solution.py:917
  59.7 2.2 %input_parts.1 = (bf16[512,768]{1,0:T(8,128)(2,1)S(1)}, f32[512,768]{1,0:T(8,128)S(1)}) custom-call(f32[512,768]{1,0:T(8,128)S(1)} %get-tuple-element.160.first_ref, bf16[1024,128]{1,0:T(8,128)(2,1)S(1)} %get-tuple-element.161.refs_0_, bf16[1024,128]{1,0:T(8,128)(2,1)S(1)} %get-tuple-element.162.refs_1_, bf16[1024,128]{1,0:T(8,128)(2,1)S(1)} %get-tuple-element.163.refs_2_, ...), custom_call_target="tpu_custom_call" | custom-call | flops 2000000000 | bytes 8388608 | tf_op jit(solution)/shard_map/input_parts/pallas_call | solution.py:421
  62.0 2.5 %collective-permute-done.10.got_ref = bf16[144,768]{1,0:T(8,128)(2,1)S(1)} collective-permute-done((bf16[144,768]{1,0:T(8,128)(2,1)S(1)}, bf16[144,768]{1,0:T(8,128)(2,1)S(1)}, u32[]{:S(2)}, u32[]{:S(2)}) %collective-permute-start.10) | collective-permute-done | bytes 221216 | tf_op jit(solution)/shard_map/ppermute | solution.py:917
  64.5 0.6 collective-permute-start.11
  65.1 2.0 %collective-permute-done.11.got_ref = bf16[144,768]{1,0:T(8,128)(2,1)S(1)} collective-permute-done((bf16[144,768]{1,0:T(8,128)(2,1)S(1)}, bf16[144,768]{1,0:T(8,128)(2,1)S(1)}, u32[]{:S(2)}, u32[]{:S(2)}) %collective-permute-start.11) | collective-permute-done | bytes 221216 | tf_op jit(solution)/shard_map/ppermute | solution.py:856
  67.1 1.9 %finish.1 = (bf16[512,768]{1,0:T(8,128)(2,1)}, f32[64,768]{1,0:T(8,128)}, f32[64]{0:T(128)}, f32[64,768]{1,0:T(8,128)}, f32[768]{0:T(1024)}, /*index=5*/f32[64,7...) custom-call(bf16[144,768]{1,0:T(8,128)(2,1)S(1)} %combine.9.held_ref, ...), custom_call_target="tpu_custom_call" | custom-call | tf_op jit(solution)/shard_map/finish/pallas_call | solution.py:841
  (45 shorter events, 0.6 us)
Async XLA Ops:
  0.6 4.7 %copy-start.5 = (bf16[768,384]{1,0:T(8,128)(2,1)S(1)}, bf16[768,384]{1,0:T(8,128)(2,1)}, u32[]{:S(2)}) copy-start(bf16[768,384]{1,0:T(8,128)(2,1)} %refs_11_.1) | copy-start | bytes 1769476
  0.7 4.7 %copy-start.4 = (bf16[768,384]{1,0:T(8,128)(2,1)S(1)}, bf16[768,384]{1,0:T(8,128)(2,1)}, u32[]{:S(2)}) copy-start(bf16[768,384]{1,0:T(8,128)(2,1)} %refs_10_.1) | copy-start | bytes 1769476
  0.7 4.7 %copy-start.3 = (bf16[768,384]{1,0:T(8,128)(2,1)S(1)}, bf16[768,384]{1,0:T(8,128)(2,1)}, u32[]{:S(2)}) copy-start(bf16[768,384]{1,0:T(8,128)(2,1)} %refs_9_.1) | copy-start | bytes 1769476
  0.7 4.6 %copy-start.2 = (bf16[384,768]{1,0:T(8,128)(2,1)S(1)}, bf16[384,768]{1,0:T(8,128)(2,1)}, u32[]{:S(2)}) copy-start(bf16[384,768]{1,0:T(8,128)(2,1)} %wo_ref.3) | copy-start | bytes 1769476
  0.7 4.0 %collective-permute-start = (bf16[512,768]{1,0:T(8,128)(2,1)}, bf16[512,768]{1,0:T(8,128)(2,1)S(1)}, u32[]{:S(2)}, u32[]{:S(2)}) collective-permute-start(bf16[512,768]{1,0:T(8,128)(2,1)} %x_ref.3), channel_id=1, source_target_pairs={{0,1},{1,0},{2,3},{3,2},{4,5},{5,4},{6,7},{7,6},{8,9},{9,8},{10,11... | collective-permute-start | bytes 2359304 | tf_op jit(solution)/shard_map/ppermute | solution.py:856
  4.7 10.4 %collective-permute-start.3 = (bf16[768,1536]{1,0:T(8,128)(2,1)}, bf16[768,1536]{1,0:T(8,128)(2,1)S(1)}, u32[]{:S(2)}, u32[]{:S(2)}) collective-permute-start(bf16[768,1536]{1,0:T(8,128)(2,1)} %w1_hbm.1), channel_id=1, source_target_pairs={{0,1},{1,0},{2,3},{3,2},{4,5},{5,4},{6,7},{7,6},{8,9},{9,8},{10,11... | collective-permute-start | bytes 7077896 | tf_op jit(solution)/shard_map/ppermute | solution.py:856
  4.9 10.2 %collective-permute-start.4 = (bf16[1536,768]{1,0:T(8,128)(2,1)}, bf16[1536,768]{1,0:T(8,128)(2,1)S(1)}, u32[]{:S(2)}, u32[]{:S(2)}) collective-permute-start(bf16[1536,768]{1,0:T(8,128)(2,1)} %w2_hbm.1), channel_id=1, source_target_pairs={{0,1},{1,0},{2,3},{3,2},{4,5},{5,4},{6,7},{7,6},{8,9},{9,8},{10,11... | collective-permute-start | bytes 7077896 | tf_op jit(solution)/shard_map/ppermute | solution.py:856
  5.3 9.8 %collective-permute-start.2 = (bf16[384,768]{1,0:T(8,128)(2,1)S(1)}, bf16[384,768]{1,0:T(8,128)(2,1)S(1)}, u32[]{:S(2)}, u32[]{:S(2)}) collective-permute-start(bf16[384,768]{1,0:T(8,128)(2,1)S(1)} %copy-done.2), channel_id=1, source_target_pairs={{0,1},{1,0},{2,3},{3,2},{4,5},{5,4},{6,7},{7,6},{8,9},{9,8},{10,11... | collective-permute-start | bytes 1769480 | tf_op jit(solution)/shard_map/ppermute | solution.py:856
  11.0 4.0 %collective-permute-start.1 = (bf16[512,384]{1,0:T(8,128)(2,1)S(1)}, bf16[512,384]{1,0:T(8,128)(2,1)S(1)}, u32[]{:S(2)}, u32[]{:S(2)}) collective-permute-start(bf16[512,384]{1,0:T(8,128)(2,1)S(1)} %get-tuple-element.111.send_ref), channel_id=1, source_target_pairs={{0,1},{1,0},{2,3},{3,2},{4,5},{5,4},{6,7},{7,6},{8,9},{9,8},{10,11... | collective-permute-start | bytes 1179656 | tf_op jit(solution)/shard_map/ppermute | solution.py:856
  11.1 4.0 %copy-start = (bf16[512,768]{1,0:T(8,128)(2,1)S(1)}, bf16[512,768]{1,0:T(8,128)(2,1)}, u32[]{:S(2)}) copy-start(bf16[512,768]{1,0:T(8,128)(2,1)} %x_ref.3) | copy-start | bytes 2359300
  11.1 4.0 %copy-start.1 = (bf16[512,768]{1,0:T(8,128)(2,1)S(1)}, bf16[512,768]{1,0:T(8,128)(2,1)}, u32[]{:S(2)}) copy-start(bf16[512,768]{1,0:T(8,128)(2,1)} %up_ref.1) | copy-start | bytes 2359300
  11.2 4.0 %copy-start.6 = (bf16[768]{0:T(1024)(128)(2,1)S(1)}, bf16[768]{0:T(1024)(128)(2,1)}, u32[]{:S(2)}) copy-start(bf16[768]{0:T(1024)(128)(2,1)} %mub_ref.1) | copy-start | bytes 4612
  11.2 4.0 %copy-start.7 = (bf16[768]{0:T(1024)(128)(2,1)S(1)}, bf16[768]{0:T(1024)(128)(2,1)}, u32[]{:S(2)}) copy-start(bf16[768]{0:T(1024)(128)(2,1)} %dub_ref.1) | copy-start | bytes 4612
  11.2 4.0 %copy-start.8 = (bf16[768]{0:T(1024)(128)(2,1)S(1)}, bf16[768]{0:T(1024)(128)(2,1)}, u32[]{:S(2)}) copy-start(bf16[768]{0:T(1024)(128)(2,1)} %fg_ref.1) | copy-start | bytes 4612
  11.2 4.0 %copy-start.9 = (bf16[768]{0:T(1024)(128)(2,1)S(1)}, bf16[768]{0:T(1024)(128)(2,1)}, u32[]{:S(2)}) copy-start(bf16[768]{0:T(1024)(128)(2,1)} %fs_ref.1) | copy-start | bytes 4612
  11.2 4.0 %copy-start.10 = (bf16[768]{0:T(1024)(128)(2,1)S(1)}, bf16[768]{0:T(1024)(128)(2,1)}, u32[]{:S(2)}) copy-start(bf16[768]{0:T(1024)(128)(2,1)} %sg_ref.1) | copy-start | bytes 4612
  32.3 2.0 %collective-permute-start.5 = (bf16[144,768]{1,0:T(8,128)(2,1)S(1)}, bf16[144,768]{1,0:T(8,128)(2,1)S(1)}, u32[]{:S(2)}, u32[]{:S(2)}) collective-permute-start(bf16[144,768]{1,0:T(8,128)(2,1)S(1)} %get-tuple-element.125), channel_id=1, source_target_pairs={{0,1},{1,0},{2,3},{3,2},{4,5},{5,4},{6,7},{7,6},{8,9},{9,8},{10,11... | collective-permute-start | bytes 663560 | tf_op jit(solution)/shard_map/ppermute | solution.py:856
  34.4 4.2 %collective-permute-start.7 = (bf16[512,384]{1,0:T(8,128)(2,1)S(1)}, bf16[512,384]{1,0:T(8,128)(2,1)S(1)}, u32[]{:S(2)}, u32[]{:S(2)}) collective-permute-start(bf16[512,384]{1,0:T(8,128)(2,1)S(1)} %get-tuple-element.131), channel_id=1, source_target_pairs={{0,1},{1,0},{2,3},{3,2},{4,5},{5,4},{6,7},{7,6},{8,9},{9,8},{10,11... | collective-permute-start | bytes 1179656 | tf_op jit(solution)/shard_map/ppermute | solution.py:856
  34.9 10.0 %collective-permute-start.6 = (bf16[144,768]{1,0:T(8,128)(2,1)S(1)}, bf16[144,768]{1,0:T(8,128)(2,1)S(1)}, u32[]{:S(2)}, u32[]{:S(2)}) collective-permute-start(bf16[144,768]{1,0:T(8,128)(2,1)S(1)} %combine.5.held_ref), channel_id=1, source_target_pairs={{0,16},{1,5},{2,18},{3,7},{4,20},{5,1},{6,22},{7,3},{8,24},{9,13},... | collective-permute-start | bytes 663560 | tf_op jit(solution)/shard_map/ppermute | solution.py:917
  44.9 6.0 %collective-permute-start.8 = (bf16[144,768]{1,0:T(8,128)(2,1)S(1)}, bf16[144,768]{1,0:T(8,128)(2,1)S(1)}, u32[]{:S(2)}, u32[]{:S(2)}) collective-permute-start(bf16[144,768]{1,0:T(8,128)(2,1)S(1)} %combine.6.held_ref), channel_id=1, source_target_pairs={{0,8},{1,3},{2,10},{3,1},{4,12},{5,7},{6,14},{7,5},{8,0},{9,11},{1... | collective-permute-start | bytes 663560 | tf_op jit(solution)/shard_map/ppermute | solution.py:917
  51.0 7.4 %collective-permute-start.9 = (bf16[144,768]{1,0:T(8,128)(2,1)S(1)}, bf16[144,768]{1,0:T(8,128)(2,1)S(1)}, u32[]{:S(2)}, u32[]{:S(2)}) collective-permute-start(bf16[144,768]{1,0:T(8,128)(2,1)S(1)} %combine.7.held_ref), channel_id=1, source_target_pairs={{0,4},{1,17},{2,6},{3,19},{4,0},{5,21},{6,2},{7,23},{8,12},{9,25},... | collective-permute-start | bytes 663560 | tf_op jit(solution)/shard_map/ppermute | solution.py:917
  58.5 6.0 %collective-permute-start.10 = (bf16[144,768]{1,0:T(8,128)(2,1)S(1)}, bf16[144,768]{1,0:T(8,128)(2,1)S(1)}, u32[]{:S(2)}, u32[]{:S(2)}) collective-permute-start(bf16[144,768]{1,0:T(8,128)(2,1)S(1)} %combine.8.held_ref), channel_id=1, source_target_pairs={{0,2},{1,9},{2,0},{3,11},{4,6},{5,13},{6,4},{7,15},{8,10},{9,1},{1... | collective-permute-start | bytes 663560 | tf_op jit(solution)/shard_map/ppermute | solution.py:917
  64.5 2.6 %collective-permute-start.12 = (bf16[512,768]{1,0:T(8,128)(2,1)S(1)}, bf16[512,768]{1,0:T(8,128)(2,1)S(1)}, u32[]{:S(2)}, u32[]{:S(2)}) collective-permute-start(bf16[512,768]{1,0:T(8,128)(2,1)S(1)} %get-tuple-element.174), channel_id=1, source_target_pairs={{0,1},{1,0},{2,3},{3,2},{4,5},{5,4},{6,7},{7,6},{8,9},{9,8},{10,11... | collective-permute-start | bytes 2359304 | tf_op jit(solution)/shard_map/ppermute | solution.py:856
  64.5 2.5 %collective-permute-start.11 = (bf16[144,768]{1,0:T(8,128)(2,1)S(1)}, bf16[144,768]{1,0:T(8,128)(2,1)S(1)}, u32[]{:S(2)}, u32[]{:S(2)}) collective-permute-start(bf16[144,768]{1,0:T(8,128)(2,1)S(1)} %combine.9.held_ref), channel_id=1, source_target_pairs={{0,1},{1,0},{2,3},{3,2},{4,5},{5,4},{6,7},{7,6},{8,9},{9,8},{10,11... | collective-permute-start | bytes 663560 | tf_op jit(solution)/shard_map/ppermute | solution.py:856
  (3 other events, 11.9 us)

commit v13 on v12

--- a/solution.py
+++ b/solution.py
@@ -107,21 +107,6 @@
             turned_ref[base + HEAD_DIM : base + TURNED, aligned(which, rows)] = ones
 
 
-def over_keys(low, high, visit):
-    odd = (high - low) % 2
-
-    def whole(t, c):
-        visit(pl.ds(pl.multiple_of(low * STEP + t * BLOCK, STEP), BLOCK), BLOCK)
-        return c
-
-    lax.fori_loop(0, (high - low) // 2 - odd, whole, 0)
-
-    @pl.when(odd == 1)
-    def _():
-        size = BLOCK + STEP
-        visit(pl.ds(pl.multiple_of(high * STEP - size, STEP), size), size)
-
-
 def over_keys_coarse(low, high, visit):
     steps = high - low
     doubles = jnp.where(steps % 4 == 0, steps // 4, (steps - 2) // 4)
@@ -371,7 +356,7 @@
                 head = slice(a * HEAD_DIM, (a + 1) * HEAD_DIM)
                 dq[head, :] += dot(turned[head, span], slopes[:, a * block : (a + 1) * block])
 
-        over_keys(rng_ref[0, g], rng_ref[1, g], visit)
+        over_keys_coarse(rng_ref[0, g], rng_ref[1, g], visit)
         dq_ref[rows, :] = (dq[...] * HEAD_DIM**-0.5).astype(BF16).T
         return carry
 

time: 69.3 us -> 68.8 us (level)
  waiting for transfers between devices: 7.06 us -> 5.57 us
  starting transfers between devices: 10.8 us -> 11.8 us
    ppermute x4, waiting for transfers between devices: 4.97 us -> 3.47 us  [per_device(): arriving = lax.ppermute(packed, ('dp', 'mp'), exchange)]
    ppermute x4, starting transfers between devices: 7.55 us -> 8.56 us  [per_device(): arriving = lax.ppermute(packed, ('dp', 'mp'), exchange)]
where the time goes in v13:
time: 68.8 us; the launch traced here: 68.7 us
  Pallas kernels  50.1 us (73%)
  starting transfers between devices  11.8 us (17%)
  waiting for transfers between devices  5.57 us (8%)
  between operations  1.18 us (2%)
    pallas_call x1, Pallas kernels, middle(): pl.pallas_call(middle_kernel, out_shape=(jax.ShapeDtypeStruct((rows, feat...  17.1 us
    pallas_call x3, Pallas kernels, pair_grad(): pl.pallas_call(functools.partial(pair_grad_kernel, p), out_shape=(jax.Sha...  14.6 us
    pallas_call x2, Pallas kernels, attention_call(): pl.pallas_call(kernel, out_shape=tuple((jax.ShapeDtypeStruct(v.shape, v.d...  9.45 us
    ppermute x4, starting transfers between devices, per_device(): arriving = lax.ppermute(packed, ('dp', 'mp'), exchange)  8.56 us
    pallas_call x1, Pallas kernels, project(): pl.pallas_call(project_kernel, out_shape=(jax.ShapeDtypeStruct((count, 2...  3.51 us
    ppermute x4, waiting for transfers between devices, per_device(): arriving = lax.ppermute(packed, ('dp', 'mp'), exchange)  3.47 us
    ppermute x9, starting transfers between devices, swap_cores(): return lax.ppermute(value, 'mp', [(0, 1), (1, 0)])  3.21 us
    pallas_call x1, Pallas kernels, input_parts(): pl.pallas_call(input_kernel, out_shape=(jax.ShapeDtypeStruct((half, featu...  2.24 us
  transfers between devices with their start and end apart: 13, of which 5 were waited for; matrix products, arithmetic and copies ran while one was open for 0% of the time, Pallas kernels for 45%

profile of v13, /device:TPU:0, one launch (start us, length us, event | category | flops | bytes accessed | tf_op | source)
XLA Modules:
  0.0 68.7 jit_solution(6521633962861527913)
XLA Ops:
  0.7 0.5 collective-permute-start
  1.2 3.5 %project.1 = (bf16[1024,768]{1,0:T(8,128)(2,1)S(1)}, bf16[3,2048,128]{2,1,0:T(8,128)(2,1)S(1)}, bf16[3,128,2048]{2,1,0:T(8,128)(2,1)S(1)}, bf16[480,1024]{1,0:T(...) custom-call(s32[1,1024]{1,0:T(1,128)} %seg_hbm.1, ...), custom_call_target="tpu_custom_call" | custom-call | flops 905969664 | bytes 5242880 | tf_op jit(solution)/shard_map/project/pallas_call | solution.py:183
  4.7 0.1 collective-permute-start.3
  4.9 0.4 collective-permute-start.4
  5.4 5.6 %attention.1 = (bf16[1024,768]{1,0:T(8,128)(2,1)S(1)}, bf16[3,2048,128]{2,1,0:T(8,128)(2,1)S(1)}, bf16[3,128,2048]{2,1,0:T(8,128)(2,1)S(1)}, bf16[480,1024]{1,0:...) custom-call(s32[2,4]{1,0:T(2,128)S(1)} %get-tuple-element.102.rng_re, ...), custom_call_target="tpu_custom_call" | custom-call | flops 5000000000 | bytes 8388608 | tf_op jit(solution)/shard_map/attention/pallas_call | solution.py:300
  11.2 3.8 %own_attention.1 = (bf16[512,384]{1,0:T(8,128)(2,1)S(1)}, f32[512,384]{1,0:T(8,128)S(1)}, bf16[1024,1024]{1,0:T(8,128)(2,1)S(1)}, bf16[1024,1024]{1,0:T(8,128)(2,1)S(1)}, bf16[1024,1024]{1,0:T(8,128)(2,1)S(1)}) custom-call(s32[2,4]{1,0:T(2,128)S(1)} %get-tuple-element.102.rng_ref, bf16[1024,128]{1,0:T(8,128)(2,1)S(1)} %get-tuple-element.105.item_ref, ...), custom_call_target="tpu_custom_call" | custom-call | flops 5000000000 | bytes 8388608 | tf_op jit(solution)/shard_map/own_attention/pallas_call | solution.py:300
  15.2 17.1 %middle.1 = (bf16[512,768]{1,0:T(8,128)(2,1)}, f32[512,768]{1,0:T(8,128)S(1)}, bf16[512,768]{1,0:T(8,128)(2,1)S(1)}, bf16[144,768]{1,0:T(8,128)(2,1)S(1)}, bf16[144,768]{1,0:T(8,128)(2,1)S(1)}) custom-call(bf16[512,768]{1,0:T(8,128)(2,1)S(1)} %copy-done, bf16[512,384]{1,0:T(8,128)(2,1)S(1)} %get-tuple-element.116.keep_ref, ...), custom_call_target="tpu_custom_call" | custom-call | flops 20000000000 | bytes 16777216 | tf_op jit(solution)/shard_map/middle/pallas_call | solution.py:716
  32.3 0.9 %collective-permute-start.5 = (bf16[144,768]{1,0:T(8,128)(2,1)S(1)}, bf16[144,768]{1,0:T(8,128)(2,1)S(1)}, u32[]{:S(2)}, u32[]{:S(2)}) collective-permute-start(bf16[144,768]{1,0:T(8,128)(2,1)S(1)} %get-tuple-element.125), channel_id=1, source_target_pairs={{0,1},{1,0},{2,3},{3,2},{4,5},{5,4},{6,7},{7,6},{8,9},{9,8},{10,11... | collective-permute-start | bytes 663560 | tf_op jit(solution)/shard_map/ppermute | solution.py:841
  33.3 1.0 %spread.1 = (bf16[512,384]{1,0:T(8,128)(2,1)S(1)}, bf16[512,384]{1,0:T(8,128)(2,1)S(1)}) custom-call(bf16[512,768]{1,0:T(8,128)(2,1)S(1)} %get-tuple-element.122.attended_ref, bf16[384,768]{1,0:T(8,128)(2,1)S(1)} %copy-done.2, bf16[384,768]{1,0:T(8,128)(2,1)S(1)} %collective-permute-done.2.wo2_ref), custom_call_target="tpu_custom_call" | custom-call | flops 603979776 | bytes 3145728 | tf_op jit(solution)/shard_map/spread/pallas_call | solution.py:751
  34.4 0.4 collective-permute-start.7
  34.9 4.0 %collective-permute-start.6 = (bf16[144,768]{1,0:T(8,128)(2,1)S(1)}, bf16[144,768]{1,0:T(8,128)(2,1)S(1)}, u32[]{:S(2)}, u32[]{:S(2)}) collective-permute-start(bf16[144,768]{1,0:T(8,128)(2,1)S(1)} %combine.5.held_ref), channel_id=1, source_target_pairs={{0,16},{1,5},{2,18},{3,7},{4,20},{5,1},{6,22},{7,3},{8,24},{9,13},... | collective-permute-start | bytes 663560 | tf_op jit(solution)/shard_map/ppermute | solution.py:902
  38.9 4.8 %pair_grad_0.1 = (bf16[1024,128]{1,0:T(8,128)(2,1)S(1)}, bf16[1024,128]{1,0:T(8,128)(2,1)S(1)}, bf16[1024,128]{1,0:T(8,128)(2,1)S(1)}) custom-call(s32[2,4]{1,0:T(2,128)S(1)} %get-tuple-element.102.rng_ref, bf16[1024,768]{1,0:T(8,128)(2,1)S(1)} %get-tuple-element.112.kv_ref, bf16[3,2048,128]{2,1,0:T(8,128)(2,1)S(1)} %get-tuple-element.129.queries_ref, ...), custom_call_target="tpu_custom_call" | custom-call | flops 4000000000 | bytes 8388608 | tf_op jit(solution)/shard_map/pair_grad_0/pallas_call | solution.py:371
  43.7 1.5 %collective-permute-done.6.got_ref = bf16[144,768]{1,0:T(8,128)(2,1)S(1)} collective-permute-done((bf16[144,768]{1,0:T(8,128)(2,1)S(1)}, bf16[144,768]{1,0:T(8,128)(2,1)S(1)}, u32[]{:S(2)}, u32[]{:S(2)}) %collective-permute-start.6) | collective-permute-done | bytes 221216 | tf_op jit(solution)/shard_map/ppermute | solution.py:902
  45.2 1.1 %collective-permute-start.8 = (bf16[144,768]{1,0:T(8,128)(2,1)S(1)}, bf16[144,768]{1,0:T(8,128)(2,1)S(1)}, u32[]{:S(2)}, u32[]{:S(2)}) collective-permute-start(bf16[144,768]{1,0:T(8,128)(2,1)S(1)} %combine.6.held_ref), channel_id=1, source_target_pairs={{0,8},{1,3},{2,10},{3,1},{4,12},{5,7},{6,14},{7,5},{8,0},{9,11},{1... | collective-permute-start | bytes 663560 | tf_op jit(solution)/shard_map/ppermute | solution.py:902
  46.3 4.8 %pair_grad_1.1 = (bf16[1024,128]{1,0:T(8,128)(2,1)S(1)}, bf16[1024,128]{1,0:T(8,128)(2,1)S(1)}, bf16[1024,128]{1,0:T(8,128)(2,1)S(1)}) custom-call(s32[2,4]{1,0:T(2,128)S(1)} %get-tuple-element.102.rng_ref, bf16[1024,768]{1,0:T(8,128)(2,1)S(1)} %get-tuple-element.112.kv_ref, bf16[3,2048,128]{2,1,0:T(8,128)(2,1)S(1)} %get-tuple-element.129.queries_ref, ...), custom_call_target="tpu_custom_call" | custom-call | flops 4000000000 | bytes 8388608 | tf_op jit(solution)/shard_map/pair_grad_1/pallas_call | solution.py:371
  51.1 0.1 collective-permute-done.8.got_ref
  51.3 1.6 %collective-permute-start.9 = (bf16[144,768]{1,0:T(8,128)(2,1)S(1)}, bf16[144,768]{1,0:T(8,128)(2,1)S(1)}, u32[]{:S(2)}, u32[]{:S(2)}) collective-permute-start(bf16[144,768]{1,0:T(8,128)(2,1)S(1)} %combine.7.held_ref), channel_id=1, source_target_pairs={{0,4},{1,17},{2,6},{3,19},{4,0},{5,21},{6,2},{7,23},{8,12},{9,25},... | collective-permute-start | bytes 663560 | tf_op jit(solution)/shard_map/ppermute | solution.py:902
  52.9 5.0 %pair_grad_2.1 = (bf16[1024,128]{1,0:T(8,128)(2,1)S(1)}, bf16[1024,128]{1,0:T(8,128)(2,1)S(1)}, bf16[1024,128]{1,0:T(8,128)(2,1)S(1)}) custom-call(s32[2,4]{1,0:T(2,128)S(1)} %get-tuple-element.102.rng_ref, bf16[1024,768]{1,0:T(8,128)(2,1)S(1)} %get-tuple-element.112.kv_ref, bf16[3,2048,128]{2,1,0:T(8,128)(2,1)S(1)} %get-tuple-element.129.queries_ref, ...), custom_call_target="tpu_custom_call" | custom-call | flops 4000000000 | bytes 8388608 | tf_op jit(solution)/shard_map/pair_grad_2/pallas_call | solution.py:371
  58.0 1.9 %collective-permute-start.10 = (bf16[144,768]{1,0:T(8,128)(2,1)S(1)}, bf16[144,768]{1,0:T(8,128)(2,1)S(1)}, u32[]{:S(2)}, u32[]{:S(2)}) collective-permute-start(bf16[144,768]{1,0:T(8,128)(2,1)S(1)} %combine.8.held_ref), channel_id=1, source_target_pairs={{0,2},{1,9},{2,0},{3,11},{4,6},{5,13},{6,4},{7,15},{8,10},{9,1},{1... | collective-permute-start | bytes 663560 | tf_op jit(solution)/shard_map/ppermute | solution.py:902
  59.9 2.2 %input_parts.1 = (bf16[512,768]{1,0:T(8,128)(2,1)S(1)}, f32[512,768]{1,0:T(8,128)S(1)}) custom-call(f32[512,768]{1,0:T(8,128)S(1)} %get-tuple-element.160.first_ref, bf16[1024,128]{1,0:T(8,128)(2,1)S(1)} %get-tuple-element.161.refs_0_, bf16[1024,128]{1,0:T(8,128)(2,1)S(1)} %get-tuple-element.162.refs_1_, bf16[1024,128]{1,0:T(8,128)(2,1)S(1)} %get-tuple-element.163.refs_2_, ...), custom_call_target="tpu_custom_call" | custom-call | flops 2000000000 | bytes 8388608 | tf_op jit(solution)/shard_map/input_parts/pallas_call | solution.py:406
  62.1 1.9 %collective-permute-done.10.got_ref = bf16[144,768]{1,0:T(8,128)(2,1)S(1)} collective-permute-done((bf16[144,768]{1,0:T(8,128)(2,1)S(1)}, bf16[144,768]{1,0:T(8,128)(2,1)S(1)}, u32[]{:S(2)}, u32[]{:S(2)}) %collective-permute-start.10) | collective-permute-done | bytes 221216 | tf_op jit(solution)/shard_map/ppermute | solution.py:902
  64.1 0.6 collective-permute-start.11
  64.7 2.0 %collective-permute-done.11.got_ref = bf16[144,768]{1,0:T(8,128)(2,1)S(1)} collective-permute-done((bf16[144,768]{1,0:T(8,128)(2,1)S(1)}, bf16[144,768]{1,0:T(8,128)(2,1)S(1)}, u32[]{:S(2)}, u32[]{:S(2)}) %collective-permute-start.11) | collective-permute-done | bytes 221216 | tf_op jit(solution)/shard_map/ppermute | solution.py:841
  66.6 1.9 %finish.1 = (bf16[512,768]{1,0:T(8,128)(2,1)}, f32[64,768]{1,0:T(8,128)}, f32[64]{0:T(128)}, f32[64,768]{1,0:T(8,128)}, f32[768]{0:T(1024)}, /*index=5*/f32[64,7...) custom-call(bf16[144,768]{1,0:T(8,128)(2,1)S(1)} %combine.9.held_ref, ...), custom_call_target="tpu_custom_call" | custom-call | tf_op jit(solution)/shard_map/finish/pallas_call | solution.py:826
  (45 shorter events, 0.7 us)
Async XLA Ops:
  0.6 4.7 %copy-start.5 = (bf16[768,384]{1,0:T(8,128)(2,1)S(1)}, bf16[768,384]{1,0:T(8,128)(2,1)}, u32[]{:S(2)}) copy-start(bf16[768,384]{1,0:T(8,128)(2,1)} %refs_11_.1) | copy-start | bytes 1769476
  0.7 4.7 %copy-start.4 = (bf16[768,384]{1,0:T(8,128)(2,1)S(1)}, bf16[768,384]{1,0:T(8,128)(2,1)}, u32[]{:S(2)}) copy-start(bf16[768,384]{1,0:T(8,128)(2,1)} %refs_10_.1) | copy-start | bytes 1769476
  0.7 4.7 %copy-start.3 = (bf16[768,384]{1,0:T(8,128)(2,1)S(1)}, bf16[768,384]{1,0:T(8,128)(2,1)}, u32[]{:S(2)}) copy-start(bf16[768,384]{1,0:T(8,128)(2,1)} %refs_9_.1) | copy-start | bytes 1769476
  0.7 4.6 %copy-start.2 = (bf16[384,768]{1,0:T(8,128)(2,1)S(1)}, bf16[384,768]{1,0:T(8,128)(2,1)}, u32[]{:S(2)}) copy-start(bf16[384,768]{1,0:T(8,128)(2,1)} %wo_ref.3) | copy-start | bytes 1769476
  0.7 4.0 %collective-permute-start = (bf16[512,768]{1,0:T(8,128)(2,1)}, bf16[512,768]{1,0:T(8,128)(2,1)S(1)}, u32[]{:S(2)}, u32[]{:S(2)}) collective-permute-start(bf16[512,768]{1,0:T(8,128)(2,1)} %x_ref.3), channel_id=1, source_target_pairs={{0,1},{1,0},{2,3},{3,2},{4,5},{5,4},{6,7},{7,6},{8,9},{9,8},{10,11... | collective-permute-start | bytes 2359304 | tf_op jit(solution)/shard_map/ppermute | solution.py:841
  4.7 10.4 %collective-permute-start.3 = (bf16[768,1536]{1,0:T(8,128)(2,1)}, bf16[768,1536]{1,0:T(8,128)(2,1)S(1)}, u32[]{:S(2)}, u32[]{:S(2)}) collective-permute-start(bf16[768,1536]{1,0:T(8,128)(2,1)} %w1_hbm.1), channel_id=1, source_target_pairs={{0,1},{1,0},{2,3},{3,2},{4,5},{5,4},{6,7},{7,6},{8,9},{9,8},{10,11... | collective-permute-start | bytes 7077896 | tf_op jit(solution)/shard_map/ppermute | solution.py:841
  4.9 10.2 %collective-permute-start.4 = (bf16[1536,768]{1,0:T(8,128)(2,1)}, bf16[1536,768]{1,0:T(8,128)(2,1)S(1)}, u32[]{:S(2)}, u32[]{:S(2)}) collective-permute-start(bf16[1536,768]{1,0:T(8,128)(2,1)} %w2_hbm.1), channel_id=1, source_target_pairs={{0,1},{1,0},{2,3},{3,2},{4,5},{5,4},{6,7},{7,6},{8,9},{9,8},{10,11... | collective-permute-start | bytes 7077896 | tf_op jit(solution)/shard_map/ppermute | solution.py:841
  5.3 9.8 %collective-permute-start.2 = (bf16[384,768]{1,0:T(8,128)(2,1)S(1)}, bf16[384,768]{1,0:T(8,128)(2,1)S(1)}, u32[]{:S(2)}, u32[]{:S(2)}) collective-permute-start(bf16[384,768]{1,0:T(8,128)(2,1)S(1)} %copy-done.2), channel_id=1, source_target_pairs={{0,1},{1,0},{2,3},{3,2},{4,5},{5,4},{6,7},{7,6},{8,9},{9,8},{10,11... | collective-permute-start | bytes 1769480 | tf_op jit(solution)/shard_map/ppermute | solution.py:841
  11.0 4.0 %collective-permute-start.1 = (bf16[512,384]{1,0:T(8,128)(2,1)S(1)}, bf16[512,384]{1,0:T(8,128)(2,1)S(1)}, u32[]{:S(2)}, u32[]{:S(2)}) collective-permute-start(bf16[512,384]{1,0:T(8,128)(2,1)S(1)} %get-tuple-element.111.send_ref), channel_id=1, source_target_pairs={{0,1},{1,0},{2,3},{3,2},{4,5},{5,4},{6,7},{7,6},{8,9},{9,8},{10,11... | collective-permute-start | bytes 1179656 | tf_op jit(solution)/shard_map/ppermute | solution.py:841
  11.1 4.0 %copy-start = (bf16[512,768]{1,0:T(8,128)(2,1)S(1)}, bf16[512,768]{1,0:T(8,128)(2,1)}, u32[]{:S(2)}) copy-start(bf16[512,768]{1,0:T(8,128)(2,1)} %x_ref.3) | copy-start | bytes 2359300
  11.1 4.0 %copy-start.1 = (bf16[512,768]{1,0:T(8,128)(2,1)S(1)}, bf16[512,768]{1,0:T(8,128)(2,1)}, u32[]{:S(2)}) copy-start(bf16[512,768]{1,0:T(8,128)(2,1)} %up_ref.1) | copy-start | bytes 2359300
  11.2 4.0 %copy-start.6 = (bf16[768]{0:T(1024)(128)(2,1)S(1)}, bf16[768]{0:T(1024)(128)(2,1)}, u32[]{:S(2)}) copy-start(bf16[768]{0:T(1024)(128)(2,1)} %mub_ref.1) | copy-start | bytes 4612
  11.2 4.0 %copy-start.7 = (bf16[768]{0:T(1024)(128)(2,1)S(1)}, bf16[768]{0:T(1024)(128)(2,1)}, u32[]{:S(2)}) copy-start(bf16[768]{0:T(1024)(128)(2,1)} %dub_ref.1) | copy-start | bytes 4612
  11.2 4.0 %copy-start.8 = (bf16[768]{0:T(1024)(128)(2,1)S(1)}, bf16[768]{0:T(1024)(128)(2,1)}, u32[]{:S(2)}) copy-start(bf16[768]{0:T(1024)(128)(2,1)} %fg_ref.1) | copy-start | bytes 4612
  11.2 4.0 %copy-start.9 = (bf16[768]{0:T(1024)(128)(2,1)S(1)}, bf16[768]{0:T(1024)(128)(2,1)}, u32[]{:S(2)}) copy-start(bf16[768]{0:T(1024)(128)(2,1)} %fs_ref.1) | copy-start | bytes 4612
  11.2 4.0 %copy-start.10 = (bf16[768]{0:T(1024)(128)(2,1)S(1)}, bf16[768]{0:T(1024)(128)(2,1)}, u32[]{:S(2)}) copy-start(bf16[768]{0:T(1024)(128)(2,1)} %sg_ref.1) | copy-start | bytes 4612
  32.3 2.0 %collective-permute-start.5 = (bf16[144,768]{1,0:T(8,128)(2,1)S(1)}, bf16[144,768]{1,0:T(8,128)(2,1)S(1)}, u32[]{:S(2)}, u32[]{:S(2)}) collective-permute-start(bf16[144,768]{1,0:T(8,128)(2,1)S(1)} %get-tuple-element.125), channel_id=1, source_target_pairs={{0,1},{1,0},{2,3},{3,2},{4,5},{5,4},{6,7},{7,6},{8,9},{9,8},{10,11... | collective-permute-start | bytes 663560 | tf_op jit(solution)/shard_map/ppermute | solution.py:841
  34.4 4.5 %collective-permute-start.7 = (bf16[512,384]{1,0:T(8,128)(2,1)S(1)}, bf16[512,384]{1,0:T(8,128)(2,1)S(1)}, u32[]{:S(2)}, u32[]{:S(2)}) collective-permute-start(bf16[512,384]{1,0:T(8,128)(2,1)S(1)} %get-tuple-element.131), channel_id=1, source_target_pairs={{0,1},{1,0},{2,3},{3,2},{4,5},{5,4},{6,7},{7,6},{8,9},{9,8},{10,11... | collective-permute-start | bytes 1179656 | tf_op jit(solution)/shard_map/ppermute | solution.py:841
  34.9 10.3 %collective-permute-start.6 = (bf16[144,768]{1,0:T(8,128)(2,1)S(1)}, bf16[144,768]{1,0:T(8,128)(2,1)S(1)}, u32[]{:S(2)}, u32[]{:S(2)}) collective-permute-start(bf16[144,768]{1,0:T(8,128)(2,1)S(1)} %combine.5.held_ref), channel_id=1, source_target_pairs={{0,16},{1,5},{2,18},{3,7},{4,20},{5,1},{6,22},{7,3},{8,24},{9,13},... | collective-permute-start | bytes 663560 | tf_op jit(solution)/shard_map/ppermute | solution.py:902
  45.2 6.0 %collective-permute-start.8 = (bf16[144,768]{1,0:T(8,128)(2,1)S(1)}, bf16[144,768]{1,0:T(8,128)(2,1)S(1)}, u32[]{:S(2)}, u32[]{:S(2)}) collective-permute-start(bf16[144,768]{1,0:T(8,128)(2,1)S(1)} %combine.6.held_ref), channel_id=1, source_target_pairs={{0,8},{1,3},{2,10},{3,1},{4,12},{5,7},{6,14},{7,5},{8,0},{9,11},{1... | collective-permute-start | bytes 663560 | tf_op jit(solution)/shard_map/ppermute | solution.py:902
  51.3 6.6 %collective-permute-start.9 = (bf16[144,768]{1,0:T(8,128)(2,1)S(1)}, bf16[144,768]{1,0:T(8,128)(2,1)S(1)}, u32[]{:S(2)}, u32[]{:S(2)}) collective-permute-start(bf16[144,768]{1,0:T(8,128)(2,1)S(1)} %combine.7.held_ref), channel_id=1, source_target_pairs={{0,4},{1,17},{2,6},{3,19},{4,0},{5,21},{6,2},{7,23},{8,12},{9,25},... | collective-permute-start | bytes 663560 | tf_op jit(solution)/shard_map/ppermute | solution.py:902
  58.0 6.0 %collective-permute-start.10 = (bf16[144,768]{1,0:T(8,128)(2,1)S(1)}, bf16[144,768]{1,0:T(8,128)(2,1)S(1)}, u32[]{:S(2)}, u32[]{:S(2)}) collective-permute-start(bf16[144,768]{1,0:T(8,128)(2,1)S(1)} %combine.8.held_ref), channel_id=1, source_target_pairs={{0,2},{1,9},{2,0},{3,11},{4,6},{5,13},{6,4},{7,15},{8,10},{9,1},{1... | collective-permute-start | bytes 663560 | tf_op jit(solution)/shard_map/ppermute | solution.py:902
  64.0 2.6 %collective-permute-start.12 = (bf16[512,768]{1,0:T(8,128)(2,1)S(1)}, bf16[512,768]{1,0:T(8,128)(2,1)S(1)}, u32[]{:S(2)}, u32[]{:S(2)}) collective-permute-start(bf16[512,768]{1,0:T(8,128)(2,1)S(1)} %get-tuple-element.174), channel_id=1, source_target_pairs={{0,1},{1,0},{2,3},{3,2},{4,5},{5,4},{6,7},{7,6},{8,9},{9,8},{10,11... | collective-permute-start | bytes 2359304 | tf_op jit(solution)/shard_map/ppermute | solution.py:841
  64.1 2.5 %collective-permute-start.11 = (bf16[144,768]{1,0:T(8,128)(2,1)S(1)}, bf16[144,768]{1,0:T(8,128)(2,1)S(1)}, u32[]{:S(2)}, u32[]{:S(2)}) collective-permute-start(bf16[144,768]{1,0:T(8,128)(2,1)S(1)} %combine.9.held_ref), channel_id=1, source_target_pairs={{0,1},{1,0},{2,3},{3,2},{4,5},{5,4},{6,7},{7,6},{8,9},{9,8},{10,11... | collective-permute-start | bytes 663560 | tf_op jit(solution)/shard_map/ppermute | solution.py:841
  (3 other events, 11.9 us)
